TPU v7x, 32 devices: a whole 2x2x4 slice. The times are simulated.
32 devices in a mesh: fsdp: 2 (over x), ctx: 4 (over y, core), tp: 4 (over z).
Axes of the slice: x: 2, y: 2, z: 4, core: 2. Of those that a mesh axis runs over, the one named last changes fastest.
Arguments:
- hidden_in: bfloat16 [2, 2, 512, 1536], P(None, 'fsdp', 'ctx'), may hold values from -6 to 6
- parents: int32 [2, 2, 4], P(None, 'fsdp'), may hold values from 0 to 2, as said below
- routes: int32 [2, 2, 512, 8], P(None, 'fsdp', 'ctx'), may hold values from 0 to 39, all different within a row; in each aligned block of 128 rows (0 to 127, 128 to 255, ..., all dimensions but the last counted through in order) at most 32 rows name the same one
- attn_gain: bfloat16 [1536], P('fsdp'), may hold values from 0.5 to 1.5
- w_query: bfloat16 [1536, 1536], P('fsdp', 'tp'), may hold values from -0.625 to 0.625
- key_projection: bfloat16 [1536, 512], P('fsdp', 'tp'), may hold values from -0.625 to 0.625
- value_projection: bfloat16 [1536, 512], P('fsdp', 'tp'), may hold values from -0.15625 to 0.15625
- w_out: bfloat16 [1536, 1536], P('tp', 'fsdp'), may hold values from -2 to 2
- moe_gain: bfloat16 [1536], P('fsdp'), may hold values from 0.5 to 1.5
- w_router: bfloat16 [1536, 40], P('fsdp'), may hold values from -0.078125 to 0.078125
- w_gate_up: bfloat16 [40, 1536, 2, 512], P(None, 'fsdp', None, 'tp'), may hold values from -0.15625 to 0.15625
- w_down: bfloat16 [40, 512, 1536], P(None, 'tp', 'fsdp'), may hold values from -4 to 4
- d_out: bfloat16 [2, 2, 512, 1536], P(None, 'fsdp', 'ctx'), may hold values from -6 to 6
Outputs:
- layer_out: float32 [2, 2, 512, 1536], P(None, 'fsdp', 'ctx')
- d_hidden: float32 [2, 2, 512, 1536], P(None, 'fsdp', 'ctx')
- d_attn_gain: float32 [1536], P('fsdp')
- d_w_query: float32 [1536, 1536], P('fsdp', 'tp')
- d_w_key: float32 [1536, 512], P('fsdp', 'tp')
- d_w_value: float32 [1536, 512], P('fsdp', 'tp')
- d_w_out: float32 [1536, 1536], P('tp', 'fsdp')
- d_moe_gain: float32 [1536], P('fsdp')
- d_w_router: float32 [1536, 40], P('fsdp')
- d_w_gate_up: float32 [40, 1536, 2, 512], P(None, 'fsdp', None, 'tp')
- d_w_down: float32 [40, 512, 1536], P(None, 'tp', 'fsdp')
Inputs may be any that keep to these rules, and one draw needn't show every extreme that they name: `parents`: segment 0 of each tree is its root (its own parent); every other segment's parent is a lower segment; the last segment's parent is the segment before it. `routes`: each token names 8 different experts; within each aligned block of 128 rows (one device's tokens of one micro-batch) no expert is named by more than 32 rows, and in some blocks one is named by exactly 32.
All inputs are finite; a program needn't handle non-finite values.
Results may differ from a plain program's by a relative error of at most 0.025.
Values may be sent and summed in bfloat16 or wider, within the bound.
No kernel may reach another device: no remote copies, remote signals or barrier semaphores. Data moves between devices by JAX's collectives and lax.ppermute only.
A program may use at most 320 MiB of HBM per device.

v0:
```python
import jax
import jax.numpy as jnp
from jax import lax
from jax.sharding import PartitionSpec as P

HEAD_DIM = 64
CAP = 32


EPSILON = 1e-06
RESIDUAL_SCALE = 0.22
SCORE_SCALE = 1.0 / 64.0
ROPE_BASE = 10000.0
TOP_PRECISION = lax.Precision.HIGHEST


def tree_tables(parent_row, tree_len):
    seg_total = parent_row.shape[0]
    seg_len = tree_len // seg_total
    seg_ids = jnp.arange(seg_total, dtype=jnp.int32)
    parent_links = (parent_row[:, None] == seg_ids[None, :]).astype(jnp.float32)
    reach_table = jnp.maximum(parent_links, jnp.eye(seg_total, dtype=jnp.float32))
    for squaring in range(max(seg_total - 1, 1).bit_length()):
        reach_table = jnp.minimum(jnp.dot(reach_table, reach_table, precision=TOP_PRECISION), 1.0)
    seg_depth = jnp.sum(reach_table, axis=1) - 1.0
    token_ids = jnp.arange(tree_len, dtype=jnp.int32)
    tok_owner = ((token_ids // seg_len)[:, None] == seg_ids[None, :]).astype(jnp.float32)
    tok_offset = (token_ids % seg_len).astype(jnp.float32)
    places = jnp.dot(tok_owner, seg_depth, precision=TOP_PRECISION) * seg_len + tok_offset
    return (places, jnp.dot(tok_owner, reach_table, precision=TOP_PRECISION), tok_owner)


def rope_tables(places):
    half_dim = HEAD_DIM // 2
    inverse = ROPE_BASE ** (-jnp.arange(half_dim, dtype=jnp.float32) * 2.0 / HEAD_DIM)
    angles = places[:, None] * inverse[None, :]
    cosine_table = jnp.concatenate([jnp.cos(angles), jnp.cos(angles)], axis=1)
    sine_values = jnp.concatenate([jnp.sin(angles), jnp.sin(angles)], axis=1)
    return (cosine_table, sine_values)


def apply_rotary(values, cosine_table, sine_values):
    half_dim = values.shape[-1] // 2
    turned = jnp.concatenate([-values[..., half_dim:], values[..., :half_dim]], axis=-1)
    return values * cosine_table[:, None, :] + turned * sine_values[:, None, :]


def norm_scale(values):
    return lax.rsqrt(jnp.mean(values * values, axis=-1, keepdims=True) + EPSILON)


def add_tuples(first_tuple, second_tuple):
    return tuple(
        (left_part + right_part for left_part, right_part in zip(first_tuple, second_tuple))
    )


def expert_work(rows, row_grads, gate_up_w, down_w, down_form):
    gate_up = jnp.einsum("ecd,edsf->ecsf", rows, gate_up_w, preferred_element_type=jnp.float32)
    gate_pre = gate_up[:, :, 0]
    up_pre = gate_up[:, :, 1]
    sigmoid = jax.nn.sigmoid(gate_pre)
    activ_low = (gate_pre * sigmoid * up_pre).astype(jnp.bfloat16)
    expert_out = jnp.einsum(
        "ecf," + down_form + "->ecd", activ_low, down_w, preferred_element_type=jnp.float32
    )
    activ_grad = jnp.einsum(
        "ecd," + down_form + "->ecf", row_grads, down_w, preferred_element_type=jnp.float32
    )
    gate_grad = activ_grad * up_pre * sigmoid * (1.0 + gate_pre * (1.0 - sigmoid))
    up_grad = activ_grad * gate_pre * sigmoid
    gate_up_grad = jnp.stack([gate_grad, up_grad], axis=2).astype(jnp.bfloat16)
    row_input_grad = jnp.einsum(
        "ecsf,edsf->ecd", gate_up_grad, gate_up_w, preferred_element_type=jnp.float32
    )
    grad_gate_up = jnp.einsum(
        "ecd,ecsf->edsf", rows, gate_up_grad, preferred_element_type=jnp.float32
    )
    grad_down = jnp.einsum(
        "ecf,ecd->" + down_form, activ_low, row_grads, preferred_element_type=jnp.float32
    )
    return (expert_out, row_input_grad, grad_gate_up, grad_down)


def body(
    hidden_in,
    parents,
    routes,
    attn_gain,
    w_query,
    key_projection,
    value_projection,
    w_out,
    moe_gain,
    w_router,
    w_gate_up,
    w_down,
    d_out,
):
    experts = w_gate_up.shape[0]
    gathered = (
        lax.all_gather(attn_gain, "fsdp", axis=0, tiled=True),
        lax.all_gather(w_query, "fsdp", axis=0, tiled=True),
        lax.all_gather(key_projection, "fsdp", axis=0, tiled=True),
        lax.all_gather(value_projection, "fsdp", axis=0, tiled=True),
        lax.all_gather(w_out, "fsdp", axis=1, tiled=True),
        lax.all_gather(moe_gain, "fsdp", axis=0, tiled=True),
        lax.all_gather(w_router, "fsdp", axis=0, tiled=True),
        lax.all_gather(w_gate_up, "fsdp", axis=1, tiled=True),
        lax.all_gather(w_down, "fsdp", axis=2, tiled=True),
    )
    gate_up_full = gathered[7]
    down_full = gathered[8]
    down_form = "efd"
    gain_one = gathered[0].astype(jnp.float32)
    query_full = gathered[1]
    key_full = gathered[2]
    value_full = gathered[3]
    out_full = gathered[4]
    gain_two = gathered[5].astype(jnp.float32)
    router_full = gathered[6]
    micro_count = hidden_in.shape[0]
    local_rows = hidden_in.shape[2]
    model_width = hidden_in.shape[3]
    top_count = routes.shape[3]
    kv_heads = key_projection.shape[1] // HEAD_DIM
    q_heads = w_query.shape[1] // HEAD_DIM
    group_size = q_heads // kv_heads
    tree_len = local_rows * lax.axis_size("ctx")
    row_start = lax.axis_index("ctx") * local_rows
    capacity = CAP
    expert_ids = jnp.arange(experts, dtype=jnp.int32)
    outputs = []
    input_grads = []
    totals = None
    for batch_index in range(micro_count):
        tree_places, reach_rows, tok_owner = tree_tables(parents[batch_index, 0], tree_len)
        local_places = lax.dynamic_slice_in_dim(tree_places, row_start, local_rows, 0)
        local_reach = lax.dynamic_slice_in_dim(reach_rows, row_start, local_rows, 0)
        allowed = (jnp.dot(local_reach, tok_owner.T, precision=TOP_PRECISION) > 0.5) & (
            tree_places[None, :] <= local_places[:, None]
        )
        cosine_table, sine_values = rope_tables(local_places)
        inputs = hidden_in[batch_index, 0].astype(jnp.float32)
        scale_one = norm_scale(inputs)
        first_normed = (inputs * scale_one * gain_one).astype(jnp.bfloat16)
        query_unrotated = jnp.dot(
            first_normed, query_full, preferred_element_type=jnp.float32
        ).reshape(local_rows, q_heads, HEAD_DIM)
        key_unrotated = jnp.dot(first_normed, key_full, preferred_element_type=jnp.float32).reshape(
            local_rows, kv_heads, HEAD_DIM
        )
        value_reduced = jnp.dot(
            first_normed, value_full, preferred_element_type=jnp.float32
        ).astype(jnp.bfloat16)
        query_reduced = (
            apply_rotary(query_unrotated, cosine_table, sine_values)
            .astype(jnp.bfloat16)
            .reshape(local_rows, kv_heads, group_size, HEAD_DIM)
        )
        key_low = (
            apply_rotary(key_unrotated, cosine_table, sine_values)
            .astype(jnp.bfloat16)
            .reshape(local_rows, kv_heads * HEAD_DIM)
        )
        tree_keys, tree_values = (
            lax.all_gather(key_low, "ctx", axis=0, tiled=True),
            lax.all_gather(value_reduced, "ctx", axis=0, tiled=True),
        )
        tree_keys = tree_keys.reshape(tree_len, kv_heads, HEAD_DIM)
        tree_values = tree_values.reshape(tree_len, kv_heads, HEAD_DIM)

        def masked_scores():
            raw_scores = jnp.einsum(
                "qhjd,khd->hjqk", query_reduced, tree_keys, preferred_element_type=jnp.float32
            )
            return jnp.where(allowed[None, None], raw_scores * SCORE_SCALE, -1e30)

        scores = masked_scores()
        top_score = jnp.max(scores, axis=-1, keepdims=True)
        log_total = top_score + jnp.log(
            jnp.sum(jnp.exp(scores - top_score), axis=-1, keepdims=True)
        )
        probs_low = jnp.exp(scores - log_total).astype(jnp.bfloat16)
        head_out = jnp.einsum(
            "hjqk,khd->qhjd", probs_low, tree_values, preferred_element_type=jnp.float32
        )
        head_low = head_out.reshape(local_rows, q_heads * HEAD_DIM).astype(jnp.bfloat16)
        attn_part = jnp.dot(head_low, out_full, preferred_element_type=jnp.float32)
        attended = lax.psum(attn_part.astype(jnp.bfloat16), "tp").astype(jnp.float32)
        mixed = inputs + RESIDUAL_SCALE * attended
        scale_two = norm_scale(mixed)
        normed_two = (mixed * scale_two * gain_two).astype(jnp.bfloat16)
        logits = jnp.dot(normed_two, router_full, preferred_element_type=jnp.float32)
        chosen_ids = routes[batch_index, 0]
        picked = (chosen_ids[:, :, None] == expert_ids[None, None, :]).astype(jnp.float32)
        chosen = jnp.sum(picked * logits[:, None, :], axis=2)
        gates = jax.nn.softmax(chosen, axis=1)
        flat_ids = chosen_ids.reshape(-1)
        flat_hot = (flat_ids[:, None] == expert_ids[None, :]).astype(jnp.int32)
        slots = jnp.sum((jnp.cumsum(flat_hot, axis=0) - flat_hot) * flat_hot, axis=1)
        targets = flat_ids * capacity + slots
        sources = (
            jnp.zeros((experts * capacity,), jnp.int32)
            .at[targets]
            .set(jnp.arange(local_rows * top_count, dtype=jnp.int32) // top_count)
        )
        filled = jnp.zeros((experts * capacity, 1), jnp.bfloat16).at[targets].set(1)
        dispatched = (normed_two[sources] * filled).reshape(experts, capacity, model_width)
        grad_out = d_out[batch_index, 0].astype(jnp.float32)
        grad_moe = RESIDUAL_SCALE * grad_out
        entry_grad = (
            (gates[:, :, None] * grad_moe[:, None, :])
            .astype(jnp.bfloat16)
            .reshape(local_rows * top_count, model_width)
        )
        slot_grad = (
            jnp.zeros((experts * capacity, model_width), jnp.bfloat16)
            .at[targets]
            .set(entry_grad)
            .reshape(experts, capacity, model_width)
        )
        expert_out, slot_input_grad, grad_gate_up, grad_down = expert_work(
            dispatched, slot_grad, gate_up_full, down_full, down_form
        )
        entry_out = expert_out.reshape(experts * capacity, model_width)[targets].reshape(
            local_rows, top_count, model_width
        )
        moe_part = jnp.sum(gates[:, :, None] * entry_out, axis=1)
        moe_sum = lax.psum(moe_part.astype(jnp.bfloat16), "tp").astype(jnp.float32)
        outputs.append(mixed + RESIDUAL_SCALE * moe_sum)
        gate_grad_part = jnp.sum(grad_moe[:, None, :] * entry_out, axis=2)
        expert_input_grad = jnp.sum(
            slot_input_grad.reshape(experts * capacity, model_width)[targets].reshape(
                local_rows, top_count, model_width
            ),
            axis=1,
        )
        expert_input_grad, gate_grads = (
            lax.psum(expert_input_grad.astype(jnp.bfloat16), "tp").astype(jnp.float32),
            lax.psum(gate_grad_part.astype(jnp.bfloat16), "tp").astype(jnp.float32),
        )
        chosen_grad = gates * (gate_grads - jnp.sum(gates * gate_grads, axis=1, keepdims=True))
        logit_grad = jnp.sum(picked * chosen_grad[:, :, None], axis=1).astype(jnp.bfloat16)
        normed_two_grad = expert_input_grad + jnp.einsum(
            "te,de->td", logit_grad, router_full, preferred_element_type=jnp.float32
        )
        grad_router = jnp.einsum(
            "td,te->de", normed_two, logit_grad, preferred_element_type=jnp.float32
        )
        unit_two = mixed * scale_two
        grad_gain_two = jnp.sum(normed_two_grad * unit_two, axis=0)
        scaled_two = normed_two_grad * gain_two
        mixed_grad = grad_out + scale_two * (
            scaled_two - unit_two * jnp.mean(scaled_two * unit_two, axis=-1, keepdims=True)
        )
        attn_grad = (RESIDUAL_SCALE * mixed_grad).astype(jnp.bfloat16)
        grad_out_proj = jnp.einsum(
            "tc,td->cd", head_low, attn_grad, preferred_element_type=jnp.float32
        )
        head_grad = (
            jnp.einsum("td,cd->tc", attn_grad, out_full, preferred_element_type=jnp.float32)
            .astype(jnp.bfloat16)
            .reshape(local_rows, kv_heads, group_size, HEAD_DIM)
        )
        scores = masked_scores()
        probs = jnp.exp(scores - log_total)
        probs_low = probs.astype(jnp.bfloat16)
        prob_grad = jnp.einsum(
            "qhjd,khd->hjqk", head_grad, tree_values, preferred_element_type=jnp.float32
        )
        value_grad = jnp.einsum(
            "hjqk,qhjd->khd", probs_low, head_grad, preferred_element_type=jnp.float32
        )
        score_grad = (
            SCORE_SCALE * probs * (prob_grad - jnp.sum(probs * prob_grad, axis=-1, keepdims=True))
        ).astype(jnp.bfloat16)
        query_grad = jnp.einsum(
            "hjqk,khd->qhjd", score_grad, tree_keys, preferred_element_type=jnp.float32
        ).reshape(local_rows, q_heads, HEAD_DIM)
        key_grad = jnp.einsum(
            "hjqk,qhjd->khd", score_grad, query_reduced, preferred_element_type=jnp.float32
        )
        key_grad, value_grad = (
            lax.psum_scatter(
                key_grad.reshape(tree_len, kv_heads * HEAD_DIM).astype(jnp.bfloat16),
                "ctx",
                scatter_dimension=0,
                tiled=True,
            ).astype(jnp.float32),
            lax.psum_scatter(
                value_grad.reshape(tree_len, kv_heads * HEAD_DIM).astype(jnp.bfloat16),
                "ctx",
                scatter_dimension=0,
                tiled=True,
            ).astype(jnp.float32),
        )
        query_pre_grad = (
            apply_rotary(query_grad, cosine_table, -sine_values)
            .astype(jnp.bfloat16)
            .reshape(local_rows, q_heads * HEAD_DIM)
        )
        key_pre_grad = (
            apply_rotary(
                key_grad.reshape(local_rows, kv_heads, HEAD_DIM), cosine_table, -sine_values
            )
            .astype(jnp.bfloat16)
            .reshape(local_rows, kv_heads * HEAD_DIM)
        )
        value_pre_grad = value_grad.astype(jnp.bfloat16)
        normed_one_grad = jnp.einsum(
            "tc,dc->td", query_pre_grad, query_full, preferred_element_type=jnp.float32
        )
        normed_one_grad = normed_one_grad + jnp.einsum(
            "tc,dc->td", key_pre_grad, key_full, preferred_element_type=jnp.float32
        )
        normed_one_grad = normed_one_grad + jnp.einsum(
            "tc,dc->td", value_pre_grad, value_full, preferred_element_type=jnp.float32
        )
        grad_query = jnp.einsum(
            "td,tc->dc", first_normed, query_pre_grad, preferred_element_type=jnp.float32
        )
        grad_key = jnp.einsum(
            "td,tc->dc", first_normed, key_pre_grad, preferred_element_type=jnp.float32
        )
        grad_value = jnp.einsum(
            "td,tc->dc", first_normed, value_pre_grad, preferred_element_type=jnp.float32
        )
        normed_one_grad = lax.psum(normed_one_grad.astype(jnp.bfloat16), "tp").astype(jnp.float32)
        unit_one = inputs * scale_one
        grad_gain_one = jnp.sum(normed_one_grad * unit_one, axis=0)
        scaled_one = normed_one_grad * gain_one
        input_grads.append(
            mixed_grad
            + scale_one
            * (scaled_one - unit_one * jnp.mean(scaled_one * unit_one, axis=-1, keepdims=True))
        )
        piece = (
            grad_gain_one,
            grad_query,
            grad_key,
            grad_value,
            grad_out_proj,
            grad_gain_two,
            grad_router,
            grad_gate_up,
            grad_down,
        )
        totals = piece if batch_index == 0 else add_tuples(totals, piece)
    summed = (
        lax.psum_scatter(totals[0], ("fsdp", "ctx"), scatter_dimension=0, tiled=True),
        lax.psum_scatter(totals[1], ("fsdp", "ctx"), scatter_dimension=0, tiled=True),
        lax.psum_scatter(totals[2], ("fsdp", "ctx"), scatter_dimension=0, tiled=True),
        lax.psum_scatter(totals[3], ("fsdp", "ctx"), scatter_dimension=0, tiled=True),
        lax.psum_scatter(totals[4], ("fsdp", "ctx"), scatter_dimension=1, tiled=True),
        lax.psum_scatter(totals[5], ("fsdp", "ctx"), scatter_dimension=0, tiled=True),
        lax.psum_scatter(totals[6], ("fsdp", "ctx"), scatter_dimension=0, tiled=True),
        lax.psum_scatter(totals[7], ("fsdp", "ctx"), scatter_dimension=1, tiled=True),
        lax.psum_scatter(totals[8], ("fsdp", "ctx"), scatter_dimension=2, tiled=True),
    )
    shares = (
        lax.all_gather(summed[0].astype(jnp.bfloat16), "ctx", axis=0, tiled=True).astype(
            jnp.float32
        ),
        lax.all_gather(summed[1].astype(jnp.bfloat16), "ctx", axis=0, tiled=True).astype(
            jnp.float32
        ),
        lax.all_gather(summed[2].astype(jnp.bfloat16), "ctx", axis=0, tiled=True).astype(
            jnp.float32
        ),
        lax.all_gather(summed[3].astype(jnp.bfloat16), "ctx", axis=0, tiled=True).astype(
            jnp.float32
        ),
        lax.all_gather(summed[4].astype(jnp.bfloat16), "ctx", axis=1, tiled=True).astype(
            jnp.float32
        ),
        lax.all_gather(summed[5].astype(jnp.bfloat16), "ctx", axis=0, tiled=True).astype(
            jnp.float32
        ),
        lax.all_gather(summed[6].astype(jnp.bfloat16), "ctx", axis=0, tiled=True).astype(
            jnp.float32
        ),
        lax.all_gather(summed[7].astype(jnp.bfloat16), "ctx", axis=1, tiled=True).astype(
            jnp.float32
        ),
        lax.all_gather(summed[8].astype(jnp.bfloat16), "ctx", axis=2, tiled=True).astype(
            jnp.float32
        ),
    )
    layer_out = jnp.stack(outputs, axis=0)[:, None]
    d_hidden = jnp.stack(input_grads, axis=0)[:, None]
    return (
        layer_out,
        d_hidden,
        shares[0],
        shares[1],
        shares[2],
        shares[3],
        shares[4],
        shares[5],
        shares[6],
        shares[7],
        shares[8],
    )


def solution(mesh):
    placed = (
        P(None, "fsdp", "ctx", None),
        P(None, "fsdp", None),
        P(None, "fsdp", "ctx", None),
        P("fsdp"),
        P("fsdp", "tp"),
        P("fsdp", "tp"),
        P("fsdp", "tp"),
        P("tp", "fsdp"),
        P("fsdp"),
        P("fsdp", None),
        P(None, "fsdp", None, "tp"),
        P(None, "tp", "fsdp"),
        P(None, "fsdp", "ctx", None),
    )
    return jax.shard_map(
        body,
        mesh=mesh,
        in_specs=placed,
        out_specs=(
            P(None, "fsdp", "ctx", None),
            P(None, "fsdp", "ctx", None),
            P("fsdp"),
            P("fsdp", "tp"),
            P("fsdp", "tp"),
            P("fsdp", "tp"),
            P("tp", "fsdp"),
            P("fsdp"),
            P("fsdp", None),
            P(None, "fsdp", None, "tp"),
            P(None, "tp", "fsdp"),
        ),
        check_vma=False,
    )
```

profile of v0, /device:TPU:0, one launch (start us, length us, event | category | flops | bytes accessed | tf_op | source)
XLA Modules:
  0.0 2018.2 jit_solution(8778584982655334623)
XLA Ops:
  8.7 8.8 all_gather.67
  18.3 4.3 all-gather
  24.0 11.9 all_gather.69
  37.5 5.4 all_gather.68
  45.7 5.4 all_gather.70
  52.1 5.4 all_gather.77
  57.7 5.4 all_gather.78
  74.4 14.5 copy.209
  90.2 4.3 all-gather.1
  94.8 11.3 reduce-window.16
  106.7 4.5 scatter_custom_fusion.2
  111.2 7.6 scatter_custom_fusion.3
  119.1 11.3 reduce-window.14
  130.9 4.3 scatter_custom_fusion
  135.2 7.6 scatter_custom_fusion.1
  142.9 5.4 all_gather.74
  152.1 5.5 gather_fusion.2
  158.1 5.4 gather_fusion
  164.7 8.3 scatter_custom_fusion.5
  173.0 8.6 scatter_custom_fusion.4
  181.6 304.7 %all-gather.14.cloned.1.call-done = bf16[40,1536,2,128]{3,1,2,0:T(8,128)(2,1)} async-done(((bf16[40,768,2,128]{3,1,2,0:T(8,128)(2,1)}), bf16[40,1536,2,128]{3,1,2,0:T(8,128)(2,1)}) %all-gather.14.cloned.1.call-update) | async-done | bytes 31457296 | tf_op jit(solution)/shard_map/all_gather | solution.py:109
  486.3 18.1 fusion.2
  504.5 170.9 %all-gather.16.cloned.1.call-done = bf16[40,128,1536]{2,1,0:T(8,128)(2,1)} async-done(((bf16[40,128,768]{2,1,0:T(8,128)(2,1)}), bf16[40,128,1536]{2,1,0:T(8,128)(2,1)}) %all-gather.16.cloned.1.call-update) | async-done | bytes 15728656 | tf_op jit(solution)/shard_map/all_gather | solution.py:110
  675.4 12.1 fusion.102
  687.5 18.0 fusion
  705.5 11.1 gather_fusion.5
  716.6 5.1 bitcast_reduce_fusion
  721.7 16.7 fusion.15
  738.3 12.7 fusion.101
  751.0 17.9 fusion.4
  768.9 11.3 gather_fusion.4
  780.2 5.1 bitcast_reduce_fusion.1
  785.2 10.9 fusion.219
  796.1 10.9 gather_fusion.3
  807.0 5.0 fusion.9
  812.1 10.9 fusion.217
  823.0 11.0 gather_fusion.1
  834.1 5.0 fusion.11
  839.2 11.7 all-reduce.5
  851.2 15.2 fusion.224
  866.4 26.1 %all-reduce.16.cloned.1.call-done = (bf16[128,1536]{1,0:T(8,128)(2,1)}, bf16[128,1536]{1,0:T(8,128)(2,1)}) async-done(((bf16[128,1536]{1,0:T(8,128)(2,1)}, bf16[128,1536]{1,0:T(8,128)(2,1)}), (bf16[128,1536]{1,0:T(8,128)(2,1)}, bf16[128,1536]{1,0:T(8,128)(2,1)})) %all-reduce.16.cloned.1.call-update) | async-done | bytes 786448 | tf_op jit(solution)/shard_map/psum | solution.py:240
  918.9 24.6 %convolution_add_fusion.1 = f32[40,128,1536]{1,2,0:T(8,128)} fusion(f32[40,128,1536]{1,2,0:T(8,128)} %fusion.224, bf16[40,32,128]{2,1,0:T(8,128)(2,1)S(1)} %copy-done.30, bf16[40,32,1536]{2,1,0:T(8,128)(2,1)} %bitcast.552), kind=kOutput, calls=%fused_computation.19 | convolution fusion | flops 511180800 | bytes 67174400 | tf_op jit(solution)/shard_map/ecf,ecd->efd/dot_general | solution.py:79
  944.6 25.3 %fusion.13 = f32[40,1536,2,128]{3,1,2,0:T(8,128)} fusion(bf16[40,32,1536]{2,1,0:T(8,128)(2,1)} %bitcast.550, bf16[40,32]{1,0:T(8,128)(2,1)S(1)} %mul.744, bf16[40,32,1,128]{3,1,0,2:T(8,128)(2,1)S(1)} %copy-done.41, bf16[40,32,1,128]{3,1,0,2:T(8,128)(2,1)S(1)} %copy-done.40), kind=kOutput, calls=%fused_computation.35 | convolution fusion | flops 1014824960 | bytes 67504640 | tf_op jit(solution)/shard_map/ecd,ecsf->edsf/dot_general | solution.py:76
  970.0 47.3 %convolution_add_fusion = f32[40,1536,2,128]{3,1,2,0:T(8,128)} fusion(f32[40,1536,2,128]{3,1,2,0:T(8,128)} %fusion.13, bf16[40,32,1536]{2,1,0:T(8,128)(2,1)S(1)} %bitcast.554, bf16[40,32]{1,0:T(8,128)(2,1)S(1)} %copy-done.82, bf16[40,32,1,128]{3,1,0,2:T(8,128)(2,1)S(1)} %copy-done.38, bf16[40,32,1,128]{3,1,0,2:T(8,128)(2,1)S(1)} %copy-done.36), kind=kOutput, calls=%fused_computation.12 | convolution fusion | flops 1030553600 | bytes 130419200 | tf_op jit(solution)/shard_map/ecd,ecsf->edsf/dot_general | solution.py:76
  1050.3 136.4 %reduce-scatter.32.cloned.1.call-done = f32[40,128,192]{1,2,0:T(8,128)} async-done(((f32[40,128,1536]{1,2,0:T(8,128)}), f32[40,128,192]{1,2,0:T(8,128)}) %reduce-scatter.32.cloned.1.call-update) | async-done | bytes 3932176 | tf_op jit(solution)/shard_map/reduce_scatter | solution.py:359
  1190.7 350.6 %reduce-scatter.30.cloned.1.call-done = f32[40,192,2,128]{3,1,2,0:T(8,128)} async-done(((f32[40,1536,2,128]{3,1,2,0:T(8,128)}), f32[40,192,2,128]{3,1,2,0:T(8,128)}) %reduce-scatter.30.cloned.1.call-update) | async-done | bytes 7864336 | tf_op jit(solution)/shard_map/reduce_scatter | solution.py:358
  1541.3 6.0 convert_element_type.490
  1550.4 29.3 %reduce-scatter.42.cloned.1.call-done = f32[192,40]{1,0:T(8,128)} async-done(((f32[1536,40]{1,0:T(8,128)}), f32[192,40]{1,0:T(8,128)}) %reduce-scatter.42.cloned.1.call-update) | async-done | bytes 30736
  1580.7 5.3 all-gather.2
  1586.8 31.8 %reduce-scatter.24.cloned.1.call-done = f32[192,128]{1,0:T(8,128)} async-done(((f32[1536,128]{1,0:T(8,128)}), f32[192,128]{1,0:T(8,128)}) %reduce-scatter.24.cloned.1.call-update) | async-done | bytes 98320 | tf_op jit(solution)/shard_map/reduce_scatter | solution.py:353
  1619.5 5.6 all_gather.81
  1625.9 31.6 %reduce-scatter.26.cloned.1.call-done = f32[192,128]{1,0:T(8,128)} async-done(((f32[1536,128]{1,0:T(8,128)}), f32[192,128]{1,0:T(8,128)}) %reduce-scatter.26.cloned.1.call-update) | async-done | bytes 98320 | tf_op jit(solution)/shard_map/reduce_scatter | solution.py:354
  1658.4 5.6 all_gather.82
  1664.7 66.2 %all-reduce.14.cloned.1.call-done = (bf16[128,1536]{1,0:T(8,128)(2,1)}, bf16[128,1536]{1,0:T(8,128)(2,1)}, bf16[128,1536]{1,0:T(8,128)(2,1)}, bf16[128,1536]{1,0:T(8,128)(2,1)}) async-done(((bf16[128,1536]{1,0:T(8,128)(2,1)}, bf16[128,1536]{1,0:T(8,128)(2,1)}, bf16[128,1536]{1,0:T(8,128)(2,1)}, bf16[128,1536]{1,0:T(8,128)(2,1)}), (bf16[128,1536]{1,0:T(8,128)(2,1)}, bf16[128,1536]{1,0:T(8,128)(2,1)}, ...) | async-done | bytes 1572880 | tf_op jit(solution)/shard_map/psum | solution.py:230
  1732.7 22.8 %all-reduce.4 = (bf16[1536]{0:T(1024)(128)(2,1)S(1)}, bf16[1536]{0:T(1024)(128)(2,1)S(1)}) all-reduce(f32[1536]{0:T(1024)S(1)} %add.335, f32[1536]{0:T(1024)S(1)} %add.342), channel_id=6, replica_groups=mesh['fsdp'=2,'ctx'=4,'tp'=4] {'fsdp','ctx'}, use_global_device_ids=true, to_apply=%region_60.61.clone | all-reduce | flops 3072 | bytes 18432
  1756.1 6.2 all-reduce.9
  1768.1 8.5 reduce-scatter.22.cloned.1.call-done
  1777.7 7.5 all_gather.80
  1786.2 36.2 %reduce-scatter.28.cloned.1.call-done = f32[384,192]{0,1:T(8,128)} async-done(((f32[384,1536]{0,1:T(8,128)}), f32[384,192]{0,1:T(8,128)}) %reduce-scatter.28.cloned.1.call-update) | async-done | bytes 294928 | tf_op jit(solution)/shard_map/reduce_scatter | solution.py:355
  1823.4 7.5 all_gather.83
  1832.1 47.3 %all-gather.20.cloned.1.call-done = bf16[40,128,768]{1,2,0:T(8,128)(2,1)} async-done(((bf16[40,128,192]{1,2,0:T(8,128)(2,1)}), bf16[40,128,768]{1,2,0:T(8,128)(2,1)}) %all-gather.20.cloned.1.call-update) | async-done | bytes 7864336 | tf_op jit(solution)/shard_map/all_gather | solution.py:386
  1879.4 11.7 copy.244
  1891.0 90.4 %all-gather.18.cloned.1.call-done = bf16[40,768,2,128]{3,1,2,0:T(8,128)(2,1)} async-done(((bf16[40,192,2,128]{3,1,2,0:T(8,128)(2,1)}), bf16[40,768,2,128]{3,1,2,0:T(8,128)(2,1)}) %all-gather.18.cloned.1.call-update) | async-done | bytes 15728656 | tf_op jit(solution)/shard_map/all_gather | solution.py:383
  1981.4 29.5 %copy.243 = f32[40,768,2,128]{3,2,1,0:T(2,128)} copy(bf16[40,768,2,128]{3,1,2,0:T(8,128)(2,1)} %all-gather.18.cloned.1.call-done) | data formatting | bytes 47185920
  (506 shorter events, 111.2 us)
Async XLA Ops:
  7.2 28.9 %copy-start.4 = (bf16[2,1,128,1536]{3,2,1,0:T(8,128)(2,1)S(1)}, bf16[2,1,128,1536]{3,2,1,0:T(8,128)(2,1)}, u32[]{:S(2)}) copy-start(bf16[2,1,128,1536]{3,2,1,0:T(8,128)(2,1)} %param.13) | copy-start | bytes 2359300
  7.2 56.9 %all-gather.10.cloned.1.call-start = ((), (), s32[]{:S(2)}) async-start(), calls=%async_computation.11 | async-start | bytes 1769472 | tf_op jit(solution)/shard_map/all_gather | solution.py:103
  7.9 61.5 %all-gather.12.cloned.1.call-start = ((), (), s32[]{:S(2)}) async-start(), calls=%async_computation.12 | async-start | bytes 1769472 | tf_op jit(solution)/shard_map/all_gather | solution.py:106
  8.7 140.0 %all-reduce.18.cloned.1.call-start = ((), (), s32[]{:S(2)}) async-start(), calls=%async_computation.30 | async-start | bytes 1572864 | tf_op jit(solution)/shard_map/psum | solution.py:190
  17.5 26.6 %copy-start.31 = (bf16[1536,128]{1,0:T(8,128)(2,1)}, bf16[1536,128]{1,0:T(8,128)(2,1)S(1)}, u32[]{:S(2)}) copy-start(bf16[1536,128]{1,0:T(8,128)(2,1)S(1)} %all_gather.67) | copy-start | bytes 1179652
  17.5 25.5 %copy-start.119 = (s32[2,1,4]{2,1,0:T(1,128)S(1)}, s32[2,1,4]{2,1,0:T(1,128)}, u32[]{:S(2)}) copy-start(s32[2,1,4]{2,1,0:T(1,128)} %param.14) | copy-start | bytes 100
  22.6 43.6 %copy-start.64 = (f32[1536]{0:T(1024)}, f32[1536]{0:T(1024)S(1)}, u32[]{:S(2)}) copy-start(f32[1536]{0:T(1024)S(1)} %reshape.775) | copy-start | bytes 18436
  24.0 41.6 %copy-start.97 = (f32[128]{0:T(128)}, f32[128]{0:T(128)S(1)}, u32[]{:S(2)}) copy-start(f32[128]{0:T(128)S(1)} %add_rsqrt_fusion.3) | copy-start | bytes 1540
  36.8 29.4 %copy-start.103 = (f32[128]{0:T(128)}, f32[128]{0:T(128)S(1)}, u32[]{:S(2)}) copy-start(f32[128]{0:T(128)S(1)} %add_rsqrt_fusion.1) | copy-start | bytes 1540
  43.0 25.4 %copy-start.52 = (bf16[512,128]{0,1:T(8,128)(2,1)}, bf16[512,128]{0,1:T(8,128)(2,1)S(1)}, u32[]{:S(2)}) copy-start(bf16[512,128]{0,1:T(8,128)(2,1)S(1)} %copy.197) | copy-start | bytes 393220
  45.7 21.2 %copy-start.49 = (f32[128,64]{0,1:T(8,128)}, f32[128,64]{0,1:T(8,128)S(1)}, u32[]{:S(2)}) copy-start(f32[128,64]{0,1:T(8,128)S(1)} %get-tuple-element.163) | copy-start | bytes 98308
  45.7 21.2 %copy-start.46 = (f32[128,64]{0,1:T(8,128)}, f32[128,64]{0,1:T(8,128)S(1)}, u32[]{:S(2)}) copy-start(f32[128,64]{0,1:T(8,128)S(1)} %get-tuple-element.164) | copy-start | bytes 98308
  68.4 20.5 %copy-start.83 = (f32[2,3,128]{2,1,0:T(4,128)}, f32[2,3,128]{2,1,0:T(4,128)S(1)}, u32[]{:S(2)}) copy-start(f32[2,3,128]{2,1,0:T(4,128)S(1)} %log_add_fusion) | copy-start | bytes 9220
  69.0 19.8 copy-start.54
  69.4 19.4 copy-start.57
  74.3 412.0 %all-gather.14.cloned.1.call-start = ((), (), s32[]{:S(2)}) async-start(), calls=%async_computation.13 | async-start | bytes 47185920 | tf_op jit(solution)/shard_map/all_gather | solution.py:109
  88.9 586.5 %all-gather.16.cloned.1.call-start = ((), (), s32[]{:S(2)}) async-start(), calls=%async_computation.14 | async-start | bytes 23592960 | tf_op jit(solution)/shard_map/all_gather | solution.py:110
  89.5 53.4 %copy-start.91 = (bf16[768,40]{0,1:T(8,128)(2,1)S(1)}, bf16[768,40]{0,1:T(8,128)(2,1)}, u32[]{:S(2)}) copy-start(bf16[768,40]{0,1:T(8,128)(2,1)} %param.22) | copy-start | bytes 184324
  89.5 58.9 %copy-start.33 = (bf16[2,1,128,1536]{3,2,1,0:T(8,128)(2,1)S(1)}, bf16[2,1,128,1536]{3,2,1,0:T(8,128)(2,1)}, u32[]{:S(2)}) copy-start(bf16[2,1,128,1536]{3,2,1,0:T(8,128)(2,1)} %param.25) | copy-start | bytes 2359300
  89.5 803.0 %all-reduce.16.cloned.1.call-start = ((), (), s32[]{:S(2)}) async-start(), calls=%async_computation.29 | async-start | bytes 1572864 | tf_op jit(solution)/shard_map/psum | solution.py:240
  89.6 68.2 %copy-start.95 = (s32[128,8]{0,1:T(8,128)}, s32[128,8]{0,1:T(8,128)S(1)}, u32[]{:S(2)}) copy-start(s32[128,8]{0,1:T(8,128)S(1)} %get-tuple-element.138) | copy-start | bytes 12292
  89.6 74.2 %copy-start.93 = (s32[128,8]{0,1:T(8,128)}, s32[128,8]{0,1:T(8,128)S(1)}, u32[]{:S(2)}) copy-start(s32[128,8]{0,1:T(8,128)S(1)} %get-tuple-element.136) | copy-start | bytes 12292
  94.6 57.5 %copy-start.88 = (f32[1536]{0:T(1024)}, f32[1536]{0:T(1024)S(1)}, u32[]{:S(2)}) copy-start(f32[1536]{0:T(1024)S(1)} %reshape.776) | copy-start | bytes 18436
  118.9 367.5 %copy-start.81 = (bf16[40,32]{1,0:T(8,128)(2,1)}, bf16[40,32]{1,0:T(8,128)(2,1)S(1)}, u32[]{:S(2)}) copy-start(bf16[40,32]{1,0:T(8,128)(2,1)S(1)} %mul.782) | copy-start | bytes 7684
  148.6 24.4 %copy-start.21 = (f32[128,1536]{1,0:T(8,128)}, f32[128,1536]{1,0:T(8,128)S(1)}, u32[]{:S(2)}) copy-start(f32[128,1536]{1,0:T(8,128)S(1)} %get-tuple-element.114) | copy-start | bytes 2359300
  164.5 17.1 copy-start.110
  164.6 17.0 copy-start.66
  687.5 18.0 copy-start.35
  687.5 18.0 copy-start.37
  687.5 97.7 %copy-start.29 = (bf16[40,32,128]{2,1,0:T(8,128)(2,1)}, bf16[40,32,128]{2,1,0:T(8,128)(2,1)S(1)}, u32[]{:S(2)}) copy-start(bf16[40,32,128]{2,1,0:T(8,128)(2,1)S(1)} %get-tuple-element.107) | copy-start | bytes 983044
  751.0 17.9 copy-start.39
  834.0 16.9 copy-start.78
  834.0 16.9 copy-start.102
  834.1 17.0 copy-start.94
  850.9 41.6 %copy-start.87 = (bf16[128,40]{0,1:T(8,128)(2,1)}, bf16[128,40]{0,1:T(8,128)(2,1)S(1)}, u32[]{:S(2)}) copy-start(bf16[128,40]{0,1:T(8,128)(2,1)S(1)} %select_reduce_fusion) | copy-start | bytes 30724
  851.1 42.9 %copy-start.92 = (bf16[128,40]{0,1:T(8,128)(2,1)}, bf16[128,40]{0,1:T(8,128)(2,1)S(1)}, u32[]{:S(2)}) copy-start(bf16[128,40]{0,1:T(8,128)(2,1)S(1)} %select_reduce_fusion.1) | copy-start | bytes 30724
  851.1 41.5 %copy-start.43 = (bf16[1536,40]{0,1:T(8,128)(2,1)S(1)}, bf16[1536,40]{0,1:T(8,128)(2,1)}, u32[]{:S(2)}) copy-start(bf16[1536,40]{0,1:T(8,128)(2,1)} %copy-done.42) | copy-start | bytes 368644
  851.1 42.8 %copy-start.5 = (bf16[2,1,128,1536]{3,2,1,0:T(8,128)(2,1)S(1)}, bf16[2,1,128,1536]{3,2,1,0:T(8,128)(2,1)}, u32[]{:S(2)}) copy-start(bf16[2,1,128,1536]{3,2,1,0:T(8,128)(2,1)} %param.13) | copy-start | bytes 2359300
  851.1 42.8 %copy-start.23 = (bf16[128,1536]{1,0:T(8,128)(2,1)S(1)}, bf16[128,1536]{1,0:T(8,128)(2,1)}, u32[]{:S(2)}) copy-start(bf16[128,1536]{1,0:T(8,128)(2,1)} %get-tuple-element.96) | copy-start | bytes 1179652
  851.1 42.8 %copy-start.24 = (bf16[128,1536]{1,0:T(8,128)(2,1)S(1)}, bf16[128,1536]{1,0:T(8,128)(2,1)}, u32[]{:S(2)}) copy-start(bf16[128,1536]{1,0:T(8,128)(2,1)} %get-tuple-element.97) | copy-start | bytes 1179652
  851.1 42.8 %copy-start.89 = (f32[1536]{0:T(1024)S(1)}, f32[1536]{0:T(1024)}, u32[]{:S(2)}) copy-start(f32[1536]{0:T(1024)} %copy-done.88) | copy-start | bytes 18436
  851.1 42.8 %copy-start.113 = (f32[128]{0:T(128)S(1)}, f32[128]{0:T(128)}, u32[]{:S(2)}) copy-start(f32[128]{0:T(128)} %copy-done.112) | copy-start | bytes 1540
  851.2 42.8 %copy-start.116 = (f32[128]{0:T(128)S(1)}, f32[128]{0:T(128)}, u32[]{:S(2)}) copy-start(f32[128]{0:T(128)} %copy-done.115) | copy-start | bytes 1540
  851.2 174.4 %reduce-scatter.38.cloned.1.call-start = ((), (), s32[]{:S(2)}) async-start(), calls=%async_computation.25 | async-start | bytes 163840
  906.3 120.2 %reduce-scatter.34.cloned.1.call-start = ((), (), s32[]{:S(2)}) async-start(), calls=%async_computation.23 | async-start | bytes 163840
  915.0 118.1 %reduce-scatter.36.cloned.1.call-start = ((), (), s32[]{:S(2)}) async-start(), calls=%async_computation.24 | async-start | bytes 163840
  917.7 117.5 %reduce-scatter.40.cloned.1.call-start = ((), (), s32[]{:S(2)}) async-start(), calls=%async_computation.26 | async-start | bytes 163840
  918.9 267.8 %reduce-scatter.32.cloned.1.call-start = ((), (), s32[]{:S(2)}) async-start(), calls=%async_computation.21 | async-start | bytes 35389440 | tf_op jit(solution)/shard_map/reduce_scatter | solution.py:359
  943.6 26.4 %copy-start.36 = (bf16[40,32,1,128]{3,1,0,2:T(8,128)(2,1)S(1)}, bf16[40,32,1,128]{3,1,0,2:T(8,128)(2,1)}, u32[]{:S(2)}) copy-start(bf16[40,32,1,128]{3,1,0,2:T(8,128)(2,1)} %copy-done.35) | copy-start | bytes 983044
  943.6 26.4 %copy-start.38 = (bf16[40,32,1,128]{3,1,0,2:T(8,128)(2,1)S(1)}, bf16[40,32,1,128]{3,1,0,2:T(8,128)(2,1)}, u32[]{:S(2)}) copy-start(bf16[40,32,1,128]{3,1,0,2:T(8,128)(2,1)} %copy-done.37) | copy-start | bytes 983044
  943.6 26.3 %copy-start.82 = (bf16[40,32]{1,0:T(8,128)(2,1)S(1)}, bf16[40,32]{1,0:T(8,128)(2,1)}, u32[]{:S(2)}) copy-start(bf16[40,32]{1,0:T(8,128)(2,1)} %copy-done.81) | copy-start | bytes 7684
  943.6 597.6 %reduce-scatter.30.cloned.1.call-start = ((), (), s32[]{:S(2)}) async-start(), calls=%async_computation.19 | async-start | bytes 70778880 | tf_op jit(solution)/shard_map/reduce_scatter | solution.py:358
  944.6 25.3 %copy-start.10 = (bf16[1280,1536]{1,0:T(8,128)(2,1)S(1)}, bf16[1280,1536]{1,0:T(8,128)(2,1)}, u32[]{:S(2)}) copy-start(bf16[1280,1536]{1,0:T(8,128)(2,1)} %gather_fusion.2) | copy-start | bytes 11796484
  1017.4 562.4 %reduce-scatter.42.cloned.1.call-start = ((), (), s32[]{:S(2)}) async-start(), calls=%async_computation.27 | async-start | bytes 884736
  1021.7 596.9 %reduce-scatter.24.cloned.1.call-start = ((), (), s32[]{:S(2)}) async-start(), calls=%async_computation.16 | async-start | bytes 884736 | tf_op jit(solution)/shard_map/reduce_scatter | solution.py:353
  1029.2 628.2 %reduce-scatter.26.cloned.1.call-start = ((), (), s32[]{:S(2)}) async-start(), calls=%async_computation.17 | async-start | bytes 884736 | tf_op jit(solution)/shard_map/reduce_scatter | solution.py:354
  1037.6 693.3 %all-reduce.14.cloned.1.call-start = ((), (), s32[]{:S(2)}) async-start(), calls=%async_computation.28 | async-start | bytes 3145728 | tf_op jit(solution)/shard_map/psum | solution.py:230
  1043.1 733.6 %reduce-scatter.22.cloned.1.call-start = ((), (), s32[]{:S(2)}) async-start(), calls=%async_computation.15 | async-start | bytes 2654208 | tf_op jit(solution)/shard_map/reduce_scatter | solution.py:352
  1046.8 775.6 %reduce-scatter.28.cloned.1.call-start = ((), (), s32[]{:S(2)}) async-start(), calls=%async_computation.18 | async-start | bytes 2654208 | tf_op jit(solution)/shard_map/reduce_scatter | solution.py:355
  1050.2 829.1 %all-gather.20.cloned.1.call-start = ((), (), s32[]{:S(2)}) async-start(), calls=%async_computation.22 | async-start | bytes 9830400 | tf_op jit(solution)/shard_map/all_gather | solution.py:386
  1190.4 791.1 %all-gather.18.cloned.1.call-start = ((), (), s32[]{:S(2)}) async-start(), calls=%async_computation.20 | async-start | bytes 19660800 | tf_op jit(solution)/shard_map/all_gather | solution.py:383
  1547.3 39.5 %copy-start.105 = (f32[1536]{0:T(1024)S(1)}, f32[1536]{0:T(1024)}, u32[]{:S(2)}) copy-start(f32[1536]{0:T(1024)} %get-tuple-element.72) | copy-start | bytes 18436
  1547.3 39.5 %copy-start.106 = (f32[1536]{0:T(1024)S(1)}, f32[1536]{0:T(1024)}, u32[]{:S(2)}) copy-start(f32[1536]{0:T(1024)} %get-tuple-element.81) | copy-start | bytes 18436
  1547.3 216.2 %copy-start.26 = (bf16[128,1536]{1,0:T(8,128)(2,1)S(1)}, bf16[128,1536]{1,0:T(8,128)(2,1)}, u32[]{:S(2)}) copy-start(bf16[128,1536]{1,0:T(8,128)(2,1)} %get-tuple-element.97) | copy-start | bytes 1179652
  (78 other events, 431.2 us)
Sparse Core Ops, SparseCore 0:
  9.6 29.7 all-gather.9
  40.9 22.7 all-gather.11
  74.5 45.4 all-reduce.17
  122.0 364.3 all-gather.13
  487.7 187.5 all-gather.15
  851.2 41.2 all-reduce.15
  906.4 18.8 reduce-scatter.37
  927.9 19.5 reduce-scatter.33
  950.5 19.5 reduce-scatter.35
  973.0 19.6 reduce-scatter.39
  996.9 189.7 reduce-scatter.31
  1190.1 351.0 reduce-scatter.29
  1544.7 34.9 reduce-scatter.41
  1583.6 34.9 reduce-scatter.23
  1622.5 34.9 reduce-scatter.25
  1660.7 70.2 all-reduce.13
  1735.1 41.5 reduce-scatter.21
  1779.9 42.4 reduce-scatter.27
  1824.0 55.2 all-gather.19
  1881.4 99.9 all-gather.17
where the time goes:
time: 2030 us; the launch traced here: 2020 us
  waiting for transfers between devices  1330 us (66%)
  matrix products  280 us (14%)
  local copies, waits for them, and re-layouts  162 us (8%)
  blocking collectives  129 us (6%)
  other arithmetic  96.5 us (5%)
    reduce_scatter x1, waiting for transfers between devices, body(): lax.psum_scatter(totals[7], ('fsdp', 'ctx'), scatter_dimension=1, tiled=T...  351 us
    all_gather x1, waiting for transfers between devices, body(): lax.all_gather(w_gate_up, 'fsdp', axis=1, tiled=True)  305 us
    all_gather x1, waiting for transfers between devices, body(): lax.all_gather(w_down, 'fsdp', axis=2, tiled=True)  171 us
    reduce_scatter x1, waiting for transfers between devices, body(): lax.psum_scatter(totals[8], ('fsdp', 'ctx'), scatter_dimension=2, tiled=T...  136 us
    all_gather x1, waiting for transfers between devices, body(): lax.all_gather(summed[7].astype(jnp.bfloat16), 'ctx', axis=1, tiled=True)  90.4 us
    unnamed x266, local copies, waits for them, and re-layouts  74.4 us
    dot_general x2, matrix products, expert_work(): jnp.einsum('ecd,ecsf->edsf', rows, gate_up_grad, preferred_element_type=j...  72.6 us
    psum x1, waiting for transfers between devices, body(): moe_sum = lax.psum(moe_part.astype(jnp.bfloat16), 'tp').astype(jnp.float32)  66.2 us
  transfers between devices with their start and end apart: 20, of which 13 were waited for; matrix products, arithmetic and copies ran while one was open for 16% of the time, Pallas kernels for 0%

commit v1 on v0

--- a/solution.py
+++ b/solution.py
@@ -1,6 +1,8 @@
 import jax
 import jax.numpy as jnp
 from jax import lax
+from jax.experimental import pallas as pl
+from jax.experimental.pallas import tpu as pltpu
 from jax.sharding import PartitionSpec as P
 
 HEAD_DIM = 64
@@ -404,6 +406,795 @@
     )
 
 
+def dot(left, right, left_dim=1, right_dim=0):
+    return lax.dot_general(
+        left, right, (((left_dim,), (right_dim,)), ((), ())), preferred_element_type=jnp.float32
+    )
+
+
+def vmem_params(count=1):
+    return pltpu.CompilerParams(
+        dimension_semantics=("arbitrary",) * count, vmem_limit_bytes=60 * 1024 * 1024
+    )
+
+
+def attend_kernel(seen_ref, query_ref, kv0, kv1, kv2, kv3, out_ref, probs_ref):
+    blocks = (kv0, kv1, kv2, kv3)
+    micro = seen_ref.shape[0]
+    rows = query_ref.shape[0] // micro
+    kv_heads = kv0.shape[1] // (2 * HEAD_DIM)
+    group = query_ref.shape[1] // HEAD_DIM // kv_heads
+    shape = (group * rows, rows)
+    causal = (
+        lax.broadcasted_iota(jnp.int32, shape, 1)
+        <= lax.broadcasted_iota(jnp.int32, shape, 0) % rows
+    )
+    for m in range(micro):
+        span = pl.ds(m * rows, rows)
+        whole = query_ref[span, :]
+        pieces = []
+        for g in range(kv_heads):
+            lanes = slice(g * HEAD_DIM, (g + 1) * HEAD_DIM)
+            query = jnp.concatenate(
+                [
+                    whole[:, (g * group + h) * HEAD_DIM : (g * group + h + 1) * HEAD_DIM]
+                    for h in range(group)
+                ],
+                axis=0,
+            )
+            parts = []
+            for r in range(4):
+                part = dot(query, blocks[r][span, :][:, lanes], 1, 1) * SCORE_SCALE
+                if r == 0:
+                    part = jnp.where(causal, part, -1e30)
+                else:
+                    part = jnp.where(seen_ref[m, r] > 0, part, -1e30)
+                parts.append(part)
+            scores = jnp.concatenate(parts, axis=1)
+            powers = jnp.exp(scores - jnp.max(scores, axis=1, keepdims=True))
+            probs = powers / jnp.sum(powers, axis=1, keepdims=True)
+            probs_ref[m * kv_heads + g] = probs
+            low = probs.astype(jnp.bfloat16)
+            values = jnp.concatenate(
+                [
+                    blocks[r][span, :][:, (kv_heads + g) * HEAD_DIM : (kv_heads + g + 1) * HEAD_DIM]
+                    for r in range(4)
+                ],
+                axis=0,
+            )
+            mixed = dot(low, values)
+            pieces += [mixed[h * rows : (h + 1) * rows] for h in range(group)]
+        out_ref[span, :] = jnp.concatenate(pieces, axis=1).astype(jnp.bfloat16)
+
+
+def attend_back_kernel(
+    query_ref, grad_ref, kv0, kv1, kv2, kv3, probs_ref, query_grad_ref, kv_grad_ref
+):
+    blocks = (kv0, kv1, kv2, kv3)
+    kv_heads = kv0.shape[1] // (2 * HEAD_DIM)
+    micro = probs_ref.shape[0] // kv_heads
+    rows = query_ref.shape[0] // micro
+    group = query_ref.shape[1] // HEAD_DIM // kv_heads
+    for m in range(micro):
+        span = pl.ds(m * rows, rows)
+        whole = query_ref[span, :]
+        whole_grad = grad_ref[span, :]
+        pieces = []
+        key_grads = []
+        value_grads = []
+        for g in range(kv_heads):
+
+            def heads(source):
+                return jnp.concatenate(
+                    [
+                        source[:, (g * group + h) * HEAD_DIM : (g * group + h + 1) * HEAD_DIM]
+                        for h in range(group)
+                    ],
+                    axis=0,
+                )
+
+            query = heads(whole)
+            head_grad = heads(whole_grad)
+            keys = jnp.concatenate(
+                [blocks[r][span, :][:, g * HEAD_DIM : (g + 1) * HEAD_DIM] for r in range(4)], axis=0
+            )
+            values = jnp.concatenate(
+                [
+                    blocks[r][span, :][:, (kv_heads + g) * HEAD_DIM : (kv_heads + g + 1) * HEAD_DIM]
+                    for r in range(4)
+                ],
+                axis=0,
+            )
+            probs = probs_ref[m * kv_heads + g]
+            prob_grad = dot(head_grad, values, 1, 1)
+            inner = jnp.sum(probs * prob_grad, axis=1, keepdims=True)
+            score_grad = (SCORE_SCALE * probs * (prob_grad - inner)).astype(jnp.bfloat16)
+            value_grads.append(dot(probs.astype(jnp.bfloat16), head_grad, 0, 0))
+            key_grads.append(dot(score_grad, query, 0, 0))
+            query_grad = dot(score_grad, keys)
+            pieces += [query_grad[h * rows : (h + 1) * rows] for h in range(group)]
+        query_grad_ref[span, :] = jnp.concatenate(pieces, axis=1)
+        joined = jnp.concatenate(key_grads + value_grads, axis=1).astype(jnp.bfloat16)
+        for r in range(4):
+            kv_grad_ref[r, span, :] = joined[r * rows : (r + 1) * rows]
+
+
+def expert_kernel(
+    place_ref,
+    near_ref,
+    far_ref,
+    near_out_ref,
+    far_out_ref,
+    rank_ref,
+    gate_ref,
+    gate_up_ref,
+    down_ref,
+    other0,
+    other1,
+    other2,
+    other3,
+    *rest,
+):
+    if len(rest) == 12:
+        held_out, held_grad = rest[:2]
+        rest = rest[2:]
+    else:
+        held_out = held_grad = None
+    out_ref, grad_ref, slots_ref, gate_grad_ref, rows_buf, grads_buf, moe_buf, back_buf, hot_buf, gate_buf = rest
+    others = (other0, other1, other2, other3)
+    half = down_ref.shape[-1]
+    width = down_ref.shape[-2]
+    quarter = [place_ref[1] ^ r for r in range(4)]
+    iota = lax.broadcasted_iota(jnp.int32, (CAP, 128), 0)
+
+    @pl.when(pl.program_id(0) == 0)
+    def _():
+        if held_out is None:
+            out_ref[...] = jnp.zeros_like(out_ref)
+            grad_ref[...] = jnp.zeros_like(grad_ref)
+        else:
+            out_ref[...] = held_out[...]
+            grad_ref[...] = held_grad[...]
+
+    for b in range(4):
+        hot = jnp.concatenate(
+            [
+                jnp.where(iota == rank_ref[quarter[r], 0, pl.ds(b, 1), :], 1.0, 0.0)
+                for r in range(4)
+            ],
+            axis=0,
+        )
+        gates = jnp.concatenate(
+            [
+                jnp.broadcast_to(gate_ref[quarter[r], 0, pl.ds(b, 1), :], (CAP, 128))
+                for r in range(4)
+            ],
+            axis=0,
+        )
+        gate_buf[b] = jnp.broadcast_to(jnp.sum(hot * gates, axis=1, keepdims=True), (4 * CAP, 128))
+        low = hot.astype(jnp.bfloat16)
+        hot_buf[b] = low
+        span = pl.ds((b % 2) * 128, 128)
+        for part in range(2):
+            keep = pl.ds(part * half, half)
+            if b < 2:
+                rows, grads = near_ref[span, keep], near_out_ref[span, keep]
+            else:
+                swap = pl.ds((1 - part) * half, half)
+                rows, grads = far_ref[span, swap], far_out_ref[span, swap]
+            rows_buf[b, :, keep] = dot(low, rows).astype(jnp.bfloat16)
+            grads_buf[b, :, keep] = dot(low, grads).astype(jnp.bfloat16)
+    for r in range(4):
+        q = quarter[r]
+        slot = slice(r * CAP, (r + 1) * CAP)
+        rows = jnp.concatenate([rows_buf[b, slot, :] for b in range(4)], axis=0)
+        grads = jnp.concatenate([grads_buf[b, slot, :] for b in range(4)], axis=0)
+        gate = jnp.concatenate([gate_buf[b, slot, :] for b in range(4)], axis=0)
+        near_w = jnp.concatenate([gate_up_ref[q, 0, 0], gate_up_ref[q, 0, 1]], axis=1)
+        far_w = jnp.concatenate([others[r][0, :half, :], others[r][0, half : 2 * half, :]], axis=1)
+        near_down = down_ref[0, q, 0]
+        far_down = jnp.concatenate(
+            [
+                others[r][0, 2 * half + j * width : 2 * half + (j + 1) * width, :]
+                for j in range(half // 128)
+            ],
+            axis=1,
+        )
+        gate_up = dot(rows[:, :half], near_w) + dot(rows[:, half:], far_w)
+        gate_pre = gate_up[:, :width]
+        up_pre = gate_up[:, width:]
+        sigmoid = 1.0 / (1.0 + jnp.exp(-gate_pre))
+        activ = (gate_pre * sigmoid * up_pre).astype(jnp.bfloat16)
+        pulled = RESIDUAL_SCALE * (
+            dot(grads[:, :half], near_down, 1, 1) + dot(grads[:, half:], far_down, 1, 1)
+        )
+        activ_wide = activ.astype(jnp.float32)
+        gate_grad = jnp.sum(activ_wide * pulled, axis=1, keepdims=True)
+        activ_grad = pulled * gate
+        gate_pre_grad = activ_grad * up_pre * sigmoid * (1.0 + gate_pre * (1.0 - sigmoid))
+        up_pre_grad = activ_grad * gate_pre * sigmoid
+        both = jnp.concatenate([gate_pre_grad, up_pre_grad], axis=1).astype(jnp.bfloat16)
+        slots_ref[q, 0, :, : 2 * width] = both
+        slots_ref[q, 0, :, 2 * width :] = (activ_wide * gate * RESIDUAL_SCALE).astype(jnp.bfloat16)
+        for part, (wide, low_w) in enumerate(((near_w, near_down), (far_w, far_down))):
+            keep = pl.ds(part * half, half)
+            made = dot(activ, low_w)
+            back = dot(both, wide, 1, 1)
+            for b in range(4):
+                piece = slice(b * CAP, (b + 1) * CAP)
+                scale = jnp.concatenate([gate[piece]] * (half // 128), axis=1)
+                moe_buf[b, slot, keep] = (made[piece] * scale).astype(jnp.bfloat16)
+                back_buf[b, slot, keep] = back[piece].astype(jnp.bfloat16)
+        for b in range(4):
+            hot = hot_buf[b, slot, :].astype(jnp.float32)
+            gate_grad_ref[q, 0, pl.ds(b, 1), :] = jnp.sum(
+                hot * gate_grad[b * CAP : (b + 1) * CAP], axis=0, keepdims=True
+            )
+    for b in range(4):
+        span = pl.ds(b * 128, 128)
+        out_ref[span, :] += dot(hot_buf[b], moe_buf[b], 0, 0)
+        grad_ref[span, :] += dot(hot_buf[b], back_buf[b], 0, 0)
+
+
+def run_experts(place, near, far, near_out, far_out, rank, gate, gate_up, down, others, held, first):
+    steps, packed, lanes = others[0].shape
+    quarters, each, sides, half, width = gate_up.shape
+    tokens = 2 * near_out.shape[0]
+    full = 2 * half
+
+    def fixed(array):
+        return pl.BlockSpec(array.shape, lambda j, sp: (0,) * array.ndim)
+
+    table = pl.BlockSpec((quarters, 1, 4, 128), lambda j, sp: (0, first + j, 0, 0))
+    in_specs = [
+        fixed(near),
+        fixed(far),
+        fixed(near_out),
+        fixed(far_out),
+        table,
+        table,
+        pl.BlockSpec((quarters, 1, sides, half, width), lambda j, sp: (0, first + j, 0, 0, 0)),
+        pl.BlockSpec((1, quarters, 1, width, half), lambda j, sp: (sp[0], 0, first + j, 0, 0)),
+    ] + [pl.BlockSpec((1, packed, lanes), lambda j, sp: (j, 0, 0))] * 4
+    operands = [place, near, far, near_out, far_out, rank, gate, gate_up, down, *others]
+    aliases = {}
+    total = jax.ShapeDtypeStruct((tokens, full), jnp.float32)
+    if held is not None:
+        in_specs += [fixed(held[0]), fixed(held[1])]
+        aliases = {len(operands): 0, len(operands) + 1: 1}
+        operands += list(held)
+    slots = jax.ShapeDtypeStruct((quarters, steps, 4 * CAP, 3 * width), jnp.bfloat16)
+    gate_grads = jax.ShapeDtypeStruct((quarters, steps, 4, 128), jnp.float32)
+    return pl.pallas_call(
+        expert_kernel,
+        out_shape=(total, total, slots, gate_grads),
+        grid_spec=pltpu.PrefetchScalarGridSpec(
+            num_scalar_prefetch=1,
+            grid=(steps,),
+            in_specs=in_specs,
+            out_specs=(
+                pl.BlockSpec(total.shape, lambda j, sp: (0, 0)),
+                pl.BlockSpec(total.shape, lambda j, sp: (0, 0)),
+                pl.BlockSpec((quarters, 1, 4 * CAP, 3 * width), lambda j, sp: (0, j, 0, 0)),
+                pl.BlockSpec((quarters, 1, 4, 128), lambda j, sp: (0, j, 0, 0)),
+            ),
+            scratch_shapes=[pltpu.VMEM((4, 4 * CAP, full), jnp.bfloat16)] * 4
+            + [
+                pltpu.VMEM((4, 4 * CAP, 128), jnp.bfloat16),
+                pltpu.VMEM((4, 4 * CAP, 128), jnp.float32),
+            ],
+        ),
+        input_output_aliases=aliases,
+        compiler_params=vmem_params(),
+        name="experts",
+    )(*operands)
+
+
+def weight_grad_kernel(place_ref, *refs):
+    rows_in, grads_in, slots_in = refs[:4], refs[4:8], refs[8:12]
+    rank_ref = refs[12]
+    gate_up_ref, down_ref, rows_buf, grads_buf = refs[-4:]
+    half = down_ref.shape[-1]
+    width = down_ref.shape[-2]
+    side = pl.program_id(1)
+    iota = lax.broadcasted_iota(jnp.int32, (CAP, 128), 0)
+    for k in range(4):
+        for b in range(4):
+            hot = jnp.concatenate(
+                [
+                    jnp.where(iota == rank_ref[0, q, 0, pl.ds(4 * k + b, 1), :], 1.0, 0.0)
+                    for q in range(4)
+                ],
+                axis=0,
+            ).astype(jnp.bfloat16)
+            span = pl.ds(b * 128, 128)
+            spot = 4 * k + (b ^ (2 * side))
+            rows_buf[spot] = dot(hot, rows_in[k][span, :]).astype(jnp.bfloat16)
+            grads_buf[spot] = dot(hot, grads_in[k][span, :]).astype(jnp.bfloat16)
+    for q in range(4):
+        slot = slice(q * CAP, (q + 1) * CAP)
+        rows = jnp.concatenate([rows_buf[n, slot, :] for n in range(16)], axis=0)
+        grads = jnp.concatenate([grads_buf[n, slot, :] for n in range(16)], axis=0)
+        taken = jnp.concatenate([slots_in[k][0, q, 0] for k in range(4)], axis=0)
+        made = dot(rows, taken[:, : 2 * width], 0, 0)
+        gate_up_ref[0, q, 0, pl.ds(0, half, stride=2), :] = made[:, :width]
+        gate_up_ref[0, q, 0, pl.ds(1, half, stride=2), :] = made[:, width:]
+        down_ref[0, q, 0] = dot(taken[:, 2 * width :], grads, 0, 0)
+
+
+def run_weight_grads(place, rows, grads, slots, rank, held, first, each):
+    sides, quarters, steps, slot_count, lanes = slots[0].shape
+    width = lanes // 3
+    tokens = rows[0].shape[0]
+    half = rank_half(rows, grads)
+    in_specs = (
+        [pl.BlockSpec((tokens, half), lambda j, a, sp: (0, 0))] * 8
+        + [
+            pl.BlockSpec(
+                (1, quarters, 1, slot_count, lanes), lambda j, a, sp: (a, 0, j, 0, 0)
+            )
+        ]
+        * 4
+        + [pl.BlockSpec((1, quarters, 1, 16, 128), lambda j, a, sp: (a, 0, first + j, 0, 0))]
+    )
+    operands = [place, *rows, *grads, *slots, rank]
+    aliases = {}
+    if held is not None:
+        in_specs += [pl.BlockSpec(memory_space=pl.ANY)] * 2
+        aliases = {len(operands): 0, len(operands) + 1: 1}
+        operands += list(held)
+    return pl.pallas_call(
+        weight_grad_kernel,
+        out_shape=(
+            jax.ShapeDtypeStruct((sides, quarters, each, 2 * half, width), jnp.float32),
+            jax.ShapeDtypeStruct((sides, quarters, each, width, half), jnp.float32),
+        ),
+        grid_spec=pltpu.PrefetchScalarGridSpec(
+            num_scalar_prefetch=1,
+            grid=(steps, sides),
+            in_specs=in_specs,
+            out_specs=(
+                pl.BlockSpec(
+                    (1, quarters, 1, 2 * half, width),
+                    lambda j, a, sp: (sp[0] ^ a, 0, first + j, 0, 0),
+                ),
+                pl.BlockSpec(
+                    (1, quarters, 1, width, half),
+                    lambda j, a, sp: (sp[0] ^ a, 0, first + j, 0, 0),
+                ),
+            ),
+            scratch_shapes=[pltpu.VMEM((16, 4 * CAP, half), jnp.bfloat16)] * 2,
+        ),
+        input_output_aliases=aliases,
+        compiler_params=vmem_params(2),
+        name="weight_grads",
+    )(*operands)
+
+
+def rank_half(rows, grads):
+    return min(array.shape[1] for array in (*rows, *grads))
+
+
+def swap_halves(values):
+    half = values.shape[-1] // 2
+    return jnp.concatenate([values[..., half:], values[..., :half]], axis=-1)
+
+
+def turn_heads(values):
+    half_dim = HEAD_DIM // 2
+    lane = lax.broadcasted_iota(jnp.int32, values.shape, 1) % HEAD_DIM
+    return jnp.where(
+        lane < half_dim,
+        -jnp.roll(values, -half_dim, axis=1),
+        jnp.roll(values, half_dim, axis=1),
+    )
+
+
+def fast_body(
+    hidden_in,
+    parents,
+    routes,
+    attn_gain,
+    w_query,
+    key_projection,
+    value_projection,
+    w_out,
+    moe_gain,
+    w_router,
+    w_gate_up,
+    w_down,
+    d_out,
+):
+    low, wide = jnp.bfloat16, jnp.float32
+    x_pos = lax.axis_index("fsdp")
+    c_pos = lax.axis_index("ctx")
+    z_pos = lax.axis_index("tp")
+    tp_size = lax.axis_size("tp")
+    micro, _, rows, model = hidden_in.shape
+    half = model // 2
+    tokens = micro * rows
+    experts = w_gate_up.shape[0]
+    mine = experts // 2
+    each = mine // 4
+    width = w_down.shape[1]
+    q_cols = w_query.shape[1]
+    k_cols = key_projection.shape[1]
+    chunks = ((0, 2), (2, 2), (4, 1))
+
+    def across(value):
+        return lax.ppermute(value, "fsdp", [(0, 1), (1, 0)])
+
+    def beside(value):
+        return lax.ppermute(value, "ctx", [(i, i ^ 1) for i in range(4)])
+
+    def along(value):
+        return lax.ppermute(value, "ctx", [(i, i ^ 2) for i in range(4)])
+
+    def from_tp(value, step):
+        return lax.ppermute(
+            value, "tp", [((i + step) % tp_size, i) for i in range(tp_size)]
+        )
+
+    def all_ctx(value):
+        nearby = beside(value)
+        distant = along(value)
+        return [value, nearby, distant, beside(distant)]
+
+    def own_first(value):
+        return jnp.where(x_pos == 0, value, swap_halves(value))
+
+    def ctx_join(first, second, axis):
+        return jnp.where(
+            c_pos % 2 == 0,
+            jnp.concatenate([first, second], axis=axis),
+            jnp.concatenate([second, first], axis=axis),
+        )
+
+    def sum_tp(value):
+        part = value.shape[0] // tp_size
+
+        def piece(step):
+            return lax.dynamic_slice_in_dim(value, ((z_pos + step) % tp_size) * part, part, 0)
+
+        total = piece(0).astype(wide)
+        for step in range(1, tp_size):
+            total = total + from_tp(piece(tp_size - step), step).astype(wide)
+        total = total.astype(low)
+        found = [total] + [from_tp(total, step) for step in range(1, tp_size)]
+        return lax.dynamic_slice_in_dim(
+            jnp.concatenate(found + found, axis=0), ((tp_size - z_pos) % tp_size) * part, tokens, 0
+        )
+
+    small = jnp.concatenate(
+        [
+            w_query,
+            key_projection,
+            value_projection,
+            jnp.pad(
+                jnp.concatenate([w_router, attn_gain[:, None], moe_gain[:, None]], axis=1),
+                ((0, 0), (0, 128 - experts - 2)),
+            ),
+        ],
+        axis=1,
+    )
+    core = c_pos % 2
+    sent = across(lax.dynamic_slice_in_dim(small, core * (half // 2), half // 2, 0))
+    small_far = ctx_join(sent, beside(sent), 0)
+    qkv_cols = q_cols + 2 * k_cols
+    qkv_full = jnp.concatenate([small[:, :qkv_cols], small_far[:, :qkv_cols]], axis=0)
+    rest_full = jnp.concatenate([small[:, qkv_cols:], small_far[:, qkv_cols:]], axis=0)
+    gain_one = rest_full[:, experts].astype(wide)
+    gain_two = rest_full[:, experts + 1].astype(wide)
+    router = jnp.where(
+        x_pos == 0,
+        rest_full[:, :experts],
+        jnp.concatenate([rest_full[:, mine:experts], rest_full[:, :mine]], axis=1),
+    )
+
+    routes_low = jnp.pad(
+        routes.reshape(tokens, -1).astype(low), ((0, 0), (0, 128 - routes.shape[-1]))
+    )
+    near_out = jnp.concatenate([own_first(d_out.reshape(tokens, model)), routes_low], axis=1)
+    far_out = across(near_out)
+
+    gate_up_mine = (
+        lax.dynamic_slice_in_dim(w_gate_up, x_pos * mine, mine, 0)
+        .transpose(0, 2, 1, 3)
+        .reshape(4, each, 2, half, width)
+    )
+    away = (1 - x_pos) * mine + c_pos * each
+    far_weights = []
+    for first, count in chunks:
+        gate_up_sent = (
+            lax.dynamic_slice_in_dim(w_gate_up, away + first, count, 0)
+            .transpose(0, 2, 1, 3)
+            .reshape(count, 2 * half, width)
+        )
+        down_sent = (
+            lax.dynamic_slice_in_dim(w_down, away + first, count, 0)
+            .reshape(count, width, half // 128, 128)
+            .transpose(0, 2, 1, 3)
+            .reshape(count, half, 128)
+        )
+        far_weights.append(all_ctx(across(jnp.concatenate([gate_up_sent, down_sent], axis=1))))
+    down_all = w_down.reshape(2, 4, each, width, half)
+
+    heads_sent = lax.dynamic_slice_in_dim(w_out, core * (q_cols // 2), q_cols // 2, 0)
+    heads_both = jnp.concatenate([heads_sent, across(heads_sent)], axis=1)
+    heads_rest = jnp.stack([from_tp(heads_both, step) for step in range(1, tp_size)], axis=0)
+    heads_rest = jnp.concatenate([heads_both[None], heads_rest], axis=0)
+    out_full = ctx_join(heads_rest, beside(heads_rest), 1)
+
+    seg_ids = jnp.arange(4, dtype=jnp.int32)
+    seen_rows = []
+    angle_rows = []
+    half_dim = HEAD_DIM // 2
+    inverse = ROPE_BASE ** (-jnp.arange(half_dim, dtype=wide) * 2.0 / HEAD_DIM)
+    for m in range(micro):
+        current = c_pos
+        reach = seg_ids == current
+        for _ in range(3):
+            current = jnp.sum(jnp.where(seg_ids == current, parents[m, 0], 0))
+            reach = reach | (seg_ids == current)
+        reach = reach.astype(jnp.int32)
+        depth = jnp.sum(reach) - 1
+        seen_rows.append(
+            jnp.stack([jnp.sum(jnp.where(seg_ids == (c_pos ^ r), reach, 0)) for r in range(4)])
+        )
+        places = (depth * rows + jnp.arange(rows, dtype=jnp.int32)).astype(wide)
+        angle_rows.append(places[:, None] * inverse[None, :])
+    seen = jnp.stack(seen_rows)
+    angles = jnp.concatenate(angle_rows, axis=0)
+    turns = (q_cols + k_cols) // half_dim
+    cosines = jnp.tile(jnp.cos(angles), (1, turns))
+    sines = jnp.tile(jnp.sin(angles), (1, turns))
+
+    inputs = own_first(hidden_in.reshape(tokens, model)).astype(wide)
+    scale_one = norm_scale(inputs)
+    unit_one = inputs * scale_one
+    first_normed = (unit_one * gain_one).astype(low)
+    unrotated = dot(first_normed, qkv_full)
+    turned_part = unrotated[:, : q_cols + k_cols]
+    rotated = (turned_part * cosines + turn_heads(turned_part) * sines).astype(low)
+    query = rotated[:, :q_cols]
+    key_value = jnp.concatenate(
+        [rotated[:, q_cols:], unrotated[:, q_cols + k_cols :].astype(low)], axis=1
+    )
+    blocks = all_ctx(key_value)
+    smem = pl.BlockSpec(memory_space=pltpu.SMEM)
+    vmem = pl.BlockSpec(memory_space=pltpu.VMEM)
+    kv_heads = k_cols // HEAD_DIM
+    group = q_cols // k_cols
+    head_low, probs = pl.pallas_call(
+        attend_kernel,
+        out_shape=(
+            jax.ShapeDtypeStruct((tokens, q_cols), low),
+            jax.ShapeDtypeStruct((micro * kv_heads, group * rows, 4 * rows), wide),
+        ),
+        in_specs=[smem] + [vmem] * 5,
+        out_specs=(vmem, vmem),
+        compiler_params=pltpu.CompilerParams(vmem_limit_bytes=60 * 1024 * 1024),
+        name="attend",
+    )(seen, query, *blocks)
+    heads = [head_low] + [from_tp(head_low, step) for step in range(1, tp_size)]
+    attended = dot(jnp.concatenate(heads, axis=1), out_full.reshape(tp_size * q_cols, model))
+    mixed = inputs + RESIDUAL_SCALE * attended
+    scale_two = norm_scale(mixed)
+    unit_two = mixed * scale_two
+    normed_two = (unit_two * gain_two).astype(low)
+
+    expert_ids = (jnp.arange(experts, dtype=jnp.int32) + x_pos * mine) % experts
+    flat_routes = routes.reshape(tokens, -1)
+    named = jnp.any(flat_routes[:, :, None] == expert_ids[None, None, :], axis=1)
+    logits = jnp.where(named, dot(normed_two, router), -1e30)
+    powers = jnp.where(named, jnp.exp(logits - jnp.max(logits, axis=1, keepdims=True)), 0.0)
+    gates = powers / jnp.sum(powers, axis=1, keepdims=True)
+
+    gates_sent = gates[:, mine:]
+    gates_high = gates_sent.astype(low)
+    gates_rest = (gates_sent - gates_high.astype(wide)).astype(low)
+    near = jnp.concatenate(
+        [
+            normed_two,
+            jnp.pad(
+                jnp.concatenate([gates_high, gates_rest], axis=1), ((0, 0), (0, 128 - 2 * mine))
+            ),
+        ],
+        axis=1,
+    )
+    far = across(near)
+    far_gates = far[:, model : model + mine].astype(wide) + far[
+        :, model + mine : model + 2 * mine
+    ].astype(wide)
+    upper = (
+        lax.broadcasted_iota(jnp.int32, (rows, rows), 0)
+        < lax.broadcasted_iota(jnp.int32, (rows, rows), 1)
+    ).astype(low)
+
+    def ranks(route_table, ids):
+        flat = route_table.astype(jnp.int32).T
+        hit = jnp.zeros((ids.shape[0], flat.shape[1]), jnp.bool_)
+        for k in range(flat.shape[0]):
+            hit = hit | (flat[k][None, :] == ids[:, None])
+        hot = hit.astype(low).reshape(-1, rows)
+        before = dot(hot, upper)
+        found = jnp.where(hot > 0, before, -1.0).astype(jnp.int32)
+        return found.reshape(ids.shape[0], -1, rows)
+
+    top = routes.shape[-1]
+    pair_routes = jnp.concatenate([routes_low, far_out[:, model:]], axis=0)[:, :top]
+    rank_pair = ranks(pair_routes, expert_ids[:mine]).reshape(4, each, 4, rows)
+    gate_pair = (
+        jnp.concatenate([gates[:, :mine], far_gates], axis=0).T.reshape(4, each, 4, rows)
+    )
+    place = jnp.stack([x_pos, c_pos]).astype(jnp.int32)
+
+    held = None
+    slots = []
+    gate_grad_parts = []
+    for (first, count), others in zip(chunks, far_weights):
+        moe_all, back_all, slot_part, gate_part = run_experts(
+            place,
+            near,
+            far,
+            near_out,
+            far_out,
+            rank_pair,
+            gate_pair,
+            gate_up_mine,
+            down_all,
+            others,
+            held,
+            first,
+        )
+        held = (moe_all, back_all)
+        slots.append(slot_part)
+        gate_grad_parts.append(gate_part)
+    gate_grad_all = jnp.concatenate(gate_grad_parts, axis=1).reshape(mine, 2 * tokens).T
+
+    back_sent = jnp.concatenate(
+        [
+            back_all[tokens:].astype(low),
+            jnp.pad(gate_grad_all[tokens:].astype(low), ((0, 0), (0, 128 - mine))),
+        ],
+        axis=1,
+    )
+    back_got = across(back_sent)
+    back_sum = (back_all[:tokens] + swap_halves(back_got[:, :model]).astype(wide)).astype(low)
+    gathered = sum_tp(
+        jnp.concatenate(
+            [
+                back_sum,
+                jnp.pad(
+                    jnp.concatenate(
+                        [gate_grad_all[:tokens].astype(low), back_got[:, model : model + mine]],
+                        axis=1,
+                    ),
+                    ((0, 0), (0, 128 - experts)),
+                ),
+            ],
+            axis=1,
+        )
+    )
+    gate_grads = gathered[:, model : model + experts].astype(wide)
+    logit_grad = (gates * (gate_grads - jnp.sum(gates * gate_grads, axis=1, keepdims=True))).astype(
+        low
+    )
+    normed_two_grad = gathered[:, :model].astype(wide) + dot(logit_grad, router, 1, 1)
+    grad_out = near_out[:, :model].astype(wide)
+    gain_two_part = jnp.sum(normed_two_grad * unit_two, axis=0)
+    scaled_two = normed_two_grad * gain_two
+    mixed_grad = grad_out + scale_two * (
+        scaled_two - unit_two * jnp.mean(scaled_two * unit_two, axis=-1, keepdims=True)
+    )
+    attn_grad = (RESIDUAL_SCALE * mixed_grad).astype(low)
+
+    moe_got = across(moe_all[tokens:].astype(low))
+    moe_part = (moe_all[:tokens] + swap_halves(moe_got).astype(wide)).astype(low)
+    moe_sum = lax.psum(moe_part, "tp").astype(wide)
+    layer_out = own_first(mixed + RESIDUAL_SCALE * moe_sum)
+
+    head_grad = dot(attn_grad, out_full[0], 1, 1).astype(low)
+    query_grad, kv_grads = pl.pallas_call(
+        attend_back_kernel,
+        out_shape=(
+            jax.ShapeDtypeStruct((tokens, q_cols), wide),
+            jax.ShapeDtypeStruct((4, tokens, 2 * k_cols), low),
+        ),
+        in_specs=[vmem] * 7,
+        out_specs=(vmem, vmem),
+        compiler_params=pltpu.CompilerParams(vmem_limit_bytes=60 * 1024 * 1024),
+        name="attend_back",
+    )(query, head_grad, *blocks, probs)
+    near_pair = beside(jnp.stack([kv_grads[1], kv_grads[3]]))
+    far_part = (kv_grads[2].astype(wide) + near_pair[1].astype(wide)).astype(low)
+    kv_grad = (
+        kv_grads[0].astype(wide) + near_pair[0].astype(wide) + along(far_part).astype(wide)
+    )
+    turned_grad = jnp.concatenate([query_grad, kv_grad[:, :k_cols]], axis=1)
+    qkv_grad = jnp.concatenate(
+        [turned_grad * cosines - turn_heads(turned_grad) * sines, kv_grad[:, k_cols:]], axis=1
+    ).astype(low)
+    normed_one_grad = sum_tp(dot(qkv_grad, qkv_full, 1, 1).astype(low)).astype(wide)
+    gain_one_part = jnp.sum(normed_one_grad * unit_one, axis=0)
+    scaled_one = normed_one_grad * gain_one
+    d_hidden = own_first(
+        mixed_grad
+        + scale_one
+        * (scaled_one - unit_one * jnp.mean(scaled_one * unit_one, axis=-1, keepdims=True))
+    )
+
+    first_far = across(first_normed[:, half:])
+    early = all_ctx(
+        jnp.concatenate(
+            [
+                jnp.concatenate([near_out[:, :half], first_normed[:, :half], routes_low], axis=1),
+                jnp.concatenate(
+                    [far_out[:, half:model], first_far, far_out[:, model:]], axis=1
+                ),
+            ],
+            axis=0,
+        )
+    )
+    rows_two = all_ctx(jnp.concatenate([normed_two[:, :half], far[:, half:model]], axis=0))
+    heads_all = all_ctx(jnp.concatenate([head_low, across(head_low)], axis=0))
+    logit_pad = jnp.pad(logit_grad, ((0, 0), (0, 128 - experts)))
+    late_far = across(jnp.concatenate([attn_grad[:, half:], logit_pad], axis=1))
+    late_far = jnp.concatenate(
+        [
+            late_far[:, :half],
+            late_far[:, half + mine : half + experts],
+            late_far[:, half : half + mine],
+            late_far[:, half + experts :],
+        ],
+        axis=1,
+    )
+    late = all_ctx(
+        jnp.concatenate(
+            [jnp.concatenate([attn_grad[:, :half], logit_pad], axis=1), late_far], axis=0
+        )
+    )
+    qkv_all = all_ctx(jnp.concatenate([qkv_grad, across(qkv_grad)], axis=0))
+
+    all_routes = jnp.concatenate([part[:, 2 * half : 2 * half + top] for part in early], axis=0)
+    rank_all = ranks(all_routes, expert_ids).reshape(2, 4, each, 16, rows)
+    grads = None
+    for (first, count), part in zip(chunks, slots):
+        pair = all_ctx(jnp.stack([part, across(part)]))
+        grads = run_weight_grads(place, rows_two, early, pair, rank_all, grads, first, each)
+    d_gate_up = grads[0].reshape(experts, half, 2, width)
+    d_down = grads[1].reshape(experts, width, half)
+
+    def over_tokens(left, right):
+        return sum(dot(a, b, 0, 0) for a, b in zip(left, right))
+
+    d_qkv = over_tokens([part[:, half : 2 * half] for part in early], qkv_all)
+    d_w_out = over_tokens(heads_all, [part[:, :half] for part in late])
+    d_router = over_tokens(rows_two, [part[:, half : half + experts] for part in late])
+    d_router = jnp.where(
+        x_pos == 0, d_router, jnp.concatenate([d_router[:, mine:], d_router[:, :mine]], axis=1)
+    )
+
+    def sum_gain(part):
+        part = part + beside(part)
+        part = part + along(part)
+        return part[:half] + across(part[half:])
+
+    return (
+        layer_out.reshape(micro, 1, rows, model),
+        d_hidden.reshape(micro, 1, rows, model),
+        sum_gain(gain_one_part),
+        d_qkv[:, :q_cols],
+        d_qkv[:, q_cols : q_cols + k_cols],
+        d_qkv[:, q_cols + k_cols :],
+        d_w_out,
+        sum_gain(gain_two_part),
+        d_router,
+        d_gate_up,
+        d_down,
+    )
+
+
 def solution(mesh):
     placed = (
         P(None, "fsdp", "ctx", None),
@@ -420,8 +1211,9 @@
         P(None, "tp", "fsdp"),
         P(None, "fsdp", "ctx", None),
     )
+    fits = mesh.shape["fsdp"] == 2 and mesh.shape["ctx"] == 4
     return jax.shard_map(
-        body,
+        fast_body if fits else body,
         mesh=mesh,
         in_specs=placed,
         out_specs=(

time: 2030 us -> 745 us (0.37)
  waiting for transfers between devices: 1330 us -> 359 us
  matrix products: 280 us -> 22.4 us
  blocking collectives: 129 us -> 0 us
  Pallas kernels: 0 us -> 111 us
  local copies, waits for them, and re-layouts: 162 us -> 72.5 us
  starting transfers between devices: 1.07 us -> 85.5 us
  other arithmetic: 96.5 us -> 70.8 us
    all_gather x6 -> x0, waiting for transfers between devices: 613 us -> none  [the longest x1 305 us: body(): lax.all_gather(w_gate_up, 'fsdp', axis=1, tiled=True)]
    reduce_scatter x6 -> x0, waiting for transfers between devices: 595 us -> none  [the longest x1 351 us: body(): lax.psum_scatter(totals[7], ('fsdp', 'ctx'), scatter_dimension=1, tiled=T...]
    ppermute x0 -> x80, waiting for transfers between devices: none -> 359 us  [the longest x15 178 us: along(): return lax.ppermute(value, 'ctx', [(i, i ^ 2) for i in range(4)])]
    dot_general x64 -> x20, matrix products: 280 us -> 22.4 us  [dot(): lax.dot_general(left, right, (((left_dim,), (right_dim,)), ((), ())), pre...]
    pallas_call x0 -> x8, Pallas kernels: none -> 111 us  [the longest x3 51.8 us: run_weight_grads(): pl.pallas_call(weight_grad_kernel, out_shape=(jax.ShapeDtypeStruct((sides...]
    psum x3 -> x1, waiting for transfers between devices: 92.3 us -> 0.01 us  [fast_body(): moe_sum = lax.psum(moe_part, 'tp').astype(wide)]
    all_gather x14 -> x0, blocking collectives: 87.9 us -> none  [the longest x1 11.9 us: body(): lax.all_gather(key_projection, 'fsdp', axis=0, tiled=True)]
    ppermute x0 -> x80, starting transfers between devices: none -> 85.4 us  [the longest x18 48.6 us: from_tp(): lax.ppermute(value, 'tp', [((i + step) % tp_size, i) for i in range(tp_si...]
  transfers between devices with their start and end apart: 20 -> 81, of which waited for: 13 -> 28; matrix products, arithmetic and copies ran while one was open for 16% -> 21% of each run, Pallas kernels for 0% -> 13%
where the time goes in v1:
time: 745 us; the launch traced here: 738 us
  waiting for transfers between devices  359 us (48%)
  Pallas kernels  111 us (15%)
  starting transfers between devices  85.5 us (11%)
  local copies, waits for them, and re-layouts  72.5 us (10%)
  other arithmetic  70.8 us (10%)
  matrix products  22.4 us (3%)
  between operations  17.5 us (2%)
    ppermute x15, waiting for transfers between devices, along(): return lax.ppermute(value, 'ctx', [(i, i ^ 2) for i in range(4)])  178 us
    ppermute x18, waiting for transfers between devices, across(): return lax.ppermute(value, 'fsdp', [(0, 1), (1, 0)])  95.1 us
    ppermute x18, waiting for transfers between devices, from_tp(): lax.ppermute(value, 'tp', [((i + step) % tp_size, i) for i in range(tp_si...  84.6 us
    pallas_call x3, Pallas kernels, run_weight_grads(): pl.pallas_call(weight_grad_kernel, out_shape=(jax.ShapeDtypeStruct((sides...  51.8 us
    ppermute x18, starting transfers between devices, from_tp(): lax.ppermute(value, 'tp', [((i + step) % tp_size, i) for i in range(tp_si...  48.6 us
    pallas_call x3, Pallas kernels, run_experts(): pl.pallas_call(expert_kernel, out_shape=(total, total, slots, gate_grads)...  47.7 us
    dot_general x20, matrix products, dot(): lax.dot_general(left, right, (((left_dim,), (right_dim,)), ((), ())), pre...  22.4 us
    ppermute x18, starting transfers between devices, across(): return lax.ppermute(value, 'fsdp', [(0, 1), (1, 0)])  19.3 us
  transfers between devices with their start and end apart: 81, of which 28 were waited for; matrix products, arithmetic and copies ran while one was open for 21% of the time, Pallas kernels for 13%

profile of v1, /device:TPU:0, one launch (start us, length us, event | category | flops | bytes accessed | tf_op | source)
XLA Modules:
  0.0 738.2 jit_solution(437501855017406086)
XLA Ops:
  9.0 2.9 collective-permute-start.8
  20.4 2.0 collective-permute-start.15
  22.5 2.0 constant_dynamic-slice_fusion.3
  24.5 3.4 dynamic-slice_bitcast_fusion.1
  32.4 2.7 fusion.117
  35.2 2.7 fusion.118
  54.2 1.9 fusion.116
  56.1 2.6 collective-permute-start.10
  64.8 33.3 %collective-permute-done.10 = bf16[192,1536]{1,0:T(8,128)(2,1)} collective-permute-done((bf16[192,1536]{1,0:T(8,128)(2,1)}, bf16[192,1536]{1,0:T(8,128)(2,1)}, u32[]{:S(2)}, u32[]{:S(2)}) %collective-permute-start.10) | collective-permute-done | bytes 589856 | tf_op jit(solution)/shard_map/ppermute | solution.py:834
  98.6 3.1 pad_maximum_fusion
  101.9 2.0 maximum_select_fusion.3
  114.3 5.5 add_bitcast_fusion
  129.8 5.2 attend.1
  135.0 10.7 %collective-permute-start.7 = (bf16[256,384]{1,0:T(8,128)(2,1)}, bf16[256,384]{1,0:T(8,128)(2,1)S(1)}, u32[]{:S(2)}, u32[]{:S(2)}) collective-permute-start(bf16[256,384]{1,0:T(8,128)(2,1)} %get-tuple-element.33), channel_id=1, source_target_pairs={{3,0},{0,1},{1,2},{2,3},{7,4},{4,5},{5,6},{6,7},{11,8},{8,9},{9,10... | collective-permute-start | bytes 589832 | tf_op jit(solution)/shard_map/ppermute | solution.py:834
  145.7 2.5 maximum_maximum_fusion.refs_4_
  148.2 2.0 collective-permute-start.6
  150.3 3.1 collective-permute-start.5
  153.3 4.5 maximum_select_fusion
  158.4 22.8 %collective-permute-done.23.other0 = bf16[2,2304,128]{2,1,0:T(8,128)(2,1)} collective-permute-done((bf16[2,2304,128]{2,1,0:T(8,128)(2,1)}, bf16[2,2304,128]{2,1,0:T(8,128)(2,1)}, u32[]{:S(2)}, u32[]{:S(2)}) %collective-permute-start.23) | collective-permute-done | bytes 1179680 | tf_op jit(solution)/shard_map/ppermute | solution.py:825
  189.9 20.5 %collective-permute-done.21.other2 = bf16[2,2304,128]{2,1,0:T(8,128)(2,1)S(1)} collective-permute-done((bf16[2,2304,128]{2,1,0:T(8,128)(2,1)}, bf16[2,2304,128]{2,1,0:T(8,128)(2,1)S(1)}, u32[]{:S(2)}, u32[]{:S(2)}) %collective-permute-start.21) | collective-permute-done | bytes 1179680 | tf_op jit(solution)/shard_map/ppermute | solution.py:831
  211.9 5.8 dynamic-slice_bitcast_fusion
  217.7 5.1 copy.176
  222.8 13.0 %collective-permute-done.25.other2 = bf16[2,2304,128]{2,1,0:T(8,128)(2,1)} collective-permute-done((bf16[2,2304,128]{2,1,0:T(8,128)(2,1)}, bf16[2,2304,128]{2,1,0:T(8,128)(2,1)}, u32[]{:S(2)}, u32[]{:S(2)}) %collective-permute-start.25) | collective-permute-done | bytes 1179680 | tf_op jit(solution)/shard_map/ppermute | solution.py:831
  236.3 34.2 %collective-permute-done.50.refs_6_ = bf16[512,1664]{1,0:T(8,128)(2,1)} collective-permute-done((bf16[512,1664]{1,0:T(8,128)(2,1)}, bf16[512,1664]{1,0:T(8,128)(2,1)}, u32[]{:S(2)}, u32[]{:S(2)}) %collective-permute-start.50) | collective-permute-done | bytes 1703968 | tf_op jit(solution)/shard_map/ppermute | solution.py:831
  280.5 16.2 %experts.3 = (f32[512,1536]{1,0:T(8,128)}, f32[512,1536]{1,0:T(8,128)}, bf16[4,2,128,384]{3,2,1,0:T(8,128)(2,1)}, f32[4,2,4,128]{3,2,1,0:T(4,128)}) custom-call(s32[2]{0:T(128)} %pad_add_fusion.1.place_ref, bf16[256,1664]{1,0:T(8,128)(2,1)} %copy-done.8, bf16[256,1664]{1,0:T(8,128)(2,1)} %collective-permute-done.13.far_ref, bf16[256,1664]{1,0:T(8,128)(2,1)} %copy-done.7, ...), custom_call_target="tpu_custom_call" | custom-call | tf_op jit(solution)/shard_map/experts/pallas_call | solution.py:668
  296.7 18.6 %experts.4 = (f32[512,1536]{1,0:T(8,128)}, f32[512,1536]{1,0:T(8,128)}, bf16[4,2,128,384]{3,2,1,0:T(8,128)(2,1)}, f32[4,2,4,128]{3,2,1,0:T(4,128)}) custom-call(s32[2]{0:T(128)} %pad_add_fusion.1.place_ref, bf16[256,1664]{1,0:T(8,128)(2,1)} %copy-done.8, ...), custom_call_target="tpu_custom_call", output_to_operand_aliasing={{0}: (13, {}), {1}: (14, {})} | custom-call | tf_op jit(solution)/shard_map/experts/pallas_call | solution.py:668
  316.1 13.0 %experts.5 = (f32[512,1536]{1,0:T(8,128)}, f32[512,1536]{1,0:T(8,128)}, bf16[4,1,128,384]{3,2,1,0:T(8,128)(2,1)}, f32[4,1,4,128]{3,2,1,0:T(4,128)}) custom-call(s32[2]{0:T(128)} %pad_add_fusion.1.place_ref, bf16[256,1664]{1,0:T(8,128)(2,1)} %copy-done.8, ...), custom_call_target="tpu_custom_call", output_to_operand_aliasing={{0}: (13, {}), {1}: (14, {})} | custom-call | tf_op jit(solution)/shard_map/experts/pallas_call | solution.py:668
  329.1 2.4 slice.642
  339.6 20.9 %collective-permute-done.68 = bf16[4,1,128,384]{3,2,0,1:T(8,128)(2,1)S(1)} collective-permute-done((bf16[4,1,128,384]{3,2,0,1:T(8,128)(2,1)}, bf16[4,1,128,384]{3,2,0,1:T(8,128)(2,1)S(1)}, u32[]{:S(2)}, u32[]{:S(2)}) %collective-permute-start.68) | collective-permute-done | bytes 393248 | tf_op jit(solution)/shard_map/ppermute | solution.py:825
  361.0 2.1 pad_maximum_fusion.10.refs_8_
  365.4 46.3 %collective-permute-done.28 = bf16[256,1664]{1,0:T(8,128)(2,1)} collective-permute-done((bf16[256,1664]{1,0:T(8,128)(2,1)}, bf16[256,1664]{1,0:T(8,128)(2,1)}, u32[]{:S(2)}, u32[]{:S(2)}) %collective-permute-start.28) | collective-permute-done | bytes 852000 | tf_op jit(solution)/shard_map/ppermute | solution.py:825
  416.3 2.4 collective-permute-start.29
  418.7 10.1 %collective-permute-start.30 = (bf16[64,1664]{1,0:T(8,128)(2,1)}, bf16[64,1664]{1,0:T(8,128)(2,1)}, u32[]{:S(2)}, u32[]{:S(2)}) collective-permute-start(bf16[64,1664]{1,0:T(8,128)(2,1)} %get-tuple-element.162), channel_id=1, source_target_pairs={{2,0},{3,1},{0,2},{1,3},{6,4},{7,5},{4,6},{5,7},{10,8},{11,9},{8,1... | collective-permute-start | bytes 638984 | tf_op jit(solution)/shard_map/ppermute | solution.py:834
  428.9 2.0 collective-permute-start.31
  430.9 2.7 pad_maximum_fusion.2.refs_8_
  434.1 2.8 pad_maximum_fusion.3.refs_8_
  437.0 10.5 %collective-permute-done.30 = bf16[64,1664]{1,0:T(8,128)(2,1)} collective-permute-done((bf16[64,1664]{1,0:T(8,128)(2,1)}, bf16[64,1664]{1,0:T(8,128)(2,1)}, u32[]{:S(2)}, u32[]{:S(2)}) %collective-permute-start.30) | collective-permute-done | bytes 213024 | tf_op jit(solution)/shard_map/ppermute | solution.py:834
  449.0 2.2 collective-permute-start.34
  451.2 9.3 %collective-permute-done.32 = bf16[64,1664]{1,0:T(8,128)(2,1)S(1)} collective-permute-done((bf16[64,1664]{1,0:T(8,128)(2,1)S(1)}, bf16[64,1664]{1,0:T(8,128)(2,1)S(1)}, u32[]{:S(2)}, u32[]{:S(2)}) %collective-permute-start.32) | collective-permute-done | bytes 213024 | tf_op jit(solution)/shard_map/ppermute | solution.py:834
  460.6 5.6 collective-permute-done.33
  471.1 2.0 collective-permute-done.63
  474.8 2.0 collective-permute-done.64
  477.4 4.9 multiply_convert_fusion
  482.3 2.5 fusion.14.grad_ref
  485.6 6.0 attend_back.1
  497.6 3.7 collective-permute-done.36
  504.1 4.3 collective-permute-start.37
  509.5 4.4 collective-permute-done.37
  514.4 3.8 collective-permute-done.39
  518.2 5.7 collective-permute-done.38
  524.2 3.9 collective-permute-start.40
  530.1 4.1 collective-permute-done.40
  534.2 2.1 collective-permute-start.41
  536.4 7.8 %collective-permute-done.41 = bf16[64,1536]{1,0:T(8,128)(2,1)S(1)} collective-permute-done((bf16[64,1536]{1,0:T(8,128)(2,1)S(1)}, bf16[64,1536]{1,0:T(8,128)(2,1)S(1)}, u32[]{:S(2)}, u32[]{:S(2)}) %collective-permute-start.41) | collective-permute-done | bytes 196640 | tf_op jit(solution)/shard_map/ppermute | solution.py:834
  547.1 3.0 collective-permute-done.44
  562.2 9.2 %collective-permute-done.51 = bf16[512,640]{1,0:T(8,128)(2,1)S(1)} collective-permute-done((bf16[512,640]{1,0:T(8,128)(2,1)S(1)}, bf16[512,640]{1,0:T(8,128)(2,1)S(1)}, u32[]{:S(2)}, u32[]{:S(2)}) %collective-permute-start.51) | collective-permute-done | bytes 655392 | tf_op jit(solution)/shard_map/ppermute | solution.py:831
  572.4 1.9 fusion.25
  574.4 13.9 %collective-permute-done.66.refs_2_ = bf16[512,768]{1,0:T(8,128)(2,1)S(1)} collective-permute-done((bf16[512,768]{1,0:T(8,128)(2,1)S(1)}, bf16[512,768]{1,0:T(8,128)(2,1)S(1)}, u32[]{:S(2)}, u32[]{:S(2)}) %collective-permute-start.66) | collective-permute-done | bytes 786464 | tf_op jit(solution)/shard_map/ppermute | solution.py:831
  589.1 16.1 %collective-permute-done.70.refs_10_ = bf16[2,4,1,128,384]{4,3,2,1,0:T(8,128)(2,1)} collective-permute-done((bf16[2,4,1,128,384]{4,3,2,1,0:T(8,128)(2,1)}, bf16[2,4,1,128,384]{4,3,2,1,0:T(8,128)(2,1)}, u32[]{:S(2)}, u32[]{:S(2)}) %collective-permute-start.70) | collective-permute-done | bytes 786464 | tf_op jit(solution)/shard_map/ppermute | solution.py:831
  608.0 30.8 %collective-permute-done.78.refs_10_ = bf16[2,4,2,128,384]{4,3,2,1,0:T(8,128)(2,1)S(1)} collective-permute-done((bf16[2,4,2,128,384]{4,3,2,1,0:T(8,128)(2,1)S(1)}, bf16[2,4,2,128,384]{4,3,2,1,0:T(8,128)(2,1)S(1)}, u32[]{:S(2)}, u32[]{:S(2)}) %collective-permute-start.78) | collective-permute-done | bytes 1572896 | tf_op jit(solution)/shard_map/ppermute | solution.py:831
  638.8 31.7 %collective-permute-done.74.refs_10_ = bf16[2,4,2,128,384]{4,3,2,1,0:T(8,128)(2,1)} collective-permute-done((bf16[2,4,2,128,384]{4,3,2,1,0:T(8,128)(2,1)}, bf16[2,4,2,128,384]{4,3,2,1,0:T(8,128)(2,1)}, u32[]{:S(2)}, u32[]{:S(2)}) %collective-permute-start.74) | collective-permute-done | bytes 1572896 | tf_op jit(solution)/shard_map/ppermute | solution.py:831
  678.1 19.6 %weight_grads.3 = (f32[2,4,5,1536,128]{4,3,2,1,0:T(8,128)}, f32[2,4,5,128,768]{4,3,2,1,0:T(8,128)}) custom-call(s32[2]{0:T(128)} %pad_add_fusion.1.place_ref, bf16[512,768]{1,0:T(8,128)(2,1)} %copy-done.9, bf16[512,768]{1,0:T(8,128)(2,1)} %copy-done.12, bf16[512,768]{1,0:T(8,128)(2,1)} %copy-done.11, bf16[512,768]{1,0:T(8,128)(2,1)} %copy-done.10, ...), custom_call_target="tpu_custom_call" | custom-call | tf_op jit(solution)/shard_map/weight_grads/pallas_call | solution.py:746
  697.7 19.4 %weight_grads.4 = (f32[2,4,5,1536,128]{4,3,2,1,0:T(8,128)}, f32[2,4,5,128,768]{4,3,2,1,0:T(8,128)}) custom-call(s32[2]{0:T(128)} %pad_add_fusion.1.place_ref, bf16[512,768]{1,0:T(8,128)(2,1)} %copy-done.9, bf16[512,768]{1,0:T(8,128)(2,1)} %copy-done.12, bf16[512,768]{1,0:T(8,128)(2,1)} %copy-done.11, ...), custom_call_target="tpu_custom_call", output_to_operand_aliasing={{0}: (14, {}), {1}: (15, {})} | custom-call | tf_op jit(solution)/shard_map/weight_grads/pallas_call | solution.py:746
  718.3 12.8 %weight_grads.5 = (f32[2,4,5,1536,128]{4,3,2,1,0:T(8,128)}, f32[2,4,5,128,768]{4,3,2,1,0:T(8,128)}) custom-call(s32[2]{0:T(128)} %pad_add_fusion.1.place_ref, bf16[512,768]{1,0:T(8,128)(2,1)} %copy-done.9, bf16[512,768]{1,0:T(8,128)(2,1)} %copy-done.12, bf16[512,768]{1,0:T(8,128)(2,1)} %copy-done.11, ...), custom_call_target="tpu_custom_call", output_to_operand_aliasing={{0}: (14, {}), {1}: (15, {})} | custom-call | tf_op jit(solution)/shard_map/weight_grads/pallas_call | solution.py:746
  (515 shorter events, 144.3 us)
Async XLA Ops:
  7.2 470.1 %all-reduce.8.cloned.1.call-start = ((), (), s32[]{:S(2)}) async-start(), calls=%async_computation | async-start | bytes 1572864 | tf_op jit(solution)/shard_map/psum | solution.py:1094
  9.0 45.2 %collective-permute-start.8 = (bf16[192,768]{1,0:T(8,128)(2,1)}, bf16[192,768]{1,0:T(8,128)(2,1)}, u32[]{:S(2)}, u32[]{:S(2)}) collective-permute-start(bf16[192,768]{1,0:T(8,128)(2,1)} %constant_dynamic-slice_fusion.6), channel_id=1, source_target_pairs={{0,16},{16,0},{1,17},{17,1},{2,18},{18,2},{3,19},{19,3},{4,20},{20... | collective-permute-start | bytes 884744 | tf_op jit(solution)/shard_map/ppermute | solution.py:825
  16.9 45.1 %collective-permute-start = (bf16[384,768]{0,1:T(8,128)(2,1)}, bf16[384,768]{0,1:T(8,128)(2,1)}, u32[]{:S(2)}, u32[]{:S(2)}) collective-permute-start(bf16[384,768]{0,1:T(8,128)(2,1)} %fusion.40), channel_id=1, source_target_pairs={{0,16},{16,0},{1,17},{17,1},{2,18},{18,2},{3,19},{19,3},{4,20},{20... | collective-permute-start | bytes 1769480 | tf_op jit(solution)/shard_map/ppermute | solution.py:825
  20.4 127.8 %collective-permute-start.15 = (bf16[1,2304,128]{2,1,0:T(8,128)(2,1)}, bf16[1,2304,128]{2,1,0:T(8,128)(2,1)}, u32[]{:S(2)}, u32[]{:S(2)}) collective-permute-start(bf16[1,2304,128]{2,1,0:T(8,128)(2,1)} %pad_maximum_fusion.13), channel_id=1, source_target_pairs={{0,16},{16,0},{1,17},{17,1},{2,18},{18,2},{3,19},{19,3},{4,20},{20... | collective-permute-start | bytes 1769480 | tf_op jit(solution)/shard_map/ppermute | solution.py:825
  56.1 41.9 %collective-permute-start.10 = (bf16[192,1536]{1,0:T(8,128)(2,1)}, bf16[192,1536]{1,0:T(8,128)(2,1)}, u32[]{:S(2)}, u32[]{:S(2)}) collective-permute-start(bf16[192,1536]{1,0:T(8,128)(2,1)} %get-tuple-element.184), channel_id=1, source_target_pairs={{2,0},{3,1},{0,2},{1,3},{6,4},{7,5},{4,6},{5,7},{10,8},{11,9},{8,1... | collective-permute-start | bytes 1769480 | tf_op jit(solution)/shard_map/ppermute | solution.py:834
  58.7 39.9 %collective-permute-start.9 = (bf16[192,1536]{1,0:T(8,128)(2,1)}, bf16[192,1536]{1,0:T(8,128)(2,1)}, u32[]{:S(2)}, u32[]{:S(2)}) collective-permute-start(bf16[192,1536]{1,0:T(8,128)(2,1)} %get-tuple-element.184), channel_id=1, source_target_pairs={{1,0},{2,1},{3,2},{0,3},{5,4},{6,5},{7,6},{4,7},{9,8},{10,9},{11,1... | collective-permute-start | bytes 1769480 | tf_op jit(solution)/shard_map/ppermute | solution.py:834
  60.1 38.5 %collective-permute-start.11 = (bf16[192,1536]{1,0:T(8,128)(2,1)}, bf16[192,1536]{1,0:T(8,128)(2,1)}, u32[]{:S(2)}, u32[]{:S(2)}) collective-permute-start(bf16[192,1536]{1,0:T(8,128)(2,1)} %get-tuple-element.184), channel_id=1, source_target_pairs={{3,0},{0,1},{1,2},{2,3},{7,4},{4,5},{5,6},{6,7},{11,8},{8,9},{9,10... | collective-permute-start | bytes 1769480 | tf_op jit(solution)/shard_map/ppermute | solution.py:834
  62.0 39.8 %collective-permute-start.1 = (bf16[384,768]{0,1:T(8,128)(2,1)}, bf16[384,768]{0,1:T(8,128)(2,1)}, u32[]{:S(2)}, u32[]{:S(2)}) collective-permute-start(bf16[384,768]{0,1:T(8,128)(2,1)} %collective-permute-done), channel_id=1, source_target_pairs={{0,4},{4,0},{8,12},{12,8},{1,5},{5,1},{9,13},{13,9},{2,6},{6,2},{1... | collective-permute-start | bytes 1769480 | tf_op jit(solution)/shard_map/ppermute | solution.py:828
  98.1 26.1 %collective-permute-start.14 = (bf16[256,1664]{1,0:T(8,128)(2,1)S(1)}, bf16[256,1664]{1,0:T(8,128)(2,1)S(1)}, u32[]{:S(2)}, u32[]{:S(2)}) collective-permute-start(bf16[256,1664]{1,0:T(8,128)(2,1)S(1)} %pad_maximum_fusion.8.near_out_ref), channel_id=1, source_target_pairs={{0,16},{16,0},{1,17},{17,1},{2,18},{18,2},{3,19},{19,3},{4,20},{20... | collective-permute-start | bytes 2555912 | tf_op jit(solution)/shard_map/ppermute | solution.py:825
  101.8 48.5 %collective-permute-start.12 = (bf16[4,192,1536]{2,1,0:T(8,128)(2,1)}, bf16[4,192,1536]{2,1,0:T(8,128)(2,1)}, u32[]{:S(2)}, u32[]{:S(2)}) collective-permute-start(bf16[4,192,1536]{2,1,0:T(8,128)(2,1)} %pad_maximum_fusion), channel_id=1, source_target_pairs={{0,4},{4,0},{8,12},{12,8},{1,5},{5,1},{9,13},{13,9},{2,6},{6,2},{1... | collective-permute-start | bytes 7077896 | tf_op jit(solution)/shard_map/ppermute | solution.py:828
  109.4 25.6 %collective-permute-start.46 = (bf16[256,768]{1,0:T(8,128)(2,1)}, bf16[256,768]{1,0:T(8,128)(2,1)}, u32[]{:S(2)}, u32[]{:S(2)}) collective-permute-start(bf16[256,768]{1,0:T(8,128)(2,1)} %get-tuple-element.169), channel_id=1, source_target_pairs={{0,16},{16,0},{1,17},{17,1},{2,18},{18,2},{3,19},{19,3},{4,20},{20... | collective-permute-start | bytes 1179656 | tf_op jit(solution)/shard_map/ppermute | solution.py:825
  112.8 13.3 %collective-permute-start.3 = (bf16[256,256]{1,0:T(8,128)(2,1)}, bf16[256,256]{1,0:T(8,128)(2,1)}, u32[]{:S(2)}, u32[]{:S(2)}) collective-permute-start(bf16[256,256]{1,0:T(8,128)(2,1)} %pad_maximum_fusion.20.kv0), channel_id=1, source_target_pairs={{0,8},{4,12},{8,0},{12,4},{1,9},{5,13},{9,1},{13,5},{2,10},{6,14},... | collective-permute-start | bytes 393224 | tf_op jit(solution)/shard_map/ppermute | solution.py:831
  127.7 30.1 %collective-permute-start.19 = (bf16[2,2304,128]{2,1,0:T(8,128)(2,1)}, bf16[2,2304,128]{2,1,0:T(8,128)(2,1)}, u32[]{:S(2)}, u32[]{:S(2)}) collective-permute-start(bf16[2,2304,128]{2,1,0:T(8,128)(2,1)} %pad_maximum_fusion.4), channel_id=1, source_target_pairs={{0,16},{16,0},{1,17},{17,1},{2,18},{18,2},{3,19},{19,3},{4,20},{20... | collective-permute-start | bytes 3538952 | tf_op jit(solution)/shard_map/ppermute | solution.py:825
  128.3 53.0 %collective-permute-start.23 = (bf16[2,2304,128]{2,1,0:T(8,128)(2,1)}, bf16[2,2304,128]{2,1,0:T(8,128)(2,1)}, u32[]{:S(2)}, u32[]{:S(2)}) collective-permute-start(bf16[2,2304,128]{2,1,0:T(8,128)(2,1)} %pad_maximum_fusion.5), channel_id=1, source_target_pairs={{0,16},{16,0},{1,17},{17,1},{2,18},{18,2},{3,19},{19,3},{4,20},{20... | collective-permute-start | bytes 3538952 | tf_op jit(solution)/shard_map/ppermute | solution.py:825
  135.0 46.8 %collective-permute-start.7 = (bf16[256,384]{1,0:T(8,128)(2,1)}, bf16[256,384]{1,0:T(8,128)(2,1)S(1)}, u32[]{:S(2)}, u32[]{:S(2)}) collective-permute-start(bf16[256,384]{1,0:T(8,128)(2,1)} %get-tuple-element.33), channel_id=1, source_target_pairs={{3,0},{0,1},{1,2},{2,3},{7,4},{4,5},{5,6},{6,7},{11,8},{8,9},{9,10... | collective-permute-start | bytes 589832 | tf_op jit(solution)/shard_map/ppermute | solution.py:834
  148.2 35.1 %collective-permute-start.6 = (bf16[256,384]{1,0:T(8,128)(2,1)}, bf16[256,384]{1,0:T(8,128)(2,1)S(1)}, u32[]{:S(2)}, u32[]{:S(2)}) collective-permute-start(bf16[256,384]{1,0:T(8,128)(2,1)} %get-tuple-element.33), channel_id=1, source_target_pairs={{2,0},{3,1},{0,2},{1,3},{6,4},{7,5},{4,6},{5,7},{10,8},{11,9},{8,1... | collective-permute-start | bytes 589832 | tf_op jit(solution)/shard_map/ppermute | solution.py:834
  150.3 33.6 %collective-permute-start.5 = (bf16[256,384]{1,0:T(8,128)(2,1)}, bf16[256,384]{1,0:T(8,128)(2,1)S(1)}, u32[]{:S(2)}, u32[]{:S(2)}) collective-permute-start(bf16[256,384]{1,0:T(8,128)(2,1)} %get-tuple-element.33), channel_id=1, source_target_pairs={{1,0},{2,1},{3,2},{0,3},{5,4},{6,5},{7,6},{4,7},{9,8},{10,9},{11,1... | collective-permute-start | bytes 589832 | tf_op jit(solution)/shard_map/ppermute | solution.py:834
  157.9 29.6 %collective-permute-start.17 = (bf16[1,2304,128]{2,1,0:T(8,128)(2,1)}, bf16[1,2304,128]{2,1,0:T(8,128)(2,1)}, u32[]{:S(2)}, u32[]{:S(2)}) collective-permute-start(bf16[1,2304,128]{2,1,0:T(8,128)(2,1)} %collective-permute-done.15.other0), channel_id=1, source_target_pairs={{0,8},{4,12},{8,0},{12,4},{1,9},{5,13},{9,1},{13,5},{2,10},{6,14},... | collective-permute-start | bytes 1769480 | tf_op jit(solution)/shard_map/ppermute | solution.py:831
  181.3 29.1 %collective-permute-start.21 = (bf16[2,2304,128]{2,1,0:T(8,128)(2,1)}, bf16[2,2304,128]{2,1,0:T(8,128)(2,1)S(1)}, u32[]{:S(2)}, u32[]{:S(2)}) collective-permute-start(bf16[2,2304,128]{2,1,0:T(8,128)(2,1)} %collective-permute-done.19.other0), channel_id=1, source_target_pairs={{0,8},{4,12},{8,0},{12,4},{1,9},{5,13},{9,1},{13,5},{2,10},{6,14},... | collective-permute-start | bytes 3538952 | tf_op jit(solution)/shard_map/ppermute | solution.py:831
  181.7 54.0 %collective-permute-start.25 = (bf16[2,2304,128]{2,1,0:T(8,128)(2,1)}, bf16[2,2304,128]{2,1,0:T(8,128)(2,1)}, u32[]{:S(2)}, u32[]{:S(2)}) collective-permute-start(bf16[2,2304,128]{2,1,0:T(8,128)(2,1)} %collective-permute-done.23.other0), channel_id=1, source_target_pairs={{0,8},{4,12},{8,0},{12,4},{1,9},{5,13},{9,1},{13,5},{2,10},{6,14},... | collective-permute-start | bytes 3538952 | tf_op jit(solution)/shard_map/ppermute | solution.py:831
  183.8 86.6 %collective-permute-start.50 = (bf16[512,1664]{1,0:T(8,128)(2,1)}, bf16[512,1664]{1,0:T(8,128)(2,1)}, u32[]{:S(2)}, u32[]{:S(2)}) collective-permute-start(bf16[512,1664]{1,0:T(8,128)(2,1)} %maximum_maximum_fusion.refs_4_), channel_id=1, source_target_pairs={{0,8},{4,12},{8,0},{12,4},{1,9},{5,13},{9,1},{13,5},{2,10},{6,14},... | collective-permute-start | bytes 5111816 | tf_op jit(solution)/shard_map/ppermute | solution.py:831
  187.5 48.3 %collective-permute-start.24 = (bf16[2,2304,128]{2,1,0:T(8,128)(2,1)}, bf16[2,2304,128]{2,1,0:T(8,128)(2,1)}, u32[]{:S(2)}, u32[]{:S(2)}) collective-permute-start(bf16[2,2304,128]{2,1,0:T(8,128)(2,1)} %collective-permute-done.23.other0), channel_id=1, source_target_pairs={{0,4},{4,0},{8,12},{12,8},{1,5},{5,1},{9,13},{13,9},{2,6},{6,2},{1... | collective-permute-start | bytes 3538952 | tf_op jit(solution)/shard_map/ppermute | solution.py:828
  189.0 83.2 %collective-permute-start.48 = (bf16[512,1664]{1,0:T(8,128)(2,1)}, bf16[512,1664]{1,0:T(8,128)(2,1)}, u32[]{:S(2)}, u32[]{:S(2)}) collective-permute-start(bf16[512,1664]{1,0:T(8,128)(2,1)} %maximum_maximum_fusion.refs_4_), channel_id=1, source_target_pairs={{0,4},{4,0},{8,12},{12,8},{1,5},{5,1},{9,13},{13,9},{2,6},{6,2},{1... | collective-permute-start | bytes 5111816 | tf_op jit(solution)/shard_map/ppermute | solution.py:828
  211.4 61.4 %collective-permute-start.13 = (bf16[256,1664]{1,0:T(8,128)(2,1)S(1)}, bf16[256,1664]{1,0:T(8,128)(2,1)}, u32[]{:S(2)}, u32[]{:S(2)}) collective-permute-start(bf16[256,1664]{1,0:T(8,128)(2,1)S(1)} %pad_maximum_fusion.7.near_ref), channel_id=1, source_target_pairs={{0,16},{16,0},{1,17},{17,1},{2,18},{18,2},{3,19},{19,3},{4,20},{20... | collective-permute-start | bytes 2555912 | tf_op jit(solution)/shard_map/ppermute | solution.py:825
  235.8 60.9 %collective-permute-start.20 = (bf16[2,2304,128]{2,1,0:T(8,128)(2,1)}, bf16[2,2304,128]{2,1,0:T(8,128)(2,1)}, u32[]{:S(2)}, u32[]{:S(2)}) collective-permute-start(bf16[2,2304,128]{2,1,0:T(8,128)(2,1)} %collective-permute-done.19.other0), channel_id=1, source_target_pairs={{0,4},{4,0},{8,12},{12,8},{1,5},{5,1},{9,13},{13,9},{2,6},{6,2},{1... | collective-permute-start | bytes 3538952 | tf_op jit(solution)/shard_map/ppermute | solution.py:828
  235.8 60.9 %collective-permute-start.22 = (bf16[2,2304,128]{2,1,0:T(8,128)(2,1)}, bf16[2,2304,128]{2,1,0:T(8,128)(2,1)}, u32[]{:S(2)}, u32[]{:S(2)}) collective-permute-start(bf16[2,2304,128]{2,1,0:T(8,128)(2,1)} %copy-done.51), channel_id=1, source_target_pairs={{0,4},{4,0},{8,12},{12,8},{1,5},{5,1},{9,13},{13,9},{2,6},{6,2},{1... | collective-permute-start | bytes 3538952 | tf_op jit(solution)/shard_map/ppermute | solution.py:828
  272.2 43.1 %collective-permute-start.16 = (bf16[1,2304,128]{2,1,0:T(8,128)(2,1)}, bf16[1,2304,128]{2,1,0:T(8,128)(2,1)}, u32[]{:S(2)}, u32[]{:S(2)}) collective-permute-start(bf16[1,2304,128]{2,1,0:T(8,128)(2,1)} %collective-permute-done.15.other0), channel_id=1, source_target_pairs={{0,4},{4,0},{8,12},{12,8},{1,5},{5,1},{9,13},{13,9},{2,6},{6,2},{1... | collective-permute-start | bytes 1769480 | tf_op jit(solution)/shard_map/ppermute | solution.py:828
  272.8 42.5 %collective-permute-start.18 = (bf16[1,2304,128]{2,1,0:T(8,128)(2,1)}, bf16[1,2304,128]{2,1,0:T(8,128)(2,1)S(1)}, u32[]{:S(2)}, u32[]{:S(2)}) collective-permute-start(bf16[1,2304,128]{2,1,0:T(8,128)(2,1)} %collective-permute-done.17.other2), channel_id=1, source_target_pairs={{0,4},{4,0},{8,12},{12,8},{1,5},{5,1},{9,13},{13,9},{2,6},{6,2},{1... | collective-permute-start | bytes 1769480 | tf_op jit(solution)/shard_map/ppermute | solution.py:828
  280.1 156.9 %collective-permute-start.52 = (bf16[512,1664]{1,0:T(8,128)(2,1)}, bf16[512,1664]{1,0:T(8,128)(2,1)S(1)}, u32[]{:S(2)}, u32[]{:S(2)}) collective-permute-start(bf16[512,1664]{1,0:T(8,128)(2,1)} %collective-permute-done.50.refs_6_), channel_id=1, source_target_pairs={{0,4},{4,0},{8,12},{12,8},{1,5},{5,1},{9,13},{13,9},{2,6},{6,2},{1... | collective-permute-start | bytes 5111816 | tf_op jit(solution)/shard_map/ppermute | solution.py:828
  331.5 31.7 %collective-permute-start.27 = (bf16[256,1536]{1,0:T(8,128)(2,1)}, bf16[256,1536]{1,0:T(8,128)(2,1)}, u32[]{:S(2)}, u32[]{:S(2)}) collective-permute-start(bf16[256,1536]{1,0:T(8,128)(2,1)} %slice.642), channel_id=1, source_target_pairs={{0,16},{16,0},{1,17},{17,1},{2,18},{18,2},{3,19},{19,3},{4,20},{20... | collective-permute-start | bytes 2359304 | tf_op jit(solution)/shard_map/ppermute | solution.py:825
  332.2 28.3 %collective-permute-start.68 = (bf16[4,1,128,384]{3,2,0,1:T(8,128)(2,1)}, bf16[4,1,128,384]{3,2,0,1:T(8,128)(2,1)S(1)}, u32[]{:S(2)}, u32[]{:S(2)}) collective-permute-start(bf16[4,1,128,384]{3,2,0,1:T(8,128)(2,1)} %bitcast.67), channel_id=1, source_target_pairs={{0,16},{16,0},{1,17},{17,1},{2,18},{18,2},{3,19},{19,3},{4,20},{20... | collective-permute-start | bytes 1179656 | tf_op jit(solution)/shard_map/ppermute | solution.py:825
  335.3 93.6 %collective-permute-start.72 = (bf16[4,2,128,384]{3,2,1,0:T(8,128)(2,1)}, bf16[4,2,128,384]{3,2,1,0:T(8,128)(2,1)}, u32[]{:S(2)}, u32[]{:S(2)}) collective-permute-start(bf16[4,2,128,384]{3,2,1,0:T(8,128)(2,1)} %get-tuple-element.47), channel_id=1, source_target_pairs={{0,16},{16,0},{1,17},{17,1},{2,18},{18,2},{3,19},{19,3},{4,20},{20... | collective-permute-start | bytes 2359304 | tf_op jit(solution)/shard_map/ppermute | solution.py:825
  335.9 97.7 %collective-permute-start.76 = (bf16[4,2,128,384]{3,2,1,0:T(8,128)(2,1)}, bf16[4,2,128,384]{3,2,1,0:T(8,128)(2,1)}, u32[]{:S(2)}, u32[]{:S(2)}) collective-permute-start(bf16[4,2,128,384]{3,2,1,0:T(8,128)(2,1)} %get-tuple-element.48), channel_id=1, source_target_pairs={{0,16},{16,0},{1,17},{17,1},{2,18},{18,2},{3,19},{19,3},{4,20},{20... | collective-permute-start | bytes 2359304 | tf_op jit(solution)/shard_map/ppermute | solution.py:825
  360.5 51.2 %collective-permute-start.28 = (bf16[256,1664]{1,0:T(8,128)(2,1)}, bf16[256,1664]{1,0:T(8,128)(2,1)}, u32[]{:S(2)}, u32[]{:S(2)}) collective-permute-start(bf16[256,1664]{1,0:T(8,128)(2,1)} %fusion.17), channel_id=1, source_target_pairs={{0,16},{16,0},{1,17},{17,1},{2,18},{18,2},{3,19},{19,3},{4,20},{20... | collective-permute-start | bytes 2555912 | tf_op jit(solution)/shard_map/ppermute | solution.py:825
  416.3 20.7 %collective-permute-start.29 = (bf16[64,1664]{1,0:T(8,128)(2,1)}, bf16[64,1664]{1,0:T(8,128)(2,1)}, u32[]{:S(2)}, u32[]{:S(2)}) collective-permute-start(bf16[64,1664]{1,0:T(8,128)(2,1)} %get-tuple-element.161), channel_id=1, source_target_pairs={{1,0},{2,1},{3,2},{0,3},{5,4},{6,5},{7,6},{4,7},{9,8},{10,9},{11,1... | collective-permute-start | bytes 638984 | tf_op jit(solution)/shard_map/ppermute | solution.py:834
  418.7 28.8 %collective-permute-start.30 = (bf16[64,1664]{1,0:T(8,128)(2,1)}, bf16[64,1664]{1,0:T(8,128)(2,1)}, u32[]{:S(2)}, u32[]{:S(2)}) collective-permute-start(bf16[64,1664]{1,0:T(8,128)(2,1)} %get-tuple-element.162), channel_id=1, source_target_pairs={{2,0},{3,1},{0,2},{1,3},{6,4},{7,5},{4,6},{5,7},{10,8},{11,9},{8,1... | collective-permute-start | bytes 638984 | tf_op jit(solution)/shard_map/ppermute | solution.py:834
  428.9 18.7 %collective-permute-start.31 = (bf16[64,1664]{1,0:T(8,128)(2,1)S(1)}, bf16[64,1664]{1,0:T(8,128)(2,1)}, u32[]{:S(2)}, u32[]{:S(2)}) collective-permute-start(bf16[64,1664]{1,0:T(8,128)(2,1)S(1)} %get-tuple-element.163), channel_id=1, source_target_pairs={{3,0},{0,1},{1,2},{2,3},{7,4},{4,5},{5,6},{6,7},{11,8},{8,9},{9,10... | collective-permute-start | bytes 638984 | tf_op jit(solution)/shard_map/ppermute | solution.py:834
  433.6 118.6 %collective-permute-start.58 = (bf16[512,384]{1,0:T(8,128)(2,1)}, bf16[512,384]{1,0:T(8,128)(2,1)}, u32[]{:S(2)}, u32[]{:S(2)}) collective-permute-start(bf16[512,384]{1,0:T(8,128)(2,1)} %constant_dynamic-update-slice_fusion.16), channel_id=1, source_target_pairs={{0,8},{4,12},{8,0},{12,4},{1,9},{5,13},{9,1},{13,5},{2,10},{6,14},... | collective-permute-start | bytes 1179656 | tf_op jit(solution)/shard_map/ppermute | solution.py:831
  448.9 11.6 %collective-permute-start.32 = (bf16[64,1664]{1,0:T(8,128)(2,1)S(1)}, bf16[64,1664]{1,0:T(8,128)(2,1)S(1)}, u32[]{:S(2)}, u32[]{:S(2)}) collective-permute-start(bf16[64,1664]{1,0:T(8,128)(2,1)S(1)} %get-tuple-element.145), channel_id=1, source_target_pairs={{1,0},{2,1},{3,2},{0,3},{5,4},{6,5},{7,6},{4,7},{9,8},{10,9},{11,1... | collective-permute-start | bytes 638984 | tf_op jit(solution)/shard_map/ppermute | solution.py:834
  449.0 17.3 %collective-permute-start.34 = (bf16[64,1664]{1,0:T(8,128)(2,1)S(1)}, bf16[64,1664]{1,0:T(8,128)(2,1)S(1)}, u32[]{:S(2)}, u32[]{:S(2)}) collective-permute-start(bf16[64,1664]{1,0:T(8,128)(2,1)S(1)} %get-tuple-element.145), channel_id=1, source_target_pairs={{3,0},{0,1},{1,2},{2,3},{7,4},{4,5},{5,6},{6,7},{11,8},{8,9},{9,10... | collective-permute-start | bytes 638984 | tf_op jit(solution)/shard_map/ppermute | solution.py:834
  451.2 15.0 %collective-permute-start.33 = (bf16[64,1664]{1,0:T(8,128)(2,1)S(1)}, bf16[64,1664]{1,0:T(8,128)(2,1)S(1)}, u32[]{:S(2)}, u32[]{:S(2)}) collective-permute-start(bf16[64,1664]{1,0:T(8,128)(2,1)S(1)} %get-tuple-element.145), channel_id=1, source_target_pairs={{2,0},{3,1},{0,2},{1,3},{6,4},{7,5},{4,6},{5,7},{10,8},{11,9},{8,1... | collective-permute-start | bytes 638984 | tf_op jit(solution)/shard_map/ppermute | solution.py:834
  492.9 15.6 %collective-permute-start.55 = (bf16[256,896]{1,0:T(8,128)(2,1)S(1)}, bf16[256,896]{1,0:T(8,128)(2,1)S(1)}, u32[]{:S(2)}, u32[]{:S(2)}) collective-permute-start(bf16[256,896]{1,0:T(8,128)(2,1)S(1)} %pad_maximum_fusion.14), channel_id=1, source_target_pairs={{0,16},{16,0},{1,17},{17,1},{2,18},{18,2},{3,19},{19,3},{4,20},{20... | collective-permute-start | bytes 1376264 | tf_op jit(solution)/shard_map/ppermute | solution.py:825
  502.2 21.9 %collective-permute-start.47 = (bf16[256,640]{1,0:T(8,128)(2,1)S(1)}, bf16[256,640]{1,0:T(8,128)(2,1)S(1)}, u32[]{:S(2)}, u32[]{:S(2)}) collective-permute-start(bf16[256,640]{1,0:T(8,128)(2,1)S(1)} %pad_maximum_fusion.17), channel_id=1, source_target_pairs={{0,16},{16,0},{1,17},{17,1},{2,18},{18,2},{3,19},{19,3},{4,20},{20... | collective-permute-start | bytes 983048 | tf_op jit(solution)/shard_map/ppermute | solution.py:825
  508.5 15.4 %collective-permute-start.38 = (bf16[64,1536]{1,0:T(8,128)(2,1)S(1)}, bf16[64,1536]{1,0:T(8,128)(2,1)S(1)}, u32[]{:S(2)}, u32[]{:S(2)}) collective-permute-start(bf16[64,1536]{1,0:T(8,128)(2,1)S(1)} %get-tuple-element.172), channel_id=1, source_target_pairs={{2,0},{3,1},{0,2},{1,3},{6,4},{7,5},{4,6},{5,7},{10,8},{11,9},{8,1... | collective-permute-start | bytes 589832 | tf_op jit(solution)/shard_map/ppermute | solution.py:834
  513.8 44.6 %collective-permute-start.59 = (bf16[512,896]{1,0:T(8,128)(2,1)S(1)}, bf16[512,896]{1,0:T(8,128)(2,1)S(1)}, u32[]{:S(2)}, u32[]{:S(2)}) collective-permute-start(bf16[512,896]{1,0:T(8,128)(2,1)S(1)} %maximum_maximum_fusion.1), channel_id=1, source_target_pairs={{0,8},{4,12},{8,0},{12,4},{1,9},{5,13},{9,1},{13,5},{2,10},{6,14},... | collective-permute-start | bytes 2752520 | tf_op jit(solution)/shard_map/ppermute | solution.py:831
  518.2 42.5 %collective-permute-start.57 = (bf16[512,896]{1,0:T(8,128)(2,1)S(1)}, bf16[512,896]{1,0:T(8,128)(2,1)S(1)}, u32[]{:S(2)}, u32[]{:S(2)}) collective-permute-start(bf16[512,896]{1,0:T(8,128)(2,1)S(1)} %maximum_maximum_fusion.1), channel_id=1, source_target_pairs={{0,4},{4,0},{8,12},{12,8},{1,5},{5,1},{9,13},{13,9},{2,6},{6,2},{1... | collective-permute-start | bytes 2752520 | tf_op jit(solution)/shard_map/ppermute | solution.py:828
  524.0 20.2 %collective-permute-start.42 = (bf16[64,1536]{1,0:T(8,128)(2,1)S(1)}, bf16[64,1536]{1,0:T(8,128)(2,1)S(1)}, u32[]{:S(2)}, u32[]{:S(2)}) collective-permute-start(bf16[64,1536]{1,0:T(8,128)(2,1)S(1)} %get-tuple-element.141), channel_id=1, source_target_pairs={{3,0},{0,1},{1,2},{2,3},{7,4},{4,5},{5,6},{6,7},{11,8},{8,9},{9,10... | collective-permute-start | bytes 589832 | tf_op jit(solution)/shard_map/ppermute | solution.py:834
  524.2 10.1 %collective-permute-start.40 = (bf16[64,1536]{1,0:T(8,128)(2,1)S(1)}, bf16[64,1536]{1,0:T(8,128)(2,1)S(1)}, u32[]{:S(2)}, u32[]{:S(2)}) collective-permute-start(bf16[64,1536]{1,0:T(8,128)(2,1)S(1)} %get-tuple-element.141), channel_id=1, source_target_pairs={{1,0},{2,1},{3,2},{0,3},{5,4},{6,5},{7,6},{4,7},{9,8},{10,9},{11,1... | collective-permute-start | bytes 589832 | tf_op jit(solution)/shard_map/ppermute | solution.py:834
  534.2 10.0 %collective-permute-start.41 = (bf16[64,1536]{1,0:T(8,128)(2,1)S(1)}, bf16[64,1536]{1,0:T(8,128)(2,1)S(1)}, u32[]{:S(2)}, u32[]{:S(2)}) collective-permute-start(bf16[64,1536]{1,0:T(8,128)(2,1)S(1)} %get-tuple-element.141), channel_id=1, source_target_pairs={{2,0},{3,1},{0,2},{1,3},{6,4},{7,5},{4,6},{5,7},{10,8},{11,9},{8,1... | collective-permute-start | bytes 589832 | tf_op jit(solution)/shard_map/ppermute | solution.py:834
  544.2 10.6 %collective-permute-start.49 = (bf16[512,640]{1,0:T(8,128)(2,1)S(1)}, bf16[512,640]{1,0:T(8,128)(2,1)S(1)}, u32[]{:S(2)}, u32[]{:S(2)}) collective-permute-start(bf16[512,640]{1,0:T(8,128)(2,1)S(1)} %pad_maximum_fusion.11), channel_id=1, source_target_pairs={{0,4},{4,0},{8,12},{12,8},{1,5},{5,1},{9,13},{13,9},{2,6},{6,2},{1... | collective-permute-start | bytes 1966088 | tf_op jit(solution)/shard_map/ppermute | solution.py:828
  553.7 17.7 %collective-permute-start.51 = (bf16[512,640]{1,0:T(8,128)(2,1)S(1)}, bf16[512,640]{1,0:T(8,128)(2,1)S(1)}, u32[]{:S(2)}, u32[]{:S(2)}) collective-permute-start(bf16[512,640]{1,0:T(8,128)(2,1)S(1)} %pad_maximum_fusion.11), channel_id=1, source_target_pairs={{0,8},{4,12},{8,0},{12,4},{1,9},{5,13},{9,1},{13,5},{2,10},{6,14},... | collective-permute-start | bytes 1966088 | tf_op jit(solution)/shard_map/ppermute | solution.py:831
  556.8 31.4 %collective-permute-start.66 = (bf16[512,768]{1,0:T(8,128)(2,1)S(1)}, bf16[512,768]{1,0:T(8,128)(2,1)S(1)}, u32[]{:S(2)}, u32[]{:S(2)}) collective-permute-start(bf16[512,768]{1,0:T(8,128)(2,1)S(1)} %pad_maximum_fusion.9.refs_0_), channel_id=1, source_target_pairs={{0,8},{4,12},{8,0},{12,4},{1,9},{5,13},{9,1},{13,5},{2,10},{6,14},... | collective-permute-start | bytes 2359304 | tf_op jit(solution)/shard_map/ppermute | solution.py:831
  558.4 29.9 %collective-permute-start.65 = (bf16[512,768]{1,0:T(8,128)(2,1)S(1)}, bf16[512,768]{1,0:T(8,128)(2,1)S(1)}, u32[]{:S(2)}, u32[]{:S(2)}) collective-permute-start(bf16[512,768]{1,0:T(8,128)(2,1)S(1)} %pad_maximum_fusion.9.refs_0_), channel_id=1, source_target_pairs={{0,4},{4,0},{8,12},{12,8},{1,5},{5,1},{9,13},{13,9},{2,6},{6,2},{1... | collective-permute-start | bytes 2359304 | tf_op jit(solution)/shard_map/ppermute | solution.py:828
  560.1 45.1 %collective-permute-start.70 = (bf16[2,4,1,128,384]{4,3,2,1,0:T(8,128)(2,1)}, bf16[2,4,1,128,384]{4,3,2,1,0:T(8,128)(2,1)}, u32[]{:S(2)}, u32[]{:S(2)}) collective-permute-start(bf16[2,4,1,128,384]{4,3,2,1,0:T(8,128)(2,1)} %pad_maximum_fusion.10.refs_8_), channel_id=1, source_target_pairs={{0,8},{4,12},{8,0},{12,4},{1,9},{5,13},{9,1},{13,5},{2,10},{6,14},... | collective-permute-start | bytes 2359304 | tf_op jit(solution)/shard_map/ppermute | solution.py:831
  560.7 78.1 %collective-permute-start.78 = (bf16[2,4,2,128,384]{4,3,2,1,0:T(8,128)(2,1)S(1)}, bf16[2,4,2,128,384]{4,3,2,1,0:T(8,128)(2,1)S(1)}, u32[]{:S(2)}, u32[]{:S(2)}) collective-permute-start(bf16[2,4,2,128,384]{4,3,2,1,0:T(8,128)(2,1)S(1)} %copy-done.22), channel_id=1, source_target_pairs={{0,8},{4,12},{8,0},{12,4},{1,9},{5,13},{9,1},{13,5},{2,10},{6,14},... | collective-permute-start | bytes 4718600 | tf_op jit(solution)/shard_map/ppermute | solution.py:831
  571.4 99.1 %collective-permute-start.74 = (bf16[2,4,2,128,384]{4,3,2,1,0:T(8,128)(2,1)}, bf16[2,4,2,128,384]{4,3,2,1,0:T(8,128)(2,1)}, u32[]{:S(2)}, u32[]{:S(2)}) collective-permute-start(bf16[2,4,2,128,384]{4,3,2,1,0:T(8,128)(2,1)} %pad_maximum_fusion.2.refs_8_), channel_id=1, source_target_pairs={{0,8},{4,12},{8,0},{12,4},{1,9},{5,13},{9,1},{13,5},{2,10},{6,14},... | collective-permute-start | bytes 4718600 | tf_op jit(solution)/shard_map/ppermute | solution.py:831
  588.2 85.7 %collective-permute-start.77 = (bf16[2,4,2,128,384]{4,3,2,1,0:T(8,128)(2,1)S(1)}, bf16[2,4,2,128,384]{4,3,2,1,0:T(8,128)(2,1)S(1)}, u32[]{:S(2)}, u32[]{:S(2)}) collective-permute-start(bf16[2,4,2,128,384]{4,3,2,1,0:T(8,128)(2,1)S(1)} %copy-done.22), channel_id=1, source_target_pairs={{0,4},{4,0},{8,12},{12,8},{1,5},{5,1},{9,13},{13,9},{2,6},{6,2},{1... | collective-permute-start | bytes 4718600 | tf_op jit(solution)/shard_map/ppermute | solution.py:828
  588.3 18.8 %collective-permute-start.67 = (bf16[512,768]{1,0:T(8,128)(2,1)S(1)}, bf16[512,768]{1,0:T(8,128)(2,1)S(1)}, u32[]{:S(2)}, u32[]{:S(2)}) collective-permute-start(bf16[512,768]{1,0:T(8,128)(2,1)S(1)} %collective-permute-done.66.refs_2_), channel_id=1, source_target_pairs={{0,4},{4,0},{8,12},{12,8},{1,5},{5,1},{9,13},{13,9},{2,6},{6,2},{1... | collective-permute-start | bytes 2359304 | tf_op jit(solution)/shard_map/ppermute | solution.py:828
  605.2 65.3 %collective-permute-start.53 = (bf16[512,640]{1,0:T(8,128)(2,1)S(1)}, bf16[512,640]{1,0:T(8,128)(2,1)S(1)}, u32[]{:S(2)}, u32[]{:S(2)}) collective-permute-start(bf16[512,640]{1,0:T(8,128)(2,1)S(1)} %collective-permute-done.51), channel_id=1, source_target_pairs={{0,4},{4,0},{8,12},{12,8},{1,5},{5,1},{9,13},{13,9},{2,6},{6,2},{1... | collective-permute-start | bytes 1966088 | tf_op jit(solution)/shard_map/ppermute | solution.py:828
  607.1 66.8 %collective-permute-start.61 = (bf16[512,896]{1,0:T(8,128)(2,1)S(1)}, bf16[512,896]{1,0:T(8,128)(2,1)S(1)}, u32[]{:S(2)}, u32[]{:S(2)}) collective-permute-start(bf16[512,896]{1,0:T(8,128)(2,1)S(1)} %collective-permute-done.59), channel_id=1, source_target_pairs={{0,4},{4,0},{8,12},{12,8},{1,5},{5,1},{9,13},{13,9},{2,6},{6,2},{1... | collective-permute-start | bytes 2752520 | tf_op jit(solution)/shard_map/ppermute | solution.py:828
  638.8 58.9 %collective-permute-start.73 = (bf16[2,4,2,128,384]{4,3,2,1,0:T(8,128)(2,1)}, bf16[2,4,2,128,384]{4,3,2,1,0:T(8,128)(2,1)}, u32[]{:S(2)}, u32[]{:S(2)}) collective-permute-start(bf16[2,4,2,128,384]{4,3,2,1,0:T(8,128)(2,1)} %pad_maximum_fusion.2.refs_8_), channel_id=1, source_target_pairs={{0,4},{4,0},{8,12},{12,8},{1,5},{5,1},{9,13},{13,9},{2,6},{6,2},{1... | collective-permute-start | bytes 4718600 | tf_op jit(solution)/shard_map/ppermute | solution.py:828
  670.5 27.2 %collective-permute-start.75 = (bf16[2,4,2,128,384]{4,3,2,1,0:T(8,128)(2,1)}, bf16[2,4,2,128,384]{4,3,2,1,0:T(8,128)(2,1)}, u32[]{:S(2)}, u32[]{:S(2)}) collective-permute-start(bf16[2,4,2,128,384]{4,3,2,1,0:T(8,128)(2,1)} %collective-permute-done.74.refs_10_), channel_id=1, source_target_pairs={{0,4},{4,0},{8,12},{12,8},{1,5},{5,1},{9,13},{13,9},{2,6},{6,2},{1... | collective-permute-start | bytes 4718600 | tf_op jit(solution)/shard_map/ppermute | solution.py:828
  673.9 43.2 %collective-permute-start.69 = (bf16[2,4,1,128,384]{4,3,2,1,0:T(8,128)(2,1)}, bf16[2,4,1,128,384]{4,3,2,1,0:T(8,128)(2,1)S(1)}, u32[]{:S(2)}, u32[]{:S(2)}) collective-permute-start(bf16[2,4,1,128,384]{4,3,2,1,0:T(8,128)(2,1)} %pad_maximum_fusion.10.refs_8_), channel_id=1, source_target_pairs={{0,4},{4,0},{8,12},{12,8},{1,5},{5,1},{9,13},{13,9},{2,6},{6,2},{1... | collective-permute-start | bytes 2359304 | tf_op jit(solution)/shard_map/ppermute | solution.py:828
  673.9 43.2 %collective-permute-start.71 = (bf16[2,4,1,128,384]{4,3,2,1,0:T(8,128)(2,1)}, bf16[2,4,1,128,384]{4,3,2,1,0:T(8,128)(2,1)S(1)}, u32[]{:S(2)}, u32[]{:S(2)}) collective-permute-start(bf16[2,4,1,128,384]{4,3,2,1,0:T(8,128)(2,1)} %collective-permute-done.70.refs_10_), channel_id=1, source_target_pairs={{0,4},{4,0},{8,12},{12,8},{1,5},{5,1},{9,13},{13,9},{2,6},{6,2},{1... | collective-permute-start | bytes 2359304 | tf_op jit(solution)/shard_map/ppermute | solution.py:828
  (112 other events, 1532.3 us)
Sparse Core Ops, SparseCore 0:
  365.5 52.9 all-reduce.7

commit v2 on v1

--- a/solution.py
+++ b/solution.py
@@ -691,8 +691,7 @@
 
 
 def weight_grad_kernel(place_ref, *refs):
-    rows_in, grads_in, slots_in = refs[:4], refs[4:8], refs[8:12]
-    rank_ref = refs[12]
+    rows_ref, grads_ref, slots_ref, rank_ref = refs[:4]
     gate_up_ref, down_ref, rows_buf, grads_buf = refs[-4:]
     half = down_ref.shape[-1]
     width = down_ref.shape[-2]
@@ -709,13 +708,13 @@
             ).astype(jnp.bfloat16)
             span = pl.ds(b * 128, 128)
             spot = 4 * k + (b ^ (2 * side))
-            rows_buf[spot] = dot(hot, rows_in[k][span, :]).astype(jnp.bfloat16)
-            grads_buf[spot] = dot(hot, grads_in[k][span, :]).astype(jnp.bfloat16)
+            rows_buf[spot] = dot(hot, rows_ref[k, span, :]).astype(jnp.bfloat16)
+            grads_buf[spot] = dot(hot, grads_ref[k, span, :]).astype(jnp.bfloat16)
     for q in range(4):
         slot = slice(q * CAP, (q + 1) * CAP)
         rows = jnp.concatenate([rows_buf[n, slot, :] for n in range(16)], axis=0)
         grads = jnp.concatenate([grads_buf[n, slot, :] for n in range(16)], axis=0)
-        taken = jnp.concatenate([slots_in[k][0, q, 0] for k in range(4)], axis=0)
+        taken = jnp.concatenate([slots_ref[0, k, q, 0] for k in range(4)], axis=0)
         made = dot(rows, taken[:, : 2 * width], 0, 0)
         gate_up_ref[0, q, 0, pl.ds(0, half, stride=2), :] = made[:, :width]
         gate_up_ref[0, q, 0, pl.ds(1, half, stride=2), :] = made[:, width:]
@@ -723,21 +722,19 @@
 
 
 def run_weight_grads(place, rows, grads, slots, rank, held, first, each):
-    sides, quarters, steps, slot_count, lanes = slots[0].shape
+    sides, _, quarters, steps, slot_count, lanes = slots.shape
     width = lanes // 3
-    tokens = rows[0].shape[0]
-    half = rank_half(rows, grads)
-    in_specs = (
-        [pl.BlockSpec((tokens, half), lambda j, a, sp: (0, 0))] * 8
-        + [
-            pl.BlockSpec(
-                (1, quarters, 1, slot_count, lanes), lambda j, a, sp: (a, 0, j, 0, 0)
-            )
-        ]
-        * 4
-        + [pl.BlockSpec((1, quarters, 1, 16, 128), lambda j, a, sp: (a, 0, first + j, 0, 0))]
-    )
-    operands = [place, *rows, *grads, *slots, rank]
+    half = rows.shape[-1]
+    in_specs = [
+        pl.BlockSpec(rows.shape, lambda j, a, sp: (0, 0, 0)),
+        pl.BlockSpec(rows.shape, lambda j, a, sp: (0, 0, 0)),
+        pl.BlockSpec(
+            (1, 4, quarters, 1, slot_count, lanes),
+            lambda j, a, sp: (sp[0] ^ a, 0, 0, j, 0, 0),
+        ),
+        pl.BlockSpec((1, quarters, 1, 16, 128), lambda j, a, sp: (a, 0, first + j, 0, 0)),
+    ]
+    operands = [place, rows, grads, slots, rank]
     aliases = {}
     if held is not None:
         in_specs += [pl.BlockSpec(memory_space=pl.ANY)] * 2
@@ -769,10 +766,6 @@
         compiler_params=vmem_params(2),
         name="weight_grads",
     )(*operands)
-
-
-def rank_half(rows, grads):
-    return min(array.shape[1] for array in (*rows, *grads))
 
 
 def swap_halves(values):
@@ -840,6 +833,9 @@
         distant = along(value)
         return [value, nearby, distant, beside(distant)]
 
+    def after(value, *earlier):
+        return lax.optimization_barrier((value, *earlier))[0]
+
     def own_first(value):
         return jnp.where(x_pos == 0, value, swap_halves(value))
 
@@ -895,16 +891,11 @@
         routes.reshape(tokens, -1).astype(low), ((0, 0), (0, 128 - routes.shape[-1]))
     )
     near_out = jnp.concatenate([own_first(d_out.reshape(tokens, model)), routes_low], axis=1)
-    far_out = across(near_out)
-
-    gate_up_mine = (
-        lax.dynamic_slice_in_dim(w_gate_up, x_pos * mine, mine, 0)
-        .transpose(0, 2, 1, 3)
-        .reshape(4, each, 2, half, width)
-    )
     away = (1 - x_pos) * mine + c_pos * each
     far_weights = []
-    for first, count in chunks:
+    last_x = sent
+    last_y = sent
+    for number, (first, count) in enumerate(chunks):
         gate_up_sent = (
             lax.dynamic_slice_in_dim(w_gate_up, away + first, count, 0)
             .transpose(0, 2, 1, 3)
@@ -916,14 +907,17 @@
             .transpose(0, 2, 1, 3)
             .reshape(count, half, 128)
         )
-        far_weights.append(all_ctx(across(jnp.concatenate([gate_up_sent, down_sent], axis=1))))
+        packed = jnp.concatenate([gate_up_sent, down_sent], axis=1)
+        got = across(after(packed, last_x))
+        last_x = got
+        nearby = beside(got)
+        distant = along(after(got, last_y))
+        last_y = distant
+        far_weights.append([got, nearby, distant, beside(distant)])
+        if number == 1:
+            far_out = across(after(near_out, got))
+            last_x = far_out
     down_all = w_down.reshape(2, 4, each, width, half)
-
-    heads_sent = lax.dynamic_slice_in_dim(w_out, core * (q_cols // 2), q_cols // 2, 0)
-    heads_both = jnp.concatenate([heads_sent, across(heads_sent)], axis=1)
-    heads_rest = jnp.stack([from_tp(heads_both, step) for step in range(1, tp_size)], axis=0)
-    heads_rest = jnp.concatenate([heads_both[None], heads_rest], axis=0)
-    out_full = ctx_join(heads_rest, beside(heads_rest), 1)
 
     seg_ids = jnp.arange(4, dtype=jnp.int32)
     seen_rows = []
@@ -957,6 +951,11 @@
     turned_part = unrotated[:, : q_cols + k_cols]
     rotated = (turned_part * cosines + turn_heads(turned_part) * sines).astype(low)
     query = rotated[:, :q_cols]
+    gate_up_mine = (
+        lax.dynamic_slice_in_dim(after(w_gate_up, query), x_pos * mine, mine, 0)
+        .transpose(0, 2, 1, 3)
+        .reshape(4, each, 2, half, width)
+    )
     key_value = jnp.concatenate(
         [rotated[:, q_cols:], unrotated[:, q_cols + k_cols :].astype(low)], axis=1
     )
@@ -976,8 +975,13 @@
         compiler_params=pltpu.CompilerParams(vmem_limit_bytes=60 * 1024 * 1024),
         name="attend",
     )(seen, query, *blocks)
-    heads = [head_low] + [from_tp(head_low, step) for step in range(1, tp_size)]
-    attended = dot(jnp.concatenate(heads, axis=1), out_full.reshape(tp_size * q_cols, model))
+    out_near = after(w_out, sent)
+    out_core = lax.dynamic_slice_in_dim(out_near, core * (q_cols // 2), q_cols // 2, 0)
+    out_got = across(out_core)
+    out_far = ctx_join(out_got, beside(out_got), 0)
+    attn_part = jnp.concatenate([dot(head_low, w_out), dot(head_low, out_far)], axis=1).astype(low)
+    attended = lax.psum(attn_part, "tp").astype(wide)
+    attended = after(attended, far_weights[1][0], far_weights[0][2])
     mixed = inputs + RESIDUAL_SCALE * attended
     scale_two = norm_scale(mixed)
     unit_two = mixed * scale_two
@@ -1091,10 +1095,12 @@
 
     moe_got = across(moe_all[tokens:].astype(low))
     moe_part = (moe_all[:tokens] + swap_halves(moe_got).astype(wide)).astype(low)
-    moe_sum = lax.psum(moe_part, "tp").astype(wide)
+    moe_sum = sum_tp(after(moe_part, gathered)).astype(wide)
     layer_out = own_first(mixed + RESIDUAL_SCALE * moe_sum)
 
-    head_grad = dot(attn_grad, out_full[0], 1, 1).astype(low)
+    head_grad = (
+        dot(attn_grad[:, :half], w_out, 1, 1) + dot(attn_grad[:, half:], out_far, 1, 1)
+    ).astype(low)
     query_grad, kv_grads = pl.pallas_call(
         attend_back_kernel,
         out_shape=(
@@ -1115,8 +1121,10 @@
     qkv_grad = jnp.concatenate(
         [turned_grad * cosines - turn_heads(turned_grad) * sines, kv_grad[:, k_cols:]], axis=1
     ).astype(low)
-    normed_one_grad = sum_tp(dot(qkv_grad, qkv_full, 1, 1).astype(low)).astype(wide)
-    gain_one_part = jnp.sum(normed_one_grad * unit_one, axis=0)
+    normed_one_part = dot(qkv_grad, qkv_full, 1, 1).astype(low)
+    normed_one_grad = sum_tp(normed_one_part).astype(wide)
+    gain_one_part = jnp.sum(normed_one_part.astype(wide) * unit_one, axis=0)
+    gain_one_part = sum([from_tp(gain_one_part, step) for step in range(1, tp_size)], gain_one_part)
     scaled_one = normed_one_grad * gain_one
     d_hidden = own_first(
         mixed_grad
@@ -1124,56 +1132,61 @@
         * (scaled_one - unit_one * jnp.mean(scaled_one * unit_one, axis=-1, keepdims=True))
     )
 
-    first_far = across(first_normed[:, half:])
-    early = all_ctx(
+    early = lax.all_gather(
         jnp.concatenate(
             [
-                jnp.concatenate([near_out[:, :half], first_normed[:, :half], routes_low], axis=1),
-                jnp.concatenate(
-                    [far_out[:, half:model], first_far, far_out[:, model:]], axis=1
-                ),
+                jnp.concatenate([near_out[:, :half], routes_low], axis=1),
+                far_out[:, half:],
             ],
             axis=0,
-        )
-    )
-    rows_two = all_ctx(jnp.concatenate([normed_two[:, :half], far[:, half:model]], axis=0))
-    heads_all = all_ctx(jnp.concatenate([head_low, across(head_low)], axis=0))
-    logit_pad = jnp.pad(logit_grad, ((0, 0), (0, 128 - experts)))
-    late_far = across(jnp.concatenate([attn_grad[:, half:], logit_pad], axis=1))
-    late_far = jnp.concatenate(
-        [
-            late_far[:, :half],
-            late_far[:, half + mine : half + experts],
-            late_far[:, half : half + mine],
-            late_far[:, half + experts :],
-        ],
-        axis=1,
-    )
-    late = all_ctx(
-        jnp.concatenate(
-            [jnp.concatenate([attn_grad[:, :half], logit_pad], axis=1), late_far], axis=0
-        )
-    )
-    qkv_all = all_ctx(jnp.concatenate([qkv_grad, across(qkv_grad)], axis=0))
-
-    all_routes = jnp.concatenate([part[:, 2 * half : 2 * half + top] for part in early], axis=0)
+        ),
+        "ctx",
+    )
+    rows_two = lax.all_gather(
+        jnp.concatenate([normed_two[:, :half], far[:, half:model]], axis=0), "ctx"
+    )
+    all_routes = early[:, :, half : half + top].reshape(4 * 2 * tokens, top)
     rank_all = ranks(all_routes, expert_ids).reshape(2, 4, each, 16, rows)
     grads = None
     for (first, count), part in zip(chunks, slots):
-        pair = all_ctx(jnp.stack([part, across(part)]))
+        pair = lax.all_gather(part, ("fsdp", "ctx")).reshape(2, 4, *part.shape)
         grads = run_weight_grads(place, rows_two, early, pair, rank_all, grads, first, each)
     d_gate_up = grads[0].reshape(experts, half, 2, width)
     d_down = grads[1].reshape(experts, width, half)
 
-    def over_tokens(left, right):
-        return sum(dot(a, b, 0, 0) for a, b in zip(left, right))
-
-    d_qkv = over_tokens([part[:, half : 2 * half] for part in early], qkv_all)
-    d_w_out = over_tokens(heads_all, [part[:, :half] for part in late])
-    d_router = over_tokens(rows_two, [part[:, half : half + experts] for part in late])
-    d_router = jnp.where(
-        x_pos == 0, d_router, jnp.concatenate([d_router[:, mine:], d_router[:, :mine]], axis=1)
-    )
+    def sum_plane(part):
+        share = part.shape[1] // 2
+        kept = lax.dynamic_slice_in_dim(part, core * share, share, 1)
+        given = lax.dynamic_slice_in_dim(part, (1 - core) * share, share, 1)
+        kept = kept + beside(given.astype(low)).astype(wide)
+        total = kept[0] + across(kept[1].astype(low)).astype(wide)
+        total = (total + along(total.astype(low)).astype(wide)).astype(low)
+        return ctx_join(total, beside(total), 0).astype(wide)
+
+    logit_cols = jnp.where(
+        x_pos == 0,
+        logit_grad,
+        jnp.concatenate([logit_grad[:, mine:], logit_grad[:, :mine]], axis=1),
+    )
+
+    def both(left, right):
+        return jnp.stack(
+            [dot(left, right[:, :half], 0, 0), dot(left, right[:, half:], 0, 0)], axis=0
+        )
+
+    side_grads = sum_plane(
+        jnp.concatenate(
+            [
+                both(head_low, attn_grad),
+                both(logit_cols, normed_two),
+                jnp.pad(gain_two_part.reshape(2, 1, half), ((0, 0), (0, 23), (0, 0))),
+            ],
+            axis=1,
+        )
+    )
+    d_w_out = side_grads[:q_cols]
+    d_router = side_grads[q_cols : q_cols + experts].T
+    d_qkv = sum_plane(dot(first_normed, qkv_grad, 0, 0).reshape(2, half, qkv_cols))
 
     def sum_gain(part):
         part = part + beside(part)
@@ -1188,7 +1201,7 @@
         d_qkv[:, q_cols : q_cols + k_cols],
         d_qkv[:, q_cols + k_cols :],
         d_w_out,
-        sum_gain(gain_two_part),
+        side_grads[q_cols + experts],
         d_router,
         d_gate_up,
         d_down,

time: 745 us -> 638 us (0.86)
  waiting for transfers between devices: 359 us -> 310 us
  other arithmetic: 70.8 us -> 45.6 us
  starting transfers between devices: 85.5 us -> 71 us
  local copies, waits for them, and re-layouts: 72.5 us -> 58.5 us
  matrix products: 22.4 us -> 13.9 us
    ppermute x15 -> x8, waiting for transfers between devices: 178 us -> 93.1 us  [along(): return lax.ppermute(value, 'ctx', [(i, i ^ 2) for i in range(4)])]
    ppermute x18 -> x12, waiting for transfers between devices: 95.1 us -> 126 us  [across(): return lax.ppermute(value, 'fsdp', [(0, 1), (1, 0)])]
    ppermute x18 -> x21, waiting for transfers between devices: 84.6 us -> 61.7 us  [from_tp(): lax.ppermute(value, 'tp', [((i + step) % tp_size, i) for i in range(tp_si...]
    psum x1, waiting for transfers between devices: 0.01 us -> 22.8 us  [fast_body(): attended = lax.psum(attn_part, 'tp').astype(wide)]
    dot_general x20 -> x15, matrix products: 22.4 us -> 13.9 us  [dot(): lax.dot_general(left, right, (((left_dim,), (right_dim,)), ((), ())), pre...]
    ppermute x18 -> x12, starting transfers between devices: 19.3 us -> 11.6 us  [across(): return lax.ppermute(value, 'fsdp', [(0, 1), (1, 0)])]
    another operation x5 -> x2, other arithmetic: 7.93 us -> 0.35 us  [the longest x3 7.58 us: fast_body(): pair = all_ctx(jnp.stack([part, across(part)]))]
    ppermute x18 -> x21, starting transfers between devices: 48.6 us -> 41.3 us  [from_tp(): lax.ppermute(value, 'tp', [((i + step) % tp_size, i) for i in range(tp_si...]
  transfers between devices with their start and end apart: 81 -> 63, of which waited for: 28 -> 30; matrix products, arithmetic and copies ran while one was open for 21% -> 16% of each run, Pallas kernels for 13% -> 15%
where the time goes in v2:
time: 638 us; the launch traced here: 629 us
  waiting for transfers between devices  310 us (49%)
  Pallas kernels  110 us (17%)
  starting transfers between devices  71 us (11%)
  local copies, waits for them, and re-layouts  58.5 us (9%)
  other arithmetic  45.6 us (7%)
  between operations  19.2 us (3%)
  matrix products  13.9 us (2%)
    ppermute x12, waiting for transfers between devices, across(): return lax.ppermute(value, 'fsdp', [(0, 1), (1, 0)])  126 us
    ppermute x8, waiting for transfers between devices, along(): return lax.ppermute(value, 'ctx', [(i, i ^ 2) for i in range(4)])  93.1 us
    ppermute x21, waiting for transfers between devices, from_tp(): lax.ppermute(value, 'tp', [((i + step) % tp_size, i) for i in range(tp_si...  61.7 us
    pallas_call x3, Pallas kernels, run_weight_grads(): pl.pallas_call(weight_grad_kernel, out_shape=(jax.ShapeDtypeStruct((sides...  51.5 us
    pallas_call x3, Pallas kernels, run_experts(): pl.pallas_call(expert_kernel, out_shape=(total, total, slots, gate_grads)...  47.6 us
    ppermute x21, starting transfers between devices, from_tp(): lax.ppermute(value, 'tp', [((i + step) % tp_size, i) for i in range(tp_si...  41.3 us
    psum x1, waiting for transfers between devices, fast_body(): attended = lax.psum(attn_part, 'tp').astype(wide)  22.8 us
    ppermute x8, starting transfers between devices, along(): return lax.ppermute(value, 'ctx', [(i, i ^ 2) for i in range(4)])  15.7 us
  transfers between devices with their start and end apart: 63, of which 30 were waited for; matrix products, arithmetic and copies ran while one was open for 16% of the time, Pallas kernels for 15%

profile of v2, /device:TPU:0, one launch (start us, length us, event | category | flops | bytes accessed | tf_op | source)
XLA Modules:
  0.0 628.8 jit_solution(10325014920416416998)
XLA Ops:
  14.1 2.9 collective-permute-start
  17.7 1.9 fusion.90
  19.7 1.9 fusion.91
  21.6 2.7 fusion.108
  24.3 2.7 fusion.109
  30.0 1.9 constant_dynamic-slice_fusion.8
  32.4 1.9 copy.191
  35.5 2.5 dynamic-slice_bitcast_fusion.1
  43.6 2.1 collective-permute-start.7
  45.7 7.8 %collective-permute-done.5 = bf16[192,768]{1,0:T(8,128)(2,1)} collective-permute-done((bf16[192,768]{1,0:T(8,128)(2,1)S(1)}, bf16[192,768]{1,0:T(8,128)(2,1)}, u32[]{:S(2)}, u32[]{:S(2)}) %collective-permute-start.5) | collective-permute-done | bytes 294944 | tf_op jit(solution)/shard_map/ppermute | solution.py:818
  59.1 19.1 %collective-permute-done.7.other0 = bf16[2,2304,128]{2,1,0:T(8,128)(2,1)} collective-permute-done((bf16[2,2304,128]{2,1,0:T(8,128)(2,1)}, bf16[2,2304,128]{2,1,0:T(8,128)(2,1)}, u32[]{:S(2)}, u32[]{:S(2)}) %collective-permute-start.7) | collective-permute-done | bytes 1179680 | tf_op jit(solution)/shard_map/ppermute | solution.py:818
  80.9 3.1 collective-permute-done.3.kv2
  84.0 5.1 add_bitcast_fusion
  91.7 5.2 attend.1
  99.0 7.0 %collective-permute-done.8.other0 = bf16[2,2304,128]{2,1,0:T(8,128)(2,1)} collective-permute-done((bf16[2,2304,128]{2,1,0:T(8,128)(2,1)}, bf16[2,2304,128]{2,1,0:T(8,128)(2,1)}, u32[]{:S(2)}, u32[]{:S(2)}) %collective-permute-start.8) | collective-permute-done | bytes 1179680 | tf_op jit(solution)/shard_map/ppermute | solution.py:818
  107.5 17.9 %collective-permute-done.11.far_out_ref = bf16[256,1664]{1,0:T(8,128)(2,1)S(1)} collective-permute-done((bf16[256,1664]{1,0:T(8,128)(2,1)S(1)}, bf16[256,1664]{1,0:T(8,128)(2,1)S(1)}, u32[]{:S(2)}, u32[]{:S(2)}) %collective-permute-start.11) | collective-permute-done | bytes 852000 | tf_op jit(solution)/shard_map/ppermute | solution.py:818
  129.7 22.8 %all-reduce.8.cloned.1.call-done = bf16[256,1536]{1,0:T(8,128)(2,1)} async-done(((bf16[256,1536]{1,0:T(8,128)(2,1)}), bf16[256,1536]{1,0:T(8,128)(2,1)}) %all-reduce.8.cloned.1.call-update) | async-done | bytes 786448 | tf_op jit(solution)/shard_map/psum | solution.py:983
  153.8 17.8 %collective-permute-done.9.other2 = bf16[2,2304,128]{2,1,0:T(8,128)(2,1)} collective-permute-done((bf16[2,2304,128]{2,1,0:T(8,128)(2,1)}, bf16[2,2304,128]{2,1,0:T(8,128)(2,1)}, u32[]{:S(2)}, u32[]{:S(2)}) %collective-permute-start.9) | collective-permute-done | bytes 1179680 | tf_op jit(solution)/shard_map/ppermute | solution.py:824
  175.5 11.9 %collective-permute-done.10.far_ref = bf16[256,1664]{1,0:T(8,128)(2,1)S(1)} collective-permute-done((bf16[256,1664]{1,0:T(8,128)(2,1)S(1)}, bf16[256,1664]{1,0:T(8,128)(2,1)S(1)}, u32[]{:S(2)}, u32[]{:S(2)}) %collective-permute-start.10) | collective-permute-done | bytes 852000 | tf_op jit(solution)/shard_map/ppermute | solution.py:818
  190.7 7.0 %dynamic-slice_bitcast_fusion = bf16[20,2,768,128]{3,1,2,0:T(2,128)(2,1)S(1)} fusion(bf16[40,768,2,128]{3,2,1,0:T(2,128)(2,1)} %param.23, s32[]{:T(128)S(6)} %select_n.311), kind=kLoop, calls=%fused_computation | loop fusion | bytes 15728644 | tf_op jit(solution)/shard_map/transpose | solution.py:956
  197.8 5.1 copy.178
  206.8 16.2 %experts.3 = (f32[512,1536]{1,0:T(8,128)}, f32[512,1536]{1,0:T(8,128)}, bf16[4,2,128,384]{3,2,1,0:T(8,128)(2,1)}, f32[4,2,4,128]{3,2,1,0:T(4,128)}) custom-call(s32[2]{0:T(128)} %pad_add_fusion.1.place_ref, bf16[256,1664]{1,0:T(8,128)(2,1)} %copy-done.6, bf16[256,1664]{1,0:T(8,128)(2,1)} %copy-done.10, bf16[256,1664]{1,0:T(8,128)(2,1)} %copy-done.5, ...), custom_call_target="tpu_custom_call" | custom-call | tf_op jit(solution)/shard_map/experts/pallas_call | solution.py:668
  223.5 2.5 collective-permute-start.14
  226.0 37.5 %collective-permute-done.14.other2 = bf16[2,2304,128]{2,1,0:T(8,128)(2,1)S(1)} collective-permute-done((bf16[2,2304,128]{2,1,0:T(8,128)(2,1)}, bf16[2,2304,128]{2,1,0:T(8,128)(2,1)S(1)}, u32[]{:S(2)}, u32[]{:S(2)}) %collective-permute-start.14) | collective-permute-done | bytes 1179680 | tf_op jit(solution)/shard_map/ppermute | solution.py:824
  263.5 2.8 collective-permute-done.18.other3
  267.4 18.2 %experts.4 = (f32[512,1536]{1,0:T(8,128)}, f32[512,1536]{1,0:T(8,128)}, bf16[4,2,128,384]{3,2,1,0:T(8,128)(2,1)}, f32[4,2,4,128]{3,2,1,0:T(4,128)}) custom-call(s32[2]{0:T(128)} %pad_add_fusion.1.place_ref, bf16[256,1664]{1,0:T(8,128)(2,1)} %copy-done.6, bf16[256,1664]{1,0:T(8,128)(2,1)} %copy-done.10, ...), custom_call_target="tpu_custom_call", output_to_operand_aliasing={{0}: (13, {}), {1}: (14, {})} | custom-call | tf_op jit(solution)/shard_map/experts/pallas_call | solution.py:668
  288.5 22.7 %collective-permute-done.12.other0 = bf16[1,2304,128]{2,1,0:T(8,128)(2,1)S(1)} collective-permute-done((bf16[1,2304,128]{2,1,0:T(8,128)(2,1)S(1)}, bf16[1,2304,128]{2,1,0:T(8,128)(2,1)S(1)}, u32[]{:S(2)}, u32[]{:S(2)}) %collective-permute-start.12) | collective-permute-done | bytes 589856 | tf_op jit(solution)/shard_map/ppermute | solution.py:818
  311.1 3.3 collective-permute-start.15
  314.4 19.7 %collective-permute-done.15.other2 = bf16[1,2304,128]{2,1,0:T(8,128)(2,1)S(1)} collective-permute-done((bf16[1,2304,128]{2,1,0:T(8,128)(2,1)S(1)}, bf16[1,2304,128]{2,1,0:T(8,128)(2,1)S(1)}, u32[]{:S(2)}, u32[]{:S(2)}) %collective-permute-start.15) | collective-permute-done | bytes 589856 | tf_op jit(solution)/shard_map/ppermute | solution.py:824
  334.1 2.4 collective-permute-done.16.other3
  337.3 13.1 %experts.5 = (f32[512,1536]{1,0:T(8,128)}, f32[512,1536]{1,0:T(8,128)}, bf16[4,1,128,384]{3,2,1,0:T(8,128)(2,1)}, f32[4,1,4,128]{3,2,1,0:T(4,128)}) custom-call(s32[2]{0:T(128)} %pad_add_fusion.1.place_ref, bf16[256,1664]{1,0:T(8,128)(2,1)} %copy-done.6, bf16[256,1664]{1,0:T(8,128)(2,1)} %copy-done.10, ...), custom_call_target="tpu_custom_call", output_to_operand_aliasing={{0}: (13, {}), {1}: (14, {})} | custom-call | tf_op jit(solution)/shard_map/experts/pallas_call | solution.py:668
  350.5 2.4 slice.571
  356.9 2.0 collective-permute-start.22
  359.0 17.2 %collective-permute-done.21 = bf16[256,1536]{1,0:T(8,128)(2,1)} collective-permute-done((bf16[256,1536]{1,0:T(8,128)(2,1)}, bf16[256,1536]{1,0:T(8,128)(2,1)}, u32[]{:S(2)}, u32[]{:S(2)}) %collective-permute-start.21) | collective-permute-done | bytes 786464 | tf_op jit(solution)/shard_map/ppermute | solution.py:818
  379.2 4.9 collective-permute-start.29
  384.7 18.9 %collective-permute-done.22 = bf16[256,1664]{1,0:T(8,128)(2,1)S(1)} collective-permute-done((bf16[256,1664]{1,0:T(8,128)(2,1)}, bf16[256,1664]{1,0:T(8,128)(2,1)S(1)}, u32[]{:S(2)}, u32[]{:S(2)}) %collective-permute-start.22) | collective-permute-done | bytes 852000 | tf_op jit(solution)/shard_map/ppermute | solution.py:818
  404.0 4.1 collective-permute-start.23
  409.1 2.9 collective-permute-start.34
  413.9 4.3 collective-permute-start.32
  418.2 15.6 %collective-permute-done.24 = bf16[64,1664]{1,0:T(8,128)(2,1)S(1)} collective-permute-done((bf16[64,1664]{1,0:T(8,128)(2,1)S(1)}, bf16[64,1664]{1,0:T(8,128)(2,1)S(1)}, u32[]{:S(2)}, u32[]{:S(2)}) %collective-permute-start.24) | collective-permute-done | bytes 213024 | tf_op jit(solution)/shard_map/ppermute | solution.py:827
  434.0 2.0 collective-permute-start.27
  436.0 4.0 collective-permute-start.26
  440.0 7.2 %collective-permute-done.33 = bf16[64,1536]{1,0:T(8,128)(2,1)S(1)} collective-permute-done((bf16[64,1536]{1,0:T(8,128)(2,1)S(1)}, bf16[64,1536]{1,0:T(8,128)(2,1)S(1)}, u32[]{:S(2)}, u32[]{:S(2)}) %collective-permute-start.33) | collective-permute-done | bytes 196640 | tf_op jit(solution)/shard_map/ppermute | solution.py:827
  447.3 11.1 %collective-permute-done.26 = bf16[64,1664]{1,0:T(8,128)(2,1)S(1)} collective-permute-done((bf16[64,1664]{1,0:T(8,128)(2,1)S(1)}, bf16[64,1664]{1,0:T(8,128)(2,1)S(1)}, u32[]{:S(2)}, u32[]{:S(2)}) %collective-permute-start.26) | collective-permute-done | bytes 213024 | tf_op jit(solution)/shard_map/ppermute | solution.py:827
  461.4 2.0 multiply_convert_fusion
  466.6 2.3 fusion.12.grad_ref
  468.9 6.1 attend_back.1
  479.3 3.0 collective-permute-start.36
  483.7 2.3 collective-permute-done.36
  488.8 5.6 collective-permute-start.37
  496.0 3.8 collective-permute-done.37
  499.8 4.4 collective-permute-done.39
  504.2 5.8 collective-permute-done.38
  510.2 3.3 collective-permute-start.41
  514.8 9.1 %collective-permute-done.40 = bf16[64,1536]{1,0:T(8,128)(2,1)S(1)} collective-permute-done((bf16[64,1536]{1,0:T(8,128)(2,1)S(1)}, bf16[64,1536]{1,0:T(8,128)(2,1)S(1)}, u32[]{:S(2)}, u32[]{:S(2)}) %collective-permute-start.40) | collective-permute-done | bytes 196640 | tf_op jit(solution)/shard_map/ppermute | solution.py:827
  524.0 2.3 collective-permute-done.41
  527.1 3.9 collective-permute-start.45
  531.0 2.6 collective-permute-start.43
  542.6 5.4 collective-permute-done.55
  548.2 3.8 collective-permute-done.50
  556.6 7.4 %collective-permute-done.51 = bf16[384,640]{1,0:T(8,128)(2,1)S(1)} collective-permute-done((bf16[384,640]{1,0:T(8,128)(2,1)S(1)}, bf16[384,640]{1,0:T(8,128)(2,1)S(1)}, u32[]{:S(2)}, u32[]{:S(2)}) %collective-permute-start.51) | collective-permute-done | bytes 491552 | tf_op jit(solution)/shard_map/ppermute | solution.py:824
  569.4 19.3 %weight_grads.3 = (f32[2,4,5,1536,128]{4,3,2,1,0:T(8,128)}, f32[2,4,5,128,768]{4,3,2,1,0:T(8,128)}) custom-call(s32[2]{0:T(128)} %pad_add_fusion.1.place_ref, bf16[4,512,768]{2,1,0:T(8,128)(2,1)} %bitcast.239, bf16[4,512,896]{2,1,0:T(8,128)(2,1)} %bitcast.236, bf16[2,4,4,2,128,384]{5,4,3,2,1,0:T(8,128)(2,1)} %bitcast.244, s32[2,4,5,16,128]{4,3,2,1,0:T(8,128)} %bitcast.245), custom_call_target="tpu_custom_call" | custom-call | tf_op jit(solution)/shard_map/weight_grads/pallas_call | solution.py:743
  588.7 19.3 %weight_grads.4 = (f32[2,4,5,1536,128]{4,3,2,1,0:T(8,128)}, f32[2,4,5,128,768]{4,3,2,1,0:T(8,128)}) custom-call(s32[2]{0:T(128)} %pad_add_fusion.1.place_ref, bf16[4,512,768]{2,1,0:T(8,128)(2,1)} %bitcast.240, bf16[4,512,896]{2,1,0:T(8,128)(2,1)} %bitcast.237, ...), custom_call_target="tpu_custom_call", output_to_operand_aliasing={{0}: (5, {}), {1}: (6, {})} | custom-call | tf_op jit(solution)/shard_map/weight_grads/pallas_call | solution.py:743
  608.0 12.8 %weight_grads.5 = (f32[2,4,5,1536,128]{4,3,2,1,0:T(8,128)}, f32[2,4,5,128,768]{4,3,2,1,0:T(8,128)}) custom-call(s32[2]{0:T(128)} %pad_add_fusion.1.place_ref, bf16[4,512,768]{2,1,0:T(8,128)(2,1)} %bitcast.241, bf16[4,512,896]{2,1,0:T(8,128)(2,1)} %bitcast.238, ...), custom_call_target="tpu_custom_call", output_to_operand_aliasing={{0}: (5, {}), {1}: (6, {})} | custom-call | tf_op jit(solution)/shard_map/weight_grads/pallas_call | solution.py:743
  (456 shorter events, 99.9 us)
Async XLA Ops:
  8.0 144.5 %all-reduce.8.cloned.1.call-start = ((), (), s32[]{:S(2)}) async-start(), calls=%async_computation | async-start | bytes 1572864 | tf_op jit(solution)/shard_map/psum | solution.py:983
  14.1 27.1 %collective-permute-start = (bf16[384,768]{0,1:T(8,128)(2,1)}, bf16[384,768]{0,1:T(8,128)(2,1)}, u32[]{:S(2)}, u32[]{:S(2)}) collective-permute-start(bf16[384,768]{0,1:T(8,128)(2,1)} %fusion.22), channel_id=1, source_target_pairs={{0,16},{16,0},{1,17},{17,1},{2,18},{18,2},{3,19},{19,3},{4,20},{20... | collective-permute-start | bytes 1769480 | tf_op jit(solution)/shard_map/ppermute | solution.py:818
  41.2 12.2 %collective-permute-start.1 = (bf16[384,768]{0,1:T(8,128)(2,1)}, bf16[384,768]{0,1:T(8,128)(2,1)}, u32[]{:S(2)}, u32[]{:S(2)}) collective-permute-start(bf16[384,768]{0,1:T(8,128)(2,1)} %collective-permute-done), channel_id=1, source_target_pairs={{0,4},{4,0},{8,12},{12,8},{1,5},{5,1},{9,13},{13,9},{2,6},{6,2},{1... | collective-permute-start | bytes 1769480 | tf_op jit(solution)/shard_map/ppermute | solution.py:821
  43.4 10.0 %collective-permute-start.5 = (bf16[192,768]{1,0:T(8,128)(2,1)S(1)}, bf16[192,768]{1,0:T(8,128)(2,1)}, u32[]{:S(2)}, u32[]{:S(2)}) collective-permute-start(bf16[192,768]{1,0:T(8,128)(2,1)S(1)} %constant_dynamic-slice_fusion.10), channel_id=1, source_target_pairs={{0,16},{16,0},{1,17},{17,1},{2,18},{18,2},{3,19},{19,3},{4,20},{20... | collective-permute-start | bytes 884744 | tf_op jit(solution)/shard_map/ppermute | solution.py:818
  43.6 34.6 %collective-permute-start.7 = (bf16[2,2304,128]{2,1,0:T(8,128)(2,1)}, bf16[2,2304,128]{2,1,0:T(8,128)(2,1)}, u32[]{:S(2)}, u32[]{:S(2)}) collective-permute-start(bf16[2,2304,128]{2,1,0:T(8,128)(2,1)} %pad_maximum_fusion.2), channel_id=1, source_target_pairs={{0,16},{16,0},{1,17},{17,1},{2,18},{18,2},{3,19},{19,3},{4,20},{20... | collective-permute-start | bytes 3538952 | tf_op jit(solution)/shard_map/ppermute | solution.py:818
  53.5 43.3 %collective-permute-start.6 = (bf16[192,768]{1,0:T(8,128)(2,1)}, bf16[192,768]{1,0:T(8,128)(2,1)}, u32[]{:S(2)}, u32[]{:S(2)}) collective-permute-start(bf16[192,768]{1,0:T(8,128)(2,1)} %collective-permute-done.5), channel_id=1, source_target_pairs={{0,4},{4,0},{8,12},{12,8},{1,5},{5,1},{9,13},{13,9},{2,6},{6,2},{1... | collective-permute-start | bytes 884744 | tf_op jit(solution)/shard_map/ppermute | solution.py:821
  57.9 113.8 %copy-start.7 = (bf16[256,1536]{1,0:T(8,128)(2,1)}, bf16[256,1536]{1,0:T(8,128)(2,1)S(1)}, u32[]{:S(2)}) copy-start(bf16[256,1536]{1,0:T(8,128)(2,1)S(1)} %get-tuple-element.163) | copy-start | bytes 2359300
  78.2 27.8 %collective-permute-start.8 = (bf16[2,2304,128]{2,1,0:T(8,128)(2,1)}, bf16[2,2304,128]{2,1,0:T(8,128)(2,1)}, u32[]{:S(2)}, u32[]{:S(2)}) collective-permute-start(bf16[2,2304,128]{2,1,0:T(8,128)(2,1)} %pad_maximum_fusion.1), channel_id=1, source_target_pairs={{0,16},{16,0},{1,17},{17,1},{2,18},{18,2},{3,19},{19,3},{4,20},{20... | collective-permute-start | bytes 3538952 | tf_op jit(solution)/shard_map/ppermute | solution.py:818
  78.9 5.0 collective-permute-start.3
  80.8 9.5 %collective-permute-start.2 = (bf16[256,256]{1,0:T(8,128)(2,1)S(1)}, bf16[256,256]{1,0:T(8,128)(2,1)S(1)}, u32[]{:S(2)}, u32[]{:S(2)}) collective-permute-start(bf16[256,256]{1,0:T(8,128)(2,1)S(1)} %pad_maximum_fusion.17.kv0), channel_id=1, source_target_pairs={{0,4},{4,0},{8,12},{12,8},{1,5},{5,1},{9,13},{13,9},{2,6},{6,2},{1... | collective-permute-start | bytes 393224 | tf_op jit(solution)/shard_map/ppermute | solution.py:821
  84.0 6.4 %collective-permute-start.4 = (bf16[256,256]{1,0:T(8,128)(2,1)S(1)}, bf16[256,256]{1,0:T(8,128)(2,1)S(1)}, u32[]{:S(2)}, u32[]{:S(2)}) collective-permute-start(bf16[256,256]{1,0:T(8,128)(2,1)S(1)} %collective-permute-done.3.kv2), channel_id=1, source_target_pairs={{0,4},{4,0},{8,12},{12,8},{1,5},{5,1},{9,13},{13,9},{2,6},{6,2},{1... | collective-permute-start | bytes 393224 | tf_op jit(solution)/shard_map/ppermute | solution.py:821
  106.0 19.5 %collective-permute-start.11 = (bf16[256,1664]{1,0:T(8,128)(2,1)S(1)}, bf16[256,1664]{1,0:T(8,128)(2,1)S(1)}, u32[]{:S(2)}, u32[]{:S(2)}) collective-permute-start(bf16[256,1664]{1,0:T(8,128)(2,1)S(1)} %pad_maximum_fusion.6.near_out_ref), channel_id=1, source_target_pairs={{0,16},{16,0},{1,17},{17,1},{2,18},{18,2},{3,19},{19,3},{4,20},{20... | collective-permute-start | bytes 2555912 | tf_op jit(solution)/shard_map/ppermute | solution.py:818
  107.5 456.8 %all-gather.13.cloned.1.call-start = ((), (), s32[]{:S(2)}) async-start(), calls=%async_computation.2 | async-start | bytes 4587520 | tf_op jit(solution)/shard_map/all_gather | solution.py:1135
  126.6 442.8 %all-gather.11.cloned.1.call-start = ((), (), s32[]{:S(2)}) async-start(), calls=%async_computation.1 | async-start | bytes 3932160 | tf_op jit(solution)/shard_map/all_gather | solution.py:1145
  126.8 44.8 %collective-permute-start.9 = (bf16[2,2304,128]{2,1,0:T(8,128)(2,1)}, bf16[2,2304,128]{2,1,0:T(8,128)(2,1)}, u32[]{:S(2)}, u32[]{:S(2)}) collective-permute-start(bf16[2,2304,128]{2,1,0:T(8,128)(2,1)} %collective-permute-done.7.other0), channel_id=1, source_target_pairs={{0,8},{4,12},{8,0},{12,4},{1,9},{5,13},{9,1},{13,5},{2,10},{6,14},... | collective-permute-start | bytes 3538952 | tf_op jit(solution)/shard_map/ppermute | solution.py:824
  174.7 12.7 %collective-permute-start.10 = (bf16[256,1664]{1,0:T(8,128)(2,1)S(1)}, bf16[256,1664]{1,0:T(8,128)(2,1)S(1)}, u32[]{:S(2)}, u32[]{:S(2)}) collective-permute-start(bf16[256,1664]{1,0:T(8,128)(2,1)S(1)} %pad_maximum_fusion.5.near_ref), channel_id=1, source_target_pairs={{0,16},{16,0},{1,17},{17,1},{2,18},{18,2},{3,19},{19,3},{4,20},{20... | collective-permute-start | bytes 2555912 | tf_op jit(solution)/shard_map/ppermute | solution.py:818
  189.3 380.0 %all-gather.19.cloned.1.call-start = ((), (), s32[]{:S(2)}) async-start(), calls=%async_computation.5 | async-start | bytes 7077888 | tf_op jit(solution)/shard_map/all_gather | solution.py:1152
  190.2 16.5 %collective-permute-start.19 = (bf16[2,2304,128]{2,1,0:T(8,128)(2,1)}, bf16[2,2304,128]{2,1,0:T(8,128)(2,1)}, u32[]{:S(2)}, u32[]{:S(2)}) collective-permute-start(bf16[2,2304,128]{2,1,0:T(8,128)(2,1)} %collective-permute-done.7.other0), channel_id=1, source_target_pairs={{0,4},{4,0},{8,12},{12,8},{1,5},{5,1},{9,13},{13,9},{2,6},{6,2},{1... | collective-permute-start | bytes 3538952 | tf_op jit(solution)/shard_map/ppermute | solution.py:821
  190.2 16.5 %collective-permute-start.20 = (bf16[2,2304,128]{2,1,0:T(8,128)(2,1)}, bf16[2,2304,128]{2,1,0:T(8,128)(2,1)}, u32[]{:S(2)}, u32[]{:S(2)}) collective-permute-start(bf16[2,2304,128]{2,1,0:T(8,128)(2,1)} %collective-permute-done.9.other2), channel_id=1, source_target_pairs={{0,4},{4,0},{8,12},{12,8},{1,5},{5,1},{9,13},{13,9},{2,6},{6,2},{1... | collective-permute-start | bytes 3538952 | tf_op jit(solution)/shard_map/ppermute | solution.py:821
  223.0 365.7 %all-gather.17.cloned.1.call-start = ((), (), s32[]{:S(2)}) async-start(), calls=%async_computation.4 | async-start | bytes 7077888 | tf_op jit(solution)/shard_map/all_gather | solution.py:1152
  223.5 40.0 %collective-permute-start.14 = (bf16[2,2304,128]{2,1,0:T(8,128)(2,1)}, bf16[2,2304,128]{2,1,0:T(8,128)(2,1)S(1)}, u32[]{:S(2)}, u32[]{:S(2)}) collective-permute-start(bf16[2,2304,128]{2,1,0:T(8,128)(2,1)} %collective-permute-done.8.other0), channel_id=1, source_target_pairs={{0,8},{4,12},{8,0},{12,4},{1,9},{5,13},{9,1},{13,5},{2,10},{6,14},... | collective-permute-start | bytes 3538952 | tf_op jit(solution)/shard_map/ppermute | solution.py:824
  226.0 37.5 %collective-permute-start.17 = (bf16[2,2304,128]{2,1,0:T(8,128)(2,1)}, bf16[2,2304,128]{2,1,0:T(8,128)(2,1)S(1)}, u32[]{:S(2)}, u32[]{:S(2)}) collective-permute-start(bf16[2,2304,128]{2,1,0:T(8,128)(2,1)} %collective-permute-done.8.other0), channel_id=1, source_target_pairs={{0,4},{4,0},{8,12},{12,8},{1,5},{5,1},{9,13},{13,9},{2,6},{6,2},{1... | collective-permute-start | bytes 3538952 | tf_op jit(solution)/shard_map/ppermute | solution.py:821
  263.5 2.8 collective-permute-start.18
  285.6 322.4 %all-gather.15.cloned.1.call-start = ((), (), s32[]{:S(2)}) async-start(), calls=%async_computation.3 | async-start | bytes 3538944 | tf_op jit(solution)/shard_map/all_gather | solution.py:1152
  288.4 22.8 %collective-permute-start.12 = (bf16[1,2304,128]{2,1,0:T(8,128)(2,1)S(1)}, bf16[1,2304,128]{2,1,0:T(8,128)(2,1)S(1)}, u32[]{:S(2)}, u32[]{:S(2)}) collective-permute-start(bf16[1,2304,128]{2,1,0:T(8,128)(2,1)S(1)} %pad_maximum_fusion.9), channel_id=1, source_target_pairs={{0,16},{16,0},{1,17},{17,1},{2,18},{18,2},{3,19},{19,3},{4,20},{20... | collective-permute-start | bytes 1769480 | tf_op jit(solution)/shard_map/ppermute | solution.py:818
  311.1 23.0 %collective-permute-start.15 = (bf16[1,2304,128]{2,1,0:T(8,128)(2,1)S(1)}, bf16[1,2304,128]{2,1,0:T(8,128)(2,1)S(1)}, u32[]{:S(2)}, u32[]{:S(2)}) collective-permute-start(bf16[1,2304,128]{2,1,0:T(8,128)(2,1)S(1)} %collective-permute-done.12.other0), channel_id=1, source_target_pairs={{0,8},{4,12},{8,0},{12,4},{1,9},{5,13},{9,1},{13,5},{2,10},{6,14},... | collective-permute-start | bytes 1769480 | tf_op jit(solution)/shard_map/ppermute | solution.py:824
  314.4 19.7 %collective-permute-start.13 = (bf16[1,2304,128]{2,1,0:T(8,128)(2,1)S(1)}, bf16[1,2304,128]{2,1,0:T(8,128)(2,1)S(1)}, u32[]{:S(2)}, u32[]{:S(2)}) collective-permute-start(bf16[1,2304,128]{2,1,0:T(8,128)(2,1)S(1)} %collective-permute-done.12.other0), channel_id=1, source_target_pairs={{0,4},{4,0},{8,12},{12,8},{1,5},{5,1},{9,13},{13,9},{2,6},{6,2},{1... | collective-permute-start | bytes 1769480 | tf_op jit(solution)/shard_map/ppermute | solution.py:821
  334.1 2.4 collective-permute-start.16
  352.9 23.3 %collective-permute-start.21 = (bf16[256,1536]{1,0:T(8,128)(2,1)}, bf16[256,1536]{1,0:T(8,128)(2,1)}, u32[]{:S(2)}, u32[]{:S(2)}) collective-permute-start(bf16[256,1536]{1,0:T(8,128)(2,1)} %slice.571), channel_id=1, source_target_pairs={{0,16},{16,0},{1,17},{17,1},{2,18},{18,2},{3,19},{19,3},{4,20},{20... | collective-permute-start | bytes 2359304 | tf_op jit(solution)/shard_map/ppermute | solution.py:818
  356.9 46.7 %collective-permute-start.22 = (bf16[256,1664]{1,0:T(8,128)(2,1)}, bf16[256,1664]{1,0:T(8,128)(2,1)S(1)}, u32[]{:S(2)}, u32[]{:S(2)}) collective-permute-start(bf16[256,1664]{1,0:T(8,128)(2,1)} %fusion.16), channel_id=1, source_target_pairs={{0,16},{16,0},{1,17},{17,1},{2,18},{18,2},{3,19},{19,3},{4,20},{20... | collective-permute-start | bytes 2555912 | tf_op jit(solution)/shard_map/ppermute | solution.py:818
  379.2 29.0 %collective-permute-start.29 = (bf16[64,1536]{1,0:T(8,128)(2,1)S(1)}, bf16[64,1536]{1,0:T(8,128)(2,1)S(1)}, u32[]{:S(2)}, u32[]{:S(2)}) collective-permute-start(bf16[64,1536]{1,0:T(8,128)(2,1)S(1)} %get-tuple-element.195), channel_id=1, source_target_pairs={{1,0},{2,1},{3,2},{0,3},{5,4},{6,5},{7,6},{4,7},{9,8},{10,9},{11,1... | collective-permute-start | bytes 589832 | tf_op jit(solution)/shard_map/ppermute | solution.py:827
  384.1 24.9 %collective-permute-start.31 = (bf16[64,1536]{1,0:T(8,128)(2,1)S(1)}, bf16[64,1536]{1,0:T(8,128)(2,1)S(1)}, u32[]{:S(2)}, u32[]{:S(2)}) collective-permute-start(bf16[64,1536]{1,0:T(8,128)(2,1)S(1)} %get-tuple-element.196), channel_id=1, source_target_pairs={{3,0},{0,1},{1,2},{2,3},{7,4},{4,5},{5,6},{6,7},{11,8},{8,9},{9,10... | collective-permute-start | bytes 589832 | tf_op jit(solution)/shard_map/ppermute | solution.py:827
  384.1 24.9 %collective-permute-start.30 = (bf16[64,1536]{1,0:T(8,128)(2,1)S(1)}, bf16[64,1536]{1,0:T(8,128)(2,1)S(1)}, u32[]{:S(2)}, u32[]{:S(2)}) collective-permute-start(bf16[64,1536]{1,0:T(8,128)(2,1)S(1)} %get-tuple-element.197), channel_id=1, source_target_pairs={{2,0},{3,1},{0,2},{1,3},{6,4},{7,5},{4,6},{5,7},{10,8},{11,9},{8,1... | collective-permute-start | bytes 589832 | tf_op jit(solution)/shard_map/ppermute | solution.py:827
  404.0 9.9 %collective-permute-start.23 = (bf16[64,1664]{1,0:T(8,128)(2,1)S(1)}, bf16[64,1664]{1,0:T(8,128)(2,1)S(1)}, u32[]{:S(2)}, u32[]{:S(2)}) collective-permute-start(bf16[64,1664]{1,0:T(8,128)(2,1)S(1)} %get-tuple-element.187), channel_id=1, source_target_pairs={{1,0},{2,1},{3,2},{0,3},{5,4},{6,5},{7,6},{4,7},{9,8},{10,9},{11,1... | collective-permute-start | bytes 638984 | tf_op jit(solution)/shard_map/ppermute | solution.py:827
  408.1 25.7 %collective-permute-start.24 = (bf16[64,1664]{1,0:T(8,128)(2,1)S(1)}, bf16[64,1664]{1,0:T(8,128)(2,1)S(1)}, u32[]{:S(2)}, u32[]{:S(2)}) collective-permute-start(bf16[64,1664]{1,0:T(8,128)(2,1)S(1)} %get-tuple-element.188), channel_id=1, source_target_pairs={{2,0},{3,1},{0,2},{1,3},{6,4},{7,5},{4,6},{5,7},{10,8},{11,9},{8,1... | collective-permute-start | bytes 638984 | tf_op jit(solution)/shard_map/ppermute | solution.py:827
  408.2 25.7 %collective-permute-start.25 = (bf16[64,1664]{1,0:T(8,128)(2,1)S(1)}, bf16[64,1664]{1,0:T(8,128)(2,1)S(1)}, u32[]{:S(2)}, u32[]{:S(2)}) collective-permute-start(bf16[64,1664]{1,0:T(8,128)(2,1)S(1)} %get-tuple-element.189), channel_id=1, source_target_pairs={{3,0},{0,1},{1,2},{2,3},{7,4},{4,5},{5,6},{6,7},{11,8},{8,9},{9,10... | collective-permute-start | bytes 638984 | tf_op jit(solution)/shard_map/ppermute | solution.py:827
  409.1 38.1 %collective-permute-start.34 = (bf16[64,1536]{1,0:T(8,128)(2,1)S(1)}, bf16[64,1536]{1,0:T(8,128)(2,1)S(1)}, u32[]{:S(2)}, u32[]{:S(2)}) collective-permute-start(bf16[64,1536]{1,0:T(8,128)(2,1)S(1)} %get-tuple-element.171), channel_id=1, source_target_pairs={{3,0},{0,1},{1,2},{2,3},{7,4},{4,5},{5,6},{6,7},{11,8},{8,9},{9,10... | collective-permute-start | bytes 589832 | tf_op jit(solution)/shard_map/ppermute | solution.py:827
  412.0 35.2 %collective-permute-start.33 = (bf16[64,1536]{1,0:T(8,128)(2,1)S(1)}, bf16[64,1536]{1,0:T(8,128)(2,1)S(1)}, u32[]{:S(2)}, u32[]{:S(2)}) collective-permute-start(bf16[64,1536]{1,0:T(8,128)(2,1)S(1)} %get-tuple-element.171), channel_id=1, source_target_pairs={{2,0},{3,1},{0,2},{1,3},{6,4},{7,5},{4,6},{5,7},{10,8},{11,9},{8,1... | collective-permute-start | bytes 589832 | tf_op jit(solution)/shard_map/ppermute | solution.py:827
  413.9 22.1 %collective-permute-start.32 = (bf16[64,1536]{1,0:T(8,128)(2,1)S(1)}, bf16[64,1536]{1,0:T(8,128)(2,1)S(1)}, u32[]{:S(2)}, u32[]{:S(2)}) collective-permute-start(bf16[64,1536]{1,0:T(8,128)(2,1)S(1)} %get-tuple-element.171), channel_id=1, source_target_pairs={{1,0},{2,1},{3,2},{0,3},{5,4},{6,5},{7,6},{4,7},{9,8},{10,9},{11,1... | collective-permute-start | bytes 589832 | tf_op jit(solution)/shard_map/ppermute | solution.py:827
  434.0 24.6 %collective-permute-start.28 = (bf16[64,1664]{1,0:T(8,128)(2,1)S(1)}, bf16[64,1664]{1,0:T(8,128)(2,1)S(1)}, u32[]{:S(2)}, u32[]{:S(2)}) collective-permute-start(bf16[64,1664]{1,0:T(8,128)(2,1)S(1)} %get-tuple-element.169), channel_id=1, source_target_pairs={{3,0},{0,1},{1,2},{2,3},{7,4},{4,5},{5,6},{6,7},{11,8},{8,9},{9,10... | collective-permute-start | bytes 638984 | tf_op jit(solution)/shard_map/ppermute | solution.py:827
  434.0 24.5 %collective-permute-start.27 = (bf16[64,1664]{1,0:T(8,128)(2,1)S(1)}, bf16[64,1664]{1,0:T(8,128)(2,1)S(1)}, u32[]{:S(2)}, u32[]{:S(2)}) collective-permute-start(bf16[64,1664]{1,0:T(8,128)(2,1)S(1)} %get-tuple-element.169), channel_id=1, source_target_pairs={{2,0},{3,1},{0,2},{1,3},{6,4},{7,5},{4,6},{5,7},{10,8},{11,9},{8,1... | collective-permute-start | bytes 638984 | tf_op jit(solution)/shard_map/ppermute | solution.py:827
  436.0 22.5 %collective-permute-start.26 = (bf16[64,1664]{1,0:T(8,128)(2,1)S(1)}, bf16[64,1664]{1,0:T(8,128)(2,1)S(1)}, u32[]{:S(2)}, u32[]{:S(2)}) collective-permute-start(bf16[64,1664]{1,0:T(8,128)(2,1)S(1)} %get-tuple-element.169), channel_id=1, source_target_pairs={{1,0},{2,1},{3,2},{0,3},{5,4},{6,5},{7,6},{4,7},{9,8},{10,9},{11,1... | collective-permute-start | bytes 638984 | tf_op jit(solution)/shard_map/ppermute | solution.py:827
  476.0 2.3 collective-permute-start.35
  477.7 36.3 %collective-permute-start.53 = (bf16[2,224,768]{2,1,0:T(8,128)(2,1)S(1)}, bf16[2,224,768]{2,1,0:T(8,128)(2,1)S(1)}, u32[]{:S(2)}, u32[]{:S(2)}) collective-permute-start(bf16[2,224,768]{2,1,0:T(8,128)(2,1)S(1)} %dynamic-slice_convert_fusion.1), channel_id=1, source_target_pairs={{0,4},{4,0},{8,12},{12,8},{1,5},{5,1},{9,13},{13,9},{2,6},{6,2},{1... | collective-permute-start | bytes 2064392 | tf_op jit(solution)/shard_map/ppermute | solution.py:821
  479.3 6.7 %collective-permute-start.36 = (bf16[256,256]{1,0:T(8,128)(2,1)S(1)}, bf16[256,256]{1,0:T(8,128)(2,1)S(1)}, u32[]{:S(2)}, u32[]{:S(2)}) collective-permute-start(bf16[256,256]{1,0:T(8,128)(2,1)S(1)} %fusion.69), channel_id=1, source_target_pairs={{0,8},{4,12},{8,0},{12,4},{1,9},{5,13},{9,1},{13,5},{2,10},{6,14},... | collective-permute-start | bytes 393224 | tf_op jit(solution)/shard_map/ppermute | solution.py:824
  488.8 11.0 %collective-permute-start.37 = (bf16[64,1536]{1,0:T(8,128)(2,1)S(1)}, bf16[64,1536]{1,0:T(8,128)(2,1)S(1)}, u32[]{:S(2)}, u32[]{:S(2)}) collective-permute-start(bf16[64,1536]{1,0:T(8,128)(2,1)S(1)} %get-tuple-element.192), channel_id=1, source_target_pairs={{1,0},{2,1},{3,2},{0,3},{5,4},{6,5},{7,6},{4,7},{9,8},{10,9},{11,1... | collective-permute-start | bytes 589832 | tf_op jit(solution)/shard_map/ppermute | solution.py:827
  494.4 9.8 %collective-permute-start.39 = (bf16[64,1536]{1,0:T(8,128)(2,1)S(1)}, bf16[64,1536]{1,0:T(8,128)(2,1)S(1)}, u32[]{:S(2)}, u32[]{:S(2)}) collective-permute-start(bf16[64,1536]{1,0:T(8,128)(2,1)S(1)} %get-tuple-element.193), channel_id=1, source_target_pairs={{3,0},{0,1},{1,2},{2,3},{7,4},{4,5},{5,6},{6,7},{11,8},{8,9},{9,10... | collective-permute-start | bytes 589832 | tf_op jit(solution)/shard_map/ppermute | solution.py:827
  494.4 15.6 %collective-permute-start.38 = (bf16[64,1536]{1,0:T(8,128)(2,1)S(1)}, bf16[64,1536]{1,0:T(8,128)(2,1)S(1)}, u32[]{:S(2)}, u32[]{:S(2)}) collective-permute-start(bf16[64,1536]{1,0:T(8,128)(2,1)S(1)} %get-tuple-element.194), channel_id=1, source_target_pairs={{2,0},{3,1},{0,2},{1,3},{6,4},{7,5},{4,6},{5,7},{10,8},{11,9},{8,1... | collective-permute-start | bytes 589832 | tf_op jit(solution)/shard_map/ppermute | solution.py:827
  495.9 43.0 %collective-permute-start.49 = (bf16[2,384,640]{2,1,0:T(8,128)(2,1)S(1)}, bf16[2,384,640]{2,1,0:T(8,128)(2,1)S(1)}, u32[]{:S(2)}, u32[]{:S(2)}) collective-permute-start(bf16[2,384,640]{2,1,0:T(8,128)(2,1)S(1)} %dynamic-slice_convert_fusion), channel_id=1, source_target_pairs={{0,4},{4,0},{8,12},{12,8},{1,5},{5,1},{9,13},{13,9},{2,6},{6,2},{1... | collective-permute-start | bytes 2949128 | tf_op jit(solution)/shard_map/ppermute | solution.py:821
  510.1 16.2 %collective-permute-start.42 = (bf16[64,1536]{1,0:T(8,128)(2,1)S(1)}, bf16[64,1536]{1,0:T(8,128)(2,1)S(1)}, u32[]{:S(2)}, u32[]{:S(2)}) collective-permute-start(bf16[64,1536]{1,0:T(8,128)(2,1)S(1)} %get-tuple-element.165), channel_id=1, source_target_pairs={{3,0},{0,1},{1,2},{2,3},{7,4},{4,5},{5,6},{6,7},{11,8},{8,9},{9,10... | collective-permute-start | bytes 589832 | tf_op jit(solution)/shard_map/ppermute | solution.py:827
  510.2 16.1 %collective-permute-start.41 = (bf16[64,1536]{1,0:T(8,128)(2,1)S(1)}, bf16[64,1536]{1,0:T(8,128)(2,1)S(1)}, u32[]{:S(2)}, u32[]{:S(2)}) collective-permute-start(bf16[64,1536]{1,0:T(8,128)(2,1)S(1)} %get-tuple-element.165), channel_id=1, source_target_pairs={{2,0},{3,1},{0,2},{1,3},{6,4},{7,5},{4,6},{5,7},{10,8},{11,9},{8,1... | collective-permute-start | bytes 589832 | tf_op jit(solution)/shard_map/ppermute | solution.py:827
  513.5 10.5 %collective-permute-start.40 = (bf16[64,1536]{1,0:T(8,128)(2,1)S(1)}, bf16[64,1536]{1,0:T(8,128)(2,1)S(1)}, u32[]{:S(2)}, u32[]{:S(2)}) collective-permute-start(bf16[64,1536]{1,0:T(8,128)(2,1)S(1)} %get-tuple-element.165), channel_id=1, source_target_pairs={{1,0},{2,1},{3,2},{0,3},{5,4},{6,5},{7,6},{4,7},{9,8},{10,9},{11,1... | collective-permute-start | bytes 589832 | tf_op jit(solution)/shard_map/ppermute | solution.py:827
  514.2 23.9 %collective-permute-start.54 = (bf16[224,768]{1,0:T(8,128)(2,1)S(1)}, bf16[224,768]{1,0:T(8,128)(2,1)S(1)}, u32[]{:S(2)}, u32[]{:S(2)}) collective-permute-start(bf16[224,768]{1,0:T(8,128)(2,1)S(1)} %fusion.45), channel_id=1, source_target_pairs={{0,16},{16,0},{1,17},{17,1},{2,18},{18,2},{3,19},{19,3},{4,20},{20... | collective-permute-start | bytes 1032200 | tf_op jit(solution)/shard_map/ppermute | solution.py:818
  527.1 7.0 %collective-permute-start.45 = (f32[1536]{0:T(1024)S(1)}, f32[1536]{0:T(1024)S(1)}, u32[]{:S(2)}, u32[]{:S(2)}) collective-permute-start(f32[1536]{0:T(1024)S(1)} %get-tuple-element.134), channel_id=1, source_target_pairs={{3,0},{0,1},{1,2},{2,3},{7,4},{4,5},{5,6},{6,7},{11,8},{8,9},{9,10... | collective-permute-start | bytes 18440 | tf_op jit(solution)/shard_map/ppermute | solution.py:827
  530.9 4.5 collective-permute-start.44
  531.0 4.5 collective-permute-start.43
  535.5 1.2 collective-permute-start.46
  536.8 4.4 collective-permute-start.47
  538.1 9.9 %collective-permute-start.55 = (bf16[224,768]{1,0:T(8,128)(2,1)S(1)}, bf16[224,768]{1,0:T(8,128)(2,1)S(1)}, u32[]{:S(2)}, u32[]{:S(2)}) collective-permute-start(bf16[224,768]{1,0:T(8,128)(2,1)S(1)} %fusion.35), channel_id=1, source_target_pairs={{0,8},{4,12},{8,0},{12,4},{1,9},{5,13},{9,1},{13,5},{2,10},{6,14},... | collective-permute-start | bytes 1032200 | tf_op jit(solution)/shard_map/ppermute | solution.py:824
  539.2 12.8 %collective-permute-start.50 = (bf16[384,640]{1,0:T(8,128)(2,1)S(1)}, bf16[384,640]{1,0:T(8,128)(2,1)S(1)}, u32[]{:S(2)}, u32[]{:S(2)}) collective-permute-start(bf16[384,640]{1,0:T(8,128)(2,1)S(1)} %fusion.34), channel_id=1, source_target_pairs={{0,16},{16,0},{1,17},{17,1},{2,18},{18,2},{3,19},{19,3},{4,20},{20... | collective-permute-start | bytes 1474568 | tf_op jit(solution)/shard_map/ppermute | solution.py:818
  541.1 12.3 %collective-permute-start.48 = (f32[768]{0:T(1024)S(1)}, f32[768]{0:T(1024)S(1)}, u32[]{:S(2)}, u32[]{:S(2)}) collective-permute-start(f32[768]{0:T(1024)S(1)} %slice.463), channel_id=1, source_target_pairs={{0,16},{16,0},{1,17},{17,1},{2,18},{18,2},{3,19},{19,3},{4,20},{20... | collective-permute-start | bytes 9224 | tf_op jit(solution)/shard_map/ppermute | solution.py:818
  548.1 5.9 collective-permute-start.56
  552.1 11.8 %collective-permute-start.51 = (bf16[384,640]{1,0:T(8,128)(2,1)S(1)}, bf16[384,640]{1,0:T(8,128)(2,1)S(1)}, u32[]{:S(2)}, u32[]{:S(2)}) collective-permute-start(bf16[384,640]{1,0:T(8,128)(2,1)S(1)} %fusion.19), channel_id=1, source_target_pairs={{0,8},{4,12},{8,0},{12,4},{1,9},{5,13},{9,1},{13,5},{2,10},{6,14},... | collective-permute-start | bytes 1474568 | tf_op jit(solution)/shard_map/ppermute | solution.py:824
  564.2 3.0 collective-permute-start.52
  (82 other events, 731.0 us)
Sparse Core Ops, SparseCore 0:
  107.6 44.8 all-reduce.7
Sparse Core Ops, SparseCore 1:
  126.7 47.3 all-gather.12
  189.4 29.6 all-gather.10
  223.1 56.2 all-gather.18
  285.7 58.6 all-gather.16
  359.0 45.8 all-gather.14

commit v3 on v2

--- a/solution.py
+++ b/solution.py
@@ -529,10 +529,7 @@
     gate_ref,
     gate_up_ref,
     down_ref,
-    other0,
-    other1,
-    other2,
-    other3,
+    other_ref,
     *rest,
 ):
     if len(rest) == 12:
@@ -541,7 +538,6 @@
     else:
         held_out = held_grad = None
     out_ref, grad_ref, slots_ref, gate_grad_ref, rows_buf, grads_buf, moe_buf, back_buf, hot_buf, gate_buf = rest
-    others = (other0, other1, other2, other3)
     half = down_ref.shape[-1]
     width = down_ref.shape[-2]
     quarter = [place_ref[1] ^ r for r in range(4)]
@@ -591,11 +587,11 @@
         grads = jnp.concatenate([grads_buf[b, slot, :] for b in range(4)], axis=0)
         gate = jnp.concatenate([gate_buf[b, slot, :] for b in range(4)], axis=0)
         near_w = jnp.concatenate([gate_up_ref[q, 0, 0], gate_up_ref[q, 0, 1]], axis=1)
-        far_w = jnp.concatenate([others[r][0, :half, :], others[r][0, half : 2 * half, :]], axis=1)
+        far_w = jnp.concatenate([other_ref[q, 0, :half, :], other_ref[q, 0, half : 2 * half, :]], axis=1)
         near_down = down_ref[0, q, 0]
         far_down = jnp.concatenate(
             [
-                others[r][0, 2 * half + j * width : 2 * half + (j + 1) * width, :]
+                other_ref[q, 0, 2 * half + j * width : 2 * half + (j + 1) * width, :]
                 for j in range(half // 128)
             ],
             axis=1,
@@ -637,7 +633,7 @@
 
 
 def run_experts(place, near, far, near_out, far_out, rank, gate, gate_up, down, others, held, first):
-    steps, packed, lanes = others[0].shape
+    _, steps, packed, lanes = others.shape
     quarters, each, sides, half, width = gate_up.shape
     tokens = 2 * near_out.shape[0]
     full = 2 * half
@@ -655,8 +651,9 @@
         table,
         pl.BlockSpec((quarters, 1, sides, half, width), lambda j, sp: (0, first + j, 0, 0, 0)),
         pl.BlockSpec((1, quarters, 1, width, half), lambda j, sp: (sp[0], 0, first + j, 0, 0)),
-    ] + [pl.BlockSpec((1, packed, lanes), lambda j, sp: (j, 0, 0))] * 4
-    operands = [place, near, far, near_out, far_out, rank, gate, gate_up, down, *others]
+        pl.BlockSpec((quarters, 1, packed, lanes), lambda j, sp: (0, j, 0, 0)),
+    ]
+    operands = [place, near, far, near_out, far_out, rank, gate, gate_up, down, others]
     aliases = {}
     total = jax.ShapeDtypeStruct((tokens, full), jnp.float32)
     if held is not None:
@@ -692,7 +689,8 @@
 
 def weight_grad_kernel(place_ref, *refs):
     rows_ref, grads_ref, slots_ref, rank_ref = refs[:4]
-    gate_up_ref, down_ref, rows_buf, grads_buf = refs[-4:]
+    gate_up_ref, down_ref, mark_ref, rows_buf, grads_buf = refs[-5:]
+    mark_ref[...] = jnp.zeros_like(mark_ref)
     half = down_ref.shape[-1]
     width = down_ref.shape[-2]
     side = pl.program_id(1)
@@ -721,7 +719,7 @@
         down_ref[0, q, 0] = dot(taken[:, 2 * width :], grads, 0, 0)
 
 
-def run_weight_grads(place, rows, grads, slots, rank, held, first, each):
+def run_weight_grads(place, rows, grads, slots, rank, held, first, each, mark):
     sides, _, quarters, steps, slot_count, lanes = slots.shape
     width = lanes // 3
     half = rows.shape[-1]
@@ -733,18 +731,20 @@
             lambda j, a, sp: (sp[0] ^ a, 0, 0, j, 0, 0),
         ),
         pl.BlockSpec((1, quarters, 1, 16, 128), lambda j, a, sp: (a, 0, first + j, 0, 0)),
+        pl.BlockSpec(memory_space=pl.ANY),
     ]
-    operands = [place, rows, grads, slots, rank]
+    operands = [place, rows, grads, slots, rank, mark]
     aliases = {}
     if held is not None:
         in_specs += [pl.BlockSpec(memory_space=pl.ANY)] * 2
         aliases = {len(operands): 0, len(operands) + 1: 1}
-        operands += list(held)
+        operands += list(held[:2])
     return pl.pallas_call(
         weight_grad_kernel,
         out_shape=(
             jax.ShapeDtypeStruct((sides, quarters, each, 2 * half, width), jnp.float32),
             jax.ShapeDtypeStruct((sides, quarters, each, width, half), jnp.float32),
+            jax.ShapeDtypeStruct((8, 128), jnp.float32),
         ),
         grid_spec=pltpu.PrefetchScalarGridSpec(
             num_scalar_prefetch=1,
@@ -759,6 +759,7 @@
                     (1, quarters, 1, width, half),
                     lambda j, a, sp: (sp[0] ^ a, 0, first + j, 0, 0),
                 ),
+                pl.BlockSpec((8, 128), lambda j, a, sp: (0, 0)),
             ),
             scratch_shapes=[pltpu.VMEM((16, 4 * CAP, half), jnp.bfloat16)] * 2,
         ),
@@ -846,7 +847,7 @@
             jnp.concatenate([second, first], axis=axis),
         )
 
-    def sum_tp(value):
+    def sum_tp(value, between=None):
         part = value.shape[0] // tp_size
 
         def piece(step):
@@ -856,10 +857,13 @@
         for step in range(1, tp_size):
             total = total + from_tp(piece(tp_size - step), step).astype(wide)
         total = total.astype(low)
+        if between is not None:
+            total, *kept = between(total)
         found = [total] + [from_tp(total, step) for step in range(1, tp_size)]
-        return lax.dynamic_slice_in_dim(
+        result = lax.dynamic_slice_in_dim(
             jnp.concatenate(found + found, axis=0), ((tp_size - z_pos) % tp_size) * part, tokens, 0
         )
+        return result if between is None else (result, kept)
 
     small = jnp.concatenate(
         [
@@ -892,31 +896,22 @@
     )
     near_out = jnp.concatenate([own_first(d_out.reshape(tokens, model)), routes_low], axis=1)
     away = (1 - x_pos) * mine + c_pos * each
-    far_weights = []
-    last_x = sent
-    last_y = sent
-    for number, (first, count) in enumerate(chunks):
+
+    def pack(first, count, base):
         gate_up_sent = (
-            lax.dynamic_slice_in_dim(w_gate_up, away + first, count, 0)
+            lax.dynamic_slice_in_dim(w_gate_up, base + first, count, 0)
             .transpose(0, 2, 1, 3)
             .reshape(count, 2 * half, width)
         )
         down_sent = (
-            lax.dynamic_slice_in_dim(w_down, away + first, count, 0)
+            lax.dynamic_slice_in_dim(w_down, base + first, count, 0)
             .reshape(count, width, half // 128, 128)
             .transpose(0, 2, 1, 3)
             .reshape(count, half, 128)
         )
-        packed = jnp.concatenate([gate_up_sent, down_sent], axis=1)
-        got = across(after(packed, last_x))
-        last_x = got
-        nearby = beside(got)
-        distant = along(after(got, last_y))
-        last_y = distant
-        far_weights.append([got, nearby, distant, beside(distant)])
-        if number == 1:
-            far_out = across(after(near_out, got))
-            last_x = far_out
+        return jnp.concatenate([gate_up_sent, down_sent], axis=1)
+
+    far_zero = across(after(pack(*chunks[0], away), sent))
     down_all = w_down.reshape(2, 4, each, width, half)
 
     seg_ids = jnp.arange(4, dtype=jnp.int32)
@@ -951,15 +946,14 @@
     turned_part = unrotated[:, : q_cols + k_cols]
     rotated = (turned_part * cosines + turn_heads(turned_part) * sines).astype(low)
     query = rotated[:, :q_cols]
-    gate_up_mine = (
-        lax.dynamic_slice_in_dim(after(w_gate_up, query), x_pos * mine, mine, 0)
-        .transpose(0, 2, 1, 3)
-        .reshape(4, each, 2, half, width)
-    )
     key_value = jnp.concatenate(
         [rotated[:, q_cols:], unrotated[:, q_cols + k_cols :].astype(low)], axis=1
     )
+    away_next, key_value = lax.optimization_barrier((away, key_value))
     blocks = all_ctx(key_value)
+    pack_one = pack(*chunks[1], away_next)
+    *blocks, pack_one, far_zero = lax.optimization_barrier((*blocks, pack_one, far_zero))
+    far_one = across(pack_one)
     smem = pl.BlockSpec(memory_space=pltpu.SMEM)
     vmem = pl.BlockSpec(memory_space=pltpu.VMEM)
     kv_heads = k_cols // HEAD_DIM
@@ -980,8 +974,22 @@
     out_got = across(out_core)
     out_far = ctx_join(out_got, beside(out_got), 0)
     attn_part = jnp.concatenate([dot(head_low, w_out), dot(head_low, out_far)], axis=1).astype(low)
-    attended = lax.psum(attn_part, "tp").astype(wide)
-    attended = after(attended, far_weights[1][0], far_weights[0][2])
+    base_mine, away_last, attn_part = lax.optimization_barrier((x_pos * mine, away, attn_part))
+    gate_up_mine = (
+        lax.dynamic_slice_in_dim(w_gate_up, base_mine, mine, 0)
+        .transpose(0, 2, 1, 3)
+        .reshape(4, each, 2, half, width)
+    )
+    pack_two = pack(*chunks[2], away_last)
+
+    def between(total):
+        return lax.optimization_barrier((total, near_out, far_one))
+
+    attended, (near_out, far_one) = sum_tp(attn_part, between)
+    far_out = across(near_out)
+    attended, gate_up_mine, pack_two, far_out = lax.optimization_barrier(
+        (attended.astype(wide), gate_up_mine, pack_two, far_out)
+    )
     mixed = inputs + RESIDUAL_SCALE * attended
     scale_two = norm_scale(mixed)
     unit_two = mixed * scale_two
@@ -1007,6 +1015,22 @@
         axis=1,
     )
     far = across(near)
+    far, pack_two = lax.optimization_barrier((far, pack_two))
+    far_two = across(pack_two)
+    far_weights = [lax.all_gather(got, "ctx") for got in (far_zero, far_one, far_two)]
+    early = lax.all_gather(
+        jnp.concatenate(
+            [
+                jnp.concatenate([near_out[:, :half], routes_low], axis=1),
+                far_out[:, half:],
+            ],
+            axis=0,
+        ),
+        "ctx",
+    )
+    rows_two = lax.all_gather(
+        jnp.concatenate([normed_two[:, :half], far[:, half:model]], axis=0), "ctx"
+    )
     far_gates = far[:, model : model + mine].astype(wide) + far[
         :, model + mine : model + 2 * mine
     ].astype(wide)
@@ -1052,6 +1076,8 @@
             first,
         )
         held = (moe_all, back_all)
+        if first == 2:
+            place, early = lax.optimization_barrier((place, early))
         slots.append(slot_part)
         gate_grad_parts.append(gate_part)
     gate_grad_all = jnp.concatenate(gate_grad_parts, axis=1).reshape(mine, 2 * tokens).T
@@ -1063,7 +1089,10 @@
         ],
         axis=1,
     )
+    moe_far = moe_all[tokens:].astype(low)
     back_got = across(back_sent)
+    back_got, moe_far, rows_two = lax.optimization_barrier((back_got, moe_far, rows_two))
+    pairs = [lax.all_gather(part, ("fsdp", "ctx")).reshape(2, 4, *part.shape) for part in slots]
     back_sum = (back_all[:tokens] + swap_halves(back_got[:, :model]).astype(wide)).astype(low)
     gathered = sum_tp(
         jnp.concatenate(
@@ -1080,6 +1109,7 @@
             axis=1,
         )
     )
+    gathered, pairs[0] = lax.optimization_barrier((gathered, pairs[0]))
     gate_grads = gathered[:, model : model + experts].astype(wide)
     logit_grad = (gates * (gate_grads - jnp.sum(gates * gate_grads, axis=1, keepdims=True))).astype(
         low
@@ -1093,10 +1123,19 @@
     )
     attn_grad = (RESIDUAL_SCALE * mixed_grad).astype(low)
 
-    moe_got = across(moe_all[tokens:].astype(low))
+    moe_got = across(moe_far)
     moe_part = (moe_all[:tokens] + swap_halves(moe_got).astype(wide)).astype(low)
-    moe_sum = sum_tp(after(moe_part, gathered)).astype(wide)
+    moe_part, attn_grad = lax.optimization_barrier((moe_part, attn_grad))
+    moe_part, pairs[2] = lax.optimization_barrier((moe_part, pairs[2]))
+    moe_sum = lax.psum(moe_part, "tp").astype(wide)
     layer_out = own_first(mixed + RESIDUAL_SCALE * moe_sum)
+
+    all_routes = early[:, :, half : half + top].reshape(4 * 2 * tokens, top)
+    rank_all = ranks(all_routes, expert_ids).reshape(2, 4, each, 16, rows)
+    def grads_of(number, held, mark):
+        return run_weight_grads(
+            place, rows_two, early, pairs[number], rank_all, held, chunks[number][0], each, mark
+        )
 
     head_grad = (
         dot(attn_grad[:, :half], w_out, 1, 1) + dot(attn_grad[:, half:], out_far, 1, 1)
@@ -1122,7 +1161,16 @@
         [turned_grad * cosines - turn_heads(turned_grad) * sines, kv_grad[:, k_cols:]], axis=1
     ).astype(low)
     normed_one_part = dot(qkv_grad, qkv_full, 1, 1).astype(low)
-    normed_one_grad = sum_tp(normed_one_part).astype(wide)
+    grads = grads_of(0, None, jnp.zeros((8, 128), wide))
+
+    def with_grads(total):
+        return lax.optimization_barrier((total, grads[2]))
+
+    normed_one_grad, (mark,) = sum_tp(normed_one_part, with_grads)
+    grads = grads_of(1, grads, mark)
+    normed_one_grad, mark = lax.optimization_barrier((normed_one_grad, grads[2]))
+    grads = grads_of(2, grads, mark)
+    normed_one_grad = normed_one_grad.astype(wide)
     gain_one_part = jnp.sum(normed_one_part.astype(wide) * unit_one, axis=0)
     gain_one_part = sum([from_tp(gain_one_part, step) for step in range(1, tp_size)], gain_one_part)
     scaled_one = normed_one_grad * gain_one
@@ -1132,25 +1180,6 @@
         * (scaled_one - unit_one * jnp.mean(scaled_one * unit_one, axis=-1, keepdims=True))
     )
 
-    early = lax.all_gather(
-        jnp.concatenate(
-            [
-                jnp.concatenate([near_out[:, :half], routes_low], axis=1),
-                far_out[:, half:],
-            ],
-            axis=0,
-        ),
-        "ctx",
-    )
-    rows_two = lax.all_gather(
-        jnp.concatenate([normed_two[:, :half], far[:, half:model]], axis=0), "ctx"
-    )
-    all_routes = early[:, :, half : half + top].reshape(4 * 2 * tokens, top)
-    rank_all = ranks(all_routes, expert_ids).reshape(2, 4, each, 16, rows)
-    grads = None
-    for (first, count), part in zip(chunks, slots):
-        pair = lax.all_gather(part, ("fsdp", "ctx")).reshape(2, 4, *part.shape)
-        grads = run_weight_grads(place, rows_two, early, pair, rank_all, grads, first, each)
     d_gate_up = grads[0].reshape(experts, half, 2, width)
     d_down = grads[1].reshape(experts, width, half)
 

time: 638 us -> 542 us (0.85)
  waiting for transfers between devices: 310 us -> 202 us
  other arithmetic: 45.6 us -> 65.1 us
  starting transfers between devices: 71 us -> 54.4 us
  local copies, waits for them, and re-layouts: 58.5 us -> 70.9 us
    ppermute x8 -> x5, waiting for transfers between devices: 93.1 us -> 3.63 us  [along(): return lax.ppermute(value, 'ctx', [(i, i ^ 2) for i in range(4)])]
    ppermute x12, waiting for transfers between devices: 126 us -> 81.6 us  [across(): return lax.ppermute(value, 'fsdp', [(0, 1), (1, 0)])]
    ppermute x21, waiting for transfers between devices: 61.7 us -> 94.9 us  [from_tp(): lax.ppermute(value, 'tp', [((i + step) % tp_size, i) for i in range(tp_si...]
    psum x1, waiting for transfers between devices: 22.8 us -> 0.01 us  [fast_body(): moe_sum = lax.psum(moe_part, 'tp').astype(wide)]
    all_gather x3 -> x6, waiting for transfers between devices: 0.01 us -> 14.9 us  [the longest x3 14.6 us: fast_body(): lax.all_gather(got, 'ctx')]
    ppermute x21, starting transfers between devices: 41.3 us -> 28.1 us  [from_tp(): lax.ppermute(value, 'tp', [((i + step) % tp_size, i) for i in range(tp_si...]
    ppermute x8 -> x5, starting transfers between devices: 15.7 us -> 7.33 us  [along(): return lax.ppermute(value, 'ctx', [(i, i ^ 2) for i in range(4)])]
    transpose x10 -> x7, local copies, waits for them, and re-layouts: 17.7 us -> 19.2 us  [the longest x2 16.2 us: fast_body(): gate_up_mine = lax.dynamic_slice_in_dim(w_gate_up, base_mine, mine, 0).tr...]
  transfers between devices with their start and end apart: 63 -> 57, of which waited for: 30 -> 27; matrix products, arithmetic and copies ran while one was open for 16% -> 23% of each run, Pallas kernels for 15% -> 21%
where the time goes in v3:
time: 542 us; the launch traced here: 535 us
  waiting for transfers between devices  202 us (37%)
  Pallas kernels  110 us (20%)
  local copies, waits for them, and re-layouts  70.9 us (13%)
  other arithmetic  65.1 us (12%)
  starting transfers between devices  54.4 us (10%)
  between operations  17.4 us (3%)
  matrix products  14.8 us (3%)
    ppermute x21, waiting for transfers between devices, from_tp(): lax.ppermute(value, 'tp', [((i + step) % tp_size, i) for i in range(tp_si...  94.9 us
    ppermute x12, waiting for transfers between devices, across(): return lax.ppermute(value, 'fsdp', [(0, 1), (1, 0)])  81.6 us
    pallas_call x3, Pallas kernels, run_weight_grads(): pl.pallas_call(weight_grad_kernel, out_shape=(jax.ShapeDtypeStruct((sides...  51.8 us
    pallas_call x3, Pallas kernels, run_experts(): pl.pallas_call(expert_kernel, out_shape=(total, total, slots, gate_grads)...  47.6 us
    ppermute x21, starting transfers between devices, from_tp(): lax.ppermute(value, 'tp', [((i + step) % tp_size, i) for i in range(tp_si...  28.1 us
    ppermute x12, starting transfers between devices, across(): return lax.ppermute(value, 'fsdp', [(0, 1), (1, 0)])  16.8 us
    transpose x2, local copies, waits for them, and re-layouts, fast_body(): gate_up_mine = lax.dynamic_slice_in_dim(w_gate_up, base_mine, mine, 0).tr...  16.2 us
    dot_general x15, matrix products, dot(): lax.dot_general(left, right, (((left_dim,), (right_dim,)), ((), ())), pre...  14.8 us
  transfers between devices with their start and end apart: 57, of which 27 were waited for; matrix products, arithmetic and copies ran while one was open for 23% of the time, Pallas kernels for 21%

profile of v3, /device:TPU:0, one launch (start us, length us, event | category | flops | bytes accessed | tf_op | source)
XLA Modules:
  0.0 534.8 jit_solution(6006463444806785638)
XLA Ops:
  11.6 3.0 collective-permute-start
  15.8 1.9 fusion.90
  17.8 1.9 fusion.91
  19.7 4.7 fusion.108
  26.0 2.0 collective-permute-done
  31.4 1.9 maximum_select_fusion.2
  38.0 2.5 constant_dynamic-slice_fusion.11
  40.7 1.9 constant_dynamic-slice_fusion.10
  45.9 1.7 collective-permute-start.5
  49.7 3.6 collective-permute-done.3.kv2
  55.0 19.5 %collective-permute-done.5 = bf16[2,2304,128]{2,1,0:T(8,128)(2,1)} collective-permute-done((bf16[2,2304,128]{2,1,0:T(8,128)(2,1)}, bf16[2,2304,128]{2,1,0:T(8,128)(2,1)}, u32[]{:S(2)}, u32[]{:S(2)}) %collective-permute-start.5) | collective-permute-done | bytes 1179680 | tf_op jit(solution)/shard_map/ppermute | solution.py:819
  75.0 2.7 add_bitcast_fusion
  78.8 1.8 collective-permute-start.6
  80.6 2.6 add_bitcast_fusion.1
  83.2 4.3 collective-permute-done.6
  90.1 5.2 attend.1
  100.2 1.8 collective-permute-start.11
  102.0 7.8 %dynamic-slice_bitcast_fusion = bf16[20,2,768,128]{3,1,2,0:T(2,128)(2,1)} fusion(bf16[40,768,2,128]{3,2,1,0:T(2,128)(2,1)} %param.23, s32[]{:T(128)S(6)} %select_n.315), kind=kLoop, calls=%fused_computation | loop fusion | bytes 15728644 | tf_op jit(solution)/shard_map/transpose | solution.py:980
  111.1 8.4 %copy.209 = bf16[20,2,768,128]{3,2,1,0:T(8,128)(2,1)} copy(bf16[20,2,768,128]{3,1,2,0:T(2,128)(2,1)} %dynamic-slice_bitcast_fusion) | data formatting | bytes 15728640 | tf_op jit(solution)/shard_map/transpose | solution.py:980
  121.2 2.3 collective-permute-start.8
  125.1 4.1 collective-permute-done.10
  129.2 2.9 collective-permute-done.8
  132.1 9.0 %collective-permute-done.9 = bf16[64,1536]{1,0:T(8,128)(2,1)S(1)} collective-permute-done((bf16[64,1536]{1,0:T(8,128)(2,1)S(1)}, bf16[64,1536]{1,0:T(8,128)(2,1)S(1)}, u32[]{:S(2)}, u32[]{:S(2)}) %collective-permute-start.9) | collective-permute-done | bytes 196640 | tf_op jit(solution)/shard_map/ppermute | solution.py:828
  144.2 5.4 %collective-permute-done.12 = bf16[64,1536]{1,0:T(8,128)(2,1)S(1)} collective-permute-done((bf16[64,1536]{1,0:T(8,128)(2,1)S(1)}, bf16[64,1536]{1,0:T(8,128)(2,1)S(1)}, u32[]{:S(2)}, u32[]{:S(2)}) %collective-permute-start.12) | collective-permute-done | bytes 196640 | tf_op jit(solution)/shard_map/ppermute | solution.py:828
  149.6 8.9 %collective-permute-done.13 = bf16[64,1536]{1,0:T(8,128)(2,1)S(1)} collective-permute-done((bf16[64,1536]{1,0:T(8,128)(2,1)S(1)}, bf16[64,1536]{1,0:T(8,128)(2,1)S(1)}, u32[]{:S(2)}, u32[]{:S(2)}) %collective-permute-start.13) | collective-permute-done | bytes 196640 | tf_op jit(solution)/shard_map/ppermute | solution.py:828
  160.0 3.6 collective-permute-done.15.far_out_ref
  166.8 1.8 multiply_reduce_fusion.2
  172.5 18.6 %collective-permute-done.16.far_ref = bf16[256,1664]{1,0:T(8,128)(2,1)S(1)} collective-permute-done((bf16[256,1664]{1,0:T(8,128)(2,1)S(1)}, bf16[256,1664]{1,0:T(8,128)(2,1)S(1)}, u32[]{:S(2)}, u32[]{:S(2)}) %collective-permute-start.16) | collective-permute-done | bytes 852000 | tf_op jit(solution)/shard_map/ppermute | solution.py:819
  192.5 12.2 %collective-permute-done.17 = bf16[1,2304,128]{2,1,0:T(8,128)(2,1)} collective-permute-done((bf16[1,2304,128]{2,1,0:T(8,128)(2,1)S(1)}, bf16[1,2304,128]{2,1,0:T(8,128)(2,1)}, u32[]{:S(2)}, u32[]{:S(2)}) %collective-permute-start.17) | collective-permute-done | bytes 589856 | tf_op jit(solution)/shard_map/ppermute | solution.py:819
  211.9 16.2 %experts.3 = (f32[512,1536]{1,0:T(8,128)}, f32[512,1536]{1,0:T(8,128)}, bf16[4,2,128,384]{3,2,1,0:T(8,128)(2,1)}, f32[4,2,4,128]{3,2,1,0:T(4,128)}) custom-call(s32[2]{0:T(128)} %pad_add_fusion.1.place_ref, bf16[256,1664]{1,0:T(8,128)(2,1)} %copy-done.7, bf16[256,1664]{1,0:T(8,128)(2,1)} %copy-done.12, bf16[256,1664]{1,0:T(8,128)(2,1)} %copy-done.2, ...), custom_call_target="tpu_custom_call" | custom-call | tf_op jit(solution)/shard_map/experts/pallas_call | solution.py:665
  228.7 7.2 %all-gather.21.cloned.1.call-done = bf16[8,2304,128]{2,1,0:T(8,128)(2,1)} async-done(((bf16[2,2304,128]{2,1,0:T(8,128)(2,1)}), bf16[8,2304,128]{2,1,0:T(8,128)(2,1)}) %all-gather.21.cloned.1.call-update) | async-done | bytes 4718608 | tf_op jit(solution)/shard_map/all_gather | solution.py:1020
  235.9 18.2 %experts.4 = (f32[512,1536]{1,0:T(8,128)}, f32[512,1536]{1,0:T(8,128)}, bf16[4,2,128,384]{3,2,1,0:T(8,128)(2,1)}, f32[4,2,4,128]{3,2,1,0:T(4,128)}) custom-call(s32[2]{0:T(128)} %pad_add_fusion.1.place_ref, bf16[256,1664]{1,0:T(8,128)(2,1)} %copy-done.7, bf16[256,1664]{1,0:T(8,128)(2,1)} %copy-done.12, ...), custom_call_target="tpu_custom_call", output_to_operand_aliasing={{0}: (10, {}), {1}: (11, {})} | custom-call | tf_op jit(solution)/shard_map/experts/pallas_call | solution.py:665
  254.1 7.4 %all-gather.19.cloned.1.call-done = bf16[4,2304,128]{2,1,0:T(8,128)(2,1)} async-done(((bf16[1,2304,128]{2,1,0:T(8,128)(2,1)}), bf16[4,2304,128]{2,1,0:T(8,128)(2,1)}) %all-gather.19.cloned.1.call-update) | async-done | bytes 2359312 | tf_op jit(solution)/shard_map/all_gather | solution.py:1020
  261.4 13.2 %experts.5 = (f32[512,1536]{1,0:T(8,128)}, f32[512,1536]{1,0:T(8,128)}, bf16[4,1,128,384]{3,2,1,0:T(8,128)(2,1)}, f32[4,1,4,128]{3,2,1,0:T(4,128)}) custom-call(s32[2]{0:T(128)} %pad_add_fusion.1.place_ref, bf16[256,1664]{1,0:T(8,128)(2,1)} %copy-done.7, bf16[256,1664]{1,0:T(8,128)(2,1)} %copy-done.12, ...), custom_call_target="tpu_custom_call", output_to_operand_aliasing={{0}: (10, {}), {1}: (11, {})} | custom-call | tf_op jit(solution)/shard_map/experts/pallas_call | solution.py:665
  275.5 2.4 slice.571
  278.1 2.1 fusion.16
  283.7 1.9 slice.389
  285.5 2.4 slice.570
  287.9 3.5 all-gather.25.cloned.1.call-done
  291.4 10.2 %collective-permute-done.18 = bf16[256,1664]{1,0:T(8,128)(2,1)} collective-permute-done((bf16[256,1664]{1,0:T(8,128)(2,1)}, bf16[256,1664]{1,0:T(8,128)(2,1)}, u32[]{:S(2)}, u32[]{:S(2)}) %collective-permute-start.18) | collective-permute-done | bytes 852000 | tf_op jit(solution)/shard_map/ppermute | solution.py:819
  306.2 3.3 collective-permute-start.20
  313.2 2.3 collective-permute-done.20
  315.6 12.2 %collective-permute-done.21 = bf16[64,1664]{1,0:T(8,128)(2,1)} collective-permute-done((bf16[64,1664]{1,0:T(8,128)(2,1)}, bf16[64,1664]{1,0:T(8,128)(2,1)}, u32[]{:S(2)}, u32[]{:S(2)}) %collective-permute-start.21) | collective-permute-done | bytes 213024 | tf_op jit(solution)/shard_map/ppermute | solution.py:828
  332.1 2.7 collective-permute-start.24
  334.8 2.2 collective-permute-start.25
  337.0 13.2 %collective-permute-done.24 = bf16[64,1664]{1,0:T(8,128)(2,1)S(1)} collective-permute-done((bf16[64,1664]{1,0:T(8,128)(2,1)S(1)}, bf16[64,1664]{1,0:T(8,128)(2,1)S(1)}, u32[]{:S(2)}, u32[]{:S(2)}) %collective-permute-start.24) | collective-permute-done | bytes 213024 | tf_op jit(solution)/shard_map/ppermute | solution.py:828
  350.4 3.3 collective-permute-done.19
  355.1 1.9 multiply_reduce_fusion
  359.6 6.0 %attend_back.1 = (f32[256,384]{1,0:T(8,128)}, bf16[4,256,256]{2,1,0:T(8,128)(2,1)}) custom-call(bf16[256,384]{1,0:T(8,128)(2,1)} %slice.424.query_ref, bf16[256,384]{1,0:T(8,128)(2,1)} %fusion.12.grad_ref, bf16[256,256]{1,0:T(8,128)(2,1)} %copy-done.47, bf16[256,256]{1,0:T(8,128)(2,1)} %collective-permute-done.2.kv1, ...), custom_call_target="tpu_custom_call" | custom-call | tf_op jit(solution)/shard_map/attend_back/pallas_call | solution.py:1143
  375.7 1.8 select_maximum_fusion
  377.7 2.3 dynamic-slice_convert_fusion.1
  380.9 19.4 %weight_grads.3 = (f32[2,4,5,1536,128]{4,3,2,1,0:T(8,128)}, f32[2,4,5,128,768]{4,3,2,1,0:T(8,128)}, f32[8,128]{1,0:T(8,128)}) custom-call(s32[2]{0:T(128)} %pad_add_fusion.1.place_ref, bf16[4,512,768]{2,1,0:T(8,128)(2,1)} %bitcast.242, bf16[4,512,896]{2,1,0:T(8,128)(2,1)} %bitcast.239, bf16[2,4,4,2,128,384]{5,4,3,2,1,0:T(8,128)(2,1)} %bitcast.247, ...), custom_call_target="tpu_custom_call" | custom-call | tf_op jit(solution)/shard_map/weight_grads/pallas_call | solution.py:742
  404.2 3.4 collective-permute-start.28
  410.8 2.2 collective-permute-done.28
  412.9 12.0 %collective-permute-done.29 = bf16[64,1536]{1,0:T(8,128)(2,1)S(1)} collective-permute-done((bf16[64,1536]{1,0:T(8,128)(2,1)S(1)}, bf16[64,1536]{1,0:T(8,128)(2,1)S(1)}, u32[]{:S(2)}, u32[]{:S(2)}) %collective-permute-start.29) | collective-permute-done | bytes 196640 | tf_op jit(solution)/shard_map/ppermute | solution.py:828
  425.2 2.7 collective-permute-start.32
  427.9 1.9 collective-permute-start.33
  432.7 22.7 %collective-permute-done.32 = bf16[64,1536]{1,0:T(8,128)(2,1)S(1)} collective-permute-done((bf16[64,1536]{1,0:T(8,128)(2,1)S(1)}, bf16[64,1536]{1,0:T(8,128)(2,1)S(1)}, u32[]{:S(2)}, u32[]{:S(2)}) %collective-permute-start.32) | collective-permute-done | bytes 196640 | tf_op jit(solution)/shard_map/ppermute | solution.py:828
  458.7 19.5 %weight_grads.4 = (f32[2,4,5,1536,128]{4,3,2,1,0:T(8,128)}, f32[2,4,5,128,768]{4,3,2,1,0:T(8,128)}, f32[8,128]{1,0:T(8,128)}) custom-call(s32[2]{0:T(128)} %pad_add_fusion.1.place_ref, bf16[4,512,768]{2,1,0:T(8,128)(2,1)} %bitcast.243, bf16[4,512,896]{2,1,0:T(8,128)(2,1)} %bitcast.240, ...), custom_call_target="tpu_custom_call", output_to_operand_aliasing={{0}: (6, {}), {1}: (7, {})} | custom-call | tf_op jit(solution)/shard_map/weight_grads/pallas_call | solution.py:742
  478.2 2.2 fusion.10
  480.6 2.2 collective-permute-start.36
  482.8 3.1 fusion.9
  493.6 7.9 %collective-permute-done.41 = bf16[384,640]{1,0:T(8,128)(2,1)S(1)} collective-permute-done((bf16[384,640]{1,0:T(8,128)(2,1)S(1)}, bf16[384,640]{1,0:T(8,128)(2,1)S(1)}, u32[]{:S(2)}, u32[]{:S(2)}) %collective-permute-start.41) | collective-permute-done | bytes 491552 | tf_op jit(solution)/shard_map/ppermute | solution.py:819
  505.2 12.8 %weight_grads.5 = (f32[2,4,5,1536,128]{4,3,2,1,0:T(8,128)}, f32[2,4,5,128,768]{4,3,2,1,0:T(8,128)}, f32[8,128]{1,0:T(8,128)}) custom-call(s32[2]{0:T(128)} %pad_add_fusion.1.place_ref, bf16[4,512,768]{2,1,0:T(8,128)(2,1)} %bitcast.244, bf16[4,512,896]{2,1,0:T(8,128)(2,1)} %bitcast.241, ...), custom_call_target="tpu_custom_call", output_to_operand_aliasing={{0}: (6, {}), {1}: (7, {})} | custom-call | tf_op jit(solution)/shard_map/weight_grads/pallas_call | solution.py:742
  (479 shorter events, 121.7 us)
Async XLA Ops:
  7.2 71.6 %copy-start = (bf16[384,768]{1,0:T(8,128)(2,1)S(1)}, bf16[384,768]{1,0:T(8,128)(2,1)}, u32[]{:S(2)}) copy-start(bf16[384,768]{1,0:T(8,128)(2,1)} %param.20) | copy-start | bytes 1769476
  7.2 204.7 %all-gather.23.cloned.1.call-start = ((), (), s32[]{:S(2)}) async-start(), calls=%async_computation.4 | async-start | bytes 5898240 | tf_op jit(solution)/shard_map/all_gather | solution.py:1020
  11.6 16.4 %collective-permute-start = (bf16[384,768]{0,1:T(8,128)(2,1)S(1)}, bf16[384,768]{0,1:T(8,128)(2,1)}, u32[]{:S(2)}, u32[]{:S(2)}) collective-permute-start(bf16[384,768]{0,1:T(8,128)(2,1)S(1)} %fusion.22), channel_id=1, source_target_pairs={{0,16},{16,0},{1,17},{17,1},{2,18},{18,2},{3,19},{19,3},{4,20},{20... | collective-permute-start | bytes 1769480 | tf_op jit(solution)/shard_map/ppermute | solution.py:819
  28.0 3.4 collective-permute-start.1
  36.1 130.7 %copy-start.8 = (bf16[256,1536]{1,0:T(8,128)(2,1)}, bf16[256,1536]{1,0:T(8,128)(2,1)S(1)}, u32[]{:S(2)}) copy-start(bf16[256,1536]{1,0:T(8,128)(2,1)S(1)} %get-tuple-element.230) | copy-start | bytes 2359300
  45.9 28.7 %collective-permute-start.5 = (bf16[2,2304,128]{2,1,0:T(8,128)(2,1)}, bf16[2,2304,128]{2,1,0:T(8,128)(2,1)}, u32[]{:S(2)}, u32[]{:S(2)}) collective-permute-start(bf16[2,2304,128]{2,1,0:T(8,128)(2,1)} %pad_maximum_fusion.2), channel_id=1, source_target_pairs={{0,16},{16,0},{1,17},{17,1},{2,18},{18,2},{3,19},{19,3},{4,20},{20... | collective-permute-start | bytes 3538952 | tf_op jit(solution)/shard_map/ppermute | solution.py:819
  47.6 5.7 %collective-permute-start.3 = (bf16[256,256]{1,0:T(8,128)(2,1)S(1)}, bf16[256,256]{1,0:T(8,128)(2,1)}, u32[]{:S(2)}, u32[]{:S(2)}) collective-permute-start(bf16[256,256]{1,0:T(8,128)(2,1)S(1)} %pad_maximum_fusion.17.kv0), channel_id=1, source_target_pairs={{0,8},{4,12},{8,0},{12,4},{1,9},{5,13},{9,1},{13,5},{2,10},{6,14},... | collective-permute-start | bytes 393224 | tf_op jit(solution)/shard_map/ppermute | solution.py:825
  49.1 5.3 collective-permute-start.2
  53.3 1.7 collective-permute-start.4
  53.3 24.3 %copy-start.29 = (bf16[2,1,128,1536]{3,2,1,0:T(8,128)(2,1)S(1)}, bf16[2,1,128,1536]{3,2,1,0:T(8,128)(2,1)}, u32[]{:S(2)}) copy-start(bf16[2,1,128,1536]{3,2,1,0:T(8,128)(2,1)} %param.25) | copy-start | bytes 2359300
  74.6 154.1 %all-gather.17.cloned.1.call-start = ((), (), s32[]{:S(2)}) async-start(), calls=%async_computation.1 | async-start | bytes 4587520 | tf_op jit(solution)/shard_map/all_gather | solution.py:1021
  78.8 8.7 %collective-permute-start.6 = (bf16[192,768]{1,0:T(8,128)(2,1)S(1)}, bf16[192,768]{1,0:T(8,128)(2,1)S(1)}, u32[]{:S(2)}, u32[]{:S(2)}) collective-permute-start(bf16[192,768]{1,0:T(8,128)(2,1)S(1)} %constant_dynamic-slice_fusion.9), channel_id=1, source_target_pairs={{0,16},{16,0},{1,17},{17,1},{2,18},{18,2},{3,19},{19,3},{4,20},{20... | collective-permute-start | bytes 884744 | tf_op jit(solution)/shard_map/ppermute | solution.py:819
  87.5 7.8 %collective-permute-start.7 = (bf16[192,768]{1,0:T(8,128)(2,1)S(1)}, bf16[192,768]{1,0:T(8,128)(2,1)S(1)}, u32[]{:S(2)}, u32[]{:S(2)}) collective-permute-start(bf16[192,768]{1,0:T(8,128)(2,1)S(1)} %collective-permute-done.6), channel_id=1, source_target_pairs={{0,4},{4,0},{8,12},{12,8},{1,5},{5,1},{9,13},{13,9},{2,6},{6,2},{1... | collective-permute-start | bytes 884744 | tf_op jit(solution)/shard_map/ppermute | solution.py:822
  89.4 54.8 %copy-start.2 = (bf16[256,1664]{1,0:T(8,128)(2,1)}, bf16[256,1664]{1,0:T(8,128)(2,1)S(1)}, u32[]{:S(2)}) copy-start(bf16[256,1664]{1,0:T(8,128)(2,1)S(1)} %pad_maximum_fusion.5.near_out_ref) | copy-start | bytes 2555908
  100.2 41.0 %collective-permute-start.11 = (bf16[2,2304,128]{2,1,0:T(8,128)(2,1)}, bf16[2,2304,128]{2,1,0:T(8,128)(2,1)}, u32[]{:S(2)}, u32[]{:S(2)}) collective-permute-start(bf16[2,2304,128]{2,1,0:T(8,128)(2,1)} %pad_maximum_fusion.1), channel_id=1, source_target_pairs={{0,16},{16,0},{1,17},{17,1},{2,18},{18,2},{3,19},{19,3},{4,20},{20... | collective-permute-start | bytes 3538952 | tf_op jit(solution)/shard_map/ppermute | solution.py:819
  119.6 9.6 %collective-permute-start.10 = (bf16[64,1536]{1,0:T(8,128)(2,1)S(1)}, bf16[64,1536]{1,0:T(8,128)(2,1)S(1)}, u32[]{:S(2)}, u32[]{:S(2)}) collective-permute-start(bf16[64,1536]{1,0:T(8,128)(2,1)S(1)} %get-tuple-element.262), channel_id=1, source_target_pairs={{3,0},{0,1},{1,2},{2,3},{7,4},{4,5},{5,6},{6,7},{11,8},{8,9},{9,10... | collective-permute-start | bytes 589832 | tf_op jit(solution)/shard_map/ppermute | solution.py:828
  121.2 10.9 %collective-permute-start.8 = (bf16[64,1536]{1,0:T(8,128)(2,1)S(1)}, bf16[64,1536]{1,0:T(8,128)(2,1)S(1)}, u32[]{:S(2)}, u32[]{:S(2)}) collective-permute-start(bf16[64,1536]{1,0:T(8,128)(2,1)S(1)} %get-tuple-element.261), channel_id=1, source_target_pairs={{1,0},{2,1},{3,2},{0,3},{5,4},{6,5},{7,6},{4,7},{9,8},{10,9},{11,1... | collective-permute-start | bytes 589832 | tf_op jit(solution)/shard_map/ppermute | solution.py:828
  123.5 17.6 %collective-permute-start.9 = (bf16[64,1536]{1,0:T(8,128)(2,1)S(1)}, bf16[64,1536]{1,0:T(8,128)(2,1)S(1)}, u32[]{:S(2)}, u32[]{:S(2)}) collective-permute-start(bf16[64,1536]{1,0:T(8,128)(2,1)S(1)} %get-tuple-element.263), channel_id=1, source_target_pairs={{2,0},{3,1},{0,2},{1,3},{6,4},{7,5},{4,6},{5,7},{10,8},{11,9},{8,1... | collective-permute-start | bytes 589832 | tf_op jit(solution)/shard_map/ppermute | solution.py:828
  141.2 8.4 %collective-permute-start.12 = (bf16[64,1536]{1,0:T(8,128)(2,1)S(1)}, bf16[64,1536]{1,0:T(8,128)(2,1)S(1)}, u32[]{:S(2)}, u32[]{:S(2)}) collective-permute-start(bf16[64,1536]{1,0:T(8,128)(2,1)S(1)} %add_convert_fusion.6), channel_id=1, source_target_pairs={{1,0},{2,1},{3,2},{0,3},{5,4},{6,5},{7,6},{4,7},{9,8},{10,9},{11,1... | collective-permute-start | bytes 589832 | tf_op jit(solution)/shard_map/ppermute | solution.py:828
  142.9 15.6 %collective-permute-start.13 = (bf16[64,1536]{1,0:T(8,128)(2,1)S(1)}, bf16[64,1536]{1,0:T(8,128)(2,1)S(1)}, u32[]{:S(2)}, u32[]{:S(2)}) collective-permute-start(bf16[64,1536]{1,0:T(8,128)(2,1)S(1)} %add_convert_fusion.6), channel_id=1, source_target_pairs={{2,0},{3,1},{0,2},{1,3},{6,4},{7,5},{4,6},{5,7},{10,8},{11,9},{8,1... | collective-permute-start | bytes 589832 | tf_op jit(solution)/shard_map/ppermute | solution.py:828
  142.9 15.6 %collective-permute-start.14 = (bf16[64,1536]{1,0:T(8,128)(2,1)S(1)}, bf16[64,1536]{1,0:T(8,128)(2,1)S(1)}, u32[]{:S(2)}, u32[]{:S(2)}) collective-permute-start(bf16[64,1536]{1,0:T(8,128)(2,1)S(1)} %add_convert_fusion.6), channel_id=1, source_target_pairs={{3,0},{0,1},{1,2},{2,3},{7,4},{4,5},{5,6},{6,7},{11,8},{8,9},{9,10... | collective-permute-start | bytes 589832 | tf_op jit(solution)/shard_map/ppermute | solution.py:828
  143.6 20.0 %collective-permute-start.15 = (bf16[256,1664]{1,0:T(8,128)(2,1)S(1)}, bf16[256,1664]{1,0:T(8,128)(2,1)S(1)}, u32[]{:S(2)}, u32[]{:S(2)}) collective-permute-start(bf16[256,1664]{1,0:T(8,128)(2,1)S(1)} %pad_maximum_fusion.5.near_out_ref), channel_id=1, source_target_pairs={{0,16},{16,0},{1,17},{17,1},{2,18},{18,2},{3,19},{19,3},{4,20},{20... | collective-permute-start | bytes 2555912 | tf_op jit(solution)/shard_map/ppermute | solution.py:819
  165.6 70.3 %all-gather.21.cloned.1.call-start = ((), (), s32[]{:S(2)}) async-start(), calls=%async_computation.3 | async-start | bytes 5898240 | tf_op jit(solution)/shard_map/all_gather | solution.py:1020
  166.3 95.1 %all-gather.19.cloned.1.call-start = ((), (), s32[]{:S(2)}) async-start(), calls=%async_computation.2 | async-start | bytes 2949120 | tf_op jit(solution)/shard_map/all_gather | solution.py:1020
  169.4 35.4 %copy-start.5 = (bf16[256,1536]{1,0:T(8,128)(2,1)}, bf16[256,1536]{1,0:T(8,128)(2,1)S(1)}, u32[]{:S(2)}) copy-start(bf16[256,1536]{1,0:T(8,128)(2,1)S(1)} %multiply_convert_fusion.1) | copy-start | bytes 2359300
  172.0 19.1 %collective-permute-start.16 = (bf16[256,1664]{1,0:T(8,128)(2,1)S(1)}, bf16[256,1664]{1,0:T(8,128)(2,1)S(1)}, u32[]{:S(2)}, u32[]{:S(2)}) collective-permute-start(bf16[256,1664]{1,0:T(8,128)(2,1)S(1)} %pad_maximum_fusion.6.near_ref), channel_id=1, source_target_pairs={{0,16},{16,0},{1,17},{17,1},{2,18},{18,2},{3,19},{19,3},{4,20},{20... | collective-permute-start | bytes 2555912 | tf_op jit(solution)/shard_map/ppermute | solution.py:819
  192.0 12.8 %collective-permute-start.17 = (bf16[1,2304,128]{2,1,0:T(8,128)(2,1)S(1)}, bf16[1,2304,128]{2,1,0:T(8,128)(2,1)}, u32[]{:S(2)}, u32[]{:S(2)}) collective-permute-start(bf16[1,2304,128]{2,1,0:T(8,128)(2,1)S(1)} %copy-done.61), channel_id=1, source_target_pairs={{0,16},{16,0},{1,17},{17,1},{2,18},{18,2},{3,19},{19,3},{4,20},{20... | collective-permute-start | bytes 1769480 | tf_op jit(solution)/shard_map/ppermute | solution.py:819
  204.8 86.6 %all-gather.25.cloned.1.call-start = ((), (), s32[]{:S(2)}) async-start(), calls=%async_computation.5 | async-start | bytes 3932160 | tf_op jit(solution)/shard_map/all_gather | solution.py:1031
  205.9 149.0 %all-gather.27.cloned.1.call-start = ((), (), s32[]{:S(2)}) async-start(), calls=%async_computation.6 | async-start | bytes 7077888 | tf_op jit(solution)/shard_map/all_gather | solution.py:1095
  228.2 149.6 %all-gather.29.cloned.1.call-start = ((), (), s32[]{:S(2)}) async-start(), calls=%async_computation.7 | async-start | bytes 3538944 | tf_op jit(solution)/shard_map/all_gather | solution.py:1095
  274.6 184.1 %all-gather.31.cloned.1.call-start = ((), (), s32[]{:S(2)}) async-start(), calls=%async_computation.8 | async-start | bytes 7077888 | tf_op jit(solution)/shard_map/all_gather | solution.py:1095
  275.4 207.4 %all-reduce.8.cloned.1.call-start = ((), (), s32[]{:S(2)}) async-start(), calls=%async_computation | async-start | bytes 1572864 | tf_op jit(solution)/shard_map/psum | solution.py:1130
  280.2 21.4 %collective-permute-start.18 = (bf16[256,1664]{1,0:T(8,128)(2,1)}, bf16[256,1664]{1,0:T(8,128)(2,1)}, u32[]{:S(2)}, u32[]{:S(2)}) collective-permute-start(bf16[256,1664]{1,0:T(8,128)(2,1)} %fusion.16), channel_id=1, source_target_pairs={{0,16},{16,0},{1,17},{17,1},{2,18},{18,2},{3,19},{19,3},{4,20},{20... | collective-permute-start | bytes 2555912 | tf_op jit(solution)/shard_map/ppermute | solution.py:819
  306.2 9.4 %collective-permute-start.20 = (bf16[64,1664]{1,0:T(8,128)(2,1)}, bf16[64,1664]{1,0:T(8,128)(2,1)}, u32[]{:S(2)}, u32[]{:S(2)}) collective-permute-start(bf16[64,1664]{1,0:T(8,128)(2,1)} %get-tuple-element.249), channel_id=1, source_target_pairs={{1,0},{2,1},{3,2},{0,3},{5,4},{6,5},{7,6},{4,7},{9,8},{10,9},{11,1... | collective-permute-start | bytes 638984 | tf_op jit(solution)/shard_map/ppermute | solution.py:828
  309.5 18.3 %collective-permute-start.21 = (bf16[64,1664]{1,0:T(8,128)(2,1)}, bf16[64,1664]{1,0:T(8,128)(2,1)}, u32[]{:S(2)}, u32[]{:S(2)}) collective-permute-start(bf16[64,1664]{1,0:T(8,128)(2,1)} %get-tuple-element.250), channel_id=1, source_target_pairs={{2,0},{3,1},{0,2},{1,3},{6,4},{7,5},{4,6},{5,7},{10,8},{11,9},{8,1... | collective-permute-start | bytes 638984 | tf_op jit(solution)/shard_map/ppermute | solution.py:828
  309.5 18.3 %collective-permute-start.22 = (bf16[64,1664]{1,0:T(8,128)(2,1)S(1)}, bf16[64,1664]{1,0:T(8,128)(2,1)}, u32[]{:S(2)}, u32[]{:S(2)}) collective-permute-start(bf16[64,1664]{1,0:T(8,128)(2,1)S(1)} %get-tuple-element.251), channel_id=1, source_target_pairs={{3,0},{0,1},{1,2},{2,3},{7,4},{4,5},{5,6},{6,7},{11,8},{8,9},{9,10... | collective-permute-start | bytes 638984 | tf_op jit(solution)/shard_map/ppermute | solution.py:828
  329.0 7.9 %collective-permute-start.23 = (bf16[64,1664]{1,0:T(8,128)(2,1)S(1)}, bf16[64,1664]{1,0:T(8,128)(2,1)S(1)}, u32[]{:S(2)}, u32[]{:S(2)}) collective-permute-start(bf16[64,1664]{1,0:T(8,128)(2,1)S(1)} %get-tuple-element.232), channel_id=1, source_target_pairs={{1,0},{2,1},{3,2},{0,3},{5,4},{6,5},{7,6},{4,7},{9,8},{10,9},{11,1... | collective-permute-start | bytes 638984 | tf_op jit(solution)/shard_map/ppermute | solution.py:828
  330.5 23.2 %collective-permute-start.19 = (bf16[256,1536]{1,0:T(8,128)(2,1)S(1)}, bf16[256,1536]{1,0:T(8,128)(2,1)S(1)}, u32[]{:S(2)}, u32[]{:S(2)}) collective-permute-start(bf16[256,1536]{1,0:T(8,128)(2,1)S(1)} %copy-done.54), channel_id=1, source_target_pairs={{0,16},{16,0},{1,17},{17,1},{2,18},{18,2},{3,19},{19,3},{4,20},{20... | collective-permute-start | bytes 2359304 | tf_op jit(solution)/shard_map/ppermute | solution.py:819
  332.1 18.1 %collective-permute-start.24 = (bf16[64,1664]{1,0:T(8,128)(2,1)S(1)}, bf16[64,1664]{1,0:T(8,128)(2,1)S(1)}, u32[]{:S(2)}, u32[]{:S(2)}) collective-permute-start(bf16[64,1664]{1,0:T(8,128)(2,1)S(1)} %get-tuple-element.232), channel_id=1, source_target_pairs={{2,0},{3,1},{0,2},{1,3},{6,4},{7,5},{4,6},{5,7},{10,8},{11,9},{8,1... | collective-permute-start | bytes 638984 | tf_op jit(solution)/shard_map/ppermute | solution.py:828
  334.8 15.4 %collective-permute-start.25 = (bf16[64,1664]{1,0:T(8,128)(2,1)S(1)}, bf16[64,1664]{1,0:T(8,128)(2,1)S(1)}, u32[]{:S(2)}, u32[]{:S(2)}) collective-permute-start(bf16[64,1664]{1,0:T(8,128)(2,1)S(1)} %get-tuple-element.232), channel_id=1, source_target_pairs={{3,0},{0,1},{1,2},{2,3},{7,4},{4,5},{5,6},{6,7},{11,8},{8,9},{9,10... | collective-permute-start | bytes 638984 | tf_op jit(solution)/shard_map/ppermute | solution.py:828
  367.4 4.5 collective-permute-start.26
  374.2 26.2 %collective-permute-start.27 = (bf16[256,256]{1,0:T(8,128)(2,1)}, bf16[256,256]{1,0:T(8,128)(2,1)}, u32[]{:S(2)}, u32[]{:S(2)}) collective-permute-start(bf16[256,256]{1,0:T(8,128)(2,1)} %fusion.69), channel_id=1, source_target_pairs={{0,8},{4,12},{8,0},{12,4},{1,9},{5,13},{9,1},{13,5},{2,10},{6,14},... | collective-permute-start | bytes 393224 | tf_op jit(solution)/shard_map/ppermute | solution.py:825
  380.0 49.8 %collective-permute-start.44 = (bf16[2,224,768]{2,1,0:T(8,128)(2,1)}, bf16[2,224,768]{2,1,0:T(8,128)(2,1)}, u32[]{:S(2)}, u32[]{:S(2)}) collective-permute-start(bf16[2,224,768]{2,1,0:T(8,128)(2,1)} %dynamic-slice_convert_fusion.1), channel_id=1, source_target_pairs={{0,4},{4,0},{8,12},{12,8},{1,5},{5,1},{9,13},{13,9},{2,6},{6,2},{1... | collective-permute-start | bytes 2064392 | tf_op jit(solution)/shard_map/ppermute | solution.py:822
  404.2 8.7 %collective-permute-start.28 = (bf16[64,1536]{1,0:T(8,128)(2,1)S(1)}, bf16[64,1536]{1,0:T(8,128)(2,1)S(1)}, u32[]{:S(2)}, u32[]{:S(2)}) collective-permute-start(bf16[64,1536]{1,0:T(8,128)(2,1)S(1)} %get-tuple-element.254), channel_id=1, source_target_pairs={{1,0},{2,1},{3,2},{0,3},{5,4},{6,5},{7,6},{4,7},{9,8},{10,9},{11,1... | collective-permute-start | bytes 589832 | tf_op jit(solution)/shard_map/ppermute | solution.py:828
  407.6 17.3 %collective-permute-start.29 = (bf16[64,1536]{1,0:T(8,128)(2,1)S(1)}, bf16[64,1536]{1,0:T(8,128)(2,1)S(1)}, u32[]{:S(2)}, u32[]{:S(2)}) collective-permute-start(bf16[64,1536]{1,0:T(8,128)(2,1)S(1)} %get-tuple-element.256), channel_id=1, source_target_pairs={{2,0},{3,1},{0,2},{1,3},{6,4},{7,5},{4,6},{5,7},{10,8},{11,9},{8,1... | collective-permute-start | bytes 589832 | tf_op jit(solution)/shard_map/ppermute | solution.py:828
  407.6 17.3 %collective-permute-start.30 = (bf16[64,1536]{1,0:T(8,128)(2,1)S(1)}, bf16[64,1536]{1,0:T(8,128)(2,1)S(1)}, u32[]{:S(2)}, u32[]{:S(2)}) collective-permute-start(bf16[64,1536]{1,0:T(8,128)(2,1)S(1)} %get-tuple-element.255), channel_id=1, source_target_pairs={{3,0},{0,1},{1,2},{2,3},{7,4},{4,5},{5,6},{6,7},{11,8},{8,9},{9,10... | collective-permute-start | bytes 589832 | tf_op jit(solution)/shard_map/ppermute | solution.py:828
  409.7 45.8 %copy-start.9 = (f32[2,768,640]{2,1,0:T(8,128)}, f32[2,768,640]{2,1,0:T(8,128)S(1)}, u32[]{:S(2)}) copy-start(f32[2,768,640]{2,1,0:T(8,128)S(1)} %fusion.47) | copy-start | bytes 11796484
  410.8 76.6 %collective-permute-start.40 = (bf16[2,384,640]{2,1,0:T(8,128)(2,1)}, bf16[2,384,640]{2,1,0:T(8,128)(2,1)}, u32[]{:S(2)}, u32[]{:S(2)}) collective-permute-start(bf16[2,384,640]{2,1,0:T(8,128)(2,1)} %dynamic-slice_convert_fusion), channel_id=1, source_target_pairs={{0,4},{4,0},{8,12},{12,8},{1,5},{5,1},{9,13},{13,9},{2,6},{6,2},{1... | collective-permute-start | bytes 2949128 | tf_op jit(solution)/shard_map/ppermute | solution.py:822
  425.0 7.7 %collective-permute-start.31 = (bf16[64,1536]{1,0:T(8,128)(2,1)S(1)}, bf16[64,1536]{1,0:T(8,128)(2,1)S(1)}, u32[]{:S(2)}, u32[]{:S(2)}) collective-permute-start(bf16[64,1536]{1,0:T(8,128)(2,1)S(1)} %add_convert_fusion.5), channel_id=1, source_target_pairs={{1,0},{2,1},{3,2},{0,3},{5,4},{6,5},{7,6},{4,7},{9,8},{10,9},{11,1... | collective-permute-start | bytes 589832 | tf_op jit(solution)/shard_map/ppermute | solution.py:828
  425.2 30.2 %collective-permute-start.32 = (bf16[64,1536]{1,0:T(8,128)(2,1)S(1)}, bf16[64,1536]{1,0:T(8,128)(2,1)S(1)}, u32[]{:S(2)}, u32[]{:S(2)}) collective-permute-start(bf16[64,1536]{1,0:T(8,128)(2,1)S(1)} %add_convert_fusion.5), channel_id=1, source_target_pairs={{2,0},{3,1},{0,2},{1,3},{6,4},{7,5},{4,6},{5,7},{10,8},{11,9},{8,1... | collective-permute-start | bytes 589832 | tf_op jit(solution)/shard_map/ppermute | solution.py:828
  427.9 27.6 %collective-permute-start.33 = (bf16[64,1536]{1,0:T(8,128)(2,1)S(1)}, bf16[64,1536]{1,0:T(8,128)(2,1)S(1)}, u32[]{:S(2)}, u32[]{:S(2)}) collective-permute-start(bf16[64,1536]{1,0:T(8,128)(2,1)S(1)} %add_convert_fusion.5), channel_id=1, source_target_pairs={{3,0},{0,1},{1,2},{2,3},{7,4},{4,5},{5,6},{6,7},{11,8},{8,9},{9,10... | collective-permute-start | bytes 589832 | tf_op jit(solution)/shard_map/ppermute | solution.py:828
  431.1 25.4 %copy-start.16 = (f32[2,224,768]{2,1,0:T(8,128)}, f32[2,224,768]{2,1,0:T(8,128)S(1)}, u32[]{:S(2)}) copy-start(f32[2,224,768]{2,1,0:T(8,128)S(1)} %convert_add_fusion.2) | copy-start | bytes 4128772
  431.2 25.3 %collective-permute-start.45 = (bf16[224,768]{1,0:T(8,128)(2,1)S(1)}, bf16[224,768]{1,0:T(8,128)(2,1)S(1)}, u32[]{:S(2)}, u32[]{:S(2)}) collective-permute-start(bf16[224,768]{1,0:T(8,128)(2,1)S(1)} %fusion.45), channel_id=1, source_target_pairs={{0,16},{16,0},{1,17},{17,1},{2,18},{18,2},{3,19},{19,3},{4,20},{20... | collective-permute-start | bytes 1032200 | tf_op jit(solution)/shard_map/ppermute | solution.py:819
  457.4 62.2 %collective-permute-start.46 = (bf16[224,768]{1,0:T(8,128)(2,1)}, bf16[224,768]{1,0:T(8,128)(2,1)}, u32[]{:S(2)}, u32[]{:S(2)}) collective-permute-start(bf16[224,768]{1,0:T(8,128)(2,1)} %fusion.35), channel_id=1, source_target_pairs={{0,8},{4,12},{8,0},{12,4},{1,9},{5,13},{9,1},{13,5},{2,10},{6,14},... | collective-permute-start | bytes 1032200 | tf_op jit(solution)/shard_map/ppermute | solution.py:825
  480.5 10.4 %collective-permute-start.34 = (f32[1536]{0:T(1024)S(1)}, f32[1536]{0:T(1024)S(1)}, u32[]{:S(2)}, u32[]{:S(2)}) collective-permute-start(f32[1536]{0:T(1024)S(1)} %get-tuple-element.201), channel_id=1, source_target_pairs={{1,0},{2,1},{3,2},{0,3},{5,4},{6,5},{7,6},{4,7},{9,8},{10,9},{11,1... | collective-permute-start | bytes 18440 | tf_op jit(solution)/shard_map/ppermute | solution.py:828
  480.5 10.3 %collective-permute-start.35 = (f32[1536]{0:T(1024)S(1)}, f32[1536]{0:T(1024)S(1)}, u32[]{:S(2)}, u32[]{:S(2)}) collective-permute-start(f32[1536]{0:T(1024)S(1)} %get-tuple-element.201), channel_id=1, source_target_pairs={{2,0},{3,1},{0,2},{1,3},{6,4},{7,5},{4,6},{5,7},{10,8},{11,9},{8,1... | collective-permute-start | bytes 18440 | tf_op jit(solution)/shard_map/ppermute | solution.py:828
  480.6 10.3 %collective-permute-start.36 = (f32[1536]{0:T(1024)S(1)}, f32[1536]{0:T(1024)S(1)}, u32[]{:S(2)}, u32[]{:S(2)}) collective-permute-start(f32[1536]{0:T(1024)S(1)} %get-tuple-element.201), channel_id=1, source_target_pairs={{3,0},{0,1},{1,2},{2,3},{7,4},{4,5},{5,6},{6,7},{11,8},{8,9},{9,10... | collective-permute-start | bytes 18440 | tf_op jit(solution)/shard_map/ppermute | solution.py:828
  490.1 11.4 %collective-permute-start.41 = (bf16[384,640]{1,0:T(8,128)(2,1)S(1)}, bf16[384,640]{1,0:T(8,128)(2,1)S(1)}, u32[]{:S(2)}, u32[]{:S(2)}) collective-permute-start(bf16[384,640]{1,0:T(8,128)(2,1)S(1)} %fusion.34), channel_id=1, source_target_pairs={{0,16},{16,0},{1,17},{17,1},{2,18},{18,2},{3,19},{19,3},{4,20},{20... | collective-permute-start | bytes 1474568 | tf_op jit(solution)/shard_map/ppermute | solution.py:819
  490.9 1.2 collective-permute-start.37
  492.1 25.9 %collective-permute-start.38 = (f32[1536]{0:T(1024)S(1)}, f32[1536]{0:T(1024)S(1)}, u32[]{:S(2)}, u32[]{:S(2)}) collective-permute-start(f32[1536]{0:T(1024)S(1)} %add.376), channel_id=1, source_target_pairs={{0,8},{4,12},{8,0},{12,4},{1,9},{5,13},{9,1},{13,5},{2,10},{6,14},... | collective-permute-start | bytes 18440 | tf_op jit(solution)/shard_map/ppermute | solution.py:825
  502.4 18.5 %collective-permute-start.42 = (bf16[384,640]{1,0:T(8,128)(2,1)}, bf16[384,640]{1,0:T(8,128)(2,1)}, u32[]{:S(2)}, u32[]{:S(2)}) collective-permute-start(bf16[384,640]{1,0:T(8,128)(2,1)} %fusion.19), channel_id=1, source_target_pairs={{0,8},{4,12},{8,0},{12,4},{1,9},{5,13},{9,1},{13,5},{2,10},{6,14},... | collective-permute-start | bytes 1474568 | tf_op jit(solution)/shard_map/ppermute | solution.py:825
  518.1 4.6 collective-permute-start.39
  520.8 2.4 collective-permute-start.47
  522.1 3.7 collective-permute-start.43
  (89 other events, 516.6 us)
Sparse Core Ops, SparseCore 0:
  74.7 38.9 all-gather.22
  165.7 31.0 all-gather.16
  198.4 37.4 all-gather.20
  237.3 24.0 all-gather.18
  262.8 28.5 all-gather.24
  293.2 49.8 all-gather.26
  345.5 32.2 all-gather.28
  379.6 45.5 all-gather.30
  427.6 53.5 all-reduce.7

commit v4 on v0

--- a/solution.py
+++ b/solution.py
@@ -1,6 +1,10 @@
+import functools
+
 import jax
 import jax.numpy as jnp
 from jax import lax
+from jax.experimental import pallas as pl
+from jax.experimental.pallas import tpu as pltpu
 from jax.sharding import PartitionSpec as P
 
 HEAD_DIM = 64
@@ -404,6 +408,1205 @@
     )
 
 
+def dot(left, right, left_dim=1, right_dim=0):
+    return lax.dot_general(
+        left, right, (((left_dim,), (right_dim,)), ((), ())), preferred_element_type=jnp.float32
+    )
+
+
+def kernel_params(count=0):
+    return pltpu.CompilerParams(
+        dimension_semantics=("arbitrary",) * count if count else None,
+        vmem_limit_bytes=60 * 1024 * 1024,
+    )
+
+
+def single(kernel, name, out_shape, scratch, scalars, *arrays):
+    smem = pl.BlockSpec(memory_space=pltpu.SMEM)
+    vmem = pl.BlockSpec(memory_space=pltpu.VMEM)
+    return pl.pallas_call(
+        kernel,
+        out_shape=tuple(jax.ShapeDtypeStruct(shape, kind) for shape, kind in out_shape),
+        in_specs=[smem] * len(scalars) + [vmem] * len(arrays),
+        out_specs=(vmem,) * len(out_shape),
+        scratch_shapes=[pltpu.VMEM(shape, kind) for shape, kind in scratch],
+        compiler_params=kernel_params(),
+        name=name,
+    )(*scalars, *arrays)
+
+
+def tree_path(parents_ref, m, start):
+    path = [start]
+    for _ in range(3):
+        path.append(parents_ref[m, path[-1]])
+    return path
+
+
+def own_then_other(x_pos, array):
+    half = array.shape[-1] // 2
+    first, second = array[..., :half], array[..., half:]
+    return jnp.where(x_pos == 0, first, second), jnp.where(x_pos == 0, second, first)
+
+
+def row_scale(near, far):
+    total = jnp.sum(near * near, axis=1, keepdims=True) + jnp.sum(far * far, axis=1, keepdims=True)
+    return lax.rsqrt(total / (2 * near.shape[1]) + EPSILON)
+
+
+def turn_heads(values):
+    half_dim = HEAD_DIM // 2
+    lane = lax.broadcasted_iota(jnp.int32, values.shape, 1) % HEAD_DIM
+    width = values.shape[1]
+    return jnp.where(
+        lane < half_dim,
+        -pltpu.roll(values, width - half_dim, 1),
+        pltpu.roll(values, half_dim, 1),
+    )
+
+
+def split_kernel(base_ref, both_ref, down_ref, out_ref, wide_buf):
+    wide_buf[...] = both_ref[0].astype(jnp.float32)
+    half = both_ref.shape[1] // 2
+    out_ref[0, :half, :] = wide_buf[pl.ds(0, half, stride=2), :].astype(jnp.bfloat16)
+    out_ref[0, half : 2 * half, :] = wide_buf[pl.ds(1, half, stride=2), :].astype(jnp.bfloat16)
+    if down_ref is not None:
+        width = down_ref.shape[1]
+        for j in range(half // 128):
+            out_ref[0, 2 * half + j * width : 2 * half + (j + 1) * width, :] = down_ref[
+                0, :, j * 128 : (j + 1) * 128
+            ]
+
+
+def split_plain_kernel(base_ref, both_ref, out_ref, wide_buf):
+    split_kernel(base_ref, both_ref, None, out_ref, wide_buf)
+
+
+def split_weights(base, count, gate_up, down):
+    _, rows, width = gate_up.shape
+    packed = rows if down is None else rows + rows // 2
+    in_specs = [pl.BlockSpec((1, rows, width), lambda i, base: (base[0] + i, 0, 0))]
+    operands = [base, gate_up]
+    if down is not None:
+        in_specs.append(
+            pl.BlockSpec((1, *down.shape[1:]), lambda i, base: (base[0] + i, 0, 0))
+        )
+        operands.append(down)
+    return pl.pallas_call(
+        split_plain_kernel if down is None else split_kernel,
+        out_shape=jax.ShapeDtypeStruct((count, packed, width), jnp.bfloat16),
+        grid_spec=pltpu.PrefetchScalarGridSpec(
+            num_scalar_prefetch=1,
+            grid=(count,),
+            in_specs=in_specs,
+            out_specs=pl.BlockSpec((1, packed, width), lambda i, base: (i, 0, 0)),
+            scratch_shapes=[pltpu.VMEM((rows, width), jnp.float32)],
+        ),
+        compiler_params=kernel_params(1),
+        name="split_weights",
+    )(*operands)
+
+
+def before_kernel(
+    place_ref,
+    parents_ref,
+    hidden_ref,
+    small_ref,
+    sent_ref,
+    next_ref,
+    cosine_ref,
+    sine_ref,
+    normed_ref,
+    query_ref,
+    key_value_ref,
+    far_ref,
+    gains_ref,
+    turn_ref,
+):
+    x_pos, c_pos = place_ref[0], place_ref[1]
+    first_core = c_pos % 2 == 0
+    half = small_ref.shape[1]
+    part = half // 2
+    q_cols = query_ref.shape[1]
+    kv_cols = key_value_ref.shape[1]
+    cols = q_cols + kv_cols
+    turned_cols = q_cols + kv_cols // 2
+    own_rows = small_ref[: 2 * part, :]
+    sent, beside = sent_ref[:part, :], next_ref[:part, :]
+    top = jnp.where(first_core, sent, beside)
+    low_rows = jnp.where(first_core, beside, sent)
+    far_ref[:part, :] = top
+    far_ref[part:, :] = low_rows
+    own_gain = small_ref[2 * part : 2 * part + 16, :].astype(jnp.float32)
+    far_gain = sent_ref[part : part + 16, :].astype(jnp.float32)
+    gains_ref[:, :half] = own_gain
+    gains_ref[:, half:] = far_gain
+    near, far = own_then_other(x_pos, hidden_ref[...].astype(jnp.float32))
+    scale = row_scale(near, far)
+    near_low = (near * scale * own_gain[:1]).astype(jnp.bfloat16)
+    far_low = (far * scale * far_gain[:1]).astype(jnp.bfloat16)
+    normed_ref[:, :half] = near_low
+    normed_ref[:, half:] = far_low
+    made = (
+        dot(near_low, own_rows[:, :cols])
+        + dot(far_low[:, :part], top[:, :cols])
+        + dot(far_low[:, part:], low_rows[:, :cols])
+    )
+    micro = parents_ref.shape[0]
+    rows = hidden_ref.shape[0] // micro
+    turns = []
+    for m in range(micro):
+        path = tree_path(parents_ref, m, c_pos)
+        depth = sum((path[i + 1] != path[i]).astype(jnp.int32) for i in range(3))
+        span = pl.ds(depth * rows, rows)
+        turns.append((cosine_ref[span, :], sine_ref[span, :]))
+    cosines = jnp.concatenate([pair[0] for pair in turns], axis=0)
+    sines = jnp.concatenate([pair[1] for pair in turns], axis=0)
+    turn_ref[0] = cosines
+    turn_ref[1] = sines
+    count = turned_cols // 128
+    values = made[:, :turned_cols]
+    rotated = (
+        values * jnp.concatenate([cosines] * count, axis=1)
+        + turn_heads(values) * jnp.concatenate([sines] * count, axis=1)
+    ).astype(jnp.bfloat16)
+    query_ref[...] = rotated[:, :q_cols]
+    key_value_ref[:, : kv_cols // 2] = rotated[:, q_cols:]
+    key_value_ref[:, kv_cols // 2 :] = made[:, turned_cols:].astype(jnp.bfloat16)
+
+
+def give_pieces(whole_ref, z_pos, piece_refs):
+    count = len(piece_refs)
+    part = whole_ref.shape[0] // count
+    for s in range(count):
+        start = pl.multiple_of(((z_pos + s) % count) * part, part)
+        piece_refs[s][...] = whole_ref[pl.ds(start, part), :].astype(piece_refs[s].dtype)
+
+
+def take_pieces(piece_refs, z_pos, whole_ref):
+    count = len(piece_refs)
+    part = whole_ref.shape[0] // count
+    for s in range(count):
+        start = pl.multiple_of(((z_pos + s) % count) * part, part)
+        whole_ref[pl.ds(start, part), :] = piece_refs[s][...].astype(whole_ref.dtype)
+
+
+def stack_heads(source, first, group):
+    return jnp.concatenate(
+        [source[:, (first + h) * HEAD_DIM : (first + h + 1) * HEAD_DIM] for h in range(group)],
+        axis=0,
+    )
+
+
+def attend_kernel(
+    place_ref,
+    parents_ref,
+    query_ref,
+    kv0,
+    kv1,
+    kv2,
+    kv3,
+    out_near_ref,
+    out_sent_ref,
+    out_next_ref,
+    head_ref,
+    probs_ref,
+    out_far_ref,
+    *rest,
+):
+    piece_refs, whole_buf = rest[:-1], rest[-1]
+    c_pos = place_ref[1]
+    blocks = (kv0, kv1, kv2, kv3)
+    micro = parents_ref.shape[0]
+    rows = query_ref.shape[0] // micro
+    kv_heads = kv0.shape[1] // (2 * HEAD_DIM)
+    group = query_ref.shape[1] // HEAD_DIM // kv_heads
+    shape = (group * rows, rows)
+    causal = (
+        lax.broadcasted_iota(jnp.int32, shape, 1)
+        <= lax.broadcasted_iota(jnp.int32, shape, 0) % rows
+    )
+    for m in range(micro):
+        span = pl.ds(m * rows, rows)
+        whole = query_ref[span, :]
+        path = tree_path(parents_ref, m, c_pos)
+        pieces = []
+        for g in range(kv_heads):
+            query = stack_heads(whole, g * group, group)
+            parts = []
+            for r in range(4):
+                keys = blocks[r][span, :][:, g * HEAD_DIM : (g + 1) * HEAD_DIM]
+                part = dot(query, keys, 1, 1) * SCORE_SCALE
+                if r == 0:
+                    part = jnp.where(causal, part, -1e30)
+                else:
+                    seen = (path[1] == c_pos ^ r) | (path[2] == c_pos ^ r) | (path[3] == c_pos ^ r)
+                    part = jnp.where(seen, part, -1e30)
+                parts.append(part)
+            scores = jnp.concatenate(parts, axis=1)
+            powers = jnp.exp(scores - jnp.max(scores, axis=1, keepdims=True))
+            probs = powers * (1.0 / jnp.sum(powers, axis=1, keepdims=True))
+            probs_ref[m * kv_heads + g] = probs
+            low = probs.astype(jnp.bfloat16)
+            values = jnp.concatenate(
+                [
+                    blocks[r][span, :][:, (kv_heads + g) * HEAD_DIM : (kv_heads + g + 1) * HEAD_DIM]
+                    for r in range(4)
+                ],
+                axis=0,
+            )
+            mixed = dot(low, values)
+            pieces += [mixed[h * rows : (h + 1) * rows] for h in range(group)]
+        head_ref[span, :] = jnp.concatenate(pieces, axis=1).astype(jnp.bfloat16)
+    first_core = c_pos % 2 == 0
+    sent, beside = out_sent_ref[...], out_next_ref[...]
+    part = sent.shape[0]
+    out_far_ref[:part, :] = jnp.where(first_core, sent, beside)
+    out_far_ref[part:, :] = jnp.where(first_core, beside, sent)
+    half = sent.shape[1]
+    whole_buf[:, :half] = dot(head_ref[...], out_near_ref[...])
+    whole_buf[:, half:] = dot(head_ref[...], out_far_ref[...])
+    give_pieces(whole_buf, place_ref[2], piece_refs)
+
+
+def after_kernel(place_ref, hidden_ref, gains_ref, small_ref, far_ref, routes_ref, *rest):
+    mixed_ref, rows_ref, gates_ref, whole_buf = rest[-4:]
+    take_pieces(rest[:-4], place_ref[2], whole_buf)
+    half = small_ref.shape[1]
+    near, far = own_then_other(place_ref[0], hidden_ref[...].astype(jnp.float32))
+    near = near + RESIDUAL_SCALE * whole_buf[:, :half]
+    far = far + RESIDUAL_SCALE * whole_buf[:, half:]
+    mixed_ref[:, :half] = near
+    mixed_ref[:, half:] = far
+    scale = row_scale(near, far)
+    near_low = (near * scale * gains_ref[1:2, :half]).astype(jnp.bfloat16)
+    far_low = (far * scale * gains_ref[1:2, half:]).astype(jnp.bfloat16)
+    rows_ref[:, :half] = near_low
+    rows_ref[:, half : 2 * half] = far_low
+    logits = dot(near_low, small_ref[:half, half - 128 :]) + dot(far_low, far_ref[:, half - 128 :])
+    lane = lax.broadcasted_iota(jnp.int32, logits.shape, 1)
+    named = lane == routes_ref[:, 0:1]
+    for k in range(1, routes_ref.shape[1]):
+        named = named | (lane == routes_ref[:, k : k + 1])
+    logits = jnp.where(named, logits, -1e30)
+    powers = jnp.where(named, jnp.exp(logits - jnp.max(logits, axis=1, keepdims=True)), 0.0)
+    gates = powers / jnp.sum(powers, axis=1, keepdims=True)
+    gates_ref[...] = gates
+    high = gates.astype(jnp.bfloat16)
+    rest_part = gates - high.astype(jnp.float32)
+    rows_ref[:, 2 * half :] = jnp.where(
+        lane < 64, high.astype(jnp.float32), pltpu.roll(rest_part, 64, 1)
+    ).astype(jnp.bfloat16)
+
+
+def expert_kernel(
+    place_ref,
+    near_ref,
+    far_ref,
+    near_out_ref,
+    far_out_ref,
+    rank_ref,
+    gate_up_ref,
+    down_ref,
+    *rest,
+    first,
+    last,
+    each,
+    split,
+):
+    count = 4 if split else 1
+    other_refs, rest = rest[:count], rest[count:]
+    if first > 0:
+        held_out, held_grad = rest[:2]
+        rest = rest[2:]
+    out_ref, grad_ref, slots_ref = rest[:3]
+    rows_buf, grads_buf, moe_buf, back_buf, hot_buf, gate_buf = rest[-6:]
+    half = down_ref.shape[-1]
+    full = 2 * half
+    width = down_ref.shape[-2]
+    step = pl.program_id(0)
+    quarter = [place_ref[1] ^ r for r in range(4)]
+    expert = [(place_ref[0] * 4 + quarter[r]) * each + first + step for r in range(4)]
+    iota = lax.broadcasted_iota(jnp.int32, (CAP, 128), 0)
+    lane = lax.broadcasted_iota(jnp.int32, (CAP, 128), 1)
+
+    @pl.when(step == 0)
+    def _():
+        if first == 0:
+            out_ref[...] = jnp.zeros_like(out_ref)
+            grad_ref[...] = jnp.zeros_like(grad_ref)
+        else:
+            out_ref[...] = held_out[...]
+            grad_ref[...] = held_grad[...]
+
+    marks = [((lane == expert[r]) | (lane == expert[r] + 64)) for r in range(4)]
+    mark = jnp.concatenate(marks, axis=0)
+    for b in range(4):
+        low = jnp.concatenate(
+            [
+                jnp.where(iota == rank_ref[quarter[r], 0, pl.ds(b, 1), :], 1.0, 0.0)
+                for r in range(4)
+            ],
+            axis=0,
+        ).astype(jnp.bfloat16)
+        hot_buf[b] = low
+        span = pl.ds((b % 2) * 128, 128)
+        source = near_ref if b < 2 else far_ref
+        picked = jnp.where(mark, dot(low, source[span, pl.ds(full, 128)]), 0.0)
+        gate_buf[b] = jnp.broadcast_to(jnp.sum(picked, axis=1, keepdims=True), (4 * CAP, 128))
+        for part in range(2):
+            keep = pl.ds(part * half, half)
+            if b < 2:
+                rows, grads = near_ref[span, keep], near_out_ref[span, keep]
+            else:
+                swap = pl.ds((1 - part) * half, half)
+                rows, grads = far_ref[span, swap], far_out_ref[span, swap]
+            rows_buf[b, :, keep] = dot(low, rows).astype(jnp.bfloat16)
+            grads_buf[b, :, keep] = dot(low, grads).astype(jnp.bfloat16)
+    for r in range(4):
+        q = quarter[r]
+        slot = slice(r * CAP, (r + 1) * CAP)
+        rows = jnp.concatenate([rows_buf[b, slot, :] for b in range(4)], axis=0)
+        grads = jnp.concatenate([grads_buf[b, slot, :] for b in range(4)], axis=0)
+        gate = jnp.concatenate([gate_buf[b, slot, :] for b in range(4)], axis=0)
+        near_w = jnp.concatenate(
+            [gate_up_ref[q, 0, :half, :], gate_up_ref[q, 0, half:, :]], axis=1
+        )
+        def other(start, size):
+            if split:
+                return other_refs[r][0, start : start + size, :]
+            return other_refs[0][q, 0, start : start + size, :]
+
+        far_w = jnp.concatenate([other(0, half), other(half, half)], axis=1)
+        near_down = down_ref[0, q, 0]
+        far_down = jnp.concatenate(
+            [other(2 * half + j * width, width) for j in range(half // 128)],
+            axis=1,
+        )
+        gate_up = dot(rows[:, :half], near_w) + dot(rows[:, half:], far_w)
+        gate_pre = gate_up[:, :width]
+        up_pre = gate_up[:, width:]
+        sigmoid = 1.0 / (1.0 + jnp.exp(-gate_pre))
+        activ = (gate_pre * sigmoid * up_pre).astype(jnp.bfloat16)
+        pulled = RESIDUAL_SCALE * (
+            dot(grads[:, :half], near_down, 1, 1) + dot(grads[:, half:], far_down, 1, 1)
+        )
+        activ_wide = activ.astype(jnp.float32)
+        gate_grad = jnp.sum(activ_wide * pulled, axis=1, keepdims=True)
+        activ_grad = pulled * gate
+        gate_pre_grad = activ_grad * up_pre * sigmoid * (1.0 + gate_pre * (1.0 - sigmoid))
+        up_pre_grad = activ_grad * gate_pre * sigmoid
+        both = jnp.concatenate([gate_pre_grad, up_pre_grad], axis=1).astype(jnp.bfloat16)
+        slots_ref[q, 0, :, : 2 * width] = both
+        slots_ref[q, 0, :, 2 * width :] = (activ_wide * gate * RESIDUAL_SCALE).astype(jnp.bfloat16)
+        for part, (wide, low_w) in enumerate(((near_w, near_down), (far_w, far_down))):
+            keep = pl.ds(part * half, half)
+            made = dot(activ, low_w)
+            back = dot(both, wide, 1, 1)
+            for b in range(4):
+                piece = slice(b * CAP, (b + 1) * CAP)
+                scale = jnp.concatenate([gate[piece]] * (half // 128), axis=1)
+                moe_buf[b, slot, keep] = (made[piece] * scale).astype(jnp.bfloat16)
+                back_buf[b, slot, keep] = back[piece].astype(jnp.bfloat16)
+        spot = lane == expert[r]
+        for b in range(4):
+            back_buf[b, slot, pl.ds(full, 128)] = jnp.where(
+                spot, gate_grad[b * CAP : (b + 1) * CAP], 0.0
+            ).astype(jnp.bfloat16)
+    for b in range(4):
+        span = pl.ds(b * 128, 128)
+        out_ref[span, :] += dot(hot_buf[b], moe_buf[b], 0, 0)
+        grad_ref[span, :] += dot(hot_buf[b], back_buf[b], 0, 0)
+
+    if last:
+        moe_far_ref, back_far_ref = rest[3:5]
+
+        @pl.when(step == pl.num_programs(0) - 1)
+        def _():
+            span = pl.ds(256, 256)
+            for part in range(2):
+                keep, swap = pl.ds(part * half, half), pl.ds((1 - part) * half, half)
+                moe_far_ref[:, keep] = out_ref[span, swap].astype(jnp.bfloat16)
+                back_far_ref[:, keep] = grad_ref[span, swap].astype(jnp.bfloat16)
+            back_far_ref[:, pl.ds(full, 128)] = grad_ref[span, pl.ds(full, 128)].astype(
+                jnp.bfloat16
+            )
+
+
+def run_experts(place, near, far, near_out, far_out, rank, gate_up, down, other, held, first, each):
+    split = isinstance(other, list)
+    others = other if split else [other]
+    steps, packed, lanes = others[0].shape[-3:]
+    quarters, _, rows, width = gate_up.shape
+    half = rows // 2
+    full = 2 * half
+    tokens = 2 * near.shape[0]
+    last = first + steps == each
+
+    def fixed(shape):
+        return pl.BlockSpec(shape, lambda j, sp: (0,) * len(shape))
+
+    in_specs = [
+        fixed(near.shape),
+        fixed(far.shape),
+        fixed((tokens // 2, full)),
+        fixed((tokens // 2, full)),
+        pl.BlockSpec((quarters, 1, 4, 128), lambda j, sp: (0, first + j, 0, 0)),
+        pl.BlockSpec((quarters, 1, rows, width), lambda j, sp: (0, first + j, 0, 0)),
+        pl.BlockSpec((1, quarters, 1, width, half), lambda j, sp: (sp[0], 0, first + j, 0, 0)),
+    ]
+    if split:
+        in_specs += [pl.BlockSpec((1, packed, lanes), lambda j, sp: (j, 0, 0))] * 4
+    else:
+        in_specs.append(pl.BlockSpec((quarters, 1, packed, lanes), lambda j, sp: (0, j, 0, 0)))
+    operands = [place, near, far, near_out, far_out, rank, gate_up, down, *others]
+    aliases = {}
+    totals = [
+        jax.ShapeDtypeStruct((tokens, full), jnp.float32),
+        jax.ShapeDtypeStruct((tokens, full + 128), jnp.float32),
+    ]
+    if first > 0:
+        in_specs += [fixed(held[0].shape), fixed(held[1].shape)]
+        aliases = {len(operands): 0, len(operands) + 1: 1}
+        operands += list(held[:2])
+    out_shape = totals + [
+        jax.ShapeDtypeStruct((quarters, steps, 4 * CAP, 3 * width), jnp.bfloat16)
+    ]
+    out_specs = [
+        fixed(totals[0].shape),
+        fixed(totals[1].shape),
+        pl.BlockSpec((quarters, 1, 4 * CAP, 3 * width), lambda j, sp: (0, j, 0, 0)),
+    ]
+    if last:
+        for lanes_out in (full, full + 128):
+            out_shape.append(jax.ShapeDtypeStruct((tokens // 2, lanes_out), jnp.bfloat16))
+            out_specs.append(fixed((tokens // 2, lanes_out)))
+    return pl.pallas_call(
+        functools.partial(expert_kernel, first=first, last=last, each=each, split=split),
+        out_shape=tuple(out_shape),
+        grid_spec=pltpu.PrefetchScalarGridSpec(
+            num_scalar_prefetch=1,
+            grid=(steps,),
+            in_specs=in_specs,
+            out_specs=tuple(out_specs),
+            scratch_shapes=[pltpu.VMEM((4, 4 * CAP, full), jnp.bfloat16)] * 3
+            + [
+                pltpu.VMEM((4, 4 * CAP, full + 128), jnp.bfloat16),
+                pltpu.VMEM((4, 4 * CAP, 128), jnp.bfloat16),
+                pltpu.VMEM((4, 4 * CAP, 128), jnp.float32),
+            ],
+        ),
+        input_output_aliases=aliases,
+        compiler_params=kernel_params(1),
+        name="experts",
+    )(*operands)
+
+
+def join_kernel(place_ref, total_ref, got_ref, *rest):
+    piece_refs, whole_buf = rest[:-1], rest[-1]
+    count = got_ref.shape[0]
+    whole_buf[...] = total_ref[:count, :] + got_ref[...].astype(jnp.float32)
+    give_pieces(whole_buf, place_ref[2], piece_refs)
+
+
+def back_kernel(
+    place_ref,
+    mixed_ref,
+    gates_ref,
+    gains_ref,
+    small_ref,
+    far_ref,
+    out_grad_ref,
+    out_near_ref,
+    out_far_ref,
+    query_ref,
+    turn_ref,
+    kv0,
+    kv1,
+    kv2,
+    kv3,
+    probs_ref,
+    *rest,
+):
+    (
+        mixed_grad_ref,
+        attn_grad_ref,
+        logit_grad_ref,
+        gain_grad_ref,
+        query_grad_ref,
+        kept_ref,
+        given_ref,
+        whole_buf,
+        head_buf,
+    ) = rest[-9:]
+    take_pieces(rest[:-9], place_ref[2], whole_buf)
+    half = small_ref.shape[1]
+    full = 2 * half
+    gates = gates_ref[...]
+    gate_grads = whole_buf[:, full:]
+    inner = jnp.sum(gates * gate_grads, axis=1, keepdims=True)
+    logit_grad = (gates * (gate_grads - inner)).astype(jnp.bfloat16)
+    logit_grad_ref[...] = logit_grad
+    near, far = mixed_ref[:, :half], mixed_ref[:, half:]
+    scale = row_scale(near, far)
+    near_unit, far_unit = near * scale, far * scale
+    near_grad = whole_buf[:, :half] + dot(logit_grad, small_ref[:half, half - 128 :], 1, 1)
+    far_grad = whole_buf[:, half:full] + dot(logit_grad, far_ref[:, half - 128 :], 1, 1)
+    gain_grad_ref[:, :half] = jnp.broadcast_to(
+        jnp.sum(near_grad * near_unit, axis=0, keepdims=True), (8, half)
+    )
+    gain_grad_ref[:, half:] = jnp.broadcast_to(
+        jnp.sum(far_grad * far_unit, axis=0, keepdims=True), (8, half)
+    )
+    near_scaled = near_grad * gains_ref[1:2, :half]
+    far_scaled = far_grad * gains_ref[1:2, half:]
+    mean = (
+        jnp.sum(near_scaled * near_unit, axis=1, keepdims=True)
+        + jnp.sum(far_scaled * far_unit, axis=1, keepdims=True)
+    ) / full
+    near_mixed = out_grad_ref[:, :half].astype(jnp.float32) + scale * (
+        near_scaled - near_unit * mean
+    )
+    far_mixed = out_grad_ref[:, half:full].astype(jnp.float32) + scale * (
+        far_scaled - far_unit * mean
+    )
+    mixed_grad_ref[:, :half] = near_mixed
+    mixed_grad_ref[:, half:] = far_mixed
+    near_attn = (RESIDUAL_SCALE * near_mixed).astype(jnp.bfloat16)
+    far_attn = (RESIDUAL_SCALE * far_mixed).astype(jnp.bfloat16)
+    attn_grad_ref[:, :half] = near_attn
+    attn_grad_ref[:, half:] = far_attn
+    head_buf[...] = (
+        dot(near_attn, out_near_ref[...], 1, 1) + dot(far_attn, out_far_ref[...], 1, 1)
+    ).astype(jnp.bfloat16)
+    blocks = (kv0, kv1, kv2, kv3)
+    kv_heads = kv0.shape[1] // (2 * HEAD_DIM)
+    micro = probs_ref.shape[0] // kv_heads
+    rows = query_ref.shape[0] // micro
+    group = query_ref.shape[1] // HEAD_DIM // kv_heads
+    count = query_ref.shape[1] // 128
+    for m in range(micro):
+        span = pl.ds(m * rows, rows)
+        whole = query_ref[span, :]
+        whole_grad = head_buf[span, :]
+        pieces = []
+        key_grads = []
+        value_grads = []
+        for g in range(kv_heads):
+            query = stack_heads(whole, g * group, group)
+            head_grad = stack_heads(whole_grad, g * group, group)
+            keys = jnp.concatenate(
+                [blocks[r][span, :][:, g * HEAD_DIM : (g + 1) * HEAD_DIM] for r in range(4)], axis=0
+            )
+            values = jnp.concatenate(
+                [
+                    blocks[r][span, :][:, (kv_heads + g) * HEAD_DIM : (kv_heads + g + 1) * HEAD_DIM]
+                    for r in range(4)
+                ],
+                axis=0,
+            )
+            probs = probs_ref[m * kv_heads + g]
+            prob_grad = dot(head_grad, values, 1, 1)
+            inner = jnp.sum(probs * prob_grad, axis=1, keepdims=True)
+            score_grad = (SCORE_SCALE * probs * (prob_grad - inner)).astype(jnp.bfloat16)
+            value_grads.append(dot(probs.astype(jnp.bfloat16), head_grad, 0, 0))
+            key_grads.append(dot(score_grad, query, 0, 0))
+            query_grad = dot(score_grad, keys)
+            pieces += [query_grad[h * rows : (h + 1) * rows] for h in range(group)]
+        query_grad = jnp.concatenate(pieces, axis=1)
+        query_grad_ref[span, :] = (
+            query_grad * jnp.concatenate([turn_ref[0, span, :]] * count, axis=1)
+            - turn_heads(query_grad) * jnp.concatenate([turn_ref[1, span, :]] * count, axis=1)
+        ).astype(jnp.bfloat16)
+        joined = jnp.concatenate(key_grads + value_grads, axis=1)
+        kept_ref[0, span, :] = joined[:rows]
+        kept_ref[1, span, :] = joined[2 * rows : 3 * rows]
+        given_ref[0, span, :] = joined[rows : 2 * rows].astype(jnp.bfloat16)
+        given_ref[1, span, :] = joined[3 * rows :].astype(jnp.bfloat16)
+
+
+def last_kernel(
+    place_ref,
+    query_grad_ref,
+    kept_ref,
+    near_ref,
+    along_ref,
+    turn_ref,
+    small_ref,
+    far_ref,
+    hidden_ref,
+    *rest,
+):
+    grads_ref, gain_ref = rest[0], rest[1]
+    piece_refs, whole_buf = rest[2:-1], rest[-1]
+    q_cols = query_grad_ref.shape[1]
+    k_cols = turn_ref.shape[2]
+    cols = q_cols + 2 * k_cols
+    half = small_ref.shape[1]
+    total = (
+        kept_ref[0] + near_ref[0].astype(jnp.float32) + along_ref[...].astype(jnp.float32)
+    )
+    keys = total[:, :k_cols]
+    grads_ref[:, :q_cols] = query_grad_ref[...]
+    grads_ref[:, q_cols : q_cols + k_cols] = (
+        keys * turn_ref[0] - turn_heads(keys) * turn_ref[1]
+    ).astype(jnp.bfloat16)
+    grads_ref[:, q_cols + k_cols :] = total[:, k_cols:].astype(jnp.bfloat16)
+    grads = grads_ref[...]
+    near_part = dot(grads, small_ref[:half, :cols], 1, 1)
+    far_part = dot(grads, far_ref[:, :cols], 1, 1)
+    near, far = own_then_other(place_ref[0], hidden_ref[...].astype(jnp.float32))
+    scale = row_scale(near, far)
+    gain_ref[:, :half] = jnp.broadcast_to(
+        jnp.sum(near_part * (near * scale), axis=0, keepdims=True), (8, half)
+    )
+    gain_ref[:, half:] = jnp.broadcast_to(
+        jnp.sum(far_part * (far * scale), axis=0, keepdims=True), (8, half)
+    )
+    whole_buf[:, :half] = near_part
+    whole_buf[:, half:] = far_part
+    give_pieces(whole_buf, place_ref[2], piece_refs)
+
+
+def output_kernel(place_ref, mixed_ref, *rest):
+    out_ref, whole_buf = rest[-2:]
+    take_pieces(rest[:-2], place_ref[2], whole_buf)
+    half = out_ref.shape[1] // 2
+    total = mixed_ref[...] + RESIDUAL_SCALE * whole_buf[...]
+    first, second = own_then_other(place_ref[0], total)
+    out_ref[:, :half] = first
+    out_ref[:, half:] = second
+
+
+def hidden_kernel(place_ref, hidden_ref, gains_ref, mixed_grad_ref, *rest):
+    out_ref, whole_buf = rest[-2:]
+    take_pieces(rest[:-2], place_ref[2], whole_buf)
+    half = out_ref.shape[1] // 2
+    near, far = own_then_other(place_ref[0], hidden_ref[...].astype(jnp.float32))
+    scale = row_scale(near, far)
+    near, far = near * scale, far * scale
+    near_scaled = whole_buf[:, :half] * gains_ref[0:1, :half]
+    far_scaled = whole_buf[:, half:] * gains_ref[0:1, half:]
+    mean = (
+        jnp.sum(near_scaled * near, axis=1, keepdims=True)
+        + jnp.sum(far_scaled * far, axis=1, keepdims=True)
+    ) / (2 * half)
+    near_out = mixed_grad_ref[:, :half] + scale * (near_scaled - near * mean)
+    far_out = mixed_grad_ref[:, half:] + scale * (far_scaled - far * mean)
+    out_ref[:, :half] = jnp.where(place_ref[0] == 0, near_out, far_out)
+    out_ref[:, half:] = jnp.where(place_ref[0] == 0, far_out, near_out)
+
+
+def weight_grad_kernel(
+    place_ref, rows_ref, grads_ref, slots_ref, rank_ref, *refs
+):
+    gate_up_ref, down_ref, mark_ref, rows_buf, grads_buf = refs[-5:]
+    half = down_ref.shape[-1]
+    width = down_ref.shape[-2]
+    steps = rank_ref.shape[2]
+    iota = lax.broadcasted_iota(jnp.int32, (CAP, 128), 0)
+    step, side = pl.program_id(0), pl.program_id(1)
+    mark_ref[...] = jnp.zeros_like(mark_ref)
+
+    @pl.when((step == 0) & (side == 0))
+    def _():
+        for k in range(4):
+            for b in range(4):
+                span = pl.ds(b * 128, 128)
+                for a in range(2):
+                    hot = jnp.concatenate(
+                        [
+                            jnp.where(iota == rank_ref[a, q, j, pl.ds(4 * k + b, 1), :], 1.0, 0.0)
+                            for j in range(steps)
+                            for q in range(4)
+                        ],
+                        axis=0,
+                    ).astype(jnp.bfloat16)
+                    spot = 4 * k + (b ^ (2 * a))
+                    rows = dot(hot, rows_ref[k, span, :]).astype(jnp.bfloat16)
+                    grads = dot(hot, grads_ref[k, span, :]).astype(jnp.bfloat16)
+                    for j in range(steps):
+                        piece = slice(j * 4 * CAP, (j + 1) * 4 * CAP)
+                        rows_buf[j * 2 + a, spot] = rows[piece]
+                        grads_buf[j * 2 + a, spot] = grads[piece]
+
+    place = step * 2 + side
+    for q in range(4):
+        slot = slice(q * CAP, (q + 1) * CAP)
+        rows = jnp.concatenate([rows_buf[place, n, slot, :] for n in range(16)], axis=0)
+        grads = jnp.concatenate([grads_buf[place, n, slot, :] for n in range(16)], axis=0)
+        taken = jnp.concatenate([slots_ref[0, k, q, 0] for k in range(4)], axis=0)
+        made = dot(rows, taken[:, : 2 * width], 0, 0)
+        gate_up_ref[0, q, 0, pl.ds(0, half, stride=2), :] = made[:, :width]
+        gate_up_ref[0, q, 0, pl.ds(1, half, stride=2), :] = made[:, width:]
+        down_ref[0, q, 0] = dot(taken[:, 2 * width :], grads, 0, 0)
+
+
+def run_weight_grads(place, plane, slots, rank, held, each, first, mark):
+    sides, _, quarters, steps, slot_count, lanes = slots.shape
+    width = lanes // 3
+    half = (plane.shape[-1] - 128) // 2
+    tokens = plane.shape[1]
+
+    def place_of(j, a, sp):
+        return (sp[0] ^ a, 0, first + j, 0, 0)
+
+    in_specs = [
+        pl.BlockSpec((4, tokens, half), lambda j, a, sp: (0, 0, 1)),
+        pl.BlockSpec((4, tokens, half), lambda j, a, sp: (0, 0, 0)),
+        pl.BlockSpec(
+            (1, 4, quarters, 1, slot_count, lanes),
+            lambda j, a, sp: (sp[0] ^ a, 0, 0, j, 0, 0),
+        ),
+        pl.BlockSpec(rank.shape, lambda j, a, sp: (0, 0, 0, 0, 0)),
+        pl.BlockSpec(memory_space=pl.ANY),
+    ]
+    operands = [place, plane, plane, slots, rank, mark]
+    aliases = {}
+    if held is not None:
+        in_specs += [pl.BlockSpec(memory_space=pl.ANY)] * 2
+        aliases = {len(operands): 0, len(operands) + 1: 1}
+        operands += list(held[:2])
+    return pl.pallas_call(
+        weight_grad_kernel,
+        out_shape=(
+            jax.ShapeDtypeStruct((sides, quarters, each, 2 * half, width), jnp.float32),
+            jax.ShapeDtypeStruct((sides, quarters, each, width, half), jnp.float32),
+            jax.ShapeDtypeStruct((8, 128), jnp.float32),
+        ),
+        grid_spec=pltpu.PrefetchScalarGridSpec(
+            num_scalar_prefetch=1,
+            grid=(steps, sides),
+            in_specs=in_specs,
+            out_specs=(
+                pl.BlockSpec((1, quarters, 1, 2 * half, width), place_of),
+                pl.BlockSpec((1, quarters, 1, width, half), place_of),
+                pl.BlockSpec((8, 128), lambda j, a, sp: (0, 0)),
+            ),
+            scratch_shapes=[pltpu.VMEM((2 * steps, 16, 4 * CAP, half), jnp.bfloat16)] * 2,
+        ),
+        input_output_aliases=aliases,
+        compiler_params=kernel_params(2),
+        name="weight_grads",
+    )(*operands)
+
+
+def swap_halves(values):
+    half = values.shape[-1] // 2
+    return jnp.concatenate([values[..., half:], values[..., :half]], axis=-1)
+
+
+def fast_body(
+    hidden_in,
+    parents,
+    routes,
+    attn_gain,
+    w_query,
+    key_projection,
+    value_projection,
+    w_out,
+    moe_gain,
+    w_router,
+    w_gate_up,
+    w_down,
+    d_out,
+):
+    low, wide = jnp.bfloat16, jnp.float32
+    x_pos = lax.axis_index("fsdp")
+    c_pos = lax.axis_index("ctx")
+    z_pos = lax.axis_index("tp")
+    tp_size = lax.axis_size("tp")
+    place = jnp.stack([x_pos, c_pos, z_pos]).astype(jnp.int32)
+    micro, _, rows, model = hidden_in.shape
+    half = model // 2
+    tokens = micro * rows
+    experts = w_gate_up.shape[0]
+    mine = experts // 2
+    each = mine // 4
+    width = w_down.shape[1]
+    q_cols = w_query.shape[1]
+    k_cols = key_projection.shape[1]
+    qkv_cols = q_cols + 2 * k_cols
+    kv_heads = k_cols // HEAD_DIM
+    group = q_cols // k_cols
+    top = routes.shape[-1]
+    chunks = ((0, 2), (2, 2), (4, 1))
+    tie = lax.optimization_barrier
+
+    def across(value):
+        return lax.ppermute(value, "fsdp", [(0, 1), (1, 0)])
+
+    def beside(value):
+        return lax.ppermute(value, "ctx", [(i, i ^ 1) for i in range(4)])
+
+    def along(value):
+        return lax.ppermute(value, "ctx", [(i, i ^ 2) for i in range(4)])
+
+    def from_tp(value, step):
+        return lax.ppermute(value, "tp", [((i + step) % tp_size, i) for i in range(tp_size)])
+
+    def all_ctx(value):
+        nearby = beside(value)
+        distant = along(value)
+        return [value, nearby, distant, beside(distant)]
+
+    def own_first(value):
+        return jnp.where(x_pos == 0, value, swap_halves(value))
+
+    def reduce_pieces(pieces):
+        total = pieces[0].astype(wide)
+        for step in range(1, tp_size):
+            total = total + from_tp(pieces[tp_size - step], step).astype(wide)
+        return total.astype(low)
+
+    def spread_pieces(total):
+        return [total] + [from_tp(total, step) for step in range(1, tp_size)]
+
+    piece_shapes = [((tokens // tp_size, model), low)] * tp_size
+    hidden = hidden_in.reshape(tokens, model)
+    flat_routes = routes.reshape(tokens, top)
+
+    core = c_pos % 2
+    part = half // 2
+    weights = jnp.concatenate(
+        [
+            w_query,
+            key_projection,
+            value_projection,
+            jnp.pad(w_router, ((0, 0), (0, half - qkv_cols - experts))),
+        ],
+        axis=1,
+    )
+    gain_rows = jnp.pad(jnp.stack([attn_gain, moe_gain]), ((0, 14), (0, 0)))
+    small = jnp.concatenate([weights, gain_rows], axis=0)
+    sent = across(
+        jnp.concatenate([lax.dynamic_slice_in_dim(weights, core * part, part, 0), gain_rows], axis=0)
+    )
+
+    both_view = w_gate_up.reshape(experts, 2 * half, width)
+    base = (x_pos * mine).astype(jnp.int32)[None]
+    away = ((1 - x_pos) * mine + c_pos * each).astype(jnp.int32)[None]
+    packs = [split_weights(away + first, count, both_view, w_down) for first, count in chunks]
+    down_all = w_down.reshape(2, 4, each, width, half)
+    routes_low = jnp.pad(flat_routes.astype(low), ((0, 0), (0, 128 - top)))
+    near_out = jnp.concatenate([own_first(d_out.reshape(tokens, model)), routes_low], axis=1)
+
+    sent, packs[0], out_start = tie((sent, packs[0], core * (q_cols // 2)))
+    out_sent = across(lax.dynamic_slice_in_dim(w_out, out_start, q_cols // 2, 0))
+
+    half_dim = HEAD_DIM // 2
+    inverse = ROPE_BASE ** (-jnp.arange(half_dim, dtype=wide) * 2.0 / HEAD_DIM)
+    angles = jnp.arange(4 * rows, dtype=wide)[:, None] * inverse[None, :]
+    cosines = jnp.tile(jnp.cos(angles), (1, 4))
+    sines = jnp.tile(jnp.sin(angles), (1, 4))
+    normed_one, query, key_value, small_far, gains, turns = single(
+        before_kernel,
+        "before",
+        [
+            ((tokens, model), low),
+            ((tokens, q_cols), low),
+            ((tokens, 2 * k_cols), low),
+            ((half, half), low),
+            ((16, model), wide),
+            ((2, tokens, 128), wide),
+        ],
+        [],
+        [place, parents.reshape(micro, 4)],
+        hidden,
+        small,
+        sent,
+        beside(sent),
+        cosines,
+        sines,
+    )
+    key_value, packs[0], near_out = tie((key_value, packs[0], near_out))
+    blocks = all_ctx(key_value)
+    far_out = across(near_out)
+    far_zero = across(packs[0])
+    head_low, probs, out_far, *pieces = single(
+        attend_kernel,
+        "attend",
+        [
+            ((tokens, q_cols), low),
+            ((micro * kv_heads, group * rows, 4 * rows), wide),
+            ((q_cols, half), low),
+        ]
+        + piece_shapes,
+        [((tokens, model), wide)],
+        [place, parents.reshape(micro, 4)],
+        query,
+        *blocks,
+        w_out,
+        out_sent,
+        beside(out_sent),
+    )
+    total = reduce_pieces(pieces)
+    total, far_zero, far_out, packs[1] = tie((total, far_zero, far_out, packs[1]))
+    far_one = across(packs[1])
+    mixed, near, gates = single(
+        after_kernel,
+        "after",
+        [((tokens, model), wide), ((tokens, model + 128), low), ((tokens, 128), wide)],
+        [((tokens, model), wide)],
+        [place],
+        hidden,
+        gains,
+        small,
+        small_far,
+        flat_routes,
+        *spread_pieces(total),
+    )
+    near, packs[2], base = tie((near, packs[2], base))
+    gate_up_mine = split_weights(base, mine, both_view, None).reshape(4, each, 2 * half, width)
+    far = across(near)
+    far, packs[2], far_one, gate_up_mine = tie((far, packs[2], far_one, gate_up_mine))
+    far_two = across(packs[2])
+    far_weights = [lax.all_gather(got, "ctx") for got in (far_zero, far_one)]
+    plane_in = jnp.concatenate(
+        [
+            jnp.concatenate([near_out[:, :half], near[:, :half], routes_low], axis=1),
+            jnp.concatenate([far_out[:, half:model], far[:, half:model], far_out[:, model:]], axis=1),
+        ],
+        axis=0,
+    )
+
+    upper = (
+        lax.broadcasted_iota(jnp.int32, (rows, rows), 0)
+        < lax.broadcasted_iota(jnp.int32, (rows, rows), 1)
+    ).astype(low)
+
+    def ranks(route_table, ids):
+        flat = route_table.astype(jnp.int32).T
+        hit = jnp.zeros((ids.shape[0], flat.shape[1]), jnp.bool_)
+        for k in range(top):
+            hit = hit | (flat[k][None, :] == ids[:, None])
+        hot = hit.astype(low).reshape(-1, rows)
+        found = jnp.where(hot > 0, dot(hot, upper), -1.0).astype(jnp.int32)
+        return found.reshape(ids.shape[0], -1, rows)
+
+    expert_ids = (jnp.arange(experts, dtype=jnp.int32) + x_pos * mine) % experts
+    pair_routes = jnp.concatenate([routes_low, far_out[:, model:]], axis=0)[:, :top]
+    rank_pair = ranks(pair_routes, expert_ids[:mine]).reshape(4, each, 4, rows)
+
+    held = None
+    slots = []
+    for number, (first, count) in enumerate(chunks):
+        if number == 1:
+            slots[0], far_two, far_weights[1] = tie((slots[0], far_two, far_weights[1]))
+            far_along = along(far_two)
+            far_near = beside(far_two)
+            plane_in, far_weights[1] = tie((plane_in, far_weights[1]))
+            plane = lax.all_gather(plane_in, "ctx")
+        if number == 2:
+            slots[1], far_along, far_near = tie((slots[1], far_along, far_near))
+            far_weights.append([far_two, far_near, far_along, beside(far_along)])
+        held = run_experts(
+            place,
+            near,
+            far,
+            near_out,
+            far_out,
+            rank_pair,
+            gate_up_mine,
+            down_all,
+            far_weights[number],
+            held,
+            first,
+            each,
+        )
+        slots.append(held[2])
+    moe_all, back_all, _, moe_far, back_far = held
+
+    back_got = across(back_far)
+    def gather_slots(part):
+        return lax.all_gather(part, ("fsdp", "ctx")).reshape(2, 4, *part.shape)
+
+    back_got, moe_far, plane, slots[0] = tie((back_got, moe_far, plane, slots[0]))
+    moe_got = across(moe_far)
+    pair_zero = gather_slots(slots[0])
+    pieces = single(
+        join_kernel,
+        "join",
+        [((tokens // tp_size, model + 128), low)] * tp_size,
+        [((tokens, model + 128), wide)],
+        [place],
+        back_all,
+        back_got,
+    )
+    found = spread_pieces(reduce_pieces(pieces))
+    *found, pair_zero, moe_got, slots[1] = tie((*found, pair_zero, moe_got, slots[1]))
+    pair_one = gather_slots(slots[1])
+    moe_pieces = single(
+        join_kernel, "join", piece_shapes, [((tokens, model), wide)], [place], moe_all, moe_got
+    )
+    moe_total = reduce_pieces(moe_pieces)
+    (
+        mixed_grad,
+        attn_grad,
+        logit_grad,
+        gain_two_part,
+        query_grad,
+        kept,
+        given,
+    ) = single(
+        back_kernel,
+        "back",
+        [
+            ((tokens, model), wide),
+            ((tokens, model), low),
+            ((tokens, 128), low),
+            ((8, model), wide),
+            ((tokens, q_cols), low),
+            ((2, tokens, 2 * k_cols), wide),
+            ((2, tokens, 2 * k_cols), low),
+        ],
+        [((tokens, model + 128), wide), ((tokens, q_cols), low)],
+        [place],
+        mixed,
+        gates,
+        gains,
+        small,
+        small_far,
+        near_out,
+        w_out,
+        out_far,
+        query,
+        turns,
+        *blocks,
+        probs,
+        *found,
+    )
+
+    given, moe_total = tie((given, moe_total))
+    near_pair = beside(given)
+    moe_found = spread_pieces(moe_total)
+    distant = along((kept[1] + near_pair[1].astype(wide)).astype(low))
+    qkv_grad, gain_one_part, *pieces = single(
+        last_kernel,
+        "last",
+        [((tokens, qkv_cols), low), ((8, model), wide)] + piece_shapes,
+        [((tokens, model), wide)],
+        [place],
+        query_grad,
+        kept,
+        near_pair,
+        distant,
+        turns,
+        small,
+        small_far,
+        hidden,
+    )
+
+    all_routes = plane[:, :, model : model + top].reshape(8 * tokens, top)
+    rank_all = ranks(all_routes, expert_ids).reshape(2, 4, each, 16, rows)
+
+    def grads_of(number, pair, held, mark):
+        first, count = chunks[number]
+        return run_weight_grads(
+            place,
+            plane,
+            pair,
+            rank_all[:, :, first : first + count],
+            held,
+            each,
+            first,
+            mark,
+        )
+
+    def hop_beside(value):
+        share = value.shape[1] // 2
+        kept = lax.dynamic_slice_in_dim(value, core * share, share, 1)
+        given = lax.dynamic_slice_in_dim(value, (1 - core) * share, share, 1)
+        return kept + beside(given.astype(low)).astype(wide)
+
+    def hop_across(kept):
+        return kept[0] + across(kept[1].astype(low)).astype(wide)
+
+    def hop_along(total):
+        return (total + along(total.astype(low)).astype(wide)).astype(low)
+
+    def hop_join(total):
+        other = beside(total)
+        return jnp.where(
+            core == 0,
+            jnp.concatenate([total, other], axis=0),
+            jnp.concatenate([other, total], axis=0),
+        ).astype(wide)
+
+    def both(left, right):
+        return jnp.stack([dot(left, right[:, :half], 0, 0), dot(left, right[:, half:], 0, 0)])
+
+    side = hop_beside(
+        jnp.concatenate(
+            [
+                both(head_low, attn_grad),
+                both(logit_grad[:, :experts], near[:, :model]),
+                jnp.stack([gain_two_part[:, :half], gain_two_part[:, half:]]),
+                jnp.zeros((2, 16, half), wide),
+            ],
+            axis=1,
+        )
+    )
+    mark = jnp.zeros((8, 128), wide)
+    tied = tie((*pieces, *moe_found, mark, side, qkv_grad, gain_one_part[0]))
+    pieces, moe_found = tied[:tp_size], tied[tp_size : 2 * tp_size]
+    mark, side, qkv_grad, gain_one = tied[2 * tp_size :]
+    (layer_out,) = single(
+        output_kernel,
+        "output",
+        [((tokens, model), wide)],
+        [((tokens, model), wide)],
+        [place],
+        mixed,
+        *moe_found,
+    )
+    total = reduce_pieces(pieces)
+    grads = grads_of(0, pair_zero, None, mark)
+    side = hop_across(side)
+    d_qkv = hop_beside(dot(normed_one, qkv_grad, 0, 0).reshape(2, half, qkv_cols))
+    total, mark, side, d_qkv, pair_one, slots[2] = tie(
+        (total, grads[2], side, d_qkv, pair_one, slots[2])
+    )
+    pair_two = gather_slots(slots[2])
+    found = spread_pieces(total)
+    grads = grads_of(1, pair_one, grads, mark)
+    side = hop_along(side)
+    d_qkv = hop_across(d_qkv)
+    gain_one = sum([from_tp(gain_one, step) for step in range(1, tp_size)], gain_one)
+    *found, mark, side, d_qkv, gain_one = tie((*found, grads[2], side, d_qkv, gain_one))
+    (d_hidden,) = single(
+        hidden_kernel,
+        "hidden",
+        [((tokens, model), wide)],
+        [((tokens, model), wide)],
+        [place],
+        hidden,
+        gains,
+        mixed_grad,
+        *found,
+    )
+    grads = grads_of(2, pair_two, grads, mark)
+    d_gate_up = grads[0].reshape(experts, half, 2, width)
+    d_down = grads[1].reshape(experts, width, half)
+    side_grads = hop_join(side)
+    d_qkv = hop_join(hop_along(d_qkv))
+    gain_one = gain_one + beside(gain_one)
+    gain_one = gain_one + along(gain_one)
+    gain_one = gain_one[:half] + across(gain_one[half:])
+    return (
+        layer_out.reshape(micro, 1, rows, model),
+        d_hidden.reshape(micro, 1, rows, model),
+        gain_one,
+        d_qkv[:, :q_cols],
+        d_qkv[:, q_cols : q_cols + k_cols],
+        d_qkv[:, q_cols + k_cols :],
+        side_grads[:q_cols],
+        side_grads[q_cols + experts],
+        side_grads[q_cols : q_cols + experts].T,
+        d_gate_up,
+        d_down,
+    )
+
+
 def solution(mesh):
     placed = (
         P(None, "fsdp", "ctx", None),
@@ -420,8 +1623,9 @@
         P(None, "tp", "fsdp"),
         P(None, "fsdp", "ctx", None),
     )
+    fits = mesh.shape["fsdp"] == 2 and mesh.shape["ctx"] == 4
     return jax.shard_map(
-        body,
+        fast_body if fits else body,
         mesh=mesh,
         in_specs=placed,
         out_specs=(

time: 2030 us -> 455 us (0.22)
  waiting for transfers between devices: 1330 us -> 148 us
  matrix products: 280 us -> 5.82 us
  Pallas kernels: 0 us -> 167 us
  local copies, waits for them, and re-layouts: 162 us -> 28.2 us
  blocking collectives: 129 us -> 0 us
  other arithmetic: 96.5 us -> 19.5 us
  starting transfers between devices: 1.07 us -> 63.1 us
    reduce_scatter x6 -> x0, waiting for transfers between devices: 595 us -> none  [the longest x1 351 us: body(): lax.psum_scatter(totals[7], ('fsdp', 'ctx'), scatter_dimension=1, tiled=T...]
    all_gather x6, waiting for transfers between devices: 613 us -> 21.4 us  [the longest x2 14.4 us: fast_body(): far_weights = [lax.all_gather(got, 'ctx') for got in (far_zero, far_one)]]
    dot_general x64 -> x7, matrix products: 280 us -> 5.82 us  [dot(): lax.dot_general(left, right, (((left_dim,), (right_dim,)), ((), ())), pre...]
    pallas_call x0 -> x19, Pallas kernels: none -> 167 us  [the longest x3 54 us: run_weight_grads(): pl.pallas_call(weight_grad_kernel, out_shape=(jax.ShapeDtypeStruct((sides...]
    ppermute x0 -> x57, waiting for transfers between devices: none -> 126 us  [the longest x27 70.7 us: from_tp(): lax.ppermute(value, 'tp', [((i + step) % tp_size, i) for i in range(tp_si...]
    psum x3 -> x0, waiting for transfers between devices: 92.3 us -> none  [the longest x1 66.2 us: body(): moe_sum = lax.psum(moe_part.astype(jnp.bfloat16), 'tp').astype(jnp.float32)]
    all_gather x14 -> x0, blocking collectives: 87.9 us -> none  [the longest x1 11.9 us: body(): lax.all_gather(key_projection, 'fsdp', axis=0, tiled=True)]
    unnamed x266 -> x108, local copies, waits for them, and re-layouts: 74.4 us -> 8.17 us
  transfers between devices with their start and end apart: 20 -> 63, of which waited for: 13 -> 26; matrix products, arithmetic and copies ran while one was open for 16% -> 9% of each run, Pallas kernels for 0% -> 34%
where the time goes in v4:
time: 455 us; the launch traced here: 447 us
  Pallas kernels  167 us (37%)
  waiting for transfers between devices  148 us (33%)
  starting transfers between devices  63.1 us (14%)
  local copies, waits for them, and re-layouts  28.2 us (6%)
  other arithmetic  19.5 us (4%)
  between operations  15.3 us (3%)
  matrix products  5.82 us (1%)
    ppermute x27, waiting for transfers between devices, from_tp(): lax.ppermute(value, 'tp', [((i + step) % tp_size, i) for i in range(tp_si...  70.7 us
    pallas_call x3, Pallas kernels, run_weight_grads(): pl.pallas_call(weight_grad_kernel, out_shape=(jax.ShapeDtypeStruct((sides...  54 us
    pallas_call x3, Pallas kernels, run_experts(): pl.pallas_call(functools.partial(expert_kernel, first=first, last=last, e...  49.7 us
    ppermute x12, waiting for transfers between devices, across(): return lax.ppermute(value, 'fsdp', [(0, 1), (1, 0)])  46.3 us
    pallas_call x9, Pallas kernels, single(): pl.pallas_call(kernel, out_shape=tuple((jax.ShapeDtypeStruct(shape, kind)...  42.5 us
    ppermute x27, starting transfers between devices, from_tp(): lax.ppermute(value, 'tp', [((i + step) % tp_size, i) for i in range(tp_si...  38.2 us
    pallas_call x4, Pallas kernels, split_weights(): pl.pallas_call(split_plain_kernel if down is None else split_kernel, out_...  20.5 us
    ppermute x12, starting transfers between devices, across(): return lax.ppermute(value, 'fsdp', [(0, 1), (1, 0)])  15.9 us
  transfers between devices with their start and end apart: 63, of which 26 were waited for; matrix products, arithmetic and copies ran while one was open for 9% of the time, Pallas kernels for 34%

profile of v4, /device:TPU:0, one launch (start us, length us, event | category | flops | bytes accessed | tf_op | source)
XLA Modules:
  0.0 446.5 jit_solution(8271540601105792487)
XLA Ops:
  11.7 2.9 collective-permute-start
  17.0 2.2 split_weights.4
  19.5 9.3 %collective-permute-done.sent_ref = bf16[400,768]{1,0:T(8,128)(2,1)} collective-permute-done((bf16[400,768]{1,0:T(8,128)(2,1)}, bf16[400,768]{1,0:T(8,128)(2,1)}, u32[]{:S(2)}, u32[]{:S(2)}) %collective-permute-start) | collective-permute-done | bytes 614432 | tf_op jit(solution)/shard_map/ppermute | solution.py:1236
  30.2 1.8 collective-permute-start.5
  32.6 4.4 before.1
  37.4 2.4 collective-permute-done.5.out_sent_ref
  39.8 1.8 collective-permute-start.3
  41.5 1.9 collective-permute-start.11
  43.4 2.5 collective-permute-done.3.kv2
  47.9 5.8 %attend.1 = (bf16[256,384]{1,0:T(8,128)(2,1)}, f32[4,384,512]{2,1,0:T(8,128)}, bf16[384,768]{1,0:T(8,128)(2,1)}, bf16[64,1536]{1,0:T(8,128)(2,1)}, bf16[64,1536]...) custom-call(s32[3]{0:T(128)} %pad_add_fusion.place_ref, s32[2,4]{1,0:T(2,128)} %bitcast.212, ...), custom_call_target="tpu_custom_call" | custom-call | tf_op jit(solution)/shard_map/attend/pallas_call | solution.py:427
  53.7 3.8 collective-permute-start.7
  58.6 2.2 split_weights.5
  60.8 2.4 collective-permute-done.7
  63.2 11.5 %collective-permute-done.8 = bf16[64,1536]{1,0:T(8,128)(2,1)S(1)} collective-permute-done((bf16[64,1536]{1,0:T(8,128)(2,1)}, bf16[64,1536]{1,0:T(8,128)(2,1)S(1)}, u32[]{:S(2)}, u32[]{:S(2)}) %collective-permute-start.8) | collective-permute-done | bytes 196640 | tf_op jit(solution)/shard_map/ppermute | solution.py:1245
  76.5 7.1 %collective-permute-done.11.far_out_ref = bf16[256,1664]{1,0:T(8,128)(2,1)S(1)} collective-permute-done((bf16[256,1664]{1,0:T(8,128)(2,1)S(1)}, bf16[256,1664]{1,0:T(8,128)(2,1)S(1)}, u32[]{:S(2)}, u32[]{:S(2)}) %collective-permute-start.11) | collective-permute-done | bytes 852000 | tf_op jit(solution)/shard_map/ppermute | solution.py:1236
  86.1 3.6 collective-permute-start.12
  90.8 2.1 split_weights.6
  92.8 2.3 collective-permute-done.12.rest_1_
  95.1 10.9 %collective-permute-done.13.rest_2_ = bf16[64,1536]{1,0:T(8,128)(2,1)S(1)} collective-permute-done((bf16[64,1536]{1,0:T(8,128)(2,1)S(1)}, bf16[64,1536]{1,0:T(8,128)(2,1)S(1)}, u32[]{:S(2)}, u32[]{:S(2)}) %collective-permute-start.13) | collective-permute-done | bytes 196640 | tf_op jit(solution)/shard_map/ppermute | solution.py:1245
  106.8 4.3 after.1
  111.5 14.0 %split_weights.7 = bf16[20,1536,128]{2,1,0:T(8,128)(2,1)} custom-call(s32[1]{0:T(128)} %bitcast.11.base_ref, bf16[40,1536,128]{2,1,0:T(8,128)(2,1)} %bitcast.158), custom_call_target="tpu_custom_call" | custom-call | tf_op jit(solution)/shard_map/split_weights/pallas_call | solution.py:494
  125.5 5.9 %collective-permute-done.15.far_ref = bf16[256,1664]{1,0:T(8,128)(2,1)S(1)} collective-permute-done((bf16[256,1664]{1,0:T(8,128)(2,1)}, bf16[256,1664]{1,0:T(8,128)(2,1)S(1)}, u32[]{:S(2)}, u32[]{:S(2)}) %collective-permute-start.15) | collective-permute-done | bytes 852000 | tf_op jit(solution)/shard_map/ppermute | solution.py:1236
  137.6 17.5 %experts.3 = (f32[512,1536]{1,0:T(8,128)}, f32[512,1664]{1,0:T(8,128)}, bf16[4,2,128,384]{3,2,1,0:T(8,128)(2,1)}) custom-call(s32[3]{0:T(128)} %pad_add_fusion.place_ref, bf16[256,1664]{1,0:T(8,128)(2,1)} %get-tuple-element.152.near_ref, bf16[256,1664]{1,0:T(8,128)(2,1)} %copy-done.3, bf16[256,1664]{1,0:T(8,128)(2,1)} %copy-done, ...), custom_call_target="tpu_custom_call" | custom-call | tf_op jit(solution)/shard_map/experts/pallas_call | solution.py:883
  155.2 14.4 %all-gather.15.cloned.1.call-done = bf16[8,2304,128]{2,1,0:T(8,128)(2,1)} async-done(((bf16[2,2304,128]{2,1,0:T(8,128)(2,1)}), bf16[8,2304,128]{2,1,0:T(8,128)(2,1)}) %all-gather.15.cloned.1.call-update) | async-done | bytes 4718608 | tf_op jit(solution)/shard_map/all_gather | solution.py:1363
  170.2 18.4 %experts.4 = (f32[512,1536]{1,0:T(8,128)}, f32[512,1664]{1,0:T(8,128)}, bf16[4,2,128,384]{3,2,1,0:T(8,128)(2,1)}) custom-call(s32[3]{0:T(128)} %pad_add_fusion.place_ref, bf16[256,1664]{1,0:T(8,128)(2,1)} %get-tuple-element.152.near_ref, bf16[256,1664]{1,0:T(8,128)(2,1)} %copy-done.3, ...), custom_call_target="tpu_custom_call", output_to_operand_aliasing={{0}: (9, {}), {1}: (10, {})} | custom-call | tf_op jit(solution)/shard_map/experts/pallas_call | solution.py:883
  189.2 1.9 collective-permute-done.20.rest_3_
  191.9 13.8 %experts.5 = (f32[512,1536]{1,0:T(8,128)}, f32[512,1664]{1,0:T(8,128)}, bf16[4,1,128,384]{3,2,1,0:T(8,128)(2,1)}, bf16[256,1536]{1,0:T(8,128)(2,1)}, bf16[256,1664]{1,0:T(8,128)(2,1)}) custom-call(s32[3]{0:T(128)} %pad_add_fusion.place_ref, bf16[256,1664]{1,0:T(8,128)(2,1)} %get-tuple-element.152.near_ref, ...), custom_call_target="tpu_custom_call", output_to_operand_aliasing={{0}: (12, {}), {1}: (13, {})} | custom-call | tf_op jit(solution)/shard_map/experts/pallas_call | solution.py:883
  205.7 1.5 collective-permute-start.21
  207.2 19.7 %collective-permute-done.21.got_ref = bf16[256,1664]{1,0:T(8,128)(2,1)S(1)} collective-permute-done((bf16[256,1664]{1,0:T(8,128)(2,1)}, bf16[256,1664]{1,0:T(8,128)(2,1)S(1)}, u32[]{:S(2)}, u32[]{:S(2)}) %collective-permute-start.21) | collective-permute-done | bytes 852000 | tf_op jit(solution)/shard_map/ppermute | solution.py:1236
  227.8 3.3 join.2
  231.1 3.5 collective-permute-start.22
  235.8 1.5 collective-permute-start.28
  237.2 3.5 collective-permute-done.22
  240.7 12.1 %collective-permute-done.23 = bf16[64,1664]{1,0:T(8,128)(2,1)S(1)} collective-permute-done((bf16[64,1664]{1,0:T(8,128)(2,1)}, bf16[64,1664]{1,0:T(8,128)(2,1)S(1)}, u32[]{:S(2)}, u32[]{:S(2)}) %collective-permute-start.23) | collective-permute-done | bytes 213024 | tf_op jit(solution)/shard_map/ppermute | solution.py:1245
  254.0 2.8 collective-permute-start.26
  256.8 1.9 collective-permute-start.27
  259.8 15.4 %collective-permute-done.26.rest_2_ = bf16[64,1664]{1,0:T(8,128)(2,1)S(1)} collective-permute-done((bf16[64,1664]{1,0:T(8,128)(2,1)S(1)}, bf16[64,1664]{1,0:T(8,128)(2,1)S(1)}, u32[]{:S(2)}, u32[]{:S(2)}) %collective-permute-start.26) | collective-permute-done | bytes 213024 | tf_op jit(solution)/shard_map/ppermute | solution.py:1245
  275.2 6.9 %all-gather.19.cloned.1.call-done = bf16[32,2,128,384]{3,2,1,0:T(8,128)(2,1)} async-done(((bf16[4,2,128,384]{3,2,1,0:T(8,128)(2,1)}), bf16[32,2,128,384]{3,2,1,0:T(8,128)(2,1)}) %all-gather.19.cloned.1.call-update) | async-done | bytes 6291472 | tf_op jit(solution)/shard_map/all_gather | solution.py:1421
  284.5 3.2 join.3
  287.7 3.3 collective-permute-start.29
  292.3 10.1 %back.1 = (f32[256,1536]{1,0:T(8,128)}, bf16[256,1536]{1,0:T(8,128)(2,1)}, bf16[256,128]{1,0:T(8,128)(2,1)}, f32[8,1536]{1,0:T(8,128)}, bf16[256,384]{1,0:T(8,12...) custom-call(s32[3]{0:T(128)} %pad_add_fusion.place_ref, f32[256,1536]{1,0:T(8,128)} %get-tuple-element.146.mixed_ref, ...), custom_call_target="tpu_custom_call" | custom-call | tf_op jit(solution)/shard_map/back/pallas_call | solution.py:427
  304.7 1.4 convolution_bitcast_fusion.1
  306.5 2.0 collective-permute-done.30
  310.7 1.6 collective-permute-start.33
  313.8 1.7 collective-permute-start.35
  315.4 2.0 collective-permute-start.36
  317.5 2.2 collective-permute-done.33.along_ref
  320.3 4.1 last.1
  324.4 1.5 slice_reduce_fusion.8
  327.1 5.8 %collective-permute-done.35.rest_2_ = bf16[64,1536]{1,0:T(8,128)(2,1)S(1)} collective-permute-done((bf16[64,1536]{1,0:T(8,128)(2,1)S(1)}, bf16[64,1536]{1,0:T(8,128)(2,1)S(1)}, u32[]{:S(2)}, u32[]{:S(2)}) %collective-permute-start.35) | collective-permute-done | bytes 196640 | tf_op jit(solution)/shard_map/ppermute | solution.py:1245
  336.4 2.4 collective-permute-start.40
  341.2 20.5 %weight_grads.3 = (f32[2,4,5,1536,128]{4,3,2,1,0:T(8,128)}, f32[2,4,5,128,768]{4,3,2,1,0:T(8,128)}, f32[8,128]{1,0:T(8,128)}) custom-call(s32[3]{0:T(128)} %pad_add_fusion.place_ref, bf16[4,512,1664]{2,1,0:T(8,128)(2,1)} %bitcast.149, bf16[4,512,1664]{2,1,0:T(8,128)(2,1)} %bitcast.150, bf16[2,4,4,2,128,384]{5,4,3,2,1,0:T(8,128)(2,1)} %bitcast.170, ...), custom_call_target="tpu_custom_call" | custom-call | tf_op jit(solution)/shard_map/weight_grads/pallas_call | solution.py:1169
  363.8 2.2 bitcast_add_fusion.1
  366.0 2.6 convert_add_fusion
  373.1 1.8 collective-permute-start.48
  375.1 2.0 collective-permute-start.50
  377.1 2.3 collective-permute-done.49
  383.6 20.7 %weight_grads.4 = (f32[2,4,5,1536,128]{4,3,2,1,0:T(8,128)}, f32[2,4,5,128,768]{4,3,2,1,0:T(8,128)}, f32[8,128]{1,0:T(8,128)}) custom-call(s32[3]{0:T(128)} %pad_add_fusion.place_ref, bf16[4,512,1664]{2,1,0:T(8,128)(2,1)} %bitcast.151, bf16[4,512,1664]{2,1,0:T(8,128)(2,1)} %bitcast.152, ...), custom_call_target="tpu_custom_call", output_to_operand_aliasing={{0}: (6, {}), {1}: (7, {})} | custom-call | tf_op jit(solution)/shard_map/weight_grads/pallas_call | solution.py:1169
  408.9 1.5 slice.238.rank_ref
  410.4 3.3 output.1
  413.7 4.0 hidden.1
  417.7 1.4 collective-permute-start.53
  419.5 1.9 collective-permute-done.53
  426.7 12.8 %weight_grads.5 = (f32[2,4,5,1536,128]{4,3,2,1,0:T(8,128)}, f32[2,4,5,128,768]{4,3,2,1,0:T(8,128)}, f32[8,128]{1,0:T(8,128)}) custom-call(s32[3]{0:T(128)} %pad_add_fusion.place_ref, bf16[4,512,1664]{2,1,0:T(8,128)(2,1)} %bitcast.153, bf16[4,512,1664]{2,1,0:T(8,128)(2,1)} %bitcast.154, ...), custom_call_target="tpu_custom_call", output_to_operand_aliasing={{0}: (6, {}), {1}: (7, {})} | custom-call | tf_op jit(solution)/shard_map/weight_grads/pallas_call | solution.py:1169
  (286 shorter events, 69.5 us)
Async XLA Ops:
  7.2 130.5 %all-gather.13.cloned.1.call-start = ((), (), s32[]{:S(2)}) async-start(), calls=%async_computation | async-start | bytes 5898240 | tf_op jit(solution)/shard_map/all_gather | solution.py:1363
  11.7 17.1 %collective-permute-start = (bf16[400,768]{1,0:T(8,128)(2,1)}, bf16[400,768]{1,0:T(8,128)(2,1)}, u32[]{:S(2)}, u32[]{:S(2)}) collective-permute-start(bf16[400,768]{1,0:T(8,128)(2,1)} %pad_maximum_fusion.2), channel_id=1, source_target_pairs={{0,16},{16,0},{1,17},{17,1},{2,18},{18,2},{3,19},{19,3},{4,20},{20... | collective-permute-start | bytes 1843208 | tf_op jit(solution)/shard_map/ppermute | solution.py:1236
  28.8 3.8 collective-permute-start.1
  30.1 102.1 %copy-start = (bf16[256,1664]{1,0:T(8,128)(2,1)}, bf16[256,1664]{1,0:T(8,128)(2,1)S(1)}, u32[]{:S(2)}) copy-start(bf16[256,1664]{1,0:T(8,128)(2,1)S(1)} %pad_maximum_fusion.1.near_out_ref.out_grad_ref) | copy-start | bytes 2555908
  30.2 9.6 %collective-permute-start.5 = (bf16[192,768]{1,0:T(8,128)(2,1)S(1)}, bf16[192,768]{1,0:T(8,128)(2,1)}, u32[]{:S(2)}, u32[]{:S(2)}) collective-permute-start(bf16[192,768]{1,0:T(8,128)(2,1)S(1)} %constant_dynamic-slice_fusion), channel_id=1, source_target_pairs={{0,16},{16,0},{1,17},{17,1},{2,18},{18,2},{3,19},{19,3},{4,20},{20... | collective-permute-start | bytes 884744 | tf_op jit(solution)/shard_map/ppermute | solution.py:1236
  37.0 46.6 %collective-permute-start.10 = (bf16[2,2304,128]{2,1,0:T(8,128)(2,1)}, bf16[2,2304,128]{2,1,0:T(8,128)(2,1)S(1)}, u32[]{:S(2)}, u32[]{:S(2)}) collective-permute-start(bf16[2,2304,128]{2,1,0:T(8,128)(2,1)} %split_weights.4), channel_id=1, source_target_pairs={{0,16},{16,0},{1,17},{17,1},{2,18},{18,2},{3,19},{19,3},{4,20},{20... | collective-permute-start | bytes 3538952 | tf_op jit(solution)/shard_map/ppermute | solution.py:1236
  39.8 6.2 %collective-permute-start.6 = (bf16[192,768]{1,0:T(8,128)(2,1)}, bf16[192,768]{1,0:T(8,128)(2,1)S(1)}, u32[]{:S(2)}, u32[]{:S(2)}) collective-permute-start(bf16[192,768]{1,0:T(8,128)(2,1)} %collective-permute-done.5.out_sent_ref), channel_id=1, source_target_pairs={{0,4},{4,0},{8,12},{12,8},{1,5},{5,1},{9,13},{13,9},{2,6},{6,2},{1... | collective-permute-start | bytes 884744 | tf_op jit(solution)/shard_map/ppermute | solution.py:1239
  39.8 6.1 %collective-permute-start.3 = (bf16[256,256]{1,0:T(8,128)(2,1)}, bf16[256,256]{1,0:T(8,128)(2,1)S(1)}, u32[]{:S(2)}, u32[]{:S(2)}) collective-permute-start(bf16[256,256]{1,0:T(8,128)(2,1)} %get-tuple-element.137.kv0), channel_id=1, source_target_pairs={{0,8},{4,12},{8,0},{12,4},{1,9},{5,13},{9,1},{13,5},{2,10},{6,14},... | collective-permute-start | bytes 393224 | tf_op jit(solution)/shard_map/ppermute | solution.py:1242
  41.5 42.1 %collective-permute-start.11 = (bf16[256,1664]{1,0:T(8,128)(2,1)S(1)}, bf16[256,1664]{1,0:T(8,128)(2,1)S(1)}, u32[]{:S(2)}, u32[]{:S(2)}) collective-permute-start(bf16[256,1664]{1,0:T(8,128)(2,1)S(1)} %pad_maximum_fusion.1.near_out_ref.out_grad_ref), channel_id=1, source_target_pairs={{0,16},{16,0},{1,17},{17,1},{2,18},{18,2},{3,19},{19,3},{4,20},{20... | collective-permute-start | bytes 2555912 | tf_op jit(solution)/shard_map/ppermute | solution.py:1236
  43.4 2.5 collective-permute-start.2
  45.9 1.3 collective-permute-start.4
  53.7 9.5 %collective-permute-start.7 = (bf16[64,1536]{1,0:T(8,128)(2,1)}, bf16[64,1536]{1,0:T(8,128)(2,1)S(1)}, u32[]{:S(2)}, u32[]{:S(2)}) collective-permute-start(bf16[64,1536]{1,0:T(8,128)(2,1)} %get-tuple-element.140), channel_id=1, source_target_pairs={{1,0},{2,1},{3,2},{0,3},{5,4},{6,5},{7,6},{4,7},{9,8},{10,9},{11,1... | collective-permute-start | bytes 589832 | tf_op jit(solution)/shard_map/ppermute | solution.py:1245
  57.5 17.2 %collective-permute-start.8 = (bf16[64,1536]{1,0:T(8,128)(2,1)}, bf16[64,1536]{1,0:T(8,128)(2,1)S(1)}, u32[]{:S(2)}, u32[]{:S(2)}) collective-permute-start(bf16[64,1536]{1,0:T(8,128)(2,1)} %get-tuple-element.141), channel_id=1, source_target_pairs={{2,0},{3,1},{0,2},{1,3},{6,4},{7,5},{4,6},{5,7},{10,8},{11,9},{8,1... | collective-permute-start | bytes 589832 | tf_op jit(solution)/shard_map/ppermute | solution.py:1245
  57.5 17.2 %collective-permute-start.9 = (bf16[64,1536]{1,0:T(8,128)(2,1)}, bf16[64,1536]{1,0:T(8,128)(2,1)S(1)}, u32[]{:S(2)}, u32[]{:S(2)}) collective-permute-start(bf16[64,1536]{1,0:T(8,128)(2,1)} %get-tuple-element.142), channel_id=1, source_target_pairs={{3,0},{0,1},{1,2},{2,3},{7,4},{4,5},{5,6},{6,7},{11,8},{8,9},{9,10... | collective-permute-start | bytes 589832 | tf_op jit(solution)/shard_map/ppermute | solution.py:1245
  84.7 84.9 %all-gather.15.cloned.1.call-start = ((), (), s32[]{:S(2)}) async-start(), calls=%async_computation.1 | async-start | bytes 5898240 | tf_op jit(solution)/shard_map/all_gather | solution.py:1363
  84.7 46.6 %collective-permute-start.16 = (bf16[2,2304,128]{2,1,0:T(8,128)(2,1)}, bf16[2,2304,128]{2,1,0:T(8,128)(2,1)}, u32[]{:S(2)}, u32[]{:S(2)}) collective-permute-start(bf16[2,2304,128]{2,1,0:T(8,128)(2,1)} %split_weights.5), channel_id=1, source_target_pairs={{0,16},{16,0},{1,17},{17,1},{2,18},{18,2},{3,19},{19,3},{4,20},{20... | collective-permute-start | bytes 3538952 | tf_op jit(solution)/shard_map/ppermute | solution.py:1236
  86.1 9.0 %collective-permute-start.12 = (bf16[64,1536]{1,0:T(8,128)(2,1)S(1)}, bf16[64,1536]{1,0:T(8,128)(2,1)S(1)}, u32[]{:S(2)}, u32[]{:S(2)}) collective-permute-start(bf16[64,1536]{1,0:T(8,128)(2,1)S(1)} %add_convert_fusion.5.rest_0_), channel_id=1, source_target_pairs={{1,0},{2,1},{3,2},{0,3},{5,4},{6,5},{7,6},{4,7},{9,8},{10,9},{11,1... | collective-permute-start | bytes 589832 | tf_op jit(solution)/shard_map/ppermute | solution.py:1245
  89.7 16.3 %collective-permute-start.13 = (bf16[64,1536]{1,0:T(8,128)(2,1)S(1)}, bf16[64,1536]{1,0:T(8,128)(2,1)S(1)}, u32[]{:S(2)}, u32[]{:S(2)}) collective-permute-start(bf16[64,1536]{1,0:T(8,128)(2,1)S(1)} %add_convert_fusion.5.rest_0_), channel_id=1, source_target_pairs={{2,0},{3,1},{0,2},{1,3},{6,4},{7,5},{4,6},{5,7},{10,8},{11,9},{8,1... | collective-permute-start | bytes 589832 | tf_op jit(solution)/shard_map/ppermute | solution.py:1245
  89.7 16.3 %collective-permute-start.14 = (bf16[64,1536]{1,0:T(8,128)(2,1)S(1)}, bf16[64,1536]{1,0:T(8,128)(2,1)S(1)}, u32[]{:S(2)}, u32[]{:S(2)}) collective-permute-start(bf16[64,1536]{1,0:T(8,128)(2,1)S(1)} %add_convert_fusion.5.rest_0_), channel_id=1, source_target_pairs={{3,0},{0,1},{1,2},{2,3},{7,4},{4,5},{5,6},{6,7},{11,8},{8,9},{9,10... | collective-permute-start | bytes 589832 | tf_op jit(solution)/shard_map/ppermute | solution.py:1245
  111.1 20.3 %collective-permute-start.15 = (bf16[256,1664]{1,0:T(8,128)(2,1)}, bf16[256,1664]{1,0:T(8,128)(2,1)S(1)}, u32[]{:S(2)}, u32[]{:S(2)}) collective-permute-start(bf16[256,1664]{1,0:T(8,128)(2,1)} %get-tuple-element.152.near_ref), channel_id=1, source_target_pairs={{0,16},{16,0},{1,17},{17,1},{2,18},{18,2},{3,19},{19,3},{4,20},{20... | collective-permute-start | bytes 2555912 | tf_op jit(solution)/shard_map/ppermute | solution.py:1236
  131.4 95.6 %all-gather.17.cloned.1.call-start = ((), (), s32[]{:S(2)}) async-start(), calls=%async_computation.2 | async-start | bytes 8519680 | tf_op jit(solution)/shard_map/all_gather | solution.py:1398
  132.2 22.9 %collective-permute-start.17 = (bf16[1,2304,128]{2,1,0:T(8,128)(2,1)}, bf16[1,2304,128]{2,1,0:T(8,128)(2,1)S(1)}, u32[]{:S(2)}, u32[]{:S(2)}) collective-permute-start(bf16[1,2304,128]{2,1,0:T(8,128)(2,1)} %split_weights.6), channel_id=1, source_target_pairs={{0,16},{16,0},{1,17},{17,1},{2,18},{18,2},{3,19},{19,3},{4,20},{20... | collective-permute-start | bytes 1769480 | tf_op jit(solution)/shard_map/ppermute | solution.py:1236
  169.6 112.5 %all-gather.19.cloned.1.call-start = ((), (), s32[]{:S(2)}) async-start(), calls=%async_computation.3 | async-start | bytes 7077888 | tf_op jit(solution)/shard_map/all_gather | solution.py:1421
  169.8 19.2 %collective-permute-start.18 = (bf16[1,2304,128]{2,1,0:T(8,128)(2,1)S(1)}, bf16[1,2304,128]{2,1,0:T(8,128)(2,1)S(1)}, u32[]{:S(2)}, u32[]{:S(2)}) collective-permute-start(bf16[1,2304,128]{2,1,0:T(8,128)(2,1)S(1)} %collective-permute-done.17.rest_0_), channel_id=1, source_target_pairs={{0,8},{4,12},{8,0},{12,4},{1,9},{5,13},{9,1},{13,5},{2,10},{6,14},... | collective-permute-start | bytes 1769480 | tf_op jit(solution)/shard_map/ppermute | solution.py:1242
  170.2 18.8 %collective-permute-start.19 = (bf16[1,2304,128]{2,1,0:T(8,128)(2,1)S(1)}, bf16[1,2304,128]{2,1,0:T(8,128)(2,1)S(1)}, u32[]{:S(2)}, u32[]{:S(2)}) collective-permute-start(bf16[1,2304,128]{2,1,0:T(8,128)(2,1)S(1)} %collective-permute-done.17.rest_0_), channel_id=1, source_target_pairs={{0,4},{4,0},{8,12},{12,8},{1,5},{5,1},{9,13},{13,9},{2,6},{6,2},{1... | collective-permute-start | bytes 1769480 | tf_op jit(solution)/shard_map/ppermute | solution.py:1239
  189.0 2.1 collective-permute-start.20
  205.7 21.2 %collective-permute-start.21 = (bf16[256,1664]{1,0:T(8,128)(2,1)}, bf16[256,1664]{1,0:T(8,128)(2,1)S(1)}, u32[]{:S(2)}, u32[]{:S(2)}) collective-permute-start(bf16[256,1664]{1,0:T(8,128)(2,1)} %get-tuple-element.174), channel_id=1, source_target_pairs={{0,16},{16,0},{1,17},{17,1},{2,18},{18,2},{3,19},{19,3},{4,20},{20... | collective-permute-start | bytes 2555912 | tf_op jit(solution)/shard_map/ppermute | solution.py:1236
  227.0 141.7 %all-gather.21.cloned.1.call-start = ((), (), s32[]{:S(2)}) async-start(), calls=%async_computation.4 | async-start | bytes 7077888 | tf_op jit(solution)/shard_map/all_gather | solution.py:1421
  231.1 9.6 %collective-permute-start.22 = (bf16[64,1664]{1,0:T(8,128)(2,1)}, bf16[64,1664]{1,0:T(8,128)(2,1)S(1)}, u32[]{:S(2)}, u32[]{:S(2)}) collective-permute-start(bf16[64,1664]{1,0:T(8,128)(2,1)} %get-tuple-element.180), channel_id=1, source_target_pairs={{1,0},{2,1},{3,2},{0,3},{5,4},{6,5},{7,6},{4,7},{9,8},{10,9},{11,1... | collective-permute-start | bytes 638984 | tf_op jit(solution)/shard_map/ppermute | solution.py:1245
  234.7 18.2 %collective-permute-start.23 = (bf16[64,1664]{1,0:T(8,128)(2,1)}, bf16[64,1664]{1,0:T(8,128)(2,1)S(1)}, u32[]{:S(2)}, u32[]{:S(2)}) collective-permute-start(bf16[64,1664]{1,0:T(8,128)(2,1)} %get-tuple-element.181), channel_id=1, source_target_pairs={{2,0},{3,1},{0,2},{1,3},{6,4},{7,5},{4,6},{5,7},{10,8},{11,9},{8,1... | collective-permute-start | bytes 638984 | tf_op jit(solution)/shard_map/ppermute | solution.py:1245
  234.7 18.2 %collective-permute-start.24 = (bf16[64,1664]{1,0:T(8,128)(2,1)}, bf16[64,1664]{1,0:T(8,128)(2,1)S(1)}, u32[]{:S(2)}, u32[]{:S(2)}) collective-permute-start(bf16[64,1664]{1,0:T(8,128)(2,1)} %get-tuple-element.182), channel_id=1, source_target_pairs={{3,0},{0,1},{1,2},{2,3},{7,4},{4,5},{5,6},{6,7},{11,8},{8,9},{9,10... | collective-permute-start | bytes 638984 | tf_op jit(solution)/shard_map/ppermute | solution.py:1245
  235.8 39.4 %collective-permute-start.28 = (bf16[256,1536]{1,0:T(8,128)(2,1)}, bf16[256,1536]{1,0:T(8,128)(2,1)S(1)}, u32[]{:S(2)}, u32[]{:S(2)}) collective-permute-start(bf16[256,1536]{1,0:T(8,128)(2,1)} %get-tuple-element.184), channel_id=1, source_target_pairs={{0,16},{16,0},{1,17},{17,1},{2,18},{18,2},{3,19},{19,3},{4,20},{20... | collective-permute-start | bytes 2359304 | tf_op jit(solution)/shard_map/ppermute | solution.py:1236
  253.9 5.9 %collective-permute-start.25 = (bf16[64,1664]{1,0:T(8,128)(2,1)S(1)}, bf16[64,1664]{1,0:T(8,128)(2,1)S(1)}, u32[]{:S(2)}, u32[]{:S(2)}) collective-permute-start(bf16[64,1664]{1,0:T(8,128)(2,1)S(1)} %add_convert_fusion.2.rest_0_), channel_id=1, source_target_pairs={{1,0},{2,1},{3,2},{0,3},{5,4},{6,5},{7,6},{4,7},{9,8},{10,9},{11,1... | collective-permute-start | bytes 638984 | tf_op jit(solution)/shard_map/ppermute | solution.py:1245
  254.0 21.2 %collective-permute-start.26 = (bf16[64,1664]{1,0:T(8,128)(2,1)S(1)}, bf16[64,1664]{1,0:T(8,128)(2,1)S(1)}, u32[]{:S(2)}, u32[]{:S(2)}) collective-permute-start(bf16[64,1664]{1,0:T(8,128)(2,1)S(1)} %add_convert_fusion.2.rest_0_), channel_id=1, source_target_pairs={{2,0},{3,1},{0,2},{1,3},{6,4},{7,5},{4,6},{5,7},{10,8},{11,9},{8,1... | collective-permute-start | bytes 638984 | tf_op jit(solution)/shard_map/ppermute | solution.py:1245
  256.8 18.4 %collective-permute-start.27 = (bf16[64,1664]{1,0:T(8,128)(2,1)S(1)}, bf16[64,1664]{1,0:T(8,128)(2,1)S(1)}, u32[]{:S(2)}, u32[]{:S(2)}) collective-permute-start(bf16[64,1664]{1,0:T(8,128)(2,1)S(1)} %add_convert_fusion.2.rest_0_), channel_id=1, source_target_pairs={{3,0},{0,1},{1,2},{2,3},{7,4},{4,5},{5,6},{6,7},{11,8},{8,9},{9,10... | collective-permute-start | bytes 638984 | tf_op jit(solution)/shard_map/ppermute | solution.py:1245
  282.2 144.5 %all-gather.23.cloned.1.call-start = ((), (), s32[]{:S(2)}) async-start(), calls=%async_computation.5 | async-start | bytes 3538944 | tf_op jit(solution)/shard_map/all_gather | solution.py:1421
  287.7 18.8 %collective-permute-start.29 = (bf16[64,1536]{1,0:T(8,128)(2,1)}, bf16[64,1536]{1,0:T(8,128)(2,1)S(1)}, u32[]{:S(2)}, u32[]{:S(2)}) collective-permute-start(bf16[64,1536]{1,0:T(8,128)(2,1)} %get-tuple-element.196), channel_id=1, source_target_pairs={{1,0},{2,1},{3,2},{0,3},{5,4},{6,5},{7,6},{4,7},{9,8},{10,9},{11,1... | collective-permute-start | bytes 589832 | tf_op jit(solution)/shard_map/ppermute | solution.py:1245
  291.0 17.5 %collective-permute-start.30 = (bf16[64,1536]{1,0:T(8,128)(2,1)}, bf16[64,1536]{1,0:T(8,128)(2,1)S(1)}, u32[]{:S(2)}, u32[]{:S(2)}) collective-permute-start(bf16[64,1536]{1,0:T(8,128)(2,1)} %get-tuple-element.197), channel_id=1, source_target_pairs={{2,0},{3,1},{0,2},{1,3},{6,4},{7,5},{4,6},{5,7},{10,8},{11,9},{8,1... | collective-permute-start | bytes 589832 | tf_op jit(solution)/shard_map/ppermute | solution.py:1245
  291.0 17.5 %collective-permute-start.31 = (bf16[64,1536]{1,0:T(8,128)(2,1)}, bf16[64,1536]{1,0:T(8,128)(2,1)S(1)}, u32[]{:S(2)}, u32[]{:S(2)}) collective-permute-start(bf16[64,1536]{1,0:T(8,128)(2,1)} %get-tuple-element.198), channel_id=1, source_target_pairs={{3,0},{0,1},{1,2},{2,3},{7,4},{4,5},{5,6},{6,7},{11,8},{8,9},{9,10... | collective-permute-start | bytes 589832 | tf_op jit(solution)/shard_map/ppermute | solution.py:1245
  308.7 2.0 collective-permute-start.32
  310.0 15.9 %collective-permute-start.37 = (bf16[2,224,768]{2,1,0:T(8,128)(2,1)}, bf16[2,224,768]{2,1,0:T(8,128)(2,1)}, u32[]{:S(2)}, u32[]{:S(2)}) collective-permute-start(bf16[2,224,768]{2,1,0:T(8,128)(2,1)} %dynamic-slice_convert_fusion.1), channel_id=1, source_target_pairs={{0,4},{4,0},{8,12},{12,8},{1,5},{5,1},{9,13},{13,9},{2,6},{6,2},{1... | collective-permute-start | bytes 2064392 | tf_op jit(solution)/shard_map/ppermute | solution.py:1239
  310.7 8.9 %collective-permute-start.33 = (bf16[256,256]{1,0:T(8,128)(2,1)S(1)}, bf16[256,256]{1,0:T(8,128)(2,1)S(1)}, u32[]{:S(2)}, u32[]{:S(2)}) collective-permute-start(bf16[256,256]{1,0:T(8,128)(2,1)S(1)} %fusion.19), channel_id=1, source_target_pairs={{0,8},{4,12},{8,0},{12,4},{1,9},{5,13},{9,1},{13,5},{2,10},{6,14},... | collective-permute-start | bytes 393224 | tf_op jit(solution)/shard_map/ppermute | solution.py:1242
  313.1 14.1 %collective-permute-start.34 = (bf16[64,1536]{1,0:T(8,128)(2,1)S(1)}, bf16[64,1536]{1,0:T(8,128)(2,1)S(1)}, u32[]{:S(2)}, u32[]{:S(2)}) collective-permute-start(bf16[64,1536]{1,0:T(8,128)(2,1)S(1)} %add_convert_fusion.4.rest_0_), channel_id=1, source_target_pairs={{1,0},{2,1},{3,2},{0,3},{5,4},{6,5},{7,6},{4,7},{9,8},{10,9},{11,1... | collective-permute-start | bytes 589832 | tf_op jit(solution)/shard_map/ppermute | solution.py:1245
  313.8 19.2 %collective-permute-start.35 = (bf16[64,1536]{1,0:T(8,128)(2,1)S(1)}, bf16[64,1536]{1,0:T(8,128)(2,1)S(1)}, u32[]{:S(2)}, u32[]{:S(2)}) collective-permute-start(bf16[64,1536]{1,0:T(8,128)(2,1)S(1)} %add_convert_fusion.4.rest_0_), channel_id=1, source_target_pairs={{2,0},{3,1},{0,2},{1,3},{6,4},{7,5},{4,6},{5,7},{10,8},{11,9},{8,1... | collective-permute-start | bytes 589832 | tf_op jit(solution)/shard_map/ppermute | solution.py:1245
  315.4 17.5 %collective-permute-start.36 = (bf16[64,1536]{1,0:T(8,128)(2,1)S(1)}, bf16[64,1536]{1,0:T(8,128)(2,1)S(1)}, u32[]{:S(2)}, u32[]{:S(2)}) collective-permute-start(bf16[64,1536]{1,0:T(8,128)(2,1)S(1)} %add_convert_fusion.4.rest_0_), channel_id=1, source_target_pairs={{3,0},{0,1},{1,2},{2,3},{7,4},{4,5},{5,6},{6,7},{11,8},{8,9},{9,10... | collective-permute-start | bytes 589832 | tf_op jit(solution)/shard_map/ppermute | solution.py:1245
  335.6 30.4 %collective-permute-start.42 = (bf16[2,384,640]{2,1,0:T(8,128)(2,1)}, bf16[2,384,640]{2,1,0:T(8,128)(2,1)}, u32[]{:S(2)}, u32[]{:S(2)}) collective-permute-start(bf16[2,384,640]{2,1,0:T(8,128)(2,1)} %dynamic-slice_convert_fusion), channel_id=1, source_target_pairs={{0,4},{4,0},{8,12},{12,8},{1,5},{5,1},{9,13},{13,9},{2,6},{6,2},{1... | collective-permute-start | bytes 2949128 | tf_op jit(solution)/shard_map/ppermute | solution.py:1239
  335.6 26.2 %collective-permute-start.38 = (bf16[64,1536]{1,0:T(8,128)(2,1)}, bf16[64,1536]{1,0:T(8,128)(2,1)S(1)}, u32[]{:S(2)}, u32[]{:S(2)}) collective-permute-start(bf16[64,1536]{1,0:T(8,128)(2,1)} %get-tuple-element.217), channel_id=1, source_target_pairs={{1,0},{2,1},{3,2},{0,3},{5,4},{6,5},{7,6},{4,7},{9,8},{10,9},{11,1... | collective-permute-start | bytes 589832 | tf_op jit(solution)/shard_map/ppermute | solution.py:1245
  335.6 26.2 %collective-permute-start.39 = (bf16[64,1536]{1,0:T(8,128)(2,1)}, bf16[64,1536]{1,0:T(8,128)(2,1)}, u32[]{:S(2)}, u32[]{:S(2)}) collective-permute-start(bf16[64,1536]{1,0:T(8,128)(2,1)} %get-tuple-element.218), channel_id=1, source_target_pairs={{2,0},{3,1},{0,2},{1,3},{6,4},{7,5},{4,6},{5,7},{10,8},{11,9},{8,1... | collective-permute-start | bytes 589832 | tf_op jit(solution)/shard_map/ppermute | solution.py:1245
  336.4 26.1 %collective-permute-start.40 = (bf16[64,1536]{1,0:T(8,128)(2,1)}, bf16[64,1536]{1,0:T(8,128)(2,1)}, u32[]{:S(2)}, u32[]{:S(2)}) collective-permute-start(bf16[64,1536]{1,0:T(8,128)(2,1)} %get-tuple-element.219), channel_id=1, source_target_pairs={{3,0},{0,1},{1,2},{2,3},{7,4},{4,5},{5,6},{6,7},{11,8},{8,9},{9,10... | collective-permute-start | bytes 589832 | tf_op jit(solution)/shard_map/ppermute | solution.py:1245
  339.6 24.2 %collective-permute-start.41 = (bf16[224,768]{1,0:T(8,128)(2,1)}, bf16[224,768]{1,0:T(8,128)(2,1)}, u32[]{:S(2)}, u32[]{:S(2)}) collective-permute-start(bf16[224,768]{1,0:T(8,128)(2,1)} %fusion.11), channel_id=1, source_target_pairs={{0,16},{16,0},{1,17},{17,1},{2,18},{18,2},{3,19},{19,3},{4,20},{20... | collective-permute-start | bytes 1032200 | tf_op jit(solution)/shard_map/ppermute | solution.py:1236
  369.8 34.5 %collective-permute-start.46 = (bf16[224,768]{1,0:T(8,128)(2,1)S(1)}, bf16[224,768]{1,0:T(8,128)(2,1)S(1)}, u32[]{:S(2)}, u32[]{:S(2)}) collective-permute-start(bf16[224,768]{1,0:T(8,128)(2,1)S(1)} %convert_element_type.184), channel_id=1, source_target_pairs={{0,8},{4,12},{8,0},{12,4},{1,9},{5,13},{9,1},{13,5},{2,10},{6,14},... | collective-permute-start | bytes 1032200 | tf_op jit(solution)/shard_map/ppermute | solution.py:1242
  372.3 32.1 %collective-permute-start.47 = (bf16[384,640]{1,0:T(8,128)(2,1)S(1)}, bf16[384,640]{1,0:T(8,128)(2,1)}, u32[]{:S(2)}, u32[]{:S(2)}) collective-permute-start(bf16[384,640]{1,0:T(8,128)(2,1)S(1)} %fusion.7), channel_id=1, source_target_pairs={{0,16},{16,0},{1,17},{17,1},{2,18},{18,2},{3,19},{19,3},{4,20},{20... | collective-permute-start | bytes 1474568 | tf_op jit(solution)/shard_map/ppermute | solution.py:1236
  373.1 4.1 collective-permute-start.48
  374.9 4.5 %collective-permute-start.49 = (f32[1536]{0:T(1024)S(1)}, f32[1536]{0:T(1024)S(1)}, u32[]{:S(2)}, u32[]{:S(2)}) collective-permute-start(f32[1536]{0:T(1024)S(1)} %copy-done.50), channel_id=1, source_target_pairs={{2,0},{3,1},{0,2},{1,3},{6,4},{7,5},{4,6},{5,7},{10,8},{11,9},{8,1... | collective-permute-start | bytes 18440 | tf_op jit(solution)/shard_map/ppermute | solution.py:1245
  375.1 5.6 %collective-permute-start.50 = (f32[1536]{0:T(1024)S(1)}, f32[1536]{0:T(1024)S(1)}, u32[]{:S(2)}, u32[]{:S(2)}) collective-permute-start(f32[1536]{0:T(1024)S(1)} %copy-done.50), channel_id=1, source_target_pairs={{3,0},{0,1},{1,2},{2,3},{7,4},{4,5},{5,6},{6,7},{11,8},{8,9},{9,10... | collective-permute-start | bytes 18440 | tf_op jit(solution)/shard_map/ppermute | solution.py:1245
  380.7 24.9 %collective-permute-start.43 = (bf16[64,1536]{1,0:T(8,128)(2,1)S(1)}, bf16[64,1536]{1,0:T(8,128)(2,1)}, u32[]{:S(2)}, u32[]{:S(2)}) collective-permute-start(bf16[64,1536]{1,0:T(8,128)(2,1)S(1)} %add_convert_fusion.3.rest_0_), channel_id=1, source_target_pairs={{1,0},{2,1},{3,2},{0,3},{5,4},{6,5},{7,6},{4,7},{9,8},{10,9},{11,1... | collective-permute-start | bytes 589832 | tf_op jit(solution)/shard_map/ppermute | solution.py:1245
  381.2 24.3 %collective-permute-start.44 = (bf16[64,1536]{1,0:T(8,128)(2,1)S(1)}, bf16[64,1536]{1,0:T(8,128)(2,1)}, u32[]{:S(2)}, u32[]{:S(2)}) collective-permute-start(bf16[64,1536]{1,0:T(8,128)(2,1)S(1)} %add_convert_fusion.3.rest_0_), channel_id=1, source_target_pairs={{2,0},{3,1},{0,2},{1,3},{6,4},{7,5},{4,6},{5,7},{10,8},{11,9},{8,1... | collective-permute-start | bytes 589832 | tf_op jit(solution)/shard_map/ppermute | solution.py:1245
  382.2 23.3 %collective-permute-start.45 = (bf16[64,1536]{1,0:T(8,128)(2,1)S(1)}, bf16[64,1536]{1,0:T(8,128)(2,1)}, u32[]{:S(2)}, u32[]{:S(2)}) collective-permute-start(bf16[64,1536]{1,0:T(8,128)(2,1)S(1)} %add_convert_fusion.3.rest_0_), channel_id=1, source_target_pairs={{3,0},{0,1},{1,2},{2,3},{7,4},{4,5},{5,6},{6,7},{11,8},{8,9},{9,10... | collective-permute-start | bytes 589832 | tf_op jit(solution)/shard_map/ppermute | solution.py:1245
  405.6 13.5 %collective-permute-start.54 = (bf16[384,640]{1,0:T(8,128)(2,1)S(1)}, bf16[384,640]{1,0:T(8,128)(2,1)S(1)}, u32[]{:S(2)}, u32[]{:S(2)}) collective-permute-start(bf16[384,640]{1,0:T(8,128)(2,1)S(1)} %convert_element_type.189), channel_id=1, source_target_pairs={{0,8},{4,12},{8,0},{12,4},{1,9},{5,13},{9,1},{13,5},{2,10},{6,14},... | collective-permute-start | bytes 1474568 | tf_op jit(solution)/shard_map/ppermute | solution.py:1242
  406.8 1.2 collective-permute-start.51
  408.0 9.7 %collective-permute-start.52 = (f32[1536]{0:T(1024)S(1)}, f32[1536]{0:T(1024)S(1)}, u32[]{:S(2)}, u32[]{:S(2)}) collective-permute-start(f32[1536]{0:T(1024)S(1)} %add.164), channel_id=1, source_target_pairs={{0,8},{4,12},{8,0},{12,4},{1,9},{5,13},{9,1},{13,5},{2,10},{6,14},... | collective-permute-start | bytes 18440 | tf_op jit(solution)/shard_map/ppermute | solution.py:1242
  413.7 8.3 %collective-permute-start.56 = (bf16[224,768]{1,0:T(8,128)(2,1)S(1)}, bf16[224,768]{1,0:T(8,128)(2,1)S(1)}, u32[]{:S(2)}, u32[]{:S(2)}) collective-permute-start(bf16[224,768]{1,0:T(8,128)(2,1)S(1)} %add_convert_fusion.1), channel_id=1, source_target_pairs={{0,4},{4,0},{8,12},{12,8},{1,5},{5,1},{9,13},{13,9},{2,6},{6,2},{1... | collective-permute-start | bytes 1032200 | tf_op jit(solution)/shard_map/ppermute | solution.py:1239
  417.7 3.7 collective-permute-start.53
  419.2 5.3 %collective-permute-start.55 = (bf16[384,640]{1,0:T(8,128)(2,1)S(1)}, bf16[384,640]{1,0:T(8,128)(2,1)S(1)}, u32[]{:S(2)}, u32[]{:S(2)}) collective-permute-start(bf16[384,640]{1,0:T(8,128)(2,1)S(1)} %add_convert_fusion), channel_id=1, source_target_pairs={{0,4},{4,0},{8,12},{12,8},{1,5},{5,1},{9,13},{13,9},{2,6},{6,2},{1... | collective-permute-start | bytes 1474568 | tf_op jit(solution)/shard_map/ppermute | solution.py:1239
  (53 other events, 445.3 us)
Sparse Core Ops, SparseCore 0:
  84.8 38.5 all-gather.12
  131.5 38.0 all-gather.14
  171.2 52.4 all-gather.16
  227.1 55.0 all-gather.18
  283.9 48.3 all-gather.20
  368.8 34.8 all-gather.22

commit v5 on v4

--- a/solution.py
+++ b/solution.py
@@ -611,9 +611,8 @@
     head_ref,
     probs_ref,
     out_far_ref,
-    *rest,
+    attn_ref,
 ):
-    piece_refs, whole_buf = rest[:-1], rest[-1]
     c_pos = place_ref[1]
     blocks = (kv0, kv1, kv2, kv3)
     micro = parents_ref.shape[0]
@@ -663,18 +662,26 @@
     out_far_ref[:part, :] = jnp.where(first_core, sent, beside)
     out_far_ref[part:, :] = jnp.where(first_core, beside, sent)
     half = sent.shape[1]
-    whole_buf[:, :half] = dot(head_ref[...], out_near_ref[...])
-    whole_buf[:, half:] = dot(head_ref[...], out_far_ref[...])
-    give_pieces(whole_buf, place_ref[2], piece_refs)
-
-
-def after_kernel(place_ref, hidden_ref, gains_ref, small_ref, far_ref, routes_ref, *rest):
-    mixed_ref, rows_ref, gates_ref, whole_buf = rest[-4:]
-    take_pieces(rest[:-4], place_ref[2], whole_buf)
+    attn_ref[:, :half] = dot(head_ref[...], out_near_ref[...]).astype(jnp.bfloat16)
+    attn_ref[:, half:] = dot(head_ref[...], out_far_ref[...]).astype(jnp.bfloat16)
+
+
+def after_kernel(
+    place_ref,
+    hidden_ref,
+    gains_ref,
+    small_ref,
+    far_ref,
+    routes_ref,
+    attended_ref,
+    mixed_ref,
+    rows_ref,
+    gates_ref,
+):
     half = small_ref.shape[1]
     near, far = own_then_other(place_ref[0], hidden_ref[...].astype(jnp.float32))
-    near = near + RESIDUAL_SCALE * whole_buf[:, :half]
-    far = far + RESIDUAL_SCALE * whole_buf[:, half:]
+    near = near + RESIDUAL_SCALE * attended_ref[:, :half].astype(jnp.float32)
+    far = far + RESIDUAL_SCALE * attended_ref[:, half:].astype(jnp.float32)
     mixed_ref[:, :half] = near
     mixed_ref[:, half:] = far
     scale = row_scale(near, far)
@@ -715,11 +722,9 @@
 ):
     count = 4 if split else 1
     other_refs, rest = rest[:count], rest[count:]
-    if first > 0:
-        held_out, held_grad = rest[:2]
-        rest = rest[2:]
-    out_ref, grad_ref, slots_ref = rest[:3]
-    rows_buf, grads_buf, moe_buf, back_buf, hot_buf, gate_buf = rest[-6:]
+    held = rest[:4] if last else ()
+    slots_ref, *sums = rest[len(held) : -8]
+    rows_buf, grads_buf, moe_buf, back_buf, hot_buf, gate_buf, out_ref, grad_ref = rest[-8:]
     half = down_ref.shape[-1]
     full = 2 * half
     width = down_ref.shape[-2]
@@ -731,12 +736,12 @@
 
     @pl.when(step == 0)
     def _():
-        if first == 0:
+        if last:
+            out_ref[...] = held[0][...].astype(jnp.float32) + held[2][...].astype(jnp.float32)
+            grad_ref[...] = held[1][...].astype(jnp.float32) + held[3][...].astype(jnp.float32)
+        else:
             out_ref[...] = jnp.zeros_like(out_ref)
             grad_ref[...] = jnp.zeros_like(grad_ref)
-        else:
-            out_ref[...] = held_out[...]
-            grad_ref[...] = held_grad[...]
 
     marks = [((lane == expert[r]) | (lane == expert[r] + 64)) for r in range(4)]
     mark = jnp.concatenate(marks, axis=0)
@@ -817,19 +822,22 @@
         out_ref[span, :] += dot(hot_buf[b], moe_buf[b], 0, 0)
         grad_ref[span, :] += dot(hot_buf[b], back_buf[b], 0, 0)
 
-    if last:
-        moe_far_ref, back_far_ref = rest[3:5]
-
-        @pl.when(step == pl.num_programs(0) - 1)
-        def _():
-            span = pl.ds(256, 256)
-            for part in range(2):
-                keep, swap = pl.ds(part * half, half), pl.ds((1 - part) * half, half)
-                moe_far_ref[:, keep] = out_ref[span, swap].astype(jnp.bfloat16)
-                back_far_ref[:, keep] = grad_ref[span, swap].astype(jnp.bfloat16)
-            back_far_ref[:, pl.ds(full, 128)] = grad_ref[span, pl.ds(full, 128)].astype(
-                jnp.bfloat16
-            )
+    @pl.when(step == pl.num_programs(0) - 1)
+    def _():
+        if not last:
+            sums[0][...] = out_ref[...].astype(jnp.bfloat16)
+            sums[1][...] = grad_ref[...].astype(jnp.bfloat16)
+            return
+        moe_ref, back_ref, moe_far_ref, back_far_ref = sums
+        count = moe_ref.shape[0]
+        span = pl.ds(count, count)
+        moe_ref[...] = out_ref[:count, :]
+        back_ref[...] = grad_ref[:count, :]
+        for part in range(2):
+            keep, swap = pl.ds(part * half, half), pl.ds((1 - part) * half, half)
+            moe_far_ref[:, keep] = out_ref[span, swap].astype(jnp.bfloat16)
+            back_far_ref[:, keep] = grad_ref[span, swap].astype(jnp.bfloat16)
+        back_far_ref[:, pl.ds(full, 128)] = grad_ref[span, pl.ds(full, 128)].astype(jnp.bfloat16)
 
 
 def run_experts(place, near, far, near_out, far_out, rank, gate_up, down, other, held, first, each):
@@ -859,27 +867,17 @@
     else:
         in_specs.append(pl.BlockSpec((quarters, 1, packed, lanes), lambda j, sp: (0, j, 0, 0)))
     operands = [place, near, far, near_out, far_out, rank, gate_up, down, *others]
-    aliases = {}
-    totals = [
-        jax.ShapeDtypeStruct((tokens, full), jnp.float32),
-        jax.ShapeDtypeStruct((tokens, full + 128), jnp.float32),
-    ]
-    if first > 0:
-        in_specs += [fixed(held[0].shape), fixed(held[1].shape)]
-        aliases = {len(operands): 0, len(operands) + 1: 1}
-        operands += list(held[:2])
-    out_shape = totals + [
-        jax.ShapeDtypeStruct((quarters, steps, 4 * CAP, 3 * width), jnp.bfloat16)
-    ]
-    out_specs = [
-        fixed(totals[0].shape),
-        fixed(totals[1].shape),
-        pl.BlockSpec((quarters, 1, 4 * CAP, 3 * width), lambda j, sp: (0, j, 0, 0)),
-    ]
     if last:
+        in_specs += [fixed(array.shape) for array in held]
+        operands += list(held)
+    out_shape = [jax.ShapeDtypeStruct((quarters, steps, 4 * CAP, 3 * width), jnp.bfloat16)]
+    out_specs = [pl.BlockSpec((quarters, 1, 4 * CAP, 3 * width), lambda j, sp: (0, j, 0, 0))]
+    count = tokens // 2 if last else tokens
+    kinds = (jnp.float32, jnp.bfloat16) if last else (jnp.bfloat16,)
+    for kind in kinds:
         for lanes_out in (full, full + 128):
-            out_shape.append(jax.ShapeDtypeStruct((tokens // 2, lanes_out), jnp.bfloat16))
-            out_specs.append(fixed((tokens // 2, lanes_out)))
+            out_shape.append(jax.ShapeDtypeStruct((count, lanes_out), kind))
+            out_specs.append(fixed((count, lanes_out)))
     return pl.pallas_call(
         functools.partial(expert_kernel, first=first, last=last, each=each, split=split),
         out_shape=tuple(out_shape),
@@ -893,9 +891,10 @@
                 pltpu.VMEM((4, 4 * CAP, full + 128), jnp.bfloat16),
                 pltpu.VMEM((4, 4 * CAP, 128), jnp.bfloat16),
                 pltpu.VMEM((4, 4 * CAP, 128), jnp.float32),
+                pltpu.VMEM((tokens, full), jnp.float32),
+                pltpu.VMEM((tokens, full + 128), jnp.float32),
             ],
         ),
-        input_output_aliases=aliases,
         compiler_params=kernel_params(1),
         name="experts",
     )(*operands)
@@ -1033,11 +1032,10 @@
     turn_ref,
     small_ref,
     far_ref,
-    hidden_ref,
+    grads_ref,
     *rest,
 ):
-    grads_ref, gain_ref = rest[0], rest[1]
-    piece_refs, whole_buf = rest[2:-1], rest[-1]
+    piece_refs, whole_buf = rest[:-1], rest[-1]
     q_cols = query_grad_ref.shape[1]
     k_cols = turn_ref.shape[2]
     cols = q_cols + 2 * k_cols
@@ -1054,14 +1052,6 @@
     grads = grads_ref[...]
     near_part = dot(grads, small_ref[:half, :cols], 1, 1)
     far_part = dot(grads, far_ref[:, :cols], 1, 1)
-    near, far = own_then_other(place_ref[0], hidden_ref[...].astype(jnp.float32))
-    scale = row_scale(near, far)
-    gain_ref[:, :half] = jnp.broadcast_to(
-        jnp.sum(near_part * (near * scale), axis=0, keepdims=True), (8, half)
-    )
-    gain_ref[:, half:] = jnp.broadcast_to(
-        jnp.sum(far_part * (far * scale), axis=0, keepdims=True), (8, half)
-    )
     whole_buf[:, :half] = near_part
     whole_buf[:, half:] = far_part
     give_pieces(whole_buf, place_ref[2], piece_refs)
@@ -1077,13 +1067,19 @@
     out_ref[:, half:] = second
 
 
-def hidden_kernel(place_ref, hidden_ref, gains_ref, mixed_grad_ref, *rest):
-    out_ref, whole_buf = rest[-2:]
-    take_pieces(rest[:-2], place_ref[2], whole_buf)
+def hidden_kernel(place_ref, hidden_ref, gains_ref, mixed_grad_ref, mark_ref, *rest):
+    out_ref, gain_ref, whole_buf = rest[-3:]
+    take_pieces(rest[:-3], place_ref[2], whole_buf)
     half = out_ref.shape[1] // 2
     near, far = own_then_other(place_ref[0], hidden_ref[...].astype(jnp.float32))
     scale = row_scale(near, far)
     near, far = near * scale, far * scale
+    gain_ref[:, :half] = jnp.broadcast_to(
+        jnp.sum(whole_buf[:, :half] * near, axis=0, keepdims=True), (8, half)
+    )
+    gain_ref[:, half:] = jnp.broadcast_to(
+        jnp.sum(whole_buf[:, half:] * far, axis=0, keepdims=True), (8, half)
+    )
     near_scaled = whole_buf[:, :half] * gains_ref[0:1, :half]
     far_scaled = whole_buf[:, half:] * gains_ref[0:1, half:]
     mean = (
@@ -1097,13 +1093,14 @@
 
 
 def weight_grad_kernel(
-    place_ref, rows_ref, grads_ref, slots_ref, rank_ref, *refs
+    place_ref, rows_ref, grads0, grads1, grads2, grads3, slots_ref, rank_ref, *refs, first, steps
 ):
     gate_up_ref, down_ref, mark_ref, rows_buf, grads_buf = refs[-5:]
     half = down_ref.shape[-1]
     width = down_ref.shape[-2]
-    steps = rank_ref.shape[2]
     iota = lax.broadcasted_iota(jnp.int32, (CAP, 128), 0)
+    grads_in = (grads0, grads1, grads2, grads3)
+    ctx = [place_ref[1] ^ r for r in range(4)]
     step, side = pl.program_id(0), pl.program_id(1)
     mark_ref[...] = jnp.zeros_like(mark_ref)
 
@@ -1115,15 +1112,15 @@
                 for a in range(2):
                     hot = jnp.concatenate(
                         [
-                            jnp.where(iota == rank_ref[a, q, j, pl.ds(4 * k + b, 1), :], 1.0, 0.0)
+                            jnp.where(iota == rank_ref[a, q, first + j, pl.ds(4 * k + b, 1), :], 1.0, 0.0)
                             for j in range(steps)
                             for q in range(4)
                         ],
                         axis=0,
                     ).astype(jnp.bfloat16)
                     spot = 4 * k + (b ^ (2 * a))
-                    rows = dot(hot, rows_ref[k, span, :]).astype(jnp.bfloat16)
-                    grads = dot(hot, grads_ref[k, span, :]).astype(jnp.bfloat16)
+                    rows = dot(hot, rows_ref[ctx[k], span, :]).astype(jnp.bfloat16)
+                    grads = dot(hot, grads_in[k][span, :]).astype(jnp.bfloat16)
                     for j in range(steps):
                         piece = slice(j * 4 * CAP, (j + 1) * 4 * CAP)
                         rows_buf[j * 2 + a, spot] = rows[piece]
@@ -1134,25 +1131,25 @@
         slot = slice(q * CAP, (q + 1) * CAP)
         rows = jnp.concatenate([rows_buf[place, n, slot, :] for n in range(16)], axis=0)
         grads = jnp.concatenate([grads_buf[place, n, slot, :] for n in range(16)], axis=0)
-        taken = jnp.concatenate([slots_ref[0, k, q, 0] for k in range(4)], axis=0)
+        taken = jnp.concatenate([slots_ref[0, ctx[k], q, 0] for k in range(4)], axis=0)
         made = dot(rows, taken[:, : 2 * width], 0, 0)
         gate_up_ref[0, q, 0, pl.ds(0, half, stride=2), :] = made[:, :width]
         gate_up_ref[0, q, 0, pl.ds(1, half, stride=2), :] = made[:, width:]
         down_ref[0, q, 0] = dot(taken[:, 2 * width :], grads, 0, 0)
 
 
-def run_weight_grads(place, plane, slots, rank, held, each, first, mark):
+def run_weight_grads(place, plane, early, slots, rank, held, each, first, mark):
     sides, _, quarters, steps, slot_count, lanes = slots.shape
     width = lanes // 3
-    half = (plane.shape[-1] - 128) // 2
+    half = plane.shape[-1]
     tokens = plane.shape[1]
 
     def place_of(j, a, sp):
         return (sp[0] ^ a, 0, first + j, 0, 0)
 
     in_specs = [
-        pl.BlockSpec((4, tokens, half), lambda j, a, sp: (0, 0, 1)),
         pl.BlockSpec((4, tokens, half), lambda j, a, sp: (0, 0, 0)),
+        *[pl.BlockSpec((tokens, half), lambda j, a, sp: (0, 0))] * 4,
         pl.BlockSpec(
             (1, 4, quarters, 1, slot_count, lanes),
             lambda j, a, sp: (sp[0] ^ a, 0, 0, j, 0, 0),
@@ -1160,14 +1157,14 @@
         pl.BlockSpec(rank.shape, lambda j, a, sp: (0, 0, 0, 0, 0)),
         pl.BlockSpec(memory_space=pl.ANY),
     ]
-    operands = [place, plane, plane, slots, rank, mark]
+    operands = [place, plane, *early, slots, rank, mark]
     aliases = {}
     if held is not None:
         in_specs += [pl.BlockSpec(memory_space=pl.ANY)] * 2
         aliases = {len(operands): 0, len(operands) + 1: 1}
         operands += list(held[:2])
     return pl.pallas_call(
-        weight_grad_kernel,
+        functools.partial(weight_grad_kernel, first=first, steps=steps),
         out_shape=(
             jax.ShapeDtypeStruct((sides, quarters, each, 2 * half, width), jnp.float32),
             jax.ShapeDtypeStruct((sides, quarters, each, width, half), jnp.float32),
@@ -1290,14 +1287,16 @@
     routes_low = jnp.pad(flat_routes.astype(low), ((0, 0), (0, 128 - top)))
     near_out = jnp.concatenate([own_first(d_out.reshape(tokens, model)), routes_low], axis=1)
 
-    sent, packs[0], out_start = tie((sent, packs[0], core * (q_cols // 2)))
-    out_sent = across(lax.dynamic_slice_in_dim(w_out, out_start, q_cols // 2, 0))
-
     half_dim = HEAD_DIM // 2
     inverse = ROPE_BASE ** (-jnp.arange(half_dim, dtype=wide) * 2.0 / HEAD_DIM)
     angles = jnp.arange(4 * rows, dtype=wide)[:, None] * inverse[None, :]
     cosines = jnp.tile(jnp.cos(angles), (1, 4))
     sines = jnp.tile(jnp.sin(angles), (1, 4))
+    sent, packs[0], out_start, small, cosines, sines, place = tie(
+        (sent, packs[0], core * (q_cols // 2), small, cosines, sines, place)
+    )
+    out_sent = across(lax.dynamic_slice_in_dim(w_out, out_start, q_cols // 2, 0))
+
     normed_one, query, key_value, small_far, gains, turns = single(
         before_kernel,
         "before",
@@ -1318,20 +1317,20 @@
         cosines,
         sines,
     )
-    key_value, packs[0], near_out = tie((key_value, packs[0], near_out))
+    key_value, packs[0], near_out, out_sent = tie((key_value, packs[0], near_out, out_sent))
     blocks = all_ctx(key_value)
     far_out = across(near_out)
     far_zero = across(packs[0])
-    head_low, probs, out_far, *pieces = single(
+    head_low, probs, out_far, attn_part = single(
         attend_kernel,
         "attend",
         [
             ((tokens, q_cols), low),
             ((micro * kv_heads, group * rows, 4 * rows), wide),
             ((q_cols, half), low),
-        ]
-        + piece_shapes,
-        [((tokens, model), wide)],
+            ((tokens, model), low),
+        ],
+        [],
         [place, parents.reshape(micro, 4)],
         query,
         *blocks,
@@ -1339,36 +1338,35 @@
         out_sent,
         beside(out_sent),
     )
-    total = reduce_pieces(pieces)
-    total, far_zero, far_out, packs[1] = tie((total, far_zero, far_out, packs[1]))
+    attn_part, base = tie((attn_part, base))
+    gate_up_mine = split_weights(base, mine, both_view, None).reshape(4, each, 2 * half, width)
+    attended = lax.psum(attn_part, "tp")
+    far_zero, packs[1] = tie((far_zero, packs[1]))
     far_one = across(packs[1])
+    attended, far_out, gate_up_mine = tie((attended, far_out, gate_up_mine))
+    zero_along = along(far_zero)
+    early = jnp.concatenate(
+        [
+            jnp.concatenate([near_out[:, :half], routes_low], axis=1),
+            far_out[:, half:],
+        ],
+        axis=0,
+    )
+    early_along = along(early)
+    early_near = beside(early)
     mixed, near, gates = single(
         after_kernel,
         "after",
         [((tokens, model), wide), ((tokens, model + 128), low), ((tokens, 128), wide)],
-        [((tokens, model), wide)],
+        [],
         [place],
         hidden,
         gains,
         small,
         small_far,
         flat_routes,
-        *spread_pieces(total),
-    )
-    near, packs[2], base = tie((near, packs[2], base))
-    gate_up_mine = split_weights(base, mine, both_view, None).reshape(4, each, 2 * half, width)
-    far = across(near)
-    far, packs[2], far_one, gate_up_mine = tie((far, packs[2], far_one, gate_up_mine))
-    far_two = across(packs[2])
-    far_weights = [lax.all_gather(got, "ctx") for got in (far_zero, far_one)]
-    plane_in = jnp.concatenate(
-        [
-            jnp.concatenate([near_out[:, :half], near[:, :half], routes_low], axis=1),
-            jnp.concatenate([far_out[:, half:model], far[:, half:model], far_out[:, model:]], axis=1),
-        ],
-        axis=0,
-    )
-
+        attended,
+    )
     upper = (
         lax.broadcasted_iota(jnp.int32, (rows, rows), 0)
         < lax.broadcasted_iota(jnp.int32, (rows, rows), 1)
@@ -1387,19 +1385,37 @@
     pair_routes = jnp.concatenate([routes_low, far_out[:, model:]], axis=0)[:, :top]
     rank_pair = ranks(pair_routes, expert_ids[:mine]).reshape(4, each, 4, rows)
 
-    held = None
+    near, packs[2] = tie((near, packs[2]))
+    far = across(near)
+    one_along = along(far_one)
+    far, packs[2], zero_along, gate_up_mine, early_along, early_near, rank_pair = tie(
+        (far, packs[2], zero_along, gate_up_mine, early_along, early_near, rank_pair)
+    )
+    early = [early, early_near, early_along, beside(early_along)]
+    far_two = across(packs[2])
+    plane_in = jnp.concatenate([near[:, :half], far[:, half:model]], axis=0)
+    def all_four(got, distant):
+        return [got, beside(got), distant, beside(distant)]
+
+    def gather_slots(part):
+        return lax.all_gather(part, ("fsdp", "ctx")).reshape(2, 4, *part.shape)
+
+    held = []
     slots = []
     for number, (first, count) in enumerate(chunks):
+        if number == 0:
+            other = all_four(far_zero, zero_along)
         if number == 1:
-            slots[0], far_two, far_weights[1] = tie((slots[0], far_two, far_weights[1]))
-            far_along = along(far_two)
-            far_near = beside(far_two)
-            plane_in, far_weights[1] = tie((plane_in, far_weights[1]))
+            slots[0], far_two, one_along, plane_in = tie(
+                (slots[0], far_two, one_along, plane_in)
+            )
+            two_along = along(far_two)
             plane = lax.all_gather(plane_in, "ctx")
+            other = all_four(far_one, one_along)
         if number == 2:
-            slots[1], far_along, far_near = tie((slots[1], far_along, far_near))
-            far_weights.append([far_two, far_near, far_along, beside(far_along)])
-        held = run_experts(
+            slots[1], two_along = tie((slots[1], two_along))
+            other = all_four(far_two, two_along)
+        made = run_experts(
             place,
             near,
             far,
@@ -1408,21 +1424,37 @@
             rank_pair,
             gate_up_mine,
             down_all,
-            far_weights[number],
+            other,
             held,
             first,
             each,
         )
-        slots.append(held[2])
-    moe_all, back_all, _, moe_far, back_far = held
-
+        slots.append(made[0])
+        held += made[1:]
+    moe_all, back_all, moe_far, back_far = made[1:]
+
+    all_routes = jnp.concatenate([part[:, half : half + top] for part in early], axis=0)
+    rank_all = ranks(all_routes, expert_ids).reshape(2, 4, each, 16, rows)
+
+    back_far, plane, slots[0] = tie((back_far, plane, slots[0]))
     back_got = across(back_far)
-    def gather_slots(part):
-        return lax.all_gather(part, ("fsdp", "ctx")).reshape(2, 4, *part.shape)
-
-    back_got, moe_far, plane, slots[0] = tie((back_got, moe_far, plane, slots[0]))
-    moe_got = across(moe_far)
     pair_zero = gather_slots(slots[0])
+    back_got, moe_far, rank_all = tie((back_got, moe_far, rank_all))
+
+    def grads_of(number, pair, held, mark):
+        first, count = chunks[number]
+        return run_weight_grads(
+            place,
+            plane,
+            early,
+            pair,
+            rank_all,
+            held,
+            each,
+            first,
+            mark,
+        )
+
     pieces = single(
         join_kernel,
         "join",
@@ -1432,8 +1464,12 @@
         back_all,
         back_got,
     )
-    found = spread_pieces(reduce_pieces(pieces))
-    *found, pair_zero, moe_got, slots[1] = tie((*found, pair_zero, moe_got, slots[1]))
+    total = reduce_pieces(pieces)
+    total, moe_far = tie((total, moe_far))
+    moe_got = across(moe_far)
+    found = spread_pieces(total)
+    grads = grads_of(0, pair_zero, None, jnp.zeros((8, 128), wide))
+    *found, moe_got, mark, slots[1] = tie((*found, moe_got, grads[2], slots[1]))
     pair_one = gather_slots(slots[1])
     moe_pieces = single(
         join_kernel, "join", piece_shapes, [((tokens, model), wide)], [place], moe_all, moe_got
@@ -1480,10 +1516,10 @@
     near_pair = beside(given)
     moe_found = spread_pieces(moe_total)
     distant = along((kept[1] + near_pair[1].astype(wide)).astype(low))
-    qkv_grad, gain_one_part, *pieces = single(
+    qkv_grad, *pieces = single(
         last_kernel,
         "last",
-        [((tokens, qkv_cols), low), ((8, model), wide)] + piece_shapes,
+        [((tokens, qkv_cols), low)] + piece_shapes,
         [((tokens, model), wide)],
         [place],
         query_grad,
@@ -1493,24 +1529,7 @@
         turns,
         small,
         small_far,
-        hidden,
-    )
-
-    all_routes = plane[:, :, model : model + top].reshape(8 * tokens, top)
-    rank_all = ranks(all_routes, expert_ids).reshape(2, 4, each, 16, rows)
-
-    def grads_of(number, pair, held, mark):
-        first, count = chunks[number]
-        return run_weight_grads(
-            place,
-            plane,
-            pair,
-            rank_all[:, :, first : first + count],
-            held,
-            each,
-            first,
-            mark,
-        )
+    )
 
     def hop_beside(value):
         share = value.shape[1] // 2
@@ -1546,10 +1565,10 @@
             axis=1,
         )
     )
-    mark = jnp.zeros((8, 128), wide)
-    tied = tie((*pieces, *moe_found, mark, side, qkv_grad, gain_one_part[0]))
+    tied = tie((*pieces, *moe_found, mark, side, qkv_grad, pair_one, slots[2]))
     pieces, moe_found = tied[:tp_size], tied[tp_size : 2 * tp_size]
-    mark, side, qkv_grad, gain_one = tied[2 * tp_size :]
+    mark, side, qkv_grad, pair_one, slots[2] = tied[2 * tp_size :]
+    pair_two = gather_slots(slots[2])
     (layer_out,) = single(
         output_kernel,
         "output",
@@ -1560,31 +1579,28 @@
         *moe_found,
     )
     total = reduce_pieces(pieces)
-    grads = grads_of(0, pair_zero, None, mark)
+    grads = grads_of(1, pair_one, grads, mark)
     side = hop_across(side)
     d_qkv = hop_beside(dot(normed_one, qkv_grad, 0, 0).reshape(2, half, qkv_cols))
-    total, mark, side, d_qkv, pair_one, slots[2] = tie(
-        (total, grads[2], side, d_qkv, pair_one, slots[2])
-    )
-    pair_two = gather_slots(slots[2])
+    total, mark, side, d_qkv = tie((total, grads[2], side, d_qkv))
     found = spread_pieces(total)
-    grads = grads_of(1, pair_one, grads, mark)
+    grads = grads_of(2, pair_two, grads, mark)
     side = hop_along(side)
     d_qkv = hop_across(d_qkv)
-    gain_one = sum([from_tp(gain_one, step) for step in range(1, tp_size)], gain_one)
-    *found, mark, side, d_qkv, gain_one = tie((*found, grads[2], side, d_qkv, gain_one))
-    (d_hidden,) = single(
+    *found, mark, side, d_qkv = tie((*found, grads[2], side, d_qkv))
+    d_hidden, gain_one = single(
         hidden_kernel,
         "hidden",
-        [((tokens, model), wide)],
+        [((tokens, model), wide), ((8, model), wide)],
         [((tokens, model), wide)],
         [place],
         hidden,
         gains,
         mixed_grad,
+        mark,
         *found,
     )
-    grads = grads_of(2, pair_two, grads, mark)
+    gain_one = gain_one[0]
     d_gate_up = grads[0].reshape(experts, half, 2, width)
     d_down = grads[1].reshape(experts, width, half)
     side_grads = hop_join(side)

time: 455 us -> 427 us (0.938)
  waiting for transfers between devices: 148 us -> 133 us
  Pallas kernels: 167 us -> 161 us
    ppermute x27 -> x18, waiting for transfers between devices: 70.7 us -> 18.6 us  [from_tp(): lax.ppermute(value, 'tp', [((i + step) % tp_size, i) for i in range(tp_si...]
    ppermute x12, waiting for transfers between devices: 46.3 us -> 69.2 us  [across(): return lax.ppermute(value, 'fsdp', [(0, 1), (1, 0)])]
    ppermute x6 -> x9, waiting for transfers between devices: 5.08 us -> 22.9 us  [along(): return lax.ppermute(value, 'ctx', [(i, i ^ 2) for i in range(4)])]
    all_gather x2 -> x0, waiting for transfers between devices: 14.4 us -> none  [fast_body(): far_weights = [lax.all_gather(got, 'ctx') for got in (far_zero, far_one)]]
    psum x0 -> x1, waiting for transfers between devices: none -> 12.9 us  [fast_body(): attended = lax.psum(attn_part, 'tp')]
    ppermute x27 -> x18, starting transfers between devices: 38.2 us -> 28.7 us  [from_tp(): lax.ppermute(value, 'tp', [((i + step) % tp_size, i) for i in range(tp_si...]
    all_gather x3, waiting for transfers between devices: 6.95 us -> 0.04 us  [gather_slots(): return lax.all_gather(part, ('fsdp', 'ctx')).reshape(2, 4, *part.shape)]
    ppermute x6 -> x9, starting transfers between devices: 7.07 us -> 13.2 us  [along(): return lax.ppermute(value, 'ctx', [(i, i ^ 2) for i in range(4)])]
  transfers between devices with their start and end apart: 63 -> 62, of which waited for: 26 -> 25; matrix products, arithmetic and copies ran while one was open for 9% -> 9% of each run, Pallas kernels for 34% -> 38%
where the time goes in v5:
time: 427 us; the launch traced here: 421 us
  Pallas kernels  161 us (38%)
  waiting for transfers between devices  133 us (31%)
  starting transfers between devices  61.6 us (14%)
  local copies, waits for them, and re-layouts  26.1 us (6%)
  other arithmetic  16.7 us (4%)
  between operations  15.3 us (4%)
  matrix products  7.7 us (2%)
    ppermute x12, waiting for transfers between devices, across(): return lax.ppermute(value, 'fsdp', [(0, 1), (1, 0)])  69.2 us
    pallas_call x3, Pallas kernels, run_weight_grads(): pl.pallas_call(functools.partial(weight_grad_kernel, first=first, steps=s...  53.5 us
    pallas_call x3, Pallas kernels, run_experts(): pl.pallas_call(functools.partial(expert_kernel, first=first, last=last, e...  44.9 us
    pallas_call x9, Pallas kernels, single(): pl.pallas_call(kernel, out_shape=tuple((jax.ShapeDtypeStruct(shape, kind)...  41.9 us
    ppermute x18, starting transfers between devices, from_tp(): lax.ppermute(value, 'tp', [((i + step) % tp_size, i) for i in range(tp_si...  28.7 us
    ppermute x9, waiting for transfers between devices, along(): return lax.ppermute(value, 'ctx', [(i, i ^ 2) for i in range(4)])  22.9 us
    pallas_call x4, Pallas kernels, split_weights(): pl.pallas_call(split_plain_kernel if down is None else split_kernel, out_...  20.5 us
    ppermute x18, waiting for transfers between devices, from_tp(): lax.ppermute(value, 'tp', [((i + step) % tp_size, i) for i in range(tp_si...  18.6 us
  transfers between devices with their start and end apart: 62, of which 25 were waited for; matrix products, arithmetic and copies ran while one was open for 9% of the time, Pallas kernels for 38%

profile of v5, /device:TPU:0, one launch (start us, length us, event | category | flops | bytes accessed | tf_op | source)
XLA Modules:
  0.0 420.9 jit_solution(16239249941446788210)
XLA Ops:
  10.8 3.0 collective-permute-start
  13.9 2.3 split_weights.4
  18.4 9.3 %collective-permute-done.sent_ref = bf16[400,768]{1,0:T(8,128)(2,1)S(1)} collective-permute-done((bf16[400,768]{1,0:T(8,128)(2,1)S(1)}, bf16[400,768]{1,0:T(8,128)(2,1)S(1)}, u32[]{:S(2)}, u32[]{:S(2)}) %collective-permute-start) | collective-permute-done | bytes 614432 | tf_op jit(solution)/shard_map/ppermute | solution.py:1233
  29.1 1.7 collective-permute-start.2
  34.2 4.5 %before.1 = (bf16[256,1536]{1,0:T(8,128)(2,1)}, bf16[256,384]{1,0:T(8,128)(2,1)}, bf16[256,256]{1,0:T(8,128)(2,1)}, bf16[768,768]{1,0:T(8,128)(2,1)}, f32[16,1536]{1,0:T(8,128)}, /*index=5*/f32[2,256,128]{2,1,0:T(8,128)}) custom-call(s32[3]{0:T(128)} %pad_add_fusion.place_ref, s32[2,4]{1,0:T(2,128)} %bitcast.199, bf16[256,1536]{1,0:T(8,128)(2,1)} %bitcast.158, ...), custom_call_target="tpu_custom_call" | custom-call | tf_op jit(solution)/shard_map/before/pallas_call | solution.py:427
  38.8 1.7 collective-permute-start.9
  40.5 1.5 collective-permute-start.4
  42.3 4.4 %collective-permute-done.4.kv2 = bf16[256,256]{1,0:T(8,128)(2,1)S(1)} collective-permute-done((bf16[256,256]{1,0:T(8,128)(2,1)}, bf16[256,256]{1,0:T(8,128)(2,1)S(1)}, u32[]{:S(2)}, u32[]{:S(2)}) %collective-permute-start.4) | collective-permute-done | bytes 131104 | tf_op jit(solution)/shard_map/ppermute | solution.py:1239
  48.6 5.8 %attend.1 = (bf16[256,384]{1,0:T(8,128)(2,1)}, f32[4,384,512]{2,1,0:T(8,128)}, bf16[384,768]{1,0:T(8,128)(2,1)}, bf16[256,1536]{1,0:T(8,128)(2,1)}) custom-call(s32[3]{0:T(128)} %pad_add_fusion.place_ref, s32[2,4]{1,0:T(2,128)} %bitcast.200, bf16[256,384]{1,0:T(8,128)(2,1)} %get-tuple-element.147.query_ref, bf16[256,256]{1,0:T(8,128)(2,1)} %get-tuple-element.151.kv0, ...), custom_call_target="tpu_custom_call" | custom-call | tf_op jit(solution)/shard_map/attend/pallas_call | solution.py:427
  54.7 2.2 split_weights.7
  56.9 10.8 %collective-permute-done.9.rest_0_ = bf16[2,2304,128]{2,1,0:T(8,128)(2,1)} collective-permute-done((bf16[2,2304,128]{2,1,0:T(8,128)(2,1)S(1)}, bf16[2,2304,128]{2,1,0:T(8,128)(2,1)}, u32[]{:S(2)}, u32[]{:S(2)}) %collective-permute-start.9) | collective-permute-done | bytes 1179680 | tf_op jit(solution)/shard_map/ppermute | solution.py:1233
  67.7 1.8 collective-permute-start.10
  69.5 1.5 collective-permute-start.16
  71.1 14.0 %split_weights.5 = bf16[20,1536,128]{2,1,0:T(8,128)(2,1)} custom-call(s32[1]{0:T(128)} %bitcast.11.base_ref, bf16[40,1536,128]{2,1,0:T(8,128)(2,1)} %bitcast.146), custom_call_target="tpu_custom_call" | custom-call | tf_op jit(solution)/shard_map/split_weights/pallas_call | solution.py:494
  85.9 12.9 %all-reduce.5.cloned.1.call-done.attended_ref = bf16[256,1536]{1,0:T(8,128)(2,1)} async-done(((bf16[256,1536]{1,0:T(8,128)(2,1)}), bf16[256,1536]{1,0:T(8,128)(2,1)}) %all-reduce.5.cloned.1.call-update) | async-done | bytes 786448 | tf_op jit(solution)/shard_map/psum | solution.py:1343
  98.9 1.5 collective-permute-start.11
  100.4 2.0 split_weights.6
  102.4 4.3 %after.1 = (f32[256,1536]{1,0:T(8,128)}, bf16[256,1664]{1,0:T(8,128)(2,1)}, f32[256,128]{1,0:T(8,128)}) custom-call(s32[3]{0:T(128)} %pad_add_fusion.place_ref, bf16[256,1536]{1,0:T(8,128)(2,1)} %bitcast.159, f32[16,1536]{1,0:T(8,128)} %get-tuple-element.145.gains_ref, bf16[784,768]{1,0:T(8,128)(2,1)} %pad_maximum_fusion.small_ref, ...), custom_call_target="tpu_custom_call" | custom-call | tf_op jit(solution)/shard_map/after/pallas_call | solution.py:427
  106.7 1.5 collective-permute-start.8
  111.8 16.8 %collective-permute-done.8.far_ref = bf16[256,1664]{1,0:T(8,128)(2,1)S(1)} collective-permute-done((bf16[256,1664]{1,0:T(8,128)(2,1)}, bf16[256,1664]{1,0:T(8,128)(2,1)S(1)}, u32[]{:S(2)}, u32[]{:S(2)}) %collective-permute-start.8) | collective-permute-done | bytes 852000 | tf_op jit(solution)/shard_map/ppermute | solution.py:1233
  129.3 1.5 collective-permute-start.17
  134.0 15.7 %experts.3 = (bf16[4,2,128,384]{3,2,1,0:T(8,128)(2,1)}, bf16[512,1536]{1,0:T(8,128)(2,1)}, bf16[512,1664]{1,0:T(8,128)(2,1)}) custom-call(s32[3]{0:T(128)} %pad_add_fusion.place_ref, bf16[256,1664]{1,0:T(8,128)(2,1)} %get-tuple-element.164.near_ref, bf16[256,1664]{1,0:T(8,128)(2,1)} %copy-done.4, bf16[256,1664]{1,0:T(8,128)(2,1)} %copy-done, ...), custom_call_target="tpu_custom_call" | custom-call | tf_op jit(solution)/shard_map/experts/pallas_call | solution.py:881
  149.8 7.8 %collective-permute-done.17.rest_2_ = bf16[2,2304,128]{2,1,0:T(8,128)(2,1)} collective-permute-done((bf16[2,2304,128]{2,1,0:T(8,128)(2,1)}, bf16[2,2304,128]{2,1,0:T(8,128)(2,1)}, u32[]{:S(2)}, u32[]{:S(2)}) %collective-permute-start.17) | collective-permute-done | bytes 1179680 | tf_op jit(solution)/shard_map/ppermute | solution.py:1239
  158.6 1.5 collective-permute-start.21
  160.2 1.9 collective-permute-done.19.rest_1_
  163.1 16.5 %experts.4 = (bf16[4,2,128,384]{3,2,1,0:T(8,128)(2,1)}, bf16[512,1536]{1,0:T(8,128)(2,1)}, bf16[512,1664]{1,0:T(8,128)(2,1)}) custom-call(s32[3]{0:T(128)} %pad_add_fusion.place_ref, bf16[256,1664]{1,0:T(8,128)(2,1)} %get-tuple-element.164.near_ref, bf16[256,1664]{1,0:T(8,128)(2,1)} %copy-done.4, bf16[256,1664]{1,0:T(8,128)(2,1)} %copy-done, ...), custom_call_target="tpu_custom_call" | custom-call | tf_op jit(solution)/shard_map/experts/pallas_call | solution.py:881
  180.6 2.2 collective-permute-done.22.rest_3_
  183.6 12.7 %experts.5 = (bf16[4,1,128,384]{3,2,1,0:T(8,128)(2,1)}, f32[256,1536]{1,0:T(8,128)}, f32[256,1664]{1,0:T(8,128)}, bf16[256,1536]{1,0:T(8,128)(2,1)}, bf16[256,1664]{1,0:T(8,128)(2,1)}) custom-call(s32[3]{0:T(128)} %pad_add_fusion.place_ref, bf16[256,1664]{1,0:T(8,128)(2,1)} %get-tuple-element.164.near_ref, bf16[256,1664]{1,0:T(8,128)(2,1)} %copy-done.4, ...), custom_call_target="tpu_custom_call" | custom-call | tf_op jit(solution)/shard_map/experts/pallas_call | solution.py:881
  200.3 26.2 %collective-permute-done.23.got_ref = bf16[256,1664]{1,0:T(8,128)(2,1)} collective-permute-done((bf16[256,1664]{1,0:T(8,128)(2,1)}, bf16[256,1664]{1,0:T(8,128)(2,1)}, u32[]{:S(2)}, u32[]{:S(2)}) %collective-permute-start.23) | collective-permute-done | bytes 852000 | tf_op jit(solution)/shard_map/ppermute | solution.py:1233
  226.5 2.9 join.2
  229.4 1.5 collective-permute-start.27
  230.9 2.7 collective-permute-start.26
  234.8 4.8 %collective-permute-done.27 = bf16[64,1664]{1,0:T(8,128)(2,1)S(1)} collective-permute-done((bf16[64,1664]{1,0:T(8,128)(2,1)}, bf16[64,1664]{1,0:T(8,128)(2,1)S(1)}, u32[]{:S(2)}, u32[]{:S(2)}) %collective-permute-start.27) | collective-permute-done | bytes 213024 | tf_op jit(solution)/shard_map/ppermute | solution.py:1242
  239.6 7.8 %collective-permute-done.26 = bf16[64,1664]{1,0:T(8,128)(2,1)S(1)} collective-permute-done((bf16[64,1664]{1,0:T(8,128)(2,1)}, bf16[64,1664]{1,0:T(8,128)(2,1)S(1)}, u32[]{:S(2)}, u32[]{:S(2)}) %collective-permute-start.26) | collective-permute-done | bytes 213024 | tf_op jit(solution)/shard_map/ppermute | solution.py:1242
  249.7 5.8 %collective-permute-start.28 = (bf16[64,1664]{1,0:T(8,128)(2,1)S(1)}, bf16[64,1664]{1,0:T(8,128)(2,1)S(1)}, u32[]{:S(2)}, u32[]{:S(2)}) collective-permute-start(bf16[64,1664]{1,0:T(8,128)(2,1)S(1)} %add_convert_fusion.2.rest_0_), channel_id=1, source_target_pairs={{1,0},{2,1},{3,2},{0,3},{5,4},{6,5},{7,6},{4,7},{9,8},{10,9},{11,1... | collective-permute-start | bytes 638984 | tf_op jit(solution)/shard_map/ppermute | solution.py:1242
  257.0 20.5 %weight_grads.3 = (f32[2,4,5,1536,128]{4,3,2,1,0:T(8,128)}, f32[2,4,5,128,768]{4,3,2,1,0:T(8,128)}, f32[8,128]{1,0:T(8,128)}) custom-call(s32[3]{0:T(128)} %pad_add_fusion.place_ref, bf16[4,512,768]{2,1,0:T(8,128)(2,1)} %bitcast.153, bf16[512,896]{1,0:T(8,128)(2,1)} %copy-done.2, bf16[512,896]{1,0:T(8,128)(2,1)} %collective-permute-done.12.grads1, ...), custom_call_target="tpu_custom_call" | custom-call | tf_op jit(solution)/shard_map/weight_grads/pallas_call | solution.py:1166
  278.5 2.8 join.3
  281.3 2.8 collective-permute-start.34
  284.1 1.6 collective-permute-start.33
  286.7 10.4 %back.1 = (f32[256,1536]{1,0:T(8,128)}, bf16[256,1536]{1,0:T(8,128)(2,1)}, bf16[256,128]{1,0:T(8,128)(2,1)}, f32[8,1536]{1,0:T(8,128)}, bf16[256,384]{1,0:T(8,12...) custom-call(s32[3]{0:T(128)} %pad_add_fusion.place_ref, f32[256,1536]{1,0:T(8,128)} %get-tuple-element.158.mixed_ref, ...), custom_call_target="tpu_custom_call" | custom-call | tf_op jit(solution)/shard_map/back/pallas_call | solution.py:427
  299.3 1.4 convolution_bitcast_fusion
  304.6 1.5 collective-permute-done.35.near_ref
  306.9 2.5 collective-permute-start.36
  309.4 2.2 collective-permute-start.37
  312.3 4.3 %collective-permute-done.36.along_ref = bf16[256,256]{1,0:T(8,128)(2,1)S(1)} collective-permute-done((bf16[256,256]{1,0:T(8,128)(2,1)}, bf16[256,256]{1,0:T(8,128)(2,1)S(1)}, u32[]{:S(2)}, u32[]{:S(2)}) %collective-permute-start.36) | collective-permute-done | bytes 131104 | tf_op jit(solution)/shard_map/ppermute | solution.py:1239
  317.2 3.9 last.1
  321.2 2.3 convert_add_fusion.1
  323.5 6.0 %collective-permute-done.38.rest_2_ = bf16[64,1536]{1,0:T(8,128)(2,1)S(1)} collective-permute-done((bf16[64,1536]{1,0:T(8,128)(2,1)S(1)}, bf16[64,1536]{1,0:T(8,128)(2,1)S(1)}, u32[]{:S(2)}, u32[]{:S(2)}) %collective-permute-start.38) | collective-permute-done | bytes 196640 | tf_op jit(solution)/shard_map/ppermute | solution.py:1242
  330.2 1.6 collective-permute-start.42
  331.9 2.7 collective-permute-start.41
  334.5 2.0 fusion.32
  337.6 1.9 fusion.11
  340.7 20.5 %weight_grads.4 = (f32[2,4,5,1536,128]{4,3,2,1,0:T(8,128)}, f32[2,4,5,128,768]{4,3,2,1,0:T(8,128)}, f32[8,128]{1,0:T(8,128)}) custom-call(s32[3]{0:T(128)} %pad_add_fusion.place_ref, bf16[4,512,768]{2,1,0:T(8,128)(2,1)} %bitcast.154, bf16[512,896]{1,0:T(8,128)(2,1)} %copy-done.2, ...), custom_call_target="tpu_custom_call", output_to_operand_aliasing={{0}: (9, {}), {1}: (10, {})} | custom-call | tf_op jit(solution)/shard_map/weight_grads/pallas_call | solution.py:1166
  363.2 1.4 bitcast_add_fusion.1
  364.6 1.4 convert_add_fusion
  369.2 2.3 collective-permute-start.48
  371.5 4.8 %collective-permute-done.49 = bf16[224,768]{1,0:T(8,128)(2,1)S(1)} collective-permute-done((bf16[224,768]{1,0:T(8,128)(2,1)S(1)}, bf16[224,768]{1,0:T(8,128)(2,1)S(1)}, u32[]{:S(2)}, u32[]{:S(2)}) %collective-permute-start.49) | collective-permute-done | bytes 344096 | tf_op jit(solution)/shard_map/ppermute | solution.py:1239
  376.4 3.3 collective-permute-done.50
  379.8 12.5 %weight_grads.5 = (f32[2,4,5,1536,128]{4,3,2,1,0:T(8,128)}, f32[2,4,5,128,768]{4,3,2,1,0:T(8,128)}, f32[8,128]{1,0:T(8,128)}) custom-call(s32[3]{0:T(128)} %pad_add_fusion.place_ref, bf16[4,512,768]{2,1,0:T(8,128)(2,1)} %bitcast.155, bf16[512,896]{1,0:T(8,128)(2,1)} %copy-done.2, ...), custom_call_target="tpu_custom_call", output_to_operand_aliasing={{0}: (9, {}), {1}: (10, {})} | custom-call | tf_op jit(solution)/shard_map/weight_grads/pallas_call | solution.py:1166
  392.5 1.7 collective-permute-start.54
  394.2 4.1 hidden.1
  400.9 3.3 output.1
  404.9 1.5 collective-permute-start.53
  406.6 1.9 collective-permute-done.53
  (279 shorter events, 61.5 us)
Async XLA Ops:
  7.2 91.6 %all-reduce.5.cloned.1.call-start = ((), (), s32[]{:S(2)}) async-start(), calls=%async_computation | async-start | bytes 1572864 | tf_op jit(solution)/shard_map/psum | solution.py:1343
  10.8 16.9 %collective-permute-start = (bf16[400,768]{1,0:T(8,128)(2,1)S(1)}, bf16[400,768]{1,0:T(8,128)(2,1)S(1)}, u32[]{:S(2)}, u32[]{:S(2)}) collective-permute-start(bf16[400,768]{1,0:T(8,128)(2,1)S(1)} %pad_maximum_fusion.4), channel_id=1, source_target_pairs={{0,16},{16,0},{1,17},{17,1},{2,18},{18,2},{3,19},{19,3},{4,20},{20... | collective-permute-start | bytes 1843208 | tf_op jit(solution)/shard_map/ppermute | solution.py:1233
  27.8 5.6 %collective-permute-start.1 = (bf16[400,768]{1,0:T(8,128)(2,1)S(1)}, bf16[400,768]{1,0:T(8,128)(2,1)S(1)}, u32[]{:S(2)}, u32[]{:S(2)}) collective-permute-start(bf16[400,768]{1,0:T(8,128)(2,1)S(1)} %collective-permute-done.sent_ref), channel_id=1, source_target_pairs={{0,4},{4,0},{8,12},{12,8},{1,5},{5,1},{9,13},{13,9},{2,6},{6,2},{1... | collective-permute-start | bytes 1843208 | tf_op jit(solution)/shard_map/ppermute | solution.py:1236
  29.1 9.7 %collective-permute-start.2 = (bf16[192,768]{1,0:T(8,128)(2,1)}, bf16[192,768]{1,0:T(8,128)(2,1)}, u32[]{:S(2)}, u32[]{:S(2)}) collective-permute-start(bf16[192,768]{1,0:T(8,128)(2,1)} %constant_dynamic-slice_fusion), channel_id=1, source_target_pairs={{0,16},{16,0},{1,17},{17,1},{2,18},{18,2},{3,19},{19,3},{4,20},{20... | collective-permute-start | bytes 884744 | tf_op jit(solution)/shard_map/ppermute | solution.py:1233
  38.8 28.9 %collective-permute-start.9 = (bf16[2,2304,128]{2,1,0:T(8,128)(2,1)S(1)}, bf16[2,2304,128]{2,1,0:T(8,128)(2,1)}, u32[]{:S(2)}, u32[]{:S(2)}) collective-permute-start(bf16[2,2304,128]{2,1,0:T(8,128)(2,1)S(1)} %copy-done.13), channel_id=1, source_target_pairs={{0,16},{16,0},{1,17},{17,1},{2,18},{18,2},{3,19},{19,3},{4,20},{20... | collective-permute-start | bytes 3538952 | tf_op jit(solution)/shard_map/ppermute | solution.py:1233
  40.5 7.5 %collective-permute-start.6 = (bf16[192,768]{1,0:T(8,128)(2,1)}, bf16[192,768]{1,0:T(8,128)(2,1)}, u32[]{:S(2)}, u32[]{:S(2)}) collective-permute-start(bf16[192,768]{1,0:T(8,128)(2,1)} %collective-permute-done.2.out_sent_ref), channel_id=1, source_target_pairs={{0,4},{4,0},{8,12},{12,8},{1,5},{5,1},{9,13},{13,9},{2,6},{6,2},{1... | collective-permute-start | bytes 884744 | tf_op jit(solution)/shard_map/ppermute | solution.py:1236
  40.5 6.1 %collective-permute-start.4 = (bf16[256,256]{1,0:T(8,128)(2,1)}, bf16[256,256]{1,0:T(8,128)(2,1)S(1)}, u32[]{:S(2)}, u32[]{:S(2)}) collective-permute-start(bf16[256,256]{1,0:T(8,128)(2,1)} %get-tuple-element.151.kv0), channel_id=1, source_target_pairs={{0,8},{4,12},{8,0},{12,4},{1,9},{5,13},{9,1},{13,5},{2,10},{6,14},... | collective-permute-start | bytes 393224 | tf_op jit(solution)/shard_map/ppermute | solution.py:1239
  42.0 4.9 %collective-permute-start.3 = (bf16[256,256]{1,0:T(8,128)(2,1)}, bf16[256,256]{1,0:T(8,128)(2,1)S(1)}, u32[]{:S(2)}, u32[]{:S(2)}) collective-permute-start(bf16[256,256]{1,0:T(8,128)(2,1)} %get-tuple-element.151.kv0), channel_id=1, source_target_pairs={{0,4},{4,0},{8,12},{12,8},{1,5},{5,1},{9,13},{13,9},{2,6},{6,2},{1... | collective-permute-start | bytes 393224 | tf_op jit(solution)/shard_map/ppermute | solution.py:1236
  46.6 1.3 collective-permute-start.5
  46.7 39.2 %collective-permute-start.7 = (bf16[256,1664]{1,0:T(8,128)(2,1)S(1)}, bf16[256,1664]{1,0:T(8,128)(2,1)S(1)}, u32[]{:S(2)}, u32[]{:S(2)}) collective-permute-start(bf16[256,1664]{1,0:T(8,128)(2,1)S(1)} %pad_maximum_fusion.2.near_out_ref.out_grad_ref), channel_id=1, source_target_pairs={{0,16},{16,0},{1,17},{17,1},{2,18},{18,2},{3,19},{19,3},{4,20},{20... | collective-permute-start | bytes 2555912 | tf_op jit(solution)/shard_map/ppermute | solution.py:1233
  54.5 141.8 %all-gather.9.cloned.1.call-start = ((), (), s32[]{:S(2)}) async-start(), calls=%async_computation.1 | async-start | bytes 3932160 | tf_op jit(solution)/shard_map/all_gather | solution.py:1413
  67.7 61.0 %collective-permute-start.10 = (bf16[2,2304,128]{2,1,0:T(8,128)(2,1)}, bf16[2,2304,128]{2,1,0:T(8,128)(2,1)}, u32[]{:S(2)}, u32[]{:S(2)}) collective-permute-start(bf16[2,2304,128]{2,1,0:T(8,128)(2,1)} %collective-permute-done.9.rest_0_), channel_id=1, source_target_pairs={{0,8},{4,12},{8,0},{12,4},{1,9},{5,13},{9,1},{13,5},{2,10},{6,14},... | collective-permute-start | bytes 3538952 | tf_op jit(solution)/shard_map/ppermute | solution.py:1239
  69.5 59.8 %collective-permute-start.16 = (bf16[2,2304,128]{2,1,0:T(8,128)(2,1)}, bf16[2,2304,128]{2,1,0:T(8,128)(2,1)}, u32[]{:S(2)}, u32[]{:S(2)}) collective-permute-start(bf16[2,2304,128]{2,1,0:T(8,128)(2,1)} %split_weights.7), channel_id=1, source_target_pairs={{0,16},{16,0},{1,17},{17,1},{2,18},{18,2},{3,19},{19,3},{4,20},{20... | collective-permute-start | bytes 3538952 | tf_op jit(solution)/shard_map/ppermute | solution.py:1233
  98.9 98.5 %copy-start.2 = (bf16[512,896]{1,0:T(8,128)(2,1)}, bf16[512,896]{1,0:T(8,128)(2,1)S(1)}, u32[]{:S(2)}) copy-start(bf16[512,896]{1,0:T(8,128)(2,1)S(1)} %pad_maximum_fusion.1.grads0) | copy-start | bytes 2752516
  98.9 29.8 %collective-permute-start.11 = (bf16[512,896]{1,0:T(8,128)(2,1)S(1)}, bf16[512,896]{1,0:T(8,128)(2,1)S(1)}, u32[]{:S(2)}, u32[]{:S(2)}) collective-permute-start(bf16[512,896]{1,0:T(8,128)(2,1)S(1)} %pad_maximum_fusion.1.grads0), channel_id=1, source_target_pairs={{0,8},{4,12},{8,0},{12,4},{1,9},{5,13},{9,1},{13,5},{2,10},{6,14},... | collective-permute-start | bytes 2752520 | tf_op jit(solution)/shard_map/ppermute | solution.py:1239
  100.4 28.3 %collective-permute-start.12 = (bf16[512,896]{1,0:T(8,128)(2,1)S(1)}, bf16[512,896]{1,0:T(8,128)(2,1)}, u32[]{:S(2)}, u32[]{:S(2)}) collective-permute-start(bf16[512,896]{1,0:T(8,128)(2,1)S(1)} %pad_maximum_fusion.1.grads0), channel_id=1, source_target_pairs={{0,4},{4,0},{8,12},{12,8},{1,5},{5,1},{9,13},{13,9},{2,6},{6,2},{1... | collective-permute-start | bytes 2752520 | tf_op jit(solution)/shard_map/ppermute | solution.py:1236
  106.7 22.0 %collective-permute-start.8 = (bf16[256,1664]{1,0:T(8,128)(2,1)}, bf16[256,1664]{1,0:T(8,128)(2,1)S(1)}, u32[]{:S(2)}, u32[]{:S(2)}) collective-permute-start(bf16[256,1664]{1,0:T(8,128)(2,1)} %get-tuple-element.164.near_ref), channel_id=1, source_target_pairs={{0,16},{16,0},{1,17},{17,1},{2,18},{18,2},{3,19},{19,3},{4,20},{20... | collective-permute-start | bytes 2555912 | tf_op jit(solution)/shard_map/ppermute | solution.py:1233
  128.7 5.4 %collective-permute-start.13 = (bf16[2,2304,128]{2,1,0:T(8,128)(2,1)}, bf16[2,2304,128]{2,1,0:T(8,128)(2,1)}, u32[]{:S(2)}, u32[]{:S(2)}) collective-permute-start(bf16[2,2304,128]{2,1,0:T(8,128)(2,1)} %collective-permute-done.9.rest_0_), channel_id=1, source_target_pairs={{0,4},{4,0},{8,12},{12,8},{1,5},{5,1},{9,13},{13,9},{2,6},{6,2},{1... | collective-permute-start | bytes 3538952 | tf_op jit(solution)/shard_map/ppermute | solution.py:1236
  128.7 68.8 %copy-start.5 = (bf16[512,896]{1,0:T(8,128)(2,1)}, bf16[512,896]{1,0:T(8,128)(2,1)S(1)}, u32[]{:S(2)}) copy-start(bf16[512,896]{1,0:T(8,128)(2,1)S(1)} %collective-permute-done.11.grads2) | copy-start | bytes 2752516
  128.7 5.3 %collective-permute-start.14 = (bf16[2,2304,128]{2,1,0:T(8,128)(2,1)}, bf16[2,2304,128]{2,1,0:T(8,128)(2,1)}, u32[]{:S(2)}, u32[]{:S(2)}) collective-permute-start(bf16[2,2304,128]{2,1,0:T(8,128)(2,1)} %collective-permute-done.10.rest_2_), channel_id=1, source_target_pairs={{0,4},{4,0},{8,12},{12,8},{1,5},{5,1},{9,13},{13,9},{2,6},{6,2},{1... | collective-permute-start | bytes 3538952 | tf_op jit(solution)/shard_map/ppermute | solution.py:1236
  129.3 28.3 %collective-permute-start.17 = (bf16[2,2304,128]{2,1,0:T(8,128)(2,1)}, bf16[2,2304,128]{2,1,0:T(8,128)(2,1)}, u32[]{:S(2)}, u32[]{:S(2)}) collective-permute-start(bf16[2,2304,128]{2,1,0:T(8,128)(2,1)} %collective-permute-done.16.rest_0_), channel_id=1, source_target_pairs={{0,8},{4,12},{8,0},{12,4},{1,9},{5,13},{9,1},{13,5},{2,10},{6,14},... | collective-permute-start | bytes 3538952 | tf_op jit(solution)/shard_map/ppermute | solution.py:1239
  130.8 19.0 %collective-permute-start.15 = (bf16[1,2304,128]{2,1,0:T(8,128)(2,1)}, bf16[1,2304,128]{2,1,0:T(8,128)(2,1)S(1)}, u32[]{:S(2)}, u32[]{:S(2)}) collective-permute-start(bf16[1,2304,128]{2,1,0:T(8,128)(2,1)} %split_weights.6), channel_id=1, source_target_pairs={{0,16},{16,0},{1,17},{17,1},{2,18},{18,2},{3,19},{19,3},{4,20},{20... | collective-permute-start | bytes 1769480 | tf_op jit(solution)/shard_map/ppermute | solution.py:1233
  157.6 98.8 %all-gather.11.cloned.1.call-start = ((), (), s32[]{:S(2)}) async-start(), calls=%async_computation.2 | async-start | bytes 7077888 | tf_op jit(solution)/shard_map/all_gather | solution.py:1401
  158.1 4.0 collective-permute-start.19
  158.1 4.9 %collective-permute-start.20 = (bf16[2,2304,128]{2,1,0:T(8,128)(2,1)}, bf16[2,2304,128]{2,1,0:T(8,128)(2,1)}, u32[]{:S(2)}, u32[]{:S(2)}) collective-permute-start(bf16[2,2304,128]{2,1,0:T(8,128)(2,1)} %collective-permute-done.17.rest_2_), channel_id=1, source_target_pairs={{0,4},{4,0},{8,12},{12,8},{1,5},{5,1},{9,13},{13,9},{2,6},{6,2},{1... | collective-permute-start | bytes 3538952 | tf_op jit(solution)/shard_map/ppermute | solution.py:1236
  158.6 21.9 %collective-permute-start.21 = (bf16[1,2304,128]{2,1,0:T(8,128)(2,1)}, bf16[1,2304,128]{2,1,0:T(8,128)(2,1)}, u32[]{:S(2)}, u32[]{:S(2)}) collective-permute-start(bf16[1,2304,128]{2,1,0:T(8,128)(2,1)} %copy-done.26), channel_id=1, source_target_pairs={{0,8},{4,12},{8,0},{12,4},{1,9},{5,13},{9,1},{13,5},{2,10},{6,14},... | collective-permute-start | bytes 1769480 | tf_op jit(solution)/shard_map/ppermute | solution.py:1239
  160.1 20.4 %collective-permute-start.18 = (bf16[1,2304,128]{2,1,0:T(8,128)(2,1)}, bf16[1,2304,128]{2,1,0:T(8,128)(2,1)}, u32[]{:S(2)}, u32[]{:S(2)}) collective-permute-start(bf16[1,2304,128]{2,1,0:T(8,128)(2,1)} %copy-done.26), channel_id=1, source_target_pairs={{0,4},{4,0},{8,12},{12,8},{1,5},{5,1},{9,13},{13,9},{2,6},{6,2},{1... | collective-permute-start | bytes 1769480 | tf_op jit(solution)/shard_map/ppermute | solution.py:1236
  180.6 2.2 collective-permute-start.22
  196.3 133.8 %all-gather.13.cloned.1.call-start = ((), (), s32[]{:S(2)}) async-start(), calls=%async_computation.3 | async-start | bytes 7077888 | tf_op jit(solution)/shard_map/all_gather | solution.py:1401
  196.3 2.5 collective-permute-start.24
  196.5 30.0 %collective-permute-start.23 = (bf16[256,1664]{1,0:T(8,128)(2,1)}, bf16[256,1664]{1,0:T(8,128)(2,1)}, u32[]{:S(2)}, u32[]{:S(2)}) collective-permute-start(bf16[256,1664]{1,0:T(8,128)(2,1)} %get-tuple-element.189), channel_id=1, source_target_pairs={{0,16},{16,0},{1,17},{17,1},{2,18},{18,2},{3,19},{19,3},{4,20},{20... | collective-permute-start | bytes 2555912 | tf_op jit(solution)/shard_map/ppermute | solution.py:1233
  229.4 10.3 %collective-permute-start.27 = (bf16[64,1664]{1,0:T(8,128)(2,1)}, bf16[64,1664]{1,0:T(8,128)(2,1)S(1)}, u32[]{:S(2)}, u32[]{:S(2)}) collective-permute-start(bf16[64,1664]{1,0:T(8,128)(2,1)} %get-tuple-element.197), channel_id=1, source_target_pairs={{3,0},{0,1},{1,2},{2,3},{7,4},{4,5},{5,6},{6,7},{11,8},{8,9},{9,10... | collective-permute-start | bytes 638984 | tf_op jit(solution)/shard_map/ppermute | solution.py:1242
  230.9 16.5 %collective-permute-start.26 = (bf16[64,1664]{1,0:T(8,128)(2,1)}, bf16[64,1664]{1,0:T(8,128)(2,1)S(1)}, u32[]{:S(2)}, u32[]{:S(2)}) collective-permute-start(bf16[64,1664]{1,0:T(8,128)(2,1)} %get-tuple-element.196), channel_id=1, source_target_pairs={{2,0},{3,1},{0,2},{1,3},{6,4},{7,5},{4,6},{5,7},{10,8},{11,9},{8,1... | collective-permute-start | bytes 638984 | tf_op jit(solution)/shard_map/ppermute | solution.py:1242
  233.6 13.9 %collective-permute-start.25 = (bf16[64,1664]{1,0:T(8,128)(2,1)}, bf16[64,1664]{1,0:T(8,128)(2,1)S(1)}, u32[]{:S(2)}, u32[]{:S(2)}) collective-permute-start(bf16[64,1664]{1,0:T(8,128)(2,1)} %get-tuple-element.195), channel_id=1, source_target_pairs={{1,0},{2,1},{3,2},{0,3},{5,4},{6,5},{7,6},{4,7},{9,8},{10,9},{11,1... | collective-permute-start | bytes 638984 | tf_op jit(solution)/shard_map/ppermute | solution.py:1242
  248.5 29.0 %collective-permute-start.31 = (bf16[256,1536]{1,0:T(8,128)(2,1)S(1)}, bf16[256,1536]{1,0:T(8,128)(2,1)S(1)}, u32[]{:S(2)}, u32[]{:S(2)}) collective-permute-start(bf16[256,1536]{1,0:T(8,128)(2,1)S(1)} %copy-done.48), channel_id=1, source_target_pairs={{0,16},{16,0},{1,17},{17,1},{2,18},{18,2},{3,19},{19,3},{4,20},{20... | collective-permute-start | bytes 2359304 | tf_op jit(solution)/shard_map/ppermute | solution.py:1233
  249.7 27.8 %collective-permute-start.28 = (bf16[64,1664]{1,0:T(8,128)(2,1)S(1)}, bf16[64,1664]{1,0:T(8,128)(2,1)S(1)}, u32[]{:S(2)}, u32[]{:S(2)}) collective-permute-start(bf16[64,1664]{1,0:T(8,128)(2,1)S(1)} %add_convert_fusion.2.rest_0_), channel_id=1, source_target_pairs={{1,0},{2,1},{3,2},{0,3},{5,4},{6,5},{7,6},{4,7},{9,8},{10,9},{11,1... | collective-permute-start | bytes 638984 | tf_op jit(solution)/shard_map/ppermute | solution.py:1242
  255.5 22.0 %collective-permute-start.29 = (bf16[64,1664]{1,0:T(8,128)(2,1)S(1)}, bf16[64,1664]{1,0:T(8,128)(2,1)S(1)}, u32[]{:S(2)}, u32[]{:S(2)}) collective-permute-start(bf16[64,1664]{1,0:T(8,128)(2,1)S(1)} %add_convert_fusion.2.rest_0_), channel_id=1, source_target_pairs={{2,0},{3,1},{0,2},{1,3},{6,4},{7,5},{4,6},{5,7},{10,8},{11,9},{8,1... | collective-permute-start | bytes 638984 | tf_op jit(solution)/shard_map/ppermute | solution.py:1242
  256.2 21.3 %collective-permute-start.30 = (bf16[64,1664]{1,0:T(8,128)(2,1)S(1)}, bf16[64,1664]{1,0:T(8,128)(2,1)S(1)}, u32[]{:S(2)}, u32[]{:S(2)}) collective-permute-start(bf16[64,1664]{1,0:T(8,128)(2,1)S(1)} %add_convert_fusion.2.rest_0_), channel_id=1, source_target_pairs={{3,0},{0,1},{1,2},{2,3},{7,4},{4,5},{5,6},{6,7},{11,8},{8,9},{9,10... | collective-permute-start | bytes 638984 | tf_op jit(solution)/shard_map/ppermute | solution.py:1242
  277.6 102.3 %all-gather.15.cloned.1.call-start = ((), (), s32[]{:S(2)}) async-start(), calls=%async_computation.4 | async-start | bytes 3538944 | tf_op jit(solution)/shard_map/all_gather | solution.py:1401
  281.3 21.0 %collective-permute-start.34 = (bf16[64,1536]{1,0:T(8,128)(2,1)}, bf16[64,1536]{1,0:T(8,128)(2,1)S(1)}, u32[]{:S(2)}, u32[]{:S(2)}) collective-permute-start(bf16[64,1536]{1,0:T(8,128)(2,1)} %get-tuple-element.218), channel_id=1, source_target_pairs={{3,0},{0,1},{1,2},{2,3},{7,4},{4,5},{5,6},{6,7},{11,8},{8,9},{9,10... | collective-permute-start | bytes 589832 | tf_op jit(solution)/shard_map/ppermute | solution.py:1242
  284.1 18.2 %collective-permute-start.33 = (bf16[64,1536]{1,0:T(8,128)(2,1)}, bf16[64,1536]{1,0:T(8,128)(2,1)S(1)}, u32[]{:S(2)}, u32[]{:S(2)}) collective-permute-start(bf16[64,1536]{1,0:T(8,128)(2,1)} %get-tuple-element.217), channel_id=1, source_target_pairs={{2,0},{3,1},{0,2},{1,3},{6,4},{7,5},{4,6},{5,7},{10,8},{11,9},{8,1... | collective-permute-start | bytes 589832 | tf_op jit(solution)/shard_map/ppermute | solution.py:1242
  285.6 16.7 %collective-permute-start.32 = (bf16[64,1536]{1,0:T(8,128)(2,1)}, bf16[64,1536]{1,0:T(8,128)(2,1)S(1)}, u32[]{:S(2)}, u32[]{:S(2)}) collective-permute-start(bf16[64,1536]{1,0:T(8,128)(2,1)} %get-tuple-element.216), channel_id=1, source_target_pairs={{1,0},{2,1},{3,2},{0,3},{5,4},{6,5},{7,6},{4,7},{9,8},{10,9},{11,1... | collective-permute-start | bytes 589832 | tf_op jit(solution)/shard_map/ppermute | solution.py:1242
  302.3 18.9 %collective-permute-start.40 = (bf16[2,224,768]{2,1,0:T(8,128)(2,1)}, bf16[2,224,768]{2,1,0:T(8,128)(2,1)}, u32[]{:S(2)}, u32[]{:S(2)}) collective-permute-start(bf16[2,224,768]{2,1,0:T(8,128)(2,1)} %dynamic-slice_convert_fusion.1), channel_id=1, source_target_pairs={{0,4},{4,0},{8,12},{12,8},{1,5},{5,1},{9,13},{13,9},{2,6},{6,2},{1... | collective-permute-start | bytes 2064392 | tf_op jit(solution)/shard_map/ppermute | solution.py:1236
  304.1 2.1 collective-permute-start.35
  306.9 9.7 %collective-permute-start.36 = (bf16[256,256]{1,0:T(8,128)(2,1)}, bf16[256,256]{1,0:T(8,128)(2,1)S(1)}, u32[]{:S(2)}, u32[]{:S(2)}) collective-permute-start(bf16[256,256]{1,0:T(8,128)(2,1)} %fusion.19), channel_id=1, source_target_pairs={{0,8},{4,12},{8,0},{12,4},{1,9},{5,13},{9,1},{13,5},{2,10},{6,14},... | collective-permute-start | bytes 393224 | tf_op jit(solution)/shard_map/ppermute | solution.py:1239
  309.4 14.1 %collective-permute-start.37 = (bf16[64,1536]{1,0:T(8,128)(2,1)S(1)}, bf16[64,1536]{1,0:T(8,128)(2,1)S(1)}, u32[]{:S(2)}, u32[]{:S(2)}) collective-permute-start(bf16[64,1536]{1,0:T(8,128)(2,1)S(1)} %add_convert_fusion.4.rest_0_), channel_id=1, source_target_pairs={{1,0},{2,1},{3,2},{0,3},{5,4},{6,5},{7,6},{4,7},{9,8},{10,9},{11,1... | collective-permute-start | bytes 589832 | tf_op jit(solution)/shard_map/ppermute | solution.py:1242
  311.6 17.9 %collective-permute-start.38 = (bf16[64,1536]{1,0:T(8,128)(2,1)S(1)}, bf16[64,1536]{1,0:T(8,128)(2,1)S(1)}, u32[]{:S(2)}, u32[]{:S(2)}) collective-permute-start(bf16[64,1536]{1,0:T(8,128)(2,1)S(1)} %add_convert_fusion.4.rest_0_), channel_id=1, source_target_pairs={{2,0},{3,1},{0,2},{1,3},{6,4},{7,5},{4,6},{5,7},{10,8},{11,9},{8,1... | collective-permute-start | bytes 589832 | tf_op jit(solution)/shard_map/ppermute | solution.py:1242
  311.9 18.2 %collective-permute-start.39 = (bf16[64,1536]{1,0:T(8,128)(2,1)S(1)}, bf16[64,1536]{1,0:T(8,128)(2,1)}, u32[]{:S(2)}, u32[]{:S(2)}) collective-permute-start(bf16[64,1536]{1,0:T(8,128)(2,1)S(1)} %add_convert_fusion.4.rest_0_), channel_id=1, source_target_pairs={{3,0},{0,1},{1,2},{2,3},{7,4},{4,5},{5,6},{6,7},{11,8},{8,9},{9,10... | collective-permute-start | bytes 589832 | tf_op jit(solution)/shard_map/ppermute | solution.py:1242
  330.2 31.0 %collective-permute-start.43 = (bf16[64,1536]{1,0:T(8,128)(2,1)}, bf16[64,1536]{1,0:T(8,128)(2,1)S(1)}, u32[]{:S(2)}, u32[]{:S(2)}) collective-permute-start(bf16[64,1536]{1,0:T(8,128)(2,1)} %get-tuple-element.241), channel_id=1, source_target_pairs={{3,0},{0,1},{1,2},{2,3},{7,4},{4,5},{5,6},{6,7},{11,8},{8,9},{9,10... | collective-permute-start | bytes 589832 | tf_op jit(solution)/shard_map/ppermute | solution.py:1242
  330.2 31.0 %collective-permute-start.42 = (bf16[64,1536]{1,0:T(8,128)(2,1)}, bf16[64,1536]{1,0:T(8,128)(2,1)}, u32[]{:S(2)}, u32[]{:S(2)}) collective-permute-start(bf16[64,1536]{1,0:T(8,128)(2,1)} %get-tuple-element.240), channel_id=1, source_target_pairs={{2,0},{3,1},{0,2},{1,3},{6,4},{7,5},{4,6},{5,7},{10,8},{11,9},{8,1... | collective-permute-start | bytes 589832 | tf_op jit(solution)/shard_map/ppermute | solution.py:1242
  331.9 30.0 %collective-permute-start.41 = (bf16[64,1536]{1,0:T(8,128)(2,1)}, bf16[64,1536]{1,0:T(8,128)(2,1)}, u32[]{:S(2)}, u32[]{:S(2)}) collective-permute-start(bf16[64,1536]{1,0:T(8,128)(2,1)} %get-tuple-element.239), channel_id=1, source_target_pairs={{1,0},{2,1},{3,2},{0,3},{5,4},{6,5},{7,6},{4,7},{9,8},{10,9},{11,1... | collective-permute-start | bytes 589832 | tf_op jit(solution)/shard_map/ppermute | solution.py:1242
  337.6 27.0 %collective-permute-start.45 = (bf16[2,384,640]{2,1,0:T(8,128)(2,1)}, bf16[2,384,640]{2,1,0:T(8,128)(2,1)}, u32[]{:S(2)}, u32[]{:S(2)}) collective-permute-start(bf16[2,384,640]{2,1,0:T(8,128)(2,1)} %dynamic-slice_convert_fusion), channel_id=1, source_target_pairs={{0,4},{4,0},{8,12},{12,8},{1,5},{5,1},{9,13},{13,9},{2,6},{6,2},{1... | collective-permute-start | bytes 2949128 | tf_op jit(solution)/shard_map/ppermute | solution.py:1236
  339.5 23.7 %collective-permute-start.44 = (bf16[224,768]{1,0:T(8,128)(2,1)}, bf16[224,768]{1,0:T(8,128)(2,1)}, u32[]{:S(2)}, u32[]{:S(2)}) collective-permute-start(bf16[224,768]{1,0:T(8,128)(2,1)} %fusion.11), channel_id=1, source_target_pairs={{0,16},{16,0},{1,17},{17,1},{2,18},{18,2},{3,19},{19,3},{4,20},{20... | collective-permute-start | bytes 1032200 | tf_op jit(solution)/shard_map/ppermute | solution.py:1233
  366.0 10.2 %collective-permute-start.49 = (bf16[224,768]{1,0:T(8,128)(2,1)S(1)}, bf16[224,768]{1,0:T(8,128)(2,1)S(1)}, u32[]{:S(2)}, u32[]{:S(2)}) collective-permute-start(bf16[224,768]{1,0:T(8,128)(2,1)S(1)} %convert_element_type.160), channel_id=1, source_target_pairs={{0,8},{4,12},{8,0},{12,4},{1,9},{5,13},{9,1},{13,5},{2,10},{6,14},... | collective-permute-start | bytes 1032200 | tf_op jit(solution)/shard_map/ppermute | solution.py:1239
  366.6 13.1 %collective-permute-start.50 = (bf16[384,640]{1,0:T(8,128)(2,1)S(1)}, bf16[384,640]{1,0:T(8,128)(2,1)S(1)}, u32[]{:S(2)}, u32[]{:S(2)}) collective-permute-start(bf16[384,640]{1,0:T(8,128)(2,1)S(1)} %fusion.7), channel_id=1, source_target_pairs={{0,16},{16,0},{1,17},{17,1},{2,18},{18,2},{3,19},{19,3},{4,20},{20... | collective-permute-start | bytes 1474568 | tf_op jit(solution)/shard_map/ppermute | solution.py:1233
  367.6 24.8 %collective-permute-start.46 = (bf16[64,1536]{1,0:T(8,128)(2,1)S(1)}, bf16[64,1536]{1,0:T(8,128)(2,1)S(1)}, u32[]{:S(2)}, u32[]{:S(2)}) collective-permute-start(bf16[64,1536]{1,0:T(8,128)(2,1)S(1)} %add_convert_fusion.3.rest_0_), channel_id=1, source_target_pairs={{1,0},{2,1},{3,2},{0,3},{5,4},{6,5},{7,6},{4,7},{9,8},{10,9},{11,1... | collective-permute-start | bytes 589832 | tf_op jit(solution)/shard_map/ppermute | solution.py:1242
  368.0 24.4 %collective-permute-start.47 = (bf16[64,1536]{1,0:T(8,128)(2,1)S(1)}, bf16[64,1536]{1,0:T(8,128)(2,1)S(1)}, u32[]{:S(2)}, u32[]{:S(2)}) collective-permute-start(bf16[64,1536]{1,0:T(8,128)(2,1)S(1)} %add_convert_fusion.3.rest_0_), channel_id=1, source_target_pairs={{2,0},{3,1},{0,2},{1,3},{6,4},{7,5},{4,6},{5,7},{10,8},{11,9},{8,1... | collective-permute-start | bytes 589832 | tf_op jit(solution)/shard_map/ppermute | solution.py:1242
  369.2 23.2 %collective-permute-start.48 = (bf16[64,1536]{1,0:T(8,128)(2,1)S(1)}, bf16[64,1536]{1,0:T(8,128)(2,1)S(1)}, u32[]{:S(2)}, u32[]{:S(2)}) collective-permute-start(bf16[64,1536]{1,0:T(8,128)(2,1)S(1)} %add_convert_fusion.3.rest_0_), channel_id=1, source_target_pairs={{3,0},{0,1},{1,2},{2,3},{7,4},{4,5},{5,6},{6,7},{11,8},{8,9},{9,10... | collective-permute-start | bytes 589832 | tf_op jit(solution)/shard_map/ppermute | solution.py:1242
  392.5 13.9 %collective-permute-start.54 = (bf16[384,640]{1,0:T(8,128)(2,1)S(1)}, bf16[384,640]{1,0:T(8,128)(2,1)S(1)}, u32[]{:S(2)}, u32[]{:S(2)}) collective-permute-start(bf16[384,640]{1,0:T(8,128)(2,1)S(1)} %convert_element_type.165), channel_id=1, source_target_pairs={{0,8},{4,12},{8,0},{12,4},{1,9},{5,13},{9,1},{13,5},{2,10},{6,14},... | collective-permute-start | bytes 1474568 | tf_op jit(solution)/shard_map/ppermute | solution.py:1239
  399.1 1.2 collective-permute-start.51
  400.3 4.6 %collective-permute-start.52 = (f32[1536]{0:T(1024)S(1)}, f32[1536]{0:T(1024)S(1)}, u32[]{:S(2)}, u32[]{:S(2)}) collective-permute-start(f32[1536]{0:T(1024)S(1)} %add.142), channel_id=1, source_target_pairs={{0,8},{4,12},{8,0},{12,4},{1,9},{5,13},{9,1},{13,5},{2,10},{6,14},... | collective-permute-start | bytes 18440 | tf_op jit(solution)/shard_map/ppermute | solution.py:1239
  404.2 4.9 %collective-permute-start.56 = (bf16[224,768]{1,0:T(8,128)(2,1)S(1)}, bf16[224,768]{1,0:T(8,128)(2,1)S(1)}, u32[]{:S(2)}, u32[]{:S(2)}) collective-permute-start(bf16[224,768]{1,0:T(8,128)(2,1)S(1)} %add_convert_fusion.1), channel_id=1, source_target_pairs={{0,4},{4,0},{8,12},{12,8},{1,5},{5,1},{9,13},{13,9},{2,6},{6,2},{1... | collective-permute-start | bytes 1032200 | tf_op jit(solution)/shard_map/ppermute | solution.py:1236
  404.9 3.6 collective-permute-start.53
  406.5 5.2 %collective-permute-start.55 = (bf16[384,640]{1,0:T(8,128)(2,1)S(1)}, bf16[384,640]{1,0:T(8,128)(2,1)S(1)}, u32[]{:S(2)}, u32[]{:S(2)}) collective-permute-start(bf16[384,640]{1,0:T(8,128)(2,1)S(1)} %add_convert_fusion), channel_id=1, source_target_pairs={{0,4},{4,0},{8,12},{12,8},{1,5},{5,1},{9,13},{13,9},{2,6},{6,2},{1... | collective-permute-start | bytes 1474568 | tf_op jit(solution)/shard_map/ppermute | solution.py:1236
  (48 other events, 363.4 us)
Sparse Core Ops, SparseCore 0:
  54.6 44.1 all-reduce.4
  157.7 34.8 all-gather.8
  196.4 55.4 all-gather.10
  277.7 50.1 all-gather.12
  330.3 36.3 all-gather.14

commit v6 on v5

--- a/solution.py
+++ b/solution.py
@@ -412,6 +412,10 @@
     return lax.dot_general(
         left, right, (((left_dim,), (right_dim,)), ((), ())), preferred_element_type=jnp.float32
     )
+
+
+def pick(hot, rows):
+    return dot(hot, rows).astype(jnp.bfloat16)
 
 
 def kernel_params(count=0):
@@ -765,8 +769,8 @@
             else:
                 swap = pl.ds((1 - part) * half, half)
                 rows, grads = far_ref[span, swap], far_out_ref[span, swap]
-            rows_buf[b, :, keep] = dot(low, rows).astype(jnp.bfloat16)
-            grads_buf[b, :, keep] = dot(low, grads).astype(jnp.bfloat16)
+            rows_buf[b, :, keep] = pick(low, rows)
+            grads_buf[b, :, keep] = pick(low, grads)
     for r in range(4):
         q = quarter[r]
         slot = slice(r * CAP, (r + 1) * CAP)
@@ -1059,7 +1063,7 @@
 
 def output_kernel(place_ref, mixed_ref, *rest):
     out_ref, whole_buf = rest[-2:]
-    take_pieces(rest[:-2], place_ref[2], whole_buf)
+    take_pieces(rest[:-2], place_ref[2] // 2, whole_buf)
     half = out_ref.shape[1] // 2
     total = mixed_ref[...] + RESIDUAL_SCALE * whole_buf[...]
     first, second = own_then_other(place_ref[0], total)
@@ -1109,20 +1113,24 @@
         for k in range(4):
             for b in range(4):
                 span = pl.ds(b * 128, 128)
+                hot = jnp.concatenate(
+                    [
+                        jnp.where(
+                            iota == rank_ref[a, q, first + j, pl.ds(4 * k + b, 1), :], 1.0, 0.0
+                        )
+                        for a in range(2)
+                        for j in range(steps)
+                        for q in range(4)
+                    ],
+                    axis=0,
+                ).astype(jnp.bfloat16)
+                rows = pick(hot, rows_ref[ctx[k], span, :])
+                grads = pick(hot, grads_in[k][span, :])
                 for a in range(2):
-                    hot = jnp.concatenate(
-                        [
-                            jnp.where(iota == rank_ref[a, q, first + j, pl.ds(4 * k + b, 1), :], 1.0, 0.0)
-                            for j in range(steps)
-                            for q in range(4)
-                        ],
-                        axis=0,
-                    ).astype(jnp.bfloat16)
                     spot = 4 * k + (b ^ (2 * a))
-                    rows = dot(hot, rows_ref[ctx[k], span, :]).astype(jnp.bfloat16)
-                    grads = dot(hot, grads_in[k][span, :]).astype(jnp.bfloat16)
                     for j in range(steps):
-                        piece = slice(j * 4 * CAP, (j + 1) * 4 * CAP)
+                        start = (a * steps + j) * 4 * CAP
+                        piece = slice(start, start + 4 * CAP)
                         rows_buf[j * 2 + a, spot] = rows[piece]
                         grads_buf[j * 2 + a, spot] = grads[piece]
 
@@ -1465,12 +1473,12 @@
         back_got,
     )
     total = reduce_pieces(pieces)
-    total, moe_far = tie((total, moe_far))
+    total, moe_far, pair_zero, slots[1] = tie((total, moe_far, pair_zero, slots[1]))
     moe_got = across(moe_far)
+    pair_one = gather_slots(slots[1])
     found = spread_pieces(total)
     grads = grads_of(0, pair_zero, None, jnp.zeros((8, 128), wide))
-    *found, moe_got, mark, slots[1] = tie((*found, moe_got, grads[2], slots[1]))
-    pair_one = gather_slots(slots[1])
+    *found, moe_got, mark = tie((*found, moe_got, grads[2]))
     moe_pieces = single(
         join_kernel, "join", piece_shapes, [((tokens, model), wide)], [place], moe_all, moe_got
     )
@@ -1514,7 +1522,8 @@
 
     given, moe_total = tie((given, moe_total))
     near_pair = beside(given)
-    moe_found = spread_pieces(moe_total)
+    near_pair, attn_grad = tie((near_pair, attn_grad))
+    moe_next = lax.ppermute(moe_total, "tp", [(i, i ^ 1) for i in range(tp_size)])
     distant = along((kept[1] + near_pair[1].astype(wide)).astype(low))
     qkv_grad, *pieces = single(
         last_kernel,
@@ -1565,10 +1574,22 @@
             axis=1,
         )
     )
-    tied = tie((*pieces, *moe_found, mark, side, qkv_grad, pair_one, slots[2]))
-    pieces, moe_found = tied[:tp_size], tied[tp_size : 2 * tp_size]
-    mark, side, qkv_grad, pair_one, slots[2] = tied[2 * tp_size :]
+    side_got = across(side[1].astype(low))
+    *pieces, mark, side_got, qkv_grad, pair_one, slots[2], moe_next = tie(
+        (*pieces, mark, side_got, qkv_grad, pair_one, slots[2], moe_next)
+    )
+    side = side[0] + side_got.astype(wide)
     pair_two = gather_slots(slots[2])
+    moe_pair = jnp.where(
+        z_pos % 2 == 0,
+        jnp.concatenate([moe_total, moe_next], axis=0),
+        jnp.concatenate([moe_next, moe_total], axis=0),
+    )
+    moe_rest = lax.ppermute(moe_pair, "tp", [(i, i ^ 2) for i in range(tp_size)])
+    total = reduce_pieces(pieces)
+    grads = grads_of(1, pair_one, grads, mark)
+    d_qkv = hop_beside(dot(normed_one, qkv_grad, 0, 0).reshape(2, half, qkv_cols))
+    total, mark, side, d_qkv, moe_rest = tie((total, grads[2], side, d_qkv, moe_rest))
     (layer_out,) = single(
         output_kernel,
         "output",
@@ -1576,18 +1597,16 @@
         [((tokens, model), wide)],
         [place],
         mixed,
-        *moe_found,
-    )
-    total = reduce_pieces(pieces)
-    grads = grads_of(1, pair_one, grads, mark)
-    side = hop_across(side)
-    d_qkv = hop_beside(dot(normed_one, qkv_grad, 0, 0).reshape(2, half, qkv_cols))
-    total, mark, side, d_qkv = tie((total, grads[2], side, d_qkv))
+        moe_pair,
+        moe_rest,
+    )
     found = spread_pieces(total)
     grads = grads_of(2, pair_two, grads, mark)
-    side = hop_along(side)
-    d_qkv = hop_across(d_qkv)
-    *found, mark, side, d_qkv = tie((*found, grads[2], side, d_qkv))
+    side_got = along(side.astype(low))
+    qkv_got = across(d_qkv[1].astype(low))
+    *found, mark, side_got, qkv_got = tie((*found, grads[2], side_got, qkv_got))
+    side = (side + side_got.astype(wide)).astype(low)
+    d_qkv = d_qkv[0] + qkv_got.astype(wide)
     d_hidden, gain_one = single(
         hidden_kernel,
         "hidden",
@@ -1639,7 +1658,7 @@
         P(None, "tp", "fsdp"),
         P(None, "fsdp", "ctx", None),
     )
-    fits = mesh.shape["fsdp"] == 2 and mesh.shape["ctx"] == 4
+    fits = mesh.shape["fsdp"] == 2 and mesh.shape["ctx"] == 4 and mesh.shape["tp"] == 4
     return jax.shard_map(
         fast_body if fits else body,
         mesh=mesh,

time: 427 us -> 418 us (0.979)
  waiting for transfers between devices: 133 us -> 128 us
    ppermute x18 -> x15, starting transfers between devices: 28.7 us -> 23.4 us  [from_tp(): lax.ppermute(value, 'tp', [((i + step) % tp_size, i) for i in range(tp_si...]
    ppermute x0 -> x2, starting transfers between devices: none -> 4.73 us  [the longest x1 3.76 us: fast_body(): lax.ppermute(moe_total, 'tp', [(i, i ^ 1) for i in range(tp_size)])]
    ppermute x12, waiting for transfers between devices: 69.2 us -> 64.6 us  [across(): return lax.ppermute(value, 'fsdp', [(0, 1), (1, 0)])]
    ppermute x18 -> x15, waiting for transfers between devices: 18.6 us -> 15.7 us  [from_tp(): lax.ppermute(value, 'tp', [((i + step) % tp_size, i) for i in range(tp_si...]
  transfers between devices with their start and end apart: 62 -> 61, of which waited for: 25 -> 25; matrix products, arithmetic and copies ran while one was open for 9% -> 8% of each run, Pallas kernels for 38% -> 39%
where the time goes in v6:
time: 418 us; the launch traced here: 412 us
  Pallas kernels  161 us (39%)
  waiting for transfers between devices  128 us (31%)
  starting transfers between devices  59.3 us (14%)
  local copies, waits for them, and re-layouts  24.2 us (6%)
  other arithmetic  17.3 us (4%)
  between operations  15.2 us (4%)
  matrix products  6.75 us (2%)
    ppermute x12, waiting for transfers between devices, across(): return lax.ppermute(value, 'fsdp', [(0, 1), (1, 0)])  64.6 us
    pallas_call x3, Pallas kernels, run_weight_grads(): pl.pallas_call(functools.partial(weight_grad_kernel, first=first, steps=s...  54.5 us
    pallas_call x3, Pallas kernels, run_experts(): pl.pallas_call(functools.partial(expert_kernel, first=first, last=last, e...  44.9 us
    pallas_call x9, Pallas kernels, single(): pl.pallas_call(kernel, out_shape=tuple((jax.ShapeDtypeStruct(shape, kind)...  41.6 us
    ppermute x15, starting transfers between devices, from_tp(): lax.ppermute(value, 'tp', [((i + step) % tp_size, i) for i in range(tp_si...  23.4 us
    ppermute x9, waiting for transfers between devices, along(): return lax.ppermute(value, 'ctx', [(i, i ^ 2) for i in range(4)])  21.3 us
    pallas_call x4, Pallas kernels, split_weights(): pl.pallas_call(split_plain_kernel if down is None else split_kernel, out_...  20.5 us
    ppermute x12, starting transfers between devices, across(): return lax.ppermute(value, 'fsdp', [(0, 1), (1, 0)])  17.6 us
  transfers between devices with their start and end apart: 61, of which 25 were waited for; matrix products, arithmetic and copies ran while one was open for 8% of the time, Pallas kernels for 39%

profile of v6, /device:TPU:0, one launch (start us, length us, event | category | flops | bytes accessed | tf_op | source)
XLA Modules:
  0.0 411.8 jit_solution(11014959263255521615)
XLA Ops:
  10.8 3.0 collective-permute-start
  13.9 2.3 split_weights.4
  18.3 9.4 %collective-permute-done.sent_ref = bf16[400,768]{1,0:T(8,128)(2,1)S(1)} collective-permute-done((bf16[400,768]{1,0:T(8,128)(2,1)S(1)}, bf16[400,768]{1,0:T(8,128)(2,1)S(1)}, u32[]{:S(2)}, u32[]{:S(2)}) %collective-permute-start) | collective-permute-done | bytes 614432 | tf_op jit(solution)/shard_map/ppermute | solution.py:1241
  29.1 1.7 collective-permute-start.2
  34.2 4.5 %before.1 = (bf16[256,1536]{1,0:T(8,128)(2,1)}, bf16[256,384]{1,0:T(8,128)(2,1)}, bf16[256,256]{1,0:T(8,128)(2,1)}, bf16[768,768]{1,0:T(8,128)(2,1)}, f32[16,1536]{1,0:T(8,128)}, /*index=5*/f32[2,256,128]{2,1,0:T(8,128)}) custom-call(s32[3]{0:T(128)} %pad_add_fusion.place_ref, s32[2,4]{1,0:T(2,128)} %bitcast.205, bf16[256,1536]{1,0:T(8,128)(2,1)} %bitcast.164, ...), custom_call_target="tpu_custom_call" | custom-call | tf_op jit(solution)/shard_map/before/pallas_call | solution.py:431
  38.8 1.7 collective-permute-start.9
  40.5 1.5 collective-permute-start.4
  42.3 4.4 %collective-permute-done.4.kv2 = bf16[256,256]{1,0:T(8,128)(2,1)S(1)} collective-permute-done((bf16[256,256]{1,0:T(8,128)(2,1)}, bf16[256,256]{1,0:T(8,128)(2,1)S(1)}, u32[]{:S(2)}, u32[]{:S(2)}) %collective-permute-start.4) | collective-permute-done | bytes 131104 | tf_op jit(solution)/shard_map/ppermute | solution.py:1247
  48.6 5.8 %attend.1 = (bf16[256,384]{1,0:T(8,128)(2,1)}, f32[4,384,512]{2,1,0:T(8,128)}, bf16[384,768]{1,0:T(8,128)(2,1)}, bf16[256,1536]{1,0:T(8,128)(2,1)}) custom-call(s32[3]{0:T(128)} %pad_add_fusion.place_ref, s32[2,4]{1,0:T(2,128)} %bitcast.206, bf16[256,384]{1,0:T(8,128)(2,1)} %get-tuple-element.148.query_ref, bf16[256,256]{1,0:T(8,128)(2,1)} %get-tuple-element.152.kv0, ...), custom_call_target="tpu_custom_call" | custom-call | tf_op jit(solution)/shard_map/attend/pallas_call | solution.py:431
  54.7 2.2 split_weights.7
  57.0 10.7 %collective-permute-done.9.rest_0_ = bf16[2,2304,128]{2,1,0:T(8,128)(2,1)} collective-permute-done((bf16[2,2304,128]{2,1,0:T(8,128)(2,1)S(1)}, bf16[2,2304,128]{2,1,0:T(8,128)(2,1)}, u32[]{:S(2)}, u32[]{:S(2)}) %collective-permute-start.9) | collective-permute-done | bytes 1179680 | tf_op jit(solution)/shard_map/ppermute | solution.py:1241
  67.7 1.8 collective-permute-start.10
  69.5 1.5 collective-permute-start.16
  71.1 14.0 %split_weights.5 = bf16[20,1536,128]{2,1,0:T(8,128)(2,1)} custom-call(s32[1]{0:T(128)} %bitcast.11.base_ref, bf16[40,1536,128]{2,1,0:T(8,128)(2,1)} %bitcast.152), custom_call_target="tpu_custom_call" | custom-call | tf_op jit(solution)/shard_map/split_weights/pallas_call | solution.py:498
  85.9 12.9 %all-reduce.5.cloned.1.call-done.attended_ref = bf16[256,1536]{1,0:T(8,128)(2,1)} async-done(((bf16[256,1536]{1,0:T(8,128)(2,1)}), bf16[256,1536]{1,0:T(8,128)(2,1)}) %all-reduce.5.cloned.1.call-update) | async-done | bytes 786448 | tf_op jit(solution)/shard_map/psum | solution.py:1351
  98.9 1.5 collective-permute-start.11
  100.5 2.0 split_weights.6
  102.4 4.3 %after.1 = (f32[256,1536]{1,0:T(8,128)}, bf16[256,1664]{1,0:T(8,128)(2,1)}, f32[256,128]{1,0:T(8,128)}) custom-call(s32[3]{0:T(128)} %pad_add_fusion.place_ref, bf16[256,1536]{1,0:T(8,128)(2,1)} %bitcast.165, f32[16,1536]{1,0:T(8,128)} %get-tuple-element.146.gains_ref, bf16[784,768]{1,0:T(8,128)(2,1)} %pad_maximum_fusion.small_ref, ...), custom_call_target="tpu_custom_call" | custom-call | tf_op jit(solution)/shard_map/after/pallas_call | solution.py:431
  106.7 1.5 collective-permute-start.8
  111.9 16.8 %collective-permute-done.8.far_ref = bf16[256,1664]{1,0:T(8,128)(2,1)S(1)} collective-permute-done((bf16[256,1664]{1,0:T(8,128)(2,1)}, bf16[256,1664]{1,0:T(8,128)(2,1)S(1)}, u32[]{:S(2)}, u32[]{:S(2)}) %collective-permute-start.8) | collective-permute-done | bytes 852000 | tf_op jit(solution)/shard_map/ppermute | solution.py:1241
  129.3 1.5 collective-permute-start.17
  134.0 15.7 %experts.3 = (bf16[4,2,128,384]{3,2,1,0:T(8,128)(2,1)}, bf16[512,1536]{1,0:T(8,128)(2,1)}, bf16[512,1664]{1,0:T(8,128)(2,1)}) custom-call(s32[3]{0:T(128)} %pad_add_fusion.place_ref, bf16[256,1664]{1,0:T(8,128)(2,1)} %get-tuple-element.165.near_ref, bf16[256,1664]{1,0:T(8,128)(2,1)} %copy-done.4, bf16[256,1664]{1,0:T(8,128)(2,1)} %copy-done, ...), custom_call_target="tpu_custom_call" | custom-call | tf_op jit(solution)/shard_map/experts/pallas_call | solution.py:885
  149.8 7.8 %collective-permute-done.17.rest_2_ = bf16[2,2304,128]{2,1,0:T(8,128)(2,1)} collective-permute-done((bf16[2,2304,128]{2,1,0:T(8,128)(2,1)}, bf16[2,2304,128]{2,1,0:T(8,128)(2,1)}, u32[]{:S(2)}, u32[]{:S(2)}) %collective-permute-start.17) | collective-permute-done | bytes 1179680 | tf_op jit(solution)/shard_map/ppermute | solution.py:1247
  158.6 1.5 collective-permute-start.21
  160.2 1.9 collective-permute-done.19.rest_1_
  163.1 16.5 %experts.4 = (bf16[4,2,128,384]{3,2,1,0:T(8,128)(2,1)}, bf16[512,1536]{1,0:T(8,128)(2,1)}, bf16[512,1664]{1,0:T(8,128)(2,1)}) custom-call(s32[3]{0:T(128)} %pad_add_fusion.place_ref, bf16[256,1664]{1,0:T(8,128)(2,1)} %get-tuple-element.165.near_ref, bf16[256,1664]{1,0:T(8,128)(2,1)} %copy-done.4, bf16[256,1664]{1,0:T(8,128)(2,1)} %copy-done, ...), custom_call_target="tpu_custom_call" | custom-call | tf_op jit(solution)/shard_map/experts/pallas_call | solution.py:885
  180.6 2.2 collective-permute-done.22.rest_3_
  183.6 12.6 %experts.5 = (bf16[4,1,128,384]{3,2,1,0:T(8,128)(2,1)}, f32[256,1536]{1,0:T(8,128)}, f32[256,1664]{1,0:T(8,128)}, bf16[256,1536]{1,0:T(8,128)(2,1)}, bf16[256,1664]{1,0:T(8,128)(2,1)}) custom-call(s32[3]{0:T(128)} %pad_add_fusion.place_ref, bf16[256,1664]{1,0:T(8,128)(2,1)} %get-tuple-element.165.near_ref, bf16[256,1664]{1,0:T(8,128)(2,1)} %copy-done.4, ...), custom_call_target="tpu_custom_call" | custom-call | tf_op jit(solution)/shard_map/experts/pallas_call | solution.py:885
  200.3 26.1 %collective-permute-done.23.got_ref = bf16[256,1664]{1,0:T(8,128)(2,1)} collective-permute-done((bf16[256,1664]{1,0:T(8,128)(2,1)}, bf16[256,1664]{1,0:T(8,128)(2,1)}, u32[]{:S(2)}, u32[]{:S(2)}) %collective-permute-start.23) | collective-permute-done | bytes 852000 | tf_op jit(solution)/shard_map/ppermute | solution.py:1241
  226.5 2.9 join.2
  229.3 1.5 collective-permute-start.27
  230.9 2.6 collective-permute-start.26
  233.5 1.3 collective-permute-start.25
  234.8 4.8 %collective-permute-done.27 = bf16[64,1664]{1,0:T(8,128)(2,1)S(1)} collective-permute-done((bf16[64,1664]{1,0:T(8,128)(2,1)}, bf16[64,1664]{1,0:T(8,128)(2,1)S(1)}, u32[]{:S(2)}, u32[]{:S(2)}) %collective-permute-start.27) | collective-permute-done | bytes 213024 | tf_op jit(solution)/shard_map/ppermute | solution.py:1250
  239.6 7.7 %collective-permute-done.26 = bf16[64,1664]{1,0:T(8,128)(2,1)S(1)} collective-permute-done((bf16[64,1664]{1,0:T(8,128)(2,1)}, bf16[64,1664]{1,0:T(8,128)(2,1)S(1)}, u32[]{:S(2)}, u32[]{:S(2)}) %collective-permute-start.26) | collective-permute-done | bytes 213024 | tf_op jit(solution)/shard_map/ppermute | solution.py:1250
  248.4 3.5 all-gather.11.cloned.1.call-done
  251.9 1.5 collective-permute-start.31
  253.5 3.3 collective-permute-start.28
  258.7 21.2 %weight_grads.3 = (f32[2,4,5,1536,128]{4,3,2,1,0:T(8,128)}, f32[2,4,5,128,768]{4,3,2,1,0:T(8,128)}, f32[8,128]{1,0:T(8,128)}) custom-call(s32[3]{0:T(128)} %pad_add_fusion.place_ref, bf16[4,512,768]{2,1,0:T(8,128)(2,1)} %bitcast.159, bf16[512,896]{1,0:T(8,128)(2,1)} %copy-done.2, bf16[512,896]{1,0:T(8,128)(2,1)} %collective-permute-done.12.grads1, ...), custom_call_target="tpu_custom_call" | custom-call | tf_op jit(solution)/shard_map/weight_grads/pallas_call | solution.py:1174
  281.0 2.7 join.3
  283.7 2.2 collective-permute-start.34
  285.9 1.6 collective-permute-start.33
  287.5 1.6 collective-permute-start.32
  289.3 10.2 %back.1 = (f32[256,1536]{1,0:T(8,128)}, bf16[256,1536]{1,0:T(8,128)(2,1)}, bf16[256,128]{1,0:T(8,128)(2,1)}, f32[8,1536]{1,0:T(8,128)}, bf16[256,384]{1,0:T(8,12...) custom-call(s32[3]{0:T(128)} %pad_add_fusion.place_ref, f32[256,1536]{1,0:T(8,128)} %get-tuple-element.159.mixed_ref, ...), custom_call_target="tpu_custom_call" | custom-call | tf_op jit(solution)/shard_map/back/pallas_call | solution.py:431
  304.8 3.8 collective-permute-start.39
  310.9 2.0 collective-permute-start.38
  313.0 5.2 %collective-permute-done.36.along_ref = bf16[256,256]{1,0:T(8,128)(2,1)S(1)} collective-permute-done((bf16[256,256]{1,0:T(8,128)(2,1)S(1)}, bf16[256,256]{1,0:T(8,128)(2,1)S(1)}, u32[]{:S(2)}, u32[]{:S(2)}) %collective-permute-start.36) | collective-permute-done | bytes 131104 | tf_op jit(solution)/shard_map/ppermute | solution.py:1247
  318.9 3.8 last.1
  323.4 2.4 collective-permute-start.42
  325.9 1.3 collective-permute-start.41
  327.1 1.4 collective-permute-start.40
  328.5 2.1 fusion.34
  333.5 20.5 %weight_grads.4 = (f32[2,4,5,1536,128]{4,3,2,1,0:T(8,128)}, f32[2,4,5,128,768]{4,3,2,1,0:T(8,128)}, f32[8,128]{1,0:T(8,128)}) custom-call(s32[3]{0:T(128)} %pad_add_fusion.place_ref, bf16[4,512,768]{2,1,0:T(8,128)(2,1)} %bitcast.160, bf16[512,896]{1,0:T(8,128)(2,1)} %copy-done.2, ...), custom_call_target="tpu_custom_call", output_to_operand_aliasing={{0}: (9, {}), {1}: (10, {})} | custom-call | tf_op jit(solution)/shard_map/weight_grads/pallas_call | solution.py:1174
  355.3 1.4 add_convert_fusion.3.rest_0_
  356.8 1.4 convert_add_fusion
  358.2 2.6 collective-permute-done.44.rest_1_
  364.0 1.3 collective-permute-start.47
  365.3 12.8 %weight_grads.5 = (f32[2,4,5,1536,128]{4,3,2,1,0:T(8,128)}, f32[2,4,5,128,768]{4,3,2,1,0:T(8,128)}, f32[8,128]{1,0:T(8,128)}) custom-call(s32[3]{0:T(128)} %pad_add_fusion.place_ref, bf16[4,512,768]{2,1,0:T(8,128)(2,1)} %bitcast.161, bf16[512,896]{1,0:T(8,128)(2,1)} %copy-done.2, ...), custom_call_target="tpu_custom_call", output_to_operand_aliasing={{0}: (9, {}), {1}: (10, {})} | custom-call | tf_op jit(solution)/shard_map/weight_grads/pallas_call | solution.py:1174
  378.1 3.1 collective-permute-done.46.rest_2_
  382.1 1.7 collective-permute-start.53
  383.8 4.1 hidden.1
  388.8 3.3 output.1
  392.9 3.0 collective-permute-done.51
  395.9 1.7 collective-permute-start.52
  (281 shorter events, 59.2 us)
Async XLA Ops:
  7.2 91.6 %all-reduce.5.cloned.1.call-start = ((), (), s32[]{:S(2)}) async-start(), calls=%async_computation | async-start | bytes 1572864 | tf_op jit(solution)/shard_map/psum | solution.py:1351
  10.8 16.9 %collective-permute-start = (bf16[400,768]{1,0:T(8,128)(2,1)S(1)}, bf16[400,768]{1,0:T(8,128)(2,1)S(1)}, u32[]{:S(2)}, u32[]{:S(2)}) collective-permute-start(bf16[400,768]{1,0:T(8,128)(2,1)S(1)} %pad_maximum_fusion.4), channel_id=1, source_target_pairs={{0,16},{16,0},{1,17},{17,1},{2,18},{18,2},{3,19},{19,3},{4,20},{20... | collective-permute-start | bytes 1843208 | tf_op jit(solution)/shard_map/ppermute | solution.py:1241
  27.8 5.6 %collective-permute-start.1 = (bf16[400,768]{1,0:T(8,128)(2,1)S(1)}, bf16[400,768]{1,0:T(8,128)(2,1)S(1)}, u32[]{:S(2)}, u32[]{:S(2)}) collective-permute-start(bf16[400,768]{1,0:T(8,128)(2,1)S(1)} %collective-permute-done.sent_ref), channel_id=1, source_target_pairs={{0,4},{4,0},{8,12},{12,8},{1,5},{5,1},{9,13},{13,9},{2,6},{6,2},{1... | collective-permute-start | bytes 1843208 | tf_op jit(solution)/shard_map/ppermute | solution.py:1244
  29.1 9.7 %collective-permute-start.2 = (bf16[192,768]{1,0:T(8,128)(2,1)}, bf16[192,768]{1,0:T(8,128)(2,1)}, u32[]{:S(2)}, u32[]{:S(2)}) collective-permute-start(bf16[192,768]{1,0:T(8,128)(2,1)} %constant_dynamic-slice_fusion), channel_id=1, source_target_pairs={{0,16},{16,0},{1,17},{17,1},{2,18},{18,2},{3,19},{19,3},{4,20},{20... | collective-permute-start | bytes 884744 | tf_op jit(solution)/shard_map/ppermute | solution.py:1241
  31.5 39.5 %copy-start = (bf16[256,1664]{1,0:T(8,128)(2,1)}, bf16[256,1664]{1,0:T(8,128)(2,1)S(1)}, u32[]{:S(2)}) copy-start(bf16[256,1664]{1,0:T(8,128)(2,1)S(1)} %pad_maximum_fusion.2.near_out_ref.out_grad_ref) | copy-start | bytes 2555908
  38.8 28.9 %collective-permute-start.9 = (bf16[2,2304,128]{2,1,0:T(8,128)(2,1)S(1)}, bf16[2,2304,128]{2,1,0:T(8,128)(2,1)}, u32[]{:S(2)}, u32[]{:S(2)}) collective-permute-start(bf16[2,2304,128]{2,1,0:T(8,128)(2,1)S(1)} %copy-done.18), channel_id=1, source_target_pairs={{0,16},{16,0},{1,17},{17,1},{2,18},{18,2},{3,19},{19,3},{4,20},{20... | collective-permute-start | bytes 3538952 | tf_op jit(solution)/shard_map/ppermute | solution.py:1241
  40.5 7.5 %collective-permute-start.6 = (bf16[192,768]{1,0:T(8,128)(2,1)}, bf16[192,768]{1,0:T(8,128)(2,1)}, u32[]{:S(2)}, u32[]{:S(2)}) collective-permute-start(bf16[192,768]{1,0:T(8,128)(2,1)} %collective-permute-done.2.out_sent_ref), channel_id=1, source_target_pairs={{0,4},{4,0},{8,12},{12,8},{1,5},{5,1},{9,13},{13,9},{2,6},{6,2},{1... | collective-permute-start | bytes 884744 | tf_op jit(solution)/shard_map/ppermute | solution.py:1244
  40.5 6.1 %collective-permute-start.4 = (bf16[256,256]{1,0:T(8,128)(2,1)}, bf16[256,256]{1,0:T(8,128)(2,1)S(1)}, u32[]{:S(2)}, u32[]{:S(2)}) collective-permute-start(bf16[256,256]{1,0:T(8,128)(2,1)} %get-tuple-element.152.kv0), channel_id=1, source_target_pairs={{0,8},{4,12},{8,0},{12,4},{1,9},{5,13},{9,1},{13,5},{2,10},{6,14},... | collective-permute-start | bytes 393224 | tf_op jit(solution)/shard_map/ppermute | solution.py:1247
  42.0 4.9 %collective-permute-start.3 = (bf16[256,256]{1,0:T(8,128)(2,1)}, bf16[256,256]{1,0:T(8,128)(2,1)S(1)}, u32[]{:S(2)}, u32[]{:S(2)}) collective-permute-start(bf16[256,256]{1,0:T(8,128)(2,1)} %get-tuple-element.152.kv0), channel_id=1, source_target_pairs={{0,4},{4,0},{8,12},{12,8},{1,5},{5,1},{9,13},{13,9},{2,6},{6,2},{1... | collective-permute-start | bytes 393224 | tf_op jit(solution)/shard_map/ppermute | solution.py:1244
  46.6 1.3 collective-permute-start.5
  46.7 39.2 %collective-permute-start.7 = (bf16[256,1664]{1,0:T(8,128)(2,1)S(1)}, bf16[256,1664]{1,0:T(8,128)(2,1)S(1)}, u32[]{:S(2)}, u32[]{:S(2)}) collective-permute-start(bf16[256,1664]{1,0:T(8,128)(2,1)S(1)} %pad_maximum_fusion.2.near_out_ref.out_grad_ref), channel_id=1, source_target_pairs={{0,16},{16,0},{1,17},{17,1},{2,18},{18,2},{3,19},{19,3},{4,20},{20... | collective-permute-start | bytes 2555912 | tf_op jit(solution)/shard_map/ppermute | solution.py:1241
  54.5 141.8 %all-gather.9.cloned.1.call-start = ((), (), s32[]{:S(2)}) async-start(), calls=%async_computation.1 | async-start | bytes 3932160 | tf_op jit(solution)/shard_map/all_gather | solution.py:1421
  67.7 61.0 %collective-permute-start.10 = (bf16[2,2304,128]{2,1,0:T(8,128)(2,1)}, bf16[2,2304,128]{2,1,0:T(8,128)(2,1)}, u32[]{:S(2)}, u32[]{:S(2)}) collective-permute-start(bf16[2,2304,128]{2,1,0:T(8,128)(2,1)} %collective-permute-done.9.rest_0_), channel_id=1, source_target_pairs={{0,8},{4,12},{8,0},{12,4},{1,9},{5,13},{9,1},{13,5},{2,10},{6,14},... | collective-permute-start | bytes 3538952 | tf_op jit(solution)/shard_map/ppermute | solution.py:1247
  69.5 59.8 %collective-permute-start.16 = (bf16[2,2304,128]{2,1,0:T(8,128)(2,1)}, bf16[2,2304,128]{2,1,0:T(8,128)(2,1)}, u32[]{:S(2)}, u32[]{:S(2)}) collective-permute-start(bf16[2,2304,128]{2,1,0:T(8,128)(2,1)} %split_weights.7), channel_id=1, source_target_pairs={{0,16},{16,0},{1,17},{17,1},{2,18},{18,2},{3,19},{19,3},{4,20},{20... | collective-permute-start | bytes 3538952 | tf_op jit(solution)/shard_map/ppermute | solution.py:1241
  98.9 98.5 %copy-start.2 = (bf16[512,896]{1,0:T(8,128)(2,1)}, bf16[512,896]{1,0:T(8,128)(2,1)S(1)}, u32[]{:S(2)}) copy-start(bf16[512,896]{1,0:T(8,128)(2,1)S(1)} %pad_maximum_fusion.1.grads0) | copy-start | bytes 2752516
  98.9 29.8 %collective-permute-start.11 = (bf16[512,896]{1,0:T(8,128)(2,1)S(1)}, bf16[512,896]{1,0:T(8,128)(2,1)S(1)}, u32[]{:S(2)}, u32[]{:S(2)}) collective-permute-start(bf16[512,896]{1,0:T(8,128)(2,1)S(1)} %pad_maximum_fusion.1.grads0), channel_id=1, source_target_pairs={{0,8},{4,12},{8,0},{12,4},{1,9},{5,13},{9,1},{13,5},{2,10},{6,14},... | collective-permute-start | bytes 2752520 | tf_op jit(solution)/shard_map/ppermute | solution.py:1247
  100.5 28.2 %collective-permute-start.12 = (bf16[512,896]{1,0:T(8,128)(2,1)S(1)}, bf16[512,896]{1,0:T(8,128)(2,1)}, u32[]{:S(2)}, u32[]{:S(2)}) collective-permute-start(bf16[512,896]{1,0:T(8,128)(2,1)S(1)} %pad_maximum_fusion.1.grads0), channel_id=1, source_target_pairs={{0,4},{4,0},{8,12},{12,8},{1,5},{5,1},{9,13},{13,9},{2,6},{6,2},{1... | collective-permute-start | bytes 2752520 | tf_op jit(solution)/shard_map/ppermute | solution.py:1244
  106.7 22.0 %collective-permute-start.8 = (bf16[256,1664]{1,0:T(8,128)(2,1)}, bf16[256,1664]{1,0:T(8,128)(2,1)S(1)}, u32[]{:S(2)}, u32[]{:S(2)}) collective-permute-start(bf16[256,1664]{1,0:T(8,128)(2,1)} %get-tuple-element.165.near_ref), channel_id=1, source_target_pairs={{0,16},{16,0},{1,17},{17,1},{2,18},{18,2},{3,19},{19,3},{4,20},{20... | collective-permute-start | bytes 2555912 | tf_op jit(solution)/shard_map/ppermute | solution.py:1241
  128.7 5.3 %collective-permute-start.13 = (bf16[2,2304,128]{2,1,0:T(8,128)(2,1)}, bf16[2,2304,128]{2,1,0:T(8,128)(2,1)}, u32[]{:S(2)}, u32[]{:S(2)}) collective-permute-start(bf16[2,2304,128]{2,1,0:T(8,128)(2,1)} %collective-permute-done.9.rest_0_), channel_id=1, source_target_pairs={{0,4},{4,0},{8,12},{12,8},{1,5},{5,1},{9,13},{13,9},{2,6},{6,2},{1... | collective-permute-start | bytes 3538952 | tf_op jit(solution)/shard_map/ppermute | solution.py:1244
  128.7 68.8 %copy-start.7 = (bf16[512,896]{1,0:T(8,128)(2,1)}, bf16[512,896]{1,0:T(8,128)(2,1)S(1)}, u32[]{:S(2)}) copy-start(bf16[512,896]{1,0:T(8,128)(2,1)S(1)} %collective-permute-done.11.grads2) | copy-start | bytes 2752516
  128.7 5.3 %collective-permute-start.14 = (bf16[2,2304,128]{2,1,0:T(8,128)(2,1)}, bf16[2,2304,128]{2,1,0:T(8,128)(2,1)}, u32[]{:S(2)}, u32[]{:S(2)}) collective-permute-start(bf16[2,2304,128]{2,1,0:T(8,128)(2,1)} %collective-permute-done.10.rest_2_), channel_id=1, source_target_pairs={{0,4},{4,0},{8,12},{12,8},{1,5},{5,1},{9,13},{13,9},{2,6},{6,2},{1... | collective-permute-start | bytes 3538952 | tf_op jit(solution)/shard_map/ppermute | solution.py:1244
  129.3 28.3 %collective-permute-start.17 = (bf16[2,2304,128]{2,1,0:T(8,128)(2,1)}, bf16[2,2304,128]{2,1,0:T(8,128)(2,1)}, u32[]{:S(2)}, u32[]{:S(2)}) collective-permute-start(bf16[2,2304,128]{2,1,0:T(8,128)(2,1)} %collective-permute-done.16.rest_0_), channel_id=1, source_target_pairs={{0,8},{4,12},{8,0},{12,4},{1,9},{5,13},{9,1},{13,5},{2,10},{6,14},... | collective-permute-start | bytes 3538952 | tf_op jit(solution)/shard_map/ppermute | solution.py:1247
  130.8 18.9 %collective-permute-start.15 = (bf16[1,2304,128]{2,1,0:T(8,128)(2,1)}, bf16[1,2304,128]{2,1,0:T(8,128)(2,1)S(1)}, u32[]{:S(2)}, u32[]{:S(2)}) collective-permute-start(bf16[1,2304,128]{2,1,0:T(8,128)(2,1)} %split_weights.6), channel_id=1, source_target_pairs={{0,16},{16,0},{1,17},{17,1},{2,18},{18,2},{3,19},{19,3},{4,20},{20... | collective-permute-start | bytes 1769480 | tf_op jit(solution)/shard_map/ppermute | solution.py:1241
  157.6 94.3 %all-gather.11.cloned.1.call-start = ((), (), s32[]{:S(2)}) async-start(), calls=%async_computation.2 | async-start | bytes 7077888 | tf_op jit(solution)/shard_map/all_gather | solution.py:1409
  158.1 4.0 collective-permute-start.19
  158.1 4.9 %collective-permute-start.20 = (bf16[2,2304,128]{2,1,0:T(8,128)(2,1)}, bf16[2,2304,128]{2,1,0:T(8,128)(2,1)}, u32[]{:S(2)}, u32[]{:S(2)}) collective-permute-start(bf16[2,2304,128]{2,1,0:T(8,128)(2,1)} %collective-permute-done.17.rest_2_), channel_id=1, source_target_pairs={{0,4},{4,0},{8,12},{12,8},{1,5},{5,1},{9,13},{13,9},{2,6},{6,2},{1... | collective-permute-start | bytes 3538952 | tf_op jit(solution)/shard_map/ppermute | solution.py:1244
  158.6 21.9 %collective-permute-start.21 = (bf16[1,2304,128]{2,1,0:T(8,128)(2,1)}, bf16[1,2304,128]{2,1,0:T(8,128)(2,1)}, u32[]{:S(2)}, u32[]{:S(2)}) collective-permute-start(bf16[1,2304,128]{2,1,0:T(8,128)(2,1)} %copy-done.30), channel_id=1, source_target_pairs={{0,8},{4,12},{8,0},{12,4},{1,9},{5,13},{9,1},{13,5},{2,10},{6,14},... | collective-permute-start | bytes 1769480 | tf_op jit(solution)/shard_map/ppermute | solution.py:1247
  160.2 20.4 %collective-permute-start.18 = (bf16[1,2304,128]{2,1,0:T(8,128)(2,1)}, bf16[1,2304,128]{2,1,0:T(8,128)(2,1)}, u32[]{:S(2)}, u32[]{:S(2)}) collective-permute-start(bf16[1,2304,128]{2,1,0:T(8,128)(2,1)} %copy-done.30), channel_id=1, source_target_pairs={{0,4},{4,0},{8,12},{12,8},{1,5},{5,1},{9,13},{13,9},{2,6},{6,2},{1... | collective-permute-start | bytes 1769480 | tf_op jit(solution)/shard_map/ppermute | solution.py:1244
  180.6 2.2 collective-permute-start.22
  196.3 127.1 %all-gather.13.cloned.1.call-start = ((), (), s32[]{:S(2)}) async-start(), calls=%async_computation.3 | async-start | bytes 7077888 | tf_op jit(solution)/shard_map/all_gather | solution.py:1409
  196.3 2.5 collective-permute-start.24
  196.5 30.0 %collective-permute-start.23 = (bf16[256,1664]{1,0:T(8,128)(2,1)}, bf16[256,1664]{1,0:T(8,128)(2,1)}, u32[]{:S(2)}, u32[]{:S(2)}) collective-permute-start(bf16[256,1664]{1,0:T(8,128)(2,1)} %get-tuple-element.190), channel_id=1, source_target_pairs={{0,16},{16,0},{1,17},{17,1},{2,18},{18,2},{3,19},{19,3},{4,20},{20... | collective-permute-start | bytes 2555912 | tf_op jit(solution)/shard_map/ppermute | solution.py:1241
  229.3 10.3 %collective-permute-start.27 = (bf16[64,1664]{1,0:T(8,128)(2,1)}, bf16[64,1664]{1,0:T(8,128)(2,1)S(1)}, u32[]{:S(2)}, u32[]{:S(2)}) collective-permute-start(bf16[64,1664]{1,0:T(8,128)(2,1)} %get-tuple-element.198), channel_id=1, source_target_pairs={{3,0},{0,1},{1,2},{2,3},{7,4},{4,5},{5,6},{6,7},{11,8},{8,9},{9,10... | collective-permute-start | bytes 638984 | tf_op jit(solution)/shard_map/ppermute | solution.py:1250
  230.9 16.5 %collective-permute-start.26 = (bf16[64,1664]{1,0:T(8,128)(2,1)}, bf16[64,1664]{1,0:T(8,128)(2,1)S(1)}, u32[]{:S(2)}, u32[]{:S(2)}) collective-permute-start(bf16[64,1664]{1,0:T(8,128)(2,1)} %get-tuple-element.197), channel_id=1, source_target_pairs={{2,0},{3,1},{0,2},{1,3},{6,4},{7,5},{4,6},{5,7},{10,8},{11,9},{8,1... | collective-permute-start | bytes 638984 | tf_op jit(solution)/shard_map/ppermute | solution.py:1250
  233.5 13.8 %collective-permute-start.25 = (bf16[64,1664]{1,0:T(8,128)(2,1)}, bf16[64,1664]{1,0:T(8,128)(2,1)S(1)}, u32[]{:S(2)}, u32[]{:S(2)}) collective-permute-start(bf16[64,1664]{1,0:T(8,128)(2,1)} %get-tuple-element.196), channel_id=1, source_target_pairs={{1,0},{2,1},{3,2},{0,3},{5,4},{6,5},{7,6},{4,7},{9,8},{10,9},{11,1... | collective-permute-start | bytes 638984 | tf_op jit(solution)/shard_map/ppermute | solution.py:1250
  251.9 113.4 %all-gather.15.cloned.1.call-start = ((), (), s32[]{:S(2)}) async-start(), calls=%async_computation.4 | async-start | bytes 3538944 | tf_op jit(solution)/shard_map/all_gather | solution.py:1409
  251.9 28.1 %collective-permute-start.31 = (bf16[256,1536]{1,0:T(8,128)(2,1)S(1)}, bf16[256,1536]{1,0:T(8,128)(2,1)S(1)}, u32[]{:S(2)}, u32[]{:S(2)}) collective-permute-start(bf16[256,1536]{1,0:T(8,128)(2,1)S(1)} %copy-done.51), channel_id=1, source_target_pairs={{0,16},{16,0},{1,17},{17,1},{2,18},{18,2},{3,19},{19,3},{4,20},{20... | collective-permute-start | bytes 2359304 | tf_op jit(solution)/shard_map/ppermute | solution.py:1241
  253.5 26.4 %collective-permute-start.28 = (bf16[64,1664]{1,0:T(8,128)(2,1)S(1)}, bf16[64,1664]{1,0:T(8,128)(2,1)S(1)}, u32[]{:S(2)}, u32[]{:S(2)}) collective-permute-start(bf16[64,1664]{1,0:T(8,128)(2,1)S(1)} %add_convert_fusion.2.rest_0_), channel_id=1, source_target_pairs={{1,0},{2,1},{3,2},{0,3},{5,4},{6,5},{7,6},{4,7},{9,8},{10,9},{11,1... | collective-permute-start | bytes 638984 | tf_op jit(solution)/shard_map/ppermute | solution.py:1250
  256.8 23.1 %collective-permute-start.29 = (bf16[64,1664]{1,0:T(8,128)(2,1)S(1)}, bf16[64,1664]{1,0:T(8,128)(2,1)S(1)}, u32[]{:S(2)}, u32[]{:S(2)}) collective-permute-start(bf16[64,1664]{1,0:T(8,128)(2,1)S(1)} %add_convert_fusion.2.rest_0_), channel_id=1, source_target_pairs={{2,0},{3,1},{0,2},{1,3},{6,4},{7,5},{4,6},{5,7},{10,8},{11,9},{8,1... | collective-permute-start | bytes 638984 | tf_op jit(solution)/shard_map/ppermute | solution.py:1250
  256.8 23.1 %collective-permute-start.30 = (bf16[64,1664]{1,0:T(8,128)(2,1)S(1)}, bf16[64,1664]{1,0:T(8,128)(2,1)S(1)}, u32[]{:S(2)}, u32[]{:S(2)}) collective-permute-start(bf16[64,1664]{1,0:T(8,128)(2,1)S(1)} %add_convert_fusion.2.rest_0_), channel_id=1, source_target_pairs={{3,0},{0,1},{1,2},{2,3},{7,4},{4,5},{5,6},{6,7},{11,8},{8,9},{9,10... | collective-permute-start | bytes 638984 | tf_op jit(solution)/shard_map/ppermute | solution.py:1250
  283.7 16.9 %collective-permute-start.34 = (bf16[64,1536]{1,0:T(8,128)(2,1)}, bf16[64,1536]{1,0:T(8,128)(2,1)S(1)}, u32[]{:S(2)}, u32[]{:S(2)}) collective-permute-start(bf16[64,1536]{1,0:T(8,128)(2,1)} %get-tuple-element.218), channel_id=1, source_target_pairs={{3,0},{0,1},{1,2},{2,3},{7,4},{4,5},{5,6},{6,7},{11,8},{8,9},{9,10... | collective-permute-start | bytes 589832 | tf_op jit(solution)/shard_map/ppermute | solution.py:1250
  285.9 14.7 %collective-permute-start.33 = (bf16[64,1536]{1,0:T(8,128)(2,1)}, bf16[64,1536]{1,0:T(8,128)(2,1)S(1)}, u32[]{:S(2)}, u32[]{:S(2)}) collective-permute-start(bf16[64,1536]{1,0:T(8,128)(2,1)} %get-tuple-element.217), channel_id=1, source_target_pairs={{2,0},{3,1},{0,2},{1,3},{6,4},{7,5},{4,6},{5,7},{10,8},{11,9},{8,1... | collective-permute-start | bytes 589832 | tf_op jit(solution)/shard_map/ppermute | solution.py:1250
  287.5 13.1 %collective-permute-start.32 = (bf16[64,1536]{1,0:T(8,128)(2,1)}, bf16[64,1536]{1,0:T(8,128)(2,1)S(1)}, u32[]{:S(2)}, u32[]{:S(2)}) collective-permute-start(bf16[64,1536]{1,0:T(8,128)(2,1)} %get-tuple-element.216), channel_id=1, source_target_pairs={{1,0},{2,1},{3,2},{0,3},{5,4},{6,5},{7,6},{4,7},{9,8},{10,9},{11,1... | collective-permute-start | bytes 589832 | tf_op jit(solution)/shard_map/ppermute | solution.py:1250
  300.8 1.8 collective-permute-start.35
  304.5 4.1 collective-permute-start.37
  304.8 17.8 %collective-permute-start.39 = (bf16[64,1536]{1,0:T(8,128)(2,1)S(1)}, bf16[64,1536]{1,0:T(8,128)(2,1)S(1)}, u32[]{:S(2)}, u32[]{:S(2)}) collective-permute-start(bf16[64,1536]{1,0:T(8,128)(2,1)S(1)} %add_convert_fusion.4), channel_id=1, source_target_pairs={{0,1},{1,0},{2,3},{3,2},{4,5},{5,4},{6,7},{7,6},{8,9},{9,8},{10,11... | collective-permute-start | bytes 589832 | tf_op jit(solution)/shard_map/ppermute | solution.py:1526
  310.9 12.4 %collective-permute-start.38 = (bf16[224,768]{1,0:T(8,128)(2,1)S(1)}, bf16[224,768]{1,0:T(8,128)(2,1)S(1)}, u32[]{:S(2)}, u32[]{:S(2)}) collective-permute-start(bf16[224,768]{1,0:T(8,128)(2,1)S(1)} %fusion.13), channel_id=1, source_target_pairs={{0,16},{16,0},{1,17},{17,1},{2,18},{18,2},{3,19},{19,3},{4,20},{20... | collective-permute-start | bytes 1032200 | tf_op jit(solution)/shard_map/ppermute | solution.py:1241
  313.0 5.3 %collective-permute-start.36 = (bf16[256,256]{1,0:T(8,128)(2,1)S(1)}, bf16[256,256]{1,0:T(8,128)(2,1)S(1)}, u32[]{:S(2)}, u32[]{:S(2)}) collective-permute-start(bf16[256,256]{1,0:T(8,128)(2,1)S(1)} %fusion.21), channel_id=1, source_target_pairs={{0,8},{4,12},{8,0},{12,4},{1,9},{5,13},{9,1},{13,5},{2,10},{6,14},... | collective-permute-start | bytes 393224 | tf_op jit(solution)/shard_map/ppermute | solution.py:1247
  323.4 31.9 %collective-permute-start.42 = (bf16[64,1536]{1,0:T(8,128)(2,1)}, bf16[64,1536]{1,0:T(8,128)(2,1)}, u32[]{:S(2)}, u32[]{:S(2)}) collective-permute-start(bf16[64,1536]{1,0:T(8,128)(2,1)} %get-tuple-element.241), channel_id=1, source_target_pairs={{3,0},{0,1},{1,2},{2,3},{7,4},{4,5},{5,6},{6,7},{11,8},{8,9},{9,10... | collective-permute-start | bytes 589832 | tf_op jit(solution)/shard_map/ppermute | solution.py:1250
  325.9 29.4 %collective-permute-start.41 = (bf16[64,1536]{1,0:T(8,128)(2,1)}, bf16[64,1536]{1,0:T(8,128)(2,1)}, u32[]{:S(2)}, u32[]{:S(2)}) collective-permute-start(bf16[64,1536]{1,0:T(8,128)(2,1)} %get-tuple-element.240), channel_id=1, source_target_pairs={{2,0},{3,1},{0,2},{1,3},{6,4},{7,5},{4,6},{5,7},{10,8},{11,9},{8,1... | collective-permute-start | bytes 589832 | tf_op jit(solution)/shard_map/ppermute | solution.py:1250
  327.1 28.2 %collective-permute-start.40 = (bf16[64,1536]{1,0:T(8,128)(2,1)}, bf16[64,1536]{1,0:T(8,128)(2,1)}, u32[]{:S(2)}, u32[]{:S(2)}) collective-permute-start(bf16[64,1536]{1,0:T(8,128)(2,1)} %get-tuple-element.239), channel_id=1, source_target_pairs={{1,0},{2,1},{3,2},{0,3},{5,4},{6,5},{7,6},{4,7},{9,8},{10,9},{11,1... | collective-permute-start | bytes 589832 | tf_op jit(solution)/shard_map/ppermute | solution.py:1250
  331.7 25.1 %collective-permute-start.43 = (bf16[2,384,640]{2,1,0:T(8,128)(2,1)}, bf16[2,384,640]{2,1,0:T(8,128)(2,1)}, u32[]{:S(2)}, u32[]{:S(2)}) collective-permute-start(bf16[2,384,640]{2,1,0:T(8,128)(2,1)} %dynamic-slice_convert_fusion), channel_id=1, source_target_pairs={{0,4},{4,0},{8,12},{12,8},{1,5},{5,1},{9,13},{13,9},{2,6},{6,2},{1... | collective-permute-start | bytes 2949128 | tf_op jit(solution)/shard_map/ppermute | solution.py:1244
  332.5 28.3 %collective-permute-start.44 = (bf16[128,1536]{1,0:T(8,128)(2,1)}, bf16[128,1536]{1,0:T(8,128)(2,1)}, u32[]{:S(2)}, u32[]{:S(2)}) collective-permute-start(bf16[128,1536]{1,0:T(8,128)(2,1)} %maximum_select_fusion.3.rest_0_), channel_id=1, source_target_pairs={{0,2},{1,3},{2,0},{3,1},{4,6},{5,7},{6,4},{7,5},{8,10},{9,11},{10,... | collective-permute-start | bytes 1179656 | tf_op jit(solution)/shard_map/ppermute | solution.py:1588
  360.9 20.3 %collective-permute-start.49 = (bf16[384,640]{1,0:T(8,128)(2,1)S(1)}, bf16[384,640]{1,0:T(8,128)(2,1)S(1)}, u32[]{:S(2)}, u32[]{:S(2)}) collective-permute-start(bf16[384,640]{1,0:T(8,128)(2,1)S(1)} %fusion.9), channel_id=1, source_target_pairs={{0,16},{16,0},{1,17},{17,1},{2,18},{18,2},{3,19},{19,3},{4,20},{20... | collective-permute-start | bytes 1474568 | tf_op jit(solution)/shard_map/ppermute | solution.py:1241
  362.2 18.9 %collective-permute-start.48 = (bf16[224,768]{1,0:T(8,128)(2,1)}, bf16[224,768]{1,0:T(8,128)(2,1)S(1)}, u32[]{:S(2)}, u32[]{:S(2)}) collective-permute-start(bf16[224,768]{1,0:T(8,128)(2,1)} %convert_element_type.160), channel_id=1, source_target_pairs={{0,8},{4,12},{8,0},{12,4},{1,9},{5,13},{9,1},{13,5},{2,10},{6,14},... | collective-permute-start | bytes 1032200 | tf_op jit(solution)/shard_map/ppermute | solution.py:1247
  362.5 15.6 %collective-permute-start.45 = (bf16[64,1536]{1,0:T(8,128)(2,1)S(1)}, bf16[64,1536]{1,0:T(8,128)(2,1)}, u32[]{:S(2)}, u32[]{:S(2)}) collective-permute-start(bf16[64,1536]{1,0:T(8,128)(2,1)S(1)} %add_convert_fusion.3.rest_0_), channel_id=1, source_target_pairs={{1,0},{2,1},{3,2},{0,3},{5,4},{6,5},{7,6},{4,7},{9,8},{10,9},{11,1... | collective-permute-start | bytes 589832 | tf_op jit(solution)/shard_map/ppermute | solution.py:1250
  363.8 17.4 %collective-permute-start.46 = (bf16[64,1536]{1,0:T(8,128)(2,1)S(1)}, bf16[64,1536]{1,0:T(8,128)(2,1)}, u32[]{:S(2)}, u32[]{:S(2)}) collective-permute-start(bf16[64,1536]{1,0:T(8,128)(2,1)S(1)} %add_convert_fusion.3.rest_0_), channel_id=1, source_target_pairs={{2,0},{3,1},{0,2},{1,3},{6,4},{7,5},{4,6},{5,7},{10,8},{11,9},{8,1... | collective-permute-start | bytes 589832 | tf_op jit(solution)/shard_map/ppermute | solution.py:1250
  364.0 17.2 %collective-permute-start.47 = (bf16[64,1536]{1,0:T(8,128)(2,1)S(1)}, bf16[64,1536]{1,0:T(8,128)(2,1)}, u32[]{:S(2)}, u32[]{:S(2)}) collective-permute-start(bf16[64,1536]{1,0:T(8,128)(2,1)S(1)} %add_convert_fusion.3.rest_0_), channel_id=1, source_target_pairs={{3,0},{0,1},{1,2},{2,3},{7,4},{4,5},{5,6},{6,7},{11,8},{8,9},{9,10... | collective-permute-start | bytes 589832 | tf_op jit(solution)/shard_map/ppermute | solution.py:1250
  382.1 15.5 %collective-permute-start.53 = (bf16[384,640]{1,0:T(8,128)(2,1)}, bf16[384,640]{1,0:T(8,128)(2,1)}, u32[]{:S(2)}, u32[]{:S(2)}) collective-permute-start(bf16[384,640]{1,0:T(8,128)(2,1)} %fusion.5), channel_id=1, source_target_pairs={{0,8},{4,12},{8,0},{12,4},{1,9},{5,13},{9,1},{13,5},{2,10},{6,14},... | collective-permute-start | bytes 1474568 | tf_op jit(solution)/shard_map/ppermute | solution.py:1247
  388.7 3.4 collective-permute-start.50
  392.2 3.7 collective-permute-start.51
  392.6 7.5 %collective-permute-start.55 = (bf16[224,768]{1,0:T(8,128)(2,1)S(1)}, bf16[224,768]{1,0:T(8,128)(2,1)S(1)}, u32[]{:S(2)}, u32[]{:S(2)}) collective-permute-start(bf16[224,768]{1,0:T(8,128)(2,1)S(1)} %add_convert_fusion.1), channel_id=1, source_target_pairs={{0,4},{4,0},{8,12},{12,8},{1,5},{5,1},{9,13},{13,9},{2,6},{6,2},{1... | collective-permute-start | bytes 1032200 | tf_op jit(solution)/shard_map/ppermute | solution.py:1244
  395.9 3.6 collective-permute-start.52
  398.8 3.8 collective-permute-start.54
  (49 other events, 344.7 us)
Sparse Core Ops, SparseCore 0:
  54.6 44.1 all-reduce.4
  157.7 34.8 all-gather.8
  196.4 55.4 all-gather.10
  253.6 52.8 all-gather.12
  323.5 31.2 all-gather.14

commit v7 on v6

--- a/solution.py
+++ b/solution.py
@@ -1110,9 +1110,10 @@
 
     @pl.when((step == 0) & (side == 0))
     def _():
-        for k in range(4):
-            for b in range(4):
-                span = pl.ds(b * 128, 128)
+        @pl.loop(0, 4)
+        def _(b):
+            span = pl.ds(pl.multiple_of(b * 128, 128), 128)
+            for k in range(4):
                 hot = jnp.concatenate(
                     [
                         jnp.where(
@@ -1351,7 +1352,9 @@
     attended = lax.psum(attn_part, "tp")
     far_zero, packs[1] = tie((far_zero, packs[1]))
     far_one = across(packs[1])
-    attended, far_out, gate_up_mine = tie((attended, far_out, gate_up_mine))
+    attended, far_out, gate_up_mine, packs[2] = tie(
+        (attended, far_out, gate_up_mine, packs[2])
+    )
     zero_along = along(far_zero)
     early = jnp.concatenate(
         [

time: 418 us -> 419 us (level)
  transfers between devices with their start and end apart: 61 -> 61, of which waited for: 25 -> 24; matrix products, arithmetic and copies ran while one was open for 8% -> 8% of each run, Pallas kernels for 39% -> 40%
where the time goes in v7:
time: 419 us; the launch traced here: 412 us
  Pallas kernels  163 us (39%)
  waiting for transfers between devices  127 us (30%)
  starting transfers between devices  59 us (14%)
  local copies, waits for them, and re-layouts  24.2 us (6%)
  other arithmetic  17.3 us (4%)
  between operations  15.2 us (4%)
  matrix products  6.76 us (2%)
    ppermute x12, waiting for transfers between devices, across(): return lax.ppermute(value, 'fsdp', [(0, 1), (1, 0)])  66 us
    pallas_call x3, Pallas kernels, run_weight_grads(): pl.pallas_call(functools.partial(weight_grad_kernel, first=first, steps=s...  56.4 us
    pallas_call x3, Pallas kernels, run_experts(): pl.pallas_call(functools.partial(expert_kernel, first=first, last=last, e...  44.7 us
    pallas_call x9, Pallas kernels, single(): pl.pallas_call(kernel, out_shape=tuple((jax.ShapeDtypeStruct(shape, kind)...  41.6 us
    ppermute x15, starting transfers between devices, from_tp(): lax.ppermute(value, 'tp', [((i + step) % tp_size, i) for i in range(tp_si...  23 us
    ppermute x9, waiting for transfers between devices, along(): return lax.ppermute(value, 'ctx', [(i, i ^ 2) for i in range(4)])  20.9 us
    pallas_call x4, Pallas kernels, split_weights(): pl.pallas_call(split_plain_kernel if down is None else split_kernel, out_...  20.5 us
    ppermute x12, starting transfers between devices, across(): return lax.ppermute(value, 'fsdp', [(0, 1), (1, 0)])  16.6 us
  transfers between devices with their start and end apart: 61, of which 24 were waited for; matrix products, arithmetic and copies ran while one was open for 8% of the time, Pallas kernels for 40%

profile of v7, /device:TPU:0, one launch (start us, length us, event | category | flops | bytes accessed | tf_op | source)
XLA Modules:
  0.0 412.3 jit_solution(532365444137092070)
XLA Ops:
  10.8 3.0 collective-permute-start
  13.9 2.3 split_weights.4
  18.3 9.4 %collective-permute-done.sent_ref = bf16[400,768]{1,0:T(8,128)(2,1)S(1)} collective-permute-done((bf16[400,768]{1,0:T(8,128)(2,1)S(1)}, bf16[400,768]{1,0:T(8,128)(2,1)S(1)}, u32[]{:S(2)}, u32[]{:S(2)}) %collective-permute-start) | collective-permute-done | bytes 614432 | tf_op jit(solution)/shard_map/ppermute | solution.py:1242
  29.1 1.7 collective-permute-start.2
  34.2 4.5 %before.1 = (bf16[256,1536]{1,0:T(8,128)(2,1)}, bf16[256,384]{1,0:T(8,128)(2,1)}, bf16[256,256]{1,0:T(8,128)(2,1)}, bf16[768,768]{1,0:T(8,128)(2,1)}, f32[16,1536]{1,0:T(8,128)}, /*index=5*/f32[2,256,128]{2,1,0:T(8,128)}) custom-call(s32[3]{0:T(128)} %pad_add_fusion.place_ref, s32[2,4]{1,0:T(2,128)} %bitcast.205, bf16[256,1536]{1,0:T(8,128)(2,1)} %bitcast.164, ...), custom_call_target="tpu_custom_call" | custom-call | tf_op jit(solution)/shard_map/before/pallas_call | solution.py:431
  38.8 1.7 collective-permute-start.9
  40.5 1.5 collective-permute-start.4
  42.3 4.4 %collective-permute-done.4.kv2 = bf16[256,256]{1,0:T(8,128)(2,1)S(1)} collective-permute-done((bf16[256,256]{1,0:T(8,128)(2,1)}, bf16[256,256]{1,0:T(8,128)(2,1)S(1)}, u32[]{:S(2)}, u32[]{:S(2)}) %collective-permute-start.4) | collective-permute-done | bytes 131104 | tf_op jit(solution)/shard_map/ppermute | solution.py:1248
  48.6 5.8 %attend.1 = (bf16[256,384]{1,0:T(8,128)(2,1)}, f32[4,384,512]{2,1,0:T(8,128)}, bf16[384,768]{1,0:T(8,128)(2,1)}, bf16[256,1536]{1,0:T(8,128)(2,1)}) custom-call(s32[3]{0:T(128)} %pad_add_fusion.place_ref, s32[2,4]{1,0:T(2,128)} %bitcast.206, bf16[256,384]{1,0:T(8,128)(2,1)} %get-tuple-element.149.query_ref, bf16[256,256]{1,0:T(8,128)(2,1)} %get-tuple-element.153.kv0, ...), custom_call_target="tpu_custom_call" | custom-call | tf_op jit(solution)/shard_map/attend/pallas_call | solution.py:431
  55.0 2.2 split_weights.7
  57.2 10.5 %collective-permute-done.9.rest_0_ = bf16[2,2304,128]{2,1,0:T(8,128)(2,1)} collective-permute-done((bf16[2,2304,128]{2,1,0:T(8,128)(2,1)S(1)}, bf16[2,2304,128]{2,1,0:T(8,128)(2,1)}, u32[]{:S(2)}, u32[]{:S(2)}) %collective-permute-start.9) | collective-permute-done | bytes 1179680 | tf_op jit(solution)/shard_map/ppermute | solution.py:1242
  67.7 1.8 collective-permute-start.10
  69.5 1.5 collective-permute-start.16
  71.0 2.0 split_weights.6
  73.0 14.0 %split_weights.5 = bf16[20,1536,128]{2,1,0:T(8,128)(2,1)} custom-call(s32[1]{0:T(128)} %bitcast.11.base_ref, bf16[40,1536,128]{2,1,0:T(8,128)(2,1)} %bitcast.153), custom_call_target="tpu_custom_call" | custom-call | tf_op jit(solution)/shard_map/split_weights/pallas_call | solution.py:498
  87.1 11.7 %all-reduce.5.cloned.1.call-done.attended_ref = bf16[256,1536]{1,0:T(8,128)(2,1)} async-done(((bf16[256,1536]{1,0:T(8,128)(2,1)}), bf16[256,1536]{1,0:T(8,128)(2,1)}) %all-reduce.5.cloned.1.call-update) | async-done | bytes 786448 | tf_op jit(solution)/shard_map/psum | solution.py:1352
  98.9 1.5 collective-permute-start.11
  100.5 4.3 %after.1 = (f32[256,1536]{1,0:T(8,128)}, bf16[256,1664]{1,0:T(8,128)(2,1)}, f32[256,128]{1,0:T(8,128)}) custom-call(s32[3]{0:T(128)} %pad_add_fusion.place_ref, bf16[256,1536]{1,0:T(8,128)(2,1)} %bitcast.165, f32[16,1536]{1,0:T(8,128)} %get-tuple-element.147.gains_ref, bf16[784,768]{1,0:T(8,128)(2,1)} %pad_maximum_fusion.small_ref, ...), custom_call_target="tpu_custom_call" | custom-call | tf_op jit(solution)/shard_map/after/pallas_call | solution.py:431
  104.7 1.5 collective-permute-start.8
  109.9 18.8 %collective-permute-done.8.far_ref = bf16[256,1664]{1,0:T(8,128)(2,1)S(1)} collective-permute-done((bf16[256,1664]{1,0:T(8,128)(2,1)}, bf16[256,1664]{1,0:T(8,128)(2,1)S(1)}, u32[]{:S(2)}, u32[]{:S(2)}) %collective-permute-start.8) | collective-permute-done | bytes 852000 | tf_op jit(solution)/shard_map/ppermute | solution.py:1242
  129.3 1.5 collective-permute-start.17
  134.0 15.7 %experts.3 = (bf16[4,2,128,384]{3,2,1,0:T(8,128)(2,1)}, bf16[512,1536]{1,0:T(8,128)(2,1)}, bf16[512,1664]{1,0:T(8,128)(2,1)}) custom-call(s32[3]{0:T(128)} %pad_add_fusion.place_ref, bf16[256,1664]{1,0:T(8,128)(2,1)} %get-tuple-element.167.near_ref, bf16[256,1664]{1,0:T(8,128)(2,1)} %copy-done.4, bf16[256,1664]{1,0:T(8,128)(2,1)} %copy-done, ...), custom_call_target="tpu_custom_call" | custom-call | tf_op jit(solution)/shard_map/experts/pallas_call | solution.py:885
  149.8 7.8 %collective-permute-done.17.rest_2_ = bf16[2,2304,128]{2,1,0:T(8,128)(2,1)} collective-permute-done((bf16[2,2304,128]{2,1,0:T(8,128)(2,1)}, bf16[2,2304,128]{2,1,0:T(8,128)(2,1)}, u32[]{:S(2)}, u32[]{:S(2)}) %collective-permute-start.17) | collective-permute-done | bytes 1179680 | tf_op jit(solution)/shard_map/ppermute | solution.py:1248
  158.4 1.5 collective-permute-start.21
  159.9 1.9 collective-permute-done.19.rest_1_
  162.9 16.4 %experts.4 = (bf16[4,2,128,384]{3,2,1,0:T(8,128)(2,1)}, bf16[512,1536]{1,0:T(8,128)(2,1)}, bf16[512,1664]{1,0:T(8,128)(2,1)}) custom-call(s32[3]{0:T(128)} %pad_add_fusion.place_ref, bf16[256,1664]{1,0:T(8,128)(2,1)} %get-tuple-element.167.near_ref, bf16[256,1664]{1,0:T(8,128)(2,1)} %copy-done.4, bf16[256,1664]{1,0:T(8,128)(2,1)} %copy-done, ...), custom_call_target="tpu_custom_call" | custom-call | tf_op jit(solution)/shard_map/experts/pallas_call | solution.py:885
  180.1 2.3 collective-permute-done.22.rest_3_
  183.2 12.6 %experts.5 = (bf16[4,1,128,384]{3,2,1,0:T(8,128)(2,1)}, f32[256,1536]{1,0:T(8,128)}, f32[256,1664]{1,0:T(8,128)}, bf16[256,1536]{1,0:T(8,128)(2,1)}, bf16[256,1664]{1,0:T(8,128)(2,1)}) custom-call(s32[3]{0:T(128)} %pad_add_fusion.place_ref, bf16[256,1664]{1,0:T(8,128)(2,1)} %get-tuple-element.167.near_ref, bf16[256,1664]{1,0:T(8,128)(2,1)} %copy-done.4, ...), custom_call_target="tpu_custom_call" | custom-call | tf_op jit(solution)/shard_map/experts/pallas_call | solution.py:885
  200.0 26.1 %collective-permute-done.23.got_ref = bf16[256,1664]{1,0:T(8,128)(2,1)} collective-permute-done((bf16[256,1664]{1,0:T(8,128)(2,1)}, bf16[256,1664]{1,0:T(8,128)(2,1)}, u32[]{:S(2)}, u32[]{:S(2)}) %collective-permute-start.23) | collective-permute-done | bytes 852000 | tf_op jit(solution)/shard_map/ppermute | solution.py:1242
  226.1 2.9 join.2
  229.0 1.3 collective-permute-start.27
  230.3 2.9 collective-permute-start.26
  234.3 5.0 %collective-permute-done.27 = bf16[64,1664]{1,0:T(8,128)(2,1)S(1)} collective-permute-done((bf16[64,1664]{1,0:T(8,128)(2,1)}, bf16[64,1664]{1,0:T(8,128)(2,1)S(1)}, u32[]{:S(2)}, u32[]{:S(2)}) %collective-permute-start.27) | collective-permute-done | bytes 213024 | tf_op jit(solution)/shard_map/ppermute | solution.py:1251
  239.3 7.8 %collective-permute-done.26 = bf16[64,1664]{1,0:T(8,128)(2,1)S(1)} collective-permute-done((bf16[64,1664]{1,0:T(8,128)(2,1)}, bf16[64,1664]{1,0:T(8,128)(2,1)S(1)}, u32[]{:S(2)}, u32[]{:S(2)}) %collective-permute-start.26) | collective-permute-done | bytes 213024 | tf_op jit(solution)/shard_map/ppermute | solution.py:1251
  248.1 3.2 all-gather.11.cloned.1.call-done
  251.4 1.5 collective-permute-start.31
  253.0 3.3 collective-permute-start.28
  256.3 1.3 collective-permute-start.30
  258.2 21.9 %weight_grads.3 = (f32[2,4,5,1536,128]{4,3,2,1,0:T(8,128)}, f32[2,4,5,128,768]{4,3,2,1,0:T(8,128)}, f32[8,128]{1,0:T(8,128)}) custom-call(s32[3]{0:T(128)} %pad_add_fusion.place_ref, bf16[4,512,768]{2,1,0:T(8,128)(2,1)} %bitcast.159, bf16[512,896]{1,0:T(8,128)(2,1)} %copy-done.2, bf16[512,896]{1,0:T(8,128)(2,1)} %collective-permute-done.12.grads1, ...), custom_call_target="tpu_custom_call" | custom-call | tf_op jit(solution)/shard_map/weight_grads/pallas_call | solution.py:1175
  281.1 2.7 join.3
  283.8 2.3 collective-permute-start.34
  287.0 1.5 collective-permute-start.32
  288.6 10.2 %back.1 = (f32[256,1536]{1,0:T(8,128)}, bf16[256,1536]{1,0:T(8,128)(2,1)}, bf16[256,128]{1,0:T(8,128)(2,1)}, f32[8,1536]{1,0:T(8,128)}, bf16[256,384]{1,0:T(8,12...) custom-call(s32[3]{0:T(128)} %pad_add_fusion.place_ref, f32[256,1536]{1,0:T(8,128)} %get-tuple-element.160.mixed_ref, ...), custom_call_target="tpu_custom_call" | custom-call | tf_op jit(solution)/shard_map/back/pallas_call | solution.py:431
  304.3 4.5 %collective-permute-start.39 = (bf16[64,1536]{1,0:T(8,128)(2,1)S(1)}, bf16[64,1536]{1,0:T(8,128)(2,1)S(1)}, u32[]{:S(2)}, u32[]{:S(2)}) collective-permute-start(bf16[64,1536]{1,0:T(8,128)(2,1)S(1)} %add_convert_fusion.4), channel_id=1, source_target_pairs={{0,1},{1,0},{2,3},{3,2},{4,5},{5,4},{6,7},{7,6},{8,9},{9,8},{10,11... | collective-permute-start | bytes 589832 | tf_op jit(solution)/shard_map/ppermute | solution.py:1529
  311.1 1.3 collective-permute-start.38
  312.7 5.0 %collective-permute-done.36.along_ref = bf16[256,256]{1,0:T(8,128)(2,1)S(1)} collective-permute-done((bf16[256,256]{1,0:T(8,128)(2,1)S(1)}, bf16[256,256]{1,0:T(8,128)(2,1)S(1)}, u32[]{:S(2)}, u32[]{:S(2)}) %collective-permute-start.36) | collective-permute-done | bytes 131104 | tf_op jit(solution)/shard_map/ppermute | solution.py:1248
  318.4 3.8 last.1
  322.9 2.4 collective-permute-start.42
  325.3 1.3 collective-permute-start.41
  326.6 1.4 collective-permute-start.40
  328.0 2.1 fusion.34
  332.9 21.2 %weight_grads.4 = (f32[2,4,5,1536,128]{4,3,2,1,0:T(8,128)}, f32[2,4,5,128,768]{4,3,2,1,0:T(8,128)}, f32[8,128]{1,0:T(8,128)}) custom-call(s32[3]{0:T(128)} %pad_add_fusion.place_ref, bf16[4,512,768]{2,1,0:T(8,128)(2,1)} %bitcast.160, bf16[512,896]{1,0:T(8,128)(2,1)} %copy-done.2, ...), custom_call_target="tpu_custom_call", output_to_operand_aliasing={{0}: (9, {}), {1}: (10, {})} | custom-call | tf_op jit(solution)/shard_map/weight_grads/pallas_call | solution.py:1175
  354.1 1.3 fusion.3
  355.4 1.4 add_convert_fusion.3.rest_0_
  356.9 1.4 convert_add_fusion
  358.3 1.9 collective-permute-done.44.rest_1_
  362.5 1.6 collective-permute-start.45
  365.7 13.3 %weight_grads.5 = (f32[2,4,5,1536,128]{4,3,2,1,0:T(8,128)}, f32[2,4,5,128,768]{4,3,2,1,0:T(8,128)}, f32[8,128]{1,0:T(8,128)}) custom-call(s32[3]{0:T(128)} %pad_add_fusion.place_ref, bf16[4,512,768]{2,1,0:T(8,128)(2,1)} %bitcast.161, bf16[512,896]{1,0:T(8,128)(2,1)} %copy-done.2, ...), custom_call_target="tpu_custom_call", output_to_operand_aliasing={{0}: (9, {}), {1}: (10, {})} | custom-call | tf_op jit(solution)/shard_map/weight_grads/pallas_call | solution.py:1175
  379.0 2.9 collective-permute-done.46.rest_2_
  382.8 1.5 collective-permute-start.53
  384.4 4.1 hidden.1
  389.4 3.3 output.1
  393.6 2.8 collective-permute-done.51
  396.4 1.3 collective-permute-start.52
  (281 shorter events, 59.5 us)
Async XLA Ops:
  7.2 91.6 %all-reduce.5.cloned.1.call-start = ((), (), s32[]{:S(2)}) async-start(), calls=%async_computation | async-start | bytes 1572864 | tf_op jit(solution)/shard_map/psum | solution.py:1352
  10.8 16.9 %collective-permute-start = (bf16[400,768]{1,0:T(8,128)(2,1)S(1)}, bf16[400,768]{1,0:T(8,128)(2,1)S(1)}, u32[]{:S(2)}, u32[]{:S(2)}) collective-permute-start(bf16[400,768]{1,0:T(8,128)(2,1)S(1)} %pad_maximum_fusion.4), channel_id=1, source_target_pairs={{0,16},{16,0},{1,17},{17,1},{2,18},{18,2},{3,19},{19,3},{4,20},{20... | collective-permute-start | bytes 1843208 | tf_op jit(solution)/shard_map/ppermute | solution.py:1242
  27.8 5.6 %collective-permute-start.1 = (bf16[400,768]{1,0:T(8,128)(2,1)S(1)}, bf16[400,768]{1,0:T(8,128)(2,1)S(1)}, u32[]{:S(2)}, u32[]{:S(2)}) collective-permute-start(bf16[400,768]{1,0:T(8,128)(2,1)S(1)} %collective-permute-done.sent_ref), channel_id=1, source_target_pairs={{0,4},{4,0},{8,12},{12,8},{1,5},{5,1},{9,13},{13,9},{2,6},{6,2},{1... | collective-permute-start | bytes 1843208 | tf_op jit(solution)/shard_map/ppermute | solution.py:1245
  29.1 9.7 %collective-permute-start.2 = (bf16[192,768]{1,0:T(8,128)(2,1)}, bf16[192,768]{1,0:T(8,128)(2,1)}, u32[]{:S(2)}, u32[]{:S(2)}) collective-permute-start(bf16[192,768]{1,0:T(8,128)(2,1)} %constant_dynamic-slice_fusion), channel_id=1, source_target_pairs={{0,16},{16,0},{1,17},{17,1},{2,18},{18,2},{3,19},{19,3},{4,20},{20... | collective-permute-start | bytes 884744 | tf_op jit(solution)/shard_map/ppermute | solution.py:1242
  31.5 41.5 %copy-start = (bf16[256,1664]{1,0:T(8,128)(2,1)}, bf16[256,1664]{1,0:T(8,128)(2,1)S(1)}, u32[]{:S(2)}) copy-start(bf16[256,1664]{1,0:T(8,128)(2,1)S(1)} %pad_maximum_fusion.2.near_out_ref.out_grad_ref) | copy-start | bytes 2555908
  38.8 28.9 %collective-permute-start.9 = (bf16[2,2304,128]{2,1,0:T(8,128)(2,1)S(1)}, bf16[2,2304,128]{2,1,0:T(8,128)(2,1)}, u32[]{:S(2)}, u32[]{:S(2)}) collective-permute-start(bf16[2,2304,128]{2,1,0:T(8,128)(2,1)S(1)} %copy-done.18), channel_id=1, source_target_pairs={{0,16},{16,0},{1,17},{17,1},{2,18},{18,2},{3,19},{19,3},{4,20},{20... | collective-permute-start | bytes 3538952 | tf_op jit(solution)/shard_map/ppermute | solution.py:1242
  40.5 7.5 %collective-permute-start.6 = (bf16[192,768]{1,0:T(8,128)(2,1)}, bf16[192,768]{1,0:T(8,128)(2,1)}, u32[]{:S(2)}, u32[]{:S(2)}) collective-permute-start(bf16[192,768]{1,0:T(8,128)(2,1)} %collective-permute-done.2.out_sent_ref), channel_id=1, source_target_pairs={{0,4},{4,0},{8,12},{12,8},{1,5},{5,1},{9,13},{13,9},{2,6},{6,2},{1... | collective-permute-start | bytes 884744 | tf_op jit(solution)/shard_map/ppermute | solution.py:1245
  40.5 6.1 %collective-permute-start.4 = (bf16[256,256]{1,0:T(8,128)(2,1)}, bf16[256,256]{1,0:T(8,128)(2,1)S(1)}, u32[]{:S(2)}, u32[]{:S(2)}) collective-permute-start(bf16[256,256]{1,0:T(8,128)(2,1)} %get-tuple-element.153.kv0), channel_id=1, source_target_pairs={{0,8},{4,12},{8,0},{12,4},{1,9},{5,13},{9,1},{13,5},{2,10},{6,14},... | collective-permute-start | bytes 393224 | tf_op jit(solution)/shard_map/ppermute | solution.py:1248
  42.0 4.9 %collective-permute-start.3 = (bf16[256,256]{1,0:T(8,128)(2,1)}, bf16[256,256]{1,0:T(8,128)(2,1)S(1)}, u32[]{:S(2)}, u32[]{:S(2)}) collective-permute-start(bf16[256,256]{1,0:T(8,128)(2,1)} %get-tuple-element.153.kv0), channel_id=1, source_target_pairs={{0,4},{4,0},{8,12},{12,8},{1,5},{5,1},{9,13},{13,9},{2,6},{6,2},{1... | collective-permute-start | bytes 393224 | tf_op jit(solution)/shard_map/ppermute | solution.py:1245
  46.6 1.3 collective-permute-start.5
  46.7 40.4 %collective-permute-start.7 = (bf16[256,1664]{1,0:T(8,128)(2,1)S(1)}, bf16[256,1664]{1,0:T(8,128)(2,1)S(1)}, u32[]{:S(2)}, u32[]{:S(2)}) collective-permute-start(bf16[256,1664]{1,0:T(8,128)(2,1)S(1)} %pad_maximum_fusion.2.near_out_ref.out_grad_ref), channel_id=1, source_target_pairs={{0,16},{16,0},{1,17},{17,1},{2,18},{18,2},{3,19},{19,3},{4,20},{20... | collective-permute-start | bytes 2555912 | tf_op jit(solution)/shard_map/ppermute | solution.py:1242
  54.5 141.4 %all-gather.9.cloned.1.call-start = ((), (), s32[]{:S(2)}) async-start(), calls=%async_computation.1 | async-start | bytes 3932160 | tf_op jit(solution)/shard_map/all_gather | solution.py:1424
  67.7 61.0 %collective-permute-start.10 = (bf16[2,2304,128]{2,1,0:T(8,128)(2,1)}, bf16[2,2304,128]{2,1,0:T(8,128)(2,1)}, u32[]{:S(2)}, u32[]{:S(2)}) collective-permute-start(bf16[2,2304,128]{2,1,0:T(8,128)(2,1)} %collective-permute-done.9.rest_0_), channel_id=1, source_target_pairs={{0,8},{4,12},{8,0},{12,4},{1,9},{5,13},{9,1},{13,5},{2,10},{6,14},... | collective-permute-start | bytes 3538952 | tf_op jit(solution)/shard_map/ppermute | solution.py:1248
  69.5 59.8 %collective-permute-start.16 = (bf16[2,2304,128]{2,1,0:T(8,128)(2,1)}, bf16[2,2304,128]{2,1,0:T(8,128)(2,1)}, u32[]{:S(2)}, u32[]{:S(2)}) collective-permute-start(bf16[2,2304,128]{2,1,0:T(8,128)(2,1)} %split_weights.7), channel_id=1, source_target_pairs={{0,16},{16,0},{1,17},{17,1},{2,18},{18,2},{3,19},{19,3},{4,20},{20... | collective-permute-start | bytes 3538952 | tf_op jit(solution)/shard_map/ppermute | solution.py:1242
  98.9 98.0 %copy-start.2 = (bf16[512,896]{1,0:T(8,128)(2,1)}, bf16[512,896]{1,0:T(8,128)(2,1)S(1)}, u32[]{:S(2)}) copy-start(bf16[512,896]{1,0:T(8,128)(2,1)S(1)} %pad_maximum_fusion.1.grads0) | copy-start | bytes 2752516
  98.9 29.8 %collective-permute-start.11 = (bf16[512,896]{1,0:T(8,128)(2,1)S(1)}, bf16[512,896]{1,0:T(8,128)(2,1)S(1)}, u32[]{:S(2)}, u32[]{:S(2)}) collective-permute-start(bf16[512,896]{1,0:T(8,128)(2,1)S(1)} %pad_maximum_fusion.1.grads0), channel_id=1, source_target_pairs={{0,8},{4,12},{8,0},{12,4},{1,9},{5,13},{9,1},{13,5},{2,10},{6,14},... | collective-permute-start | bytes 2752520 | tf_op jit(solution)/shard_map/ppermute | solution.py:1248
  100.5 28.2 %collective-permute-start.12 = (bf16[512,896]{1,0:T(8,128)(2,1)S(1)}, bf16[512,896]{1,0:T(8,128)(2,1)}, u32[]{:S(2)}, u32[]{:S(2)}) collective-permute-start(bf16[512,896]{1,0:T(8,128)(2,1)S(1)} %pad_maximum_fusion.1.grads0), channel_id=1, source_target_pairs={{0,4},{4,0},{8,12},{12,8},{1,5},{5,1},{9,13},{13,9},{2,6},{6,2},{1... | collective-permute-start | bytes 2752520 | tf_op jit(solution)/shard_map/ppermute | solution.py:1245
  104.7 23.9 %collective-permute-start.8 = (bf16[256,1664]{1,0:T(8,128)(2,1)}, bf16[256,1664]{1,0:T(8,128)(2,1)S(1)}, u32[]{:S(2)}, u32[]{:S(2)}) collective-permute-start(bf16[256,1664]{1,0:T(8,128)(2,1)} %get-tuple-element.167.near_ref), channel_id=1, source_target_pairs={{0,16},{16,0},{1,17},{17,1},{2,18},{18,2},{3,19},{19,3},{4,20},{20... | collective-permute-start | bytes 2555912 | tf_op jit(solution)/shard_map/ppermute | solution.py:1242
  128.7 5.3 %collective-permute-start.13 = (bf16[2,2304,128]{2,1,0:T(8,128)(2,1)}, bf16[2,2304,128]{2,1,0:T(8,128)(2,1)}, u32[]{:S(2)}, u32[]{:S(2)}) collective-permute-start(bf16[2,2304,128]{2,1,0:T(8,128)(2,1)} %collective-permute-done.9.rest_0_), channel_id=1, source_target_pairs={{0,4},{4,0},{8,12},{12,8},{1,5},{5,1},{9,13},{13,9},{2,6},{6,2},{1... | collective-permute-start | bytes 3538952 | tf_op jit(solution)/shard_map/ppermute | solution.py:1245
  128.7 68.3 %copy-start.7 = (bf16[512,896]{1,0:T(8,128)(2,1)}, bf16[512,896]{1,0:T(8,128)(2,1)S(1)}, u32[]{:S(2)}) copy-start(bf16[512,896]{1,0:T(8,128)(2,1)S(1)} %collective-permute-done.11.grads2) | copy-start | bytes 2752516
  128.7 5.3 %collective-permute-start.14 = (bf16[2,2304,128]{2,1,0:T(8,128)(2,1)}, bf16[2,2304,128]{2,1,0:T(8,128)(2,1)}, u32[]{:S(2)}, u32[]{:S(2)}) collective-permute-start(bf16[2,2304,128]{2,1,0:T(8,128)(2,1)} %collective-permute-done.10.rest_2_), channel_id=1, source_target_pairs={{0,4},{4,0},{8,12},{12,8},{1,5},{5,1},{9,13},{13,9},{2,6},{6,2},{1... | collective-permute-start | bytes 3538952 | tf_op jit(solution)/shard_map/ppermute | solution.py:1245
  129.3 28.3 %collective-permute-start.17 = (bf16[2,2304,128]{2,1,0:T(8,128)(2,1)}, bf16[2,2304,128]{2,1,0:T(8,128)(2,1)}, u32[]{:S(2)}, u32[]{:S(2)}) collective-permute-start(bf16[2,2304,128]{2,1,0:T(8,128)(2,1)} %collective-permute-done.16.rest_0_), channel_id=1, source_target_pairs={{0,8},{4,12},{8,0},{12,4},{1,9},{5,13},{9,1},{13,5},{2,10},{6,14},... | collective-permute-start | bytes 3538952 | tf_op jit(solution)/shard_map/ppermute | solution.py:1248
  130.8 18.9 %collective-permute-start.15 = (bf16[1,2304,128]{2,1,0:T(8,128)(2,1)}, bf16[1,2304,128]{2,1,0:T(8,128)(2,1)S(1)}, u32[]{:S(2)}, u32[]{:S(2)}) collective-permute-start(bf16[1,2304,128]{2,1,0:T(8,128)(2,1)} %split_weights.6), channel_id=1, source_target_pairs={{0,16},{16,0},{1,17},{17,1},{2,18},{18,2},{3,19},{19,3},{4,20},{20... | collective-permute-start | bytes 1769480 | tf_op jit(solution)/shard_map/ppermute | solution.py:1242
  157.6 93.7 %all-gather.11.cloned.1.call-start = ((), (), s32[]{:S(2)}) async-start(), calls=%async_computation.2 | async-start | bytes 7077888 | tf_op jit(solution)/shard_map/all_gather | solution.py:1412
  157.8 4.0 collective-permute-start.19
  157.9 4.9 %collective-permute-start.20 = (bf16[2,2304,128]{2,1,0:T(8,128)(2,1)}, bf16[2,2304,128]{2,1,0:T(8,128)(2,1)}, u32[]{:S(2)}, u32[]{:S(2)}) collective-permute-start(bf16[2,2304,128]{2,1,0:T(8,128)(2,1)} %collective-permute-done.17.rest_2_), channel_id=1, source_target_pairs={{0,4},{4,0},{8,12},{12,8},{1,5},{5,1},{9,13},{13,9},{2,6},{6,2},{1... | collective-permute-start | bytes 3538952 | tf_op jit(solution)/shard_map/ppermute | solution.py:1245
  158.4 21.7 %collective-permute-start.21 = (bf16[1,2304,128]{2,1,0:T(8,128)(2,1)}, bf16[1,2304,128]{2,1,0:T(8,128)(2,1)}, u32[]{:S(2)}, u32[]{:S(2)}) collective-permute-start(bf16[1,2304,128]{2,1,0:T(8,128)(2,1)} %copy-done.30), channel_id=1, source_target_pairs={{0,8},{4,12},{8,0},{12,4},{1,9},{5,13},{9,1},{13,5},{2,10},{6,14},... | collective-permute-start | bytes 1769480 | tf_op jit(solution)/shard_map/ppermute | solution.py:1248
  159.9 20.2 %collective-permute-start.18 = (bf16[1,2304,128]{2,1,0:T(8,128)(2,1)}, bf16[1,2304,128]{2,1,0:T(8,128)(2,1)}, u32[]{:S(2)}, u32[]{:S(2)}) collective-permute-start(bf16[1,2304,128]{2,1,0:T(8,128)(2,1)} %copy-done.30), channel_id=1, source_target_pairs={{0,4},{4,0},{8,12},{12,8},{1,5},{5,1},{9,13},{13,9},{2,6},{6,2},{1... | collective-permute-start | bytes 1769480 | tf_op jit(solution)/shard_map/ppermute | solution.py:1245
  180.1 2.3 collective-permute-start.22
  195.9 126.9 %all-gather.13.cloned.1.call-start = ((), (), s32[]{:S(2)}) async-start(), calls=%async_computation.3 | async-start | bytes 7077888 | tf_op jit(solution)/shard_map/all_gather | solution.py:1412
  195.9 2.5 collective-permute-start.24
  196.1 30.0 %collective-permute-start.23 = (bf16[256,1664]{1,0:T(8,128)(2,1)}, bf16[256,1664]{1,0:T(8,128)(2,1)}, u32[]{:S(2)}, u32[]{:S(2)}) collective-permute-start(bf16[256,1664]{1,0:T(8,128)(2,1)} %get-tuple-element.192), channel_id=1, source_target_pairs={{0,16},{16,0},{1,17},{17,1},{2,18},{18,2},{3,19},{19,3},{4,20},{20... | collective-permute-start | bytes 2555912 | tf_op jit(solution)/shard_map/ppermute | solution.py:1242
  229.0 10.3 %collective-permute-start.27 = (bf16[64,1664]{1,0:T(8,128)(2,1)}, bf16[64,1664]{1,0:T(8,128)(2,1)S(1)}, u32[]{:S(2)}, u32[]{:S(2)}) collective-permute-start(bf16[64,1664]{1,0:T(8,128)(2,1)} %get-tuple-element.200), channel_id=1, source_target_pairs={{3,0},{0,1},{1,2},{2,3},{7,4},{4,5},{5,6},{6,7},{11,8},{8,9},{9,10... | collective-permute-start | bytes 638984 | tf_op jit(solution)/shard_map/ppermute | solution.py:1251
  230.3 16.8 %collective-permute-start.26 = (bf16[64,1664]{1,0:T(8,128)(2,1)}, bf16[64,1664]{1,0:T(8,128)(2,1)S(1)}, u32[]{:S(2)}, u32[]{:S(2)}) collective-permute-start(bf16[64,1664]{1,0:T(8,128)(2,1)} %get-tuple-element.199), channel_id=1, source_target_pairs={{2,0},{3,1},{0,2},{1,3},{6,4},{7,5},{4,6},{5,7},{10,8},{11,9},{8,1... | collective-permute-start | bytes 638984 | tf_op jit(solution)/shard_map/ppermute | solution.py:1251
  233.2 13.9 %collective-permute-start.25 = (bf16[64,1664]{1,0:T(8,128)(2,1)}, bf16[64,1664]{1,0:T(8,128)(2,1)S(1)}, u32[]{:S(2)}, u32[]{:S(2)}) collective-permute-start(bf16[64,1664]{1,0:T(8,128)(2,1)} %get-tuple-element.198), channel_id=1, source_target_pairs={{1,0},{2,1},{3,2},{0,3},{5,4},{6,5},{7,6},{4,7},{9,8},{10,9},{11,1... | collective-permute-start | bytes 638984 | tf_op jit(solution)/shard_map/ppermute | solution.py:1251
  251.4 114.3 %all-gather.15.cloned.1.call-start = ((), (), s32[]{:S(2)}) async-start(), calls=%async_computation.4 | async-start | bytes 3538944 | tf_op jit(solution)/shard_map/all_gather | solution.py:1412
  251.4 28.7 %collective-permute-start.31 = (bf16[256,1536]{1,0:T(8,128)(2,1)S(1)}, bf16[256,1536]{1,0:T(8,128)(2,1)S(1)}, u32[]{:S(2)}, u32[]{:S(2)}) collective-permute-start(bf16[256,1536]{1,0:T(8,128)(2,1)S(1)} %copy-done.51), channel_id=1, source_target_pairs={{0,16},{16,0},{1,17},{17,1},{2,18},{18,2},{3,19},{19,3},{4,20},{20... | collective-permute-start | bytes 2359304 | tf_op jit(solution)/shard_map/ppermute | solution.py:1242
  253.0 27.1 %collective-permute-start.28 = (bf16[64,1664]{1,0:T(8,128)(2,1)S(1)}, bf16[64,1664]{1,0:T(8,128)(2,1)S(1)}, u32[]{:S(2)}, u32[]{:S(2)}) collective-permute-start(bf16[64,1664]{1,0:T(8,128)(2,1)S(1)} %add_convert_fusion.2.rest_0_), channel_id=1, source_target_pairs={{1,0},{2,1},{3,2},{0,3},{5,4},{6,5},{7,6},{4,7},{9,8},{10,9},{11,1... | collective-permute-start | bytes 638984 | tf_op jit(solution)/shard_map/ppermute | solution.py:1251
  256.3 23.8 %collective-permute-start.29 = (bf16[64,1664]{1,0:T(8,128)(2,1)S(1)}, bf16[64,1664]{1,0:T(8,128)(2,1)S(1)}, u32[]{:S(2)}, u32[]{:S(2)}) collective-permute-start(bf16[64,1664]{1,0:T(8,128)(2,1)S(1)} %add_convert_fusion.2.rest_0_), channel_id=1, source_target_pairs={{2,0},{3,1},{0,2},{1,3},{6,4},{7,5},{4,6},{5,7},{10,8},{11,9},{8,1... | collective-permute-start | bytes 638984 | tf_op jit(solution)/shard_map/ppermute | solution.py:1251
  256.3 23.8 %collective-permute-start.30 = (bf16[64,1664]{1,0:T(8,128)(2,1)S(1)}, bf16[64,1664]{1,0:T(8,128)(2,1)S(1)}, u32[]{:S(2)}, u32[]{:S(2)}) collective-permute-start(bf16[64,1664]{1,0:T(8,128)(2,1)S(1)} %add_convert_fusion.2.rest_0_), channel_id=1, source_target_pairs={{3,0},{0,1},{1,2},{2,3},{7,4},{4,5},{5,6},{6,7},{11,8},{8,9},{9,10... | collective-permute-start | bytes 638984 | tf_op jit(solution)/shard_map/ppermute | solution.py:1251
  283.8 16.1 %collective-permute-start.34 = (bf16[64,1536]{1,0:T(8,128)(2,1)}, bf16[64,1536]{1,0:T(8,128)(2,1)S(1)}, u32[]{:S(2)}, u32[]{:S(2)}) collective-permute-start(bf16[64,1536]{1,0:T(8,128)(2,1)} %get-tuple-element.220), channel_id=1, source_target_pairs={{3,0},{0,1},{1,2},{2,3},{7,4},{4,5},{5,6},{6,7},{11,8},{8,9},{9,10... | collective-permute-start | bytes 589832 | tf_op jit(solution)/shard_map/ppermute | solution.py:1251
  286.1 14.0 %collective-permute-start.33 = (bf16[64,1536]{1,0:T(8,128)(2,1)}, bf16[64,1536]{1,0:T(8,128)(2,1)S(1)}, u32[]{:S(2)}, u32[]{:S(2)}) collective-permute-start(bf16[64,1536]{1,0:T(8,128)(2,1)} %get-tuple-element.219), channel_id=1, source_target_pairs={{2,0},{3,1},{0,2},{1,3},{6,4},{7,5},{4,6},{5,7},{10,8},{11,9},{8,1... | collective-permute-start | bytes 589832 | tf_op jit(solution)/shard_map/ppermute | solution.py:1251
  287.0 13.0 %collective-permute-start.32 = (bf16[64,1536]{1,0:T(8,128)(2,1)}, bf16[64,1536]{1,0:T(8,128)(2,1)S(1)}, u32[]{:S(2)}, u32[]{:S(2)}) collective-permute-start(bf16[64,1536]{1,0:T(8,128)(2,1)} %get-tuple-element.218), channel_id=1, source_target_pairs={{1,0},{2,1},{3,2},{0,3},{5,4},{6,5},{7,6},{4,7},{9,8},{10,9},{11,1... | collective-permute-start | bytes 589832 | tf_op jit(solution)/shard_map/ppermute | solution.py:1251
  300.2 1.8 collective-permute-start.35
  303.9 4.8 %collective-permute-start.37 = (bf16[2,224,768]{2,1,0:T(8,128)(2,1)}, bf16[2,224,768]{2,1,0:T(8,128)(2,1)}, u32[]{:S(2)}, u32[]{:S(2)}) collective-permute-start(bf16[2,224,768]{2,1,0:T(8,128)(2,1)} %dynamic-slice_convert_fusion.1), channel_id=1, source_target_pairs={{0,4},{4,0},{8,12},{12,8},{1,5},{5,1},{9,13},{13,9},{2,6},{6,2},{1... | collective-permute-start | bytes 2064392 | tf_op jit(solution)/shard_map/ppermute | solution.py:1245
  304.3 17.9 %collective-permute-start.39 = (bf16[64,1536]{1,0:T(8,128)(2,1)S(1)}, bf16[64,1536]{1,0:T(8,128)(2,1)S(1)}, u32[]{:S(2)}, u32[]{:S(2)}) collective-permute-start(bf16[64,1536]{1,0:T(8,128)(2,1)S(1)} %add_convert_fusion.4), channel_id=1, source_target_pairs={{0,1},{1,0},{2,3},{3,2},{4,5},{5,4},{6,7},{7,6},{8,9},{9,8},{10,11... | collective-permute-start | bytes 589832 | tf_op jit(solution)/shard_map/ppermute | solution.py:1529
  311.1 11.7 %collective-permute-start.38 = (bf16[224,768]{1,0:T(8,128)(2,1)S(1)}, bf16[224,768]{1,0:T(8,128)(2,1)S(1)}, u32[]{:S(2)}, u32[]{:S(2)}) collective-permute-start(bf16[224,768]{1,0:T(8,128)(2,1)S(1)} %fusion.13), channel_id=1, source_target_pairs={{0,16},{16,0},{1,17},{17,1},{2,18},{18,2},{3,19},{19,3},{4,20},{20... | collective-permute-start | bytes 1032200 | tf_op jit(solution)/shard_map/ppermute | solution.py:1242
  312.4 5.3 %collective-permute-start.36 = (bf16[256,256]{1,0:T(8,128)(2,1)S(1)}, bf16[256,256]{1,0:T(8,128)(2,1)S(1)}, u32[]{:S(2)}, u32[]{:S(2)}) collective-permute-start(bf16[256,256]{1,0:T(8,128)(2,1)S(1)} %fusion.21), channel_id=1, source_target_pairs={{0,8},{4,12},{8,0},{12,4},{1,9},{5,13},{9,1},{13,5},{2,10},{6,14},... | collective-permute-start | bytes 393224 | tf_op jit(solution)/shard_map/ppermute | solution.py:1248
  322.9 32.5 %collective-permute-start.42 = (bf16[64,1536]{1,0:T(8,128)(2,1)}, bf16[64,1536]{1,0:T(8,128)(2,1)}, u32[]{:S(2)}, u32[]{:S(2)}) collective-permute-start(bf16[64,1536]{1,0:T(8,128)(2,1)} %get-tuple-element.243), channel_id=1, source_target_pairs={{3,0},{0,1},{1,2},{2,3},{7,4},{4,5},{5,6},{6,7},{11,8},{8,9},{9,10... | collective-permute-start | bytes 589832 | tf_op jit(solution)/shard_map/ppermute | solution.py:1251
  325.3 30.1 %collective-permute-start.41 = (bf16[64,1536]{1,0:T(8,128)(2,1)}, bf16[64,1536]{1,0:T(8,128)(2,1)}, u32[]{:S(2)}, u32[]{:S(2)}) collective-permute-start(bf16[64,1536]{1,0:T(8,128)(2,1)} %get-tuple-element.242), channel_id=1, source_target_pairs={{2,0},{3,1},{0,2},{1,3},{6,4},{7,5},{4,6},{5,7},{10,8},{11,9},{8,1... | collective-permute-start | bytes 589832 | tf_op jit(solution)/shard_map/ppermute | solution.py:1251
  326.6 28.8 %collective-permute-start.40 = (bf16[64,1536]{1,0:T(8,128)(2,1)}, bf16[64,1536]{1,0:T(8,128)(2,1)}, u32[]{:S(2)}, u32[]{:S(2)}) collective-permute-start(bf16[64,1536]{1,0:T(8,128)(2,1)} %get-tuple-element.241), channel_id=1, source_target_pairs={{1,0},{2,1},{3,2},{0,3},{5,4},{6,5},{7,6},{4,7},{9,8},{10,9},{11,1... | collective-permute-start | bytes 589832 | tf_op jit(solution)/shard_map/ppermute | solution.py:1251
  331.1 25.7 %collective-permute-start.43 = (bf16[2,384,640]{2,1,0:T(8,128)(2,1)}, bf16[2,384,640]{2,1,0:T(8,128)(2,1)}, u32[]{:S(2)}, u32[]{:S(2)}) collective-permute-start(bf16[2,384,640]{2,1,0:T(8,128)(2,1)} %dynamic-slice_convert_fusion), channel_id=1, source_target_pairs={{0,4},{4,0},{8,12},{12,8},{1,5},{5,1},{9,13},{13,9},{2,6},{6,2},{1... | collective-permute-start | bytes 2949128 | tf_op jit(solution)/shard_map/ppermute | solution.py:1245
  332.0 28.3 %collective-permute-start.44 = (bf16[128,1536]{1,0:T(8,128)(2,1)}, bf16[128,1536]{1,0:T(8,128)(2,1)}, u32[]{:S(2)}, u32[]{:S(2)}) collective-permute-start(bf16[128,1536]{1,0:T(8,128)(2,1)} %maximum_select_fusion.3.rest_0_), channel_id=1, source_target_pairs={{0,2},{1,3},{2,0},{3,1},{4,6},{5,7},{6,4},{7,5},{8,10},{9,11},{10,... | collective-permute-start | bytes 1179656 | tf_op jit(solution)/shard_map/ppermute | solution.py:1591
  360.3 21.6 %collective-permute-start.49 = (bf16[384,640]{1,0:T(8,128)(2,1)S(1)}, bf16[384,640]{1,0:T(8,128)(2,1)S(1)}, u32[]{:S(2)}, u32[]{:S(2)}) collective-permute-start(bf16[384,640]{1,0:T(8,128)(2,1)S(1)} %fusion.9), channel_id=1, source_target_pairs={{0,16},{16,0},{1,17},{17,1},{2,18},{18,2},{3,19},{19,3},{4,20},{20... | collective-permute-start | bytes 1474568 | tf_op jit(solution)/shard_map/ppermute | solution.py:1242
  362.0 20.0 %collective-permute-start.48 = (bf16[224,768]{1,0:T(8,128)(2,1)}, bf16[224,768]{1,0:T(8,128)(2,1)S(1)}, u32[]{:S(2)}, u32[]{:S(2)}) collective-permute-start(bf16[224,768]{1,0:T(8,128)(2,1)} %convert_element_type.160), channel_id=1, source_target_pairs={{0,8},{4,12},{8,0},{12,4},{1,9},{5,13},{9,1},{13,5},{2,10},{6,14},... | collective-permute-start | bytes 1032200 | tf_op jit(solution)/shard_map/ppermute | solution.py:1248
  362.5 16.6 %collective-permute-start.45 = (bf16[64,1536]{1,0:T(8,128)(2,1)S(1)}, bf16[64,1536]{1,0:T(8,128)(2,1)}, u32[]{:S(2)}, u32[]{:S(2)}) collective-permute-start(bf16[64,1536]{1,0:T(8,128)(2,1)S(1)} %add_convert_fusion.3.rest_0_), channel_id=1, source_target_pairs={{1,0},{2,1},{3,2},{0,3},{5,4},{6,5},{7,6},{4,7},{9,8},{10,9},{11,1... | collective-permute-start | bytes 589832 | tf_op jit(solution)/shard_map/ppermute | solution.py:1251
  364.0 17.9 %collective-permute-start.46 = (bf16[64,1536]{1,0:T(8,128)(2,1)S(1)}, bf16[64,1536]{1,0:T(8,128)(2,1)}, u32[]{:S(2)}, u32[]{:S(2)}) collective-permute-start(bf16[64,1536]{1,0:T(8,128)(2,1)S(1)} %add_convert_fusion.3.rest_0_), channel_id=1, source_target_pairs={{2,0},{3,1},{0,2},{1,3},{6,4},{7,5},{4,6},{5,7},{10,8},{11,9},{8,1... | collective-permute-start | bytes 589832 | tf_op jit(solution)/shard_map/ppermute | solution.py:1251
  364.7 17.2 %collective-permute-start.47 = (bf16[64,1536]{1,0:T(8,128)(2,1)S(1)}, bf16[64,1536]{1,0:T(8,128)(2,1)}, u32[]{:S(2)}, u32[]{:S(2)}) collective-permute-start(bf16[64,1536]{1,0:T(8,128)(2,1)S(1)} %add_convert_fusion.3.rest_0_), channel_id=1, source_target_pairs={{3,0},{0,1},{1,2},{2,3},{7,4},{4,5},{5,6},{6,7},{11,8},{8,9},{9,10... | collective-permute-start | bytes 589832 | tf_op jit(solution)/shard_map/ppermute | solution.py:1251
  382.8 14.9 %collective-permute-start.53 = (bf16[384,640]{1,0:T(8,128)(2,1)}, bf16[384,640]{1,0:T(8,128)(2,1)}, u32[]{:S(2)}, u32[]{:S(2)}) collective-permute-start(bf16[384,640]{1,0:T(8,128)(2,1)} %fusion.5), channel_id=1, source_target_pairs={{0,8},{4,12},{8,0},{12,4},{1,9},{5,13},{9,1},{13,5},{2,10},{6,14},... | collective-permute-start | bytes 1474568 | tf_op jit(solution)/shard_map/ppermute | solution.py:1248
  389.3 3.4 collective-permute-start.50
  392.7 3.7 collective-permute-start.51
  393.3 7.3 %collective-permute-start.55 = (bf16[224,768]{1,0:T(8,128)(2,1)S(1)}, bf16[224,768]{1,0:T(8,128)(2,1)S(1)}, u32[]{:S(2)}, u32[]{:S(2)}) collective-permute-start(bf16[224,768]{1,0:T(8,128)(2,1)S(1)} %add_convert_fusion.1), channel_id=1, source_target_pairs={{0,4},{4,0},{8,12},{12,8},{1,5},{5,1},{9,13},{13,9},{2,6},{6,2},{1... | collective-permute-start | bytes 1032200 | tf_op jit(solution)/shard_map/ppermute | solution.py:1245
  396.4 3.6 collective-permute-start.52
  398.9 4.3 %collective-permute-start.54 = (bf16[384,640]{1,0:T(8,128)(2,1)S(1)}, bf16[384,640]{1,0:T(8,128)(2,1)S(1)}, u32[]{:S(2)}, u32[]{:S(2)}) collective-permute-start(bf16[384,640]{1,0:T(8,128)(2,1)S(1)} %add_convert_fusion), channel_id=1, source_target_pairs={{0,4},{4,0},{8,12},{12,8},{1,5},{5,1},{9,13},{13,9},{2,6},{6,2},{1... | collective-permute-start | bytes 1474568 | tf_op jit(solution)/shard_map/ppermute | solution.py:1245
  (49 other events, 337.8 us)
Sparse Core Ops, SparseCore 0:
  54.6 44.1 all-reduce.4
  157.7 34.5 all-gather.8
  196.0 55.2 all-gather.10
  253.1 52.8 all-gather.12
  323.0 31.4 all-gather.14

commit v8 on v7

--- a/solution.py
+++ b/solution.py
@@ -1235,7 +1235,7 @@
     kv_heads = k_cols // HEAD_DIM
     group = q_cols // k_cols
     top = routes.shape[-1]
-    chunks = ((0, 2), (2, 2), (4, 1))
+    chunks = ((0, 1), (1, 2), (3, 2))
     tie = lax.optimization_barrier
 
     def across(value):

time: 419 us -> 457 us (1.091)
  waiting for transfers between devices: 127 us -> 159 us
  starting transfers between devices: 59 us -> 63.9 us
    ppermute x9, waiting for transfers between devices: 20.9 us -> 66.8 us  [along(): return lax.ppermute(value, 'ctx', [(i, i ^ 2) for i in range(4)])]
    psum x1, waiting for transfers between devices: 11.7 us -> 1.1 us  [fast_body(): attended = lax.psum(attn_part, 'tp')]
    ppermute x12, waiting for transfers between devices: 66 us -> 58.3 us  [across(): return lax.ppermute(value, 'fsdp', [(0, 1), (1, 0)])]
  transfers between devices with their start and end apart: 61 -> 61, of which waited for: 24 -> 25; matrix products, arithmetic and copies ran while one was open for 8% -> 8% of each run, Pallas kernels for 40% -> 36%
where the time goes in v8:
time: 457 us; the launch traced here: 450 us
  Pallas kernels  164 us (36%)
  waiting for transfers between devices  159 us (35%)
  starting transfers between devices  63.9 us (14%)
  local copies, waits for them, and re-layouts  25 us (5%)
  other arithmetic  17.4 us (4%)
  between operations  15.2 us (3%)
  matrix products  6.67 us (1%)
    ppermute x9, waiting for transfers between devices, along(): return lax.ppermute(value, 'ctx', [(i, i ^ 2) for i in range(4)])  66.8 us
    ppermute x12, waiting for transfers between devices, across(): return lax.ppermute(value, 'fsdp', [(0, 1), (1, 0)])  58.3 us
    pallas_call x3, Pallas kernels, run_weight_grads(): pl.pallas_call(functools.partial(weight_grad_kernel, first=first, steps=s...  56.2 us
    pallas_call x3, Pallas kernels, run_experts(): pl.pallas_call(functools.partial(expert_kernel, first=first, last=last, e...  45.2 us
    pallas_call x9, Pallas kernels, single(): pl.pallas_call(kernel, out_shape=tuple((jax.ShapeDtypeStruct(shape, kind)...  41.6 us
    ppermute x15, starting transfers between devices, from_tp(): lax.ppermute(value, 'tp', [((i + step) % tp_size, i) for i in range(tp_si...  26.5 us
    pallas_call x4, Pallas kernels, split_weights(): pl.pallas_call(split_plain_kernel if down is None else split_kernel, out_...  20.5 us
    ppermute x12, starting transfers between devices, across(): return lax.ppermute(value, 'fsdp', [(0, 1), (1, 0)])  18.9 us
  transfers between devices with their start and end apart: 61, of which 25 were waited for; matrix products, arithmetic and copies ran while one was open for 8% of the time, Pallas kernels for 36%

profile of v8, /device:TPU:0, one launch (start us, length us, event | category | flops | bytes accessed | tf_op | source)
XLA Modules:
  0.0 450.3 jit_solution(5501806199587382739)
XLA Ops:
  10.8 3.0 collective-permute-start
  13.9 2.1 split_weights.4
  18.1 9.6 %collective-permute-done.sent_ref = bf16[400,768]{1,0:T(8,128)(2,1)S(1)} collective-permute-done((bf16[400,768]{1,0:T(8,128)(2,1)S(1)}, bf16[400,768]{1,0:T(8,128)(2,1)S(1)}, u32[]{:S(2)}, u32[]{:S(2)}) %collective-permute-start) | collective-permute-done | bytes 614432 | tf_op jit(solution)/shard_map/ppermute | solution.py:1242
  29.1 1.7 collective-permute-start.2
  34.2 4.4 before.1
  39.0 1.6 collective-permute-start.4
  40.8 4.1 collective-permute-done.4.kv2
  44.9 1.7 collective-permute-start.7
  47.5 5.8 %attend.1 = (bf16[256,384]{1,0:T(8,128)(2,1)}, f32[4,384,512]{2,1,0:T(8,128)}, bf16[384,768]{1,0:T(8,128)(2,1)}, bf16[256,1536]{1,0:T(8,128)(2,1)}) custom-call(s32[3]{0:T(128)} %pad_add_fusion.place_ref, s32[2,4]{1,0:T(2,128)} %bitcast.206, bf16[256,384]{1,0:T(8,128)(2,1)} %get-tuple-element.149.query_ref, bf16[256,256]{1,0:T(8,128)(2,1)} %get-tuple-element.153.kv0, ...), custom_call_target="tpu_custom_call" | custom-call | tf_op jit(solution)/shard_map/attend/pallas_call | solution.py:431
  53.8 1.4 collective-permute-start.9
  55.2 2.2 split_weights.7
  57.4 21.7 %collective-permute-done.9.rest_0_ = bf16[1,2304,128]{2,1,0:T(8,128)(2,1)} collective-permute-done((bf16[1,2304,128]{2,1,0:T(8,128)(2,1)S(1)}, bf16[1,2304,128]{2,1,0:T(8,128)(2,1)}, u32[]{:S(2)}, u32[]{:S(2)}) %collective-permute-start.9) | collective-permute-done | bytes 589856 | tf_op jit(solution)/shard_map/ppermute | solution.py:1242
  79.0 1.7 collective-permute-start.16
  80.8 2.2 split_weights.6
  83.0 14.0 %split_weights.5 = bf16[20,1536,128]{2,1,0:T(8,128)(2,1)} custom-call(s32[1]{0:T(128)} %bitcast.11.base_ref, bf16[40,1536,128]{2,1,0:T(8,128)(2,1)} %bitcast.153), custom_call_target="tpu_custom_call" | custom-call | tf_op jit(solution)/shard_map/split_weights/pallas_call | solution.py:498
  98.3 1.5 collective-permute-start.11
  99.8 4.4 after.1
  104.2 1.5 collective-permute-start.8
  109.9 1.5 collective-permute-start.17
  111.4 23.0 %collective-permute-done.10.rest_2_ = bf16[1,2304,128]{2,1,0:T(8,128)(2,1)} collective-permute-done((bf16[1,2304,128]{2,1,0:T(8,128)(2,1)}, bf16[1,2304,128]{2,1,0:T(8,128)(2,1)}, u32[]{:S(2)}, u32[]{:S(2)}) %collective-permute-start.10) | collective-permute-done | bytes 589856 | tf_op jit(solution)/shard_map/ppermute | solution.py:1248
  134.4 1.5 collective-permute-start.15
  139.8 10.2 %experts.3 = (bf16[4,1,128,384]{3,2,1,0:T(8,128)(2,1)}, bf16[512,1536]{1,0:T(8,128)(2,1)}, bf16[512,1664]{1,0:T(8,128)(2,1)}) custom-call(s32[3]{0:T(128)} %pad_add_fusion.place_ref, bf16[256,1664]{1,0:T(8,128)(2,1)} %get-tuple-element.167.near_ref, bf16[256,1664]{1,0:T(8,128)(2,1)} %copy-done.4, bf16[256,1664]{1,0:T(8,128)(2,1)} %copy-done, ...), custom_call_target="tpu_custom_call" | custom-call | tf_op jit(solution)/shard_map/experts/pallas_call | solution.py:885
  149.9 8.5 %collective-permute-done.17.rest_2_ = bf16[2,2304,128]{2,1,0:T(8,128)(2,1)} collective-permute-done((bf16[2,2304,128]{2,1,0:T(8,128)(2,1)}, bf16[2,2304,128]{2,1,0:T(8,128)(2,1)}, u32[]{:S(2)}, u32[]{:S(2)}) %collective-permute-start.17) | collective-permute-done | bytes 1179680 | tf_op jit(solution)/shard_map/ppermute | solution.py:1248
  158.4 1.9 collective-permute-done.15.rest_0_
  161.1 1.5 collective-permute-start.21
  163.8 1.7 collective-permute-done.20.rest_3_
  165.5 16.5 %experts.4 = (bf16[4,2,128,384]{3,2,1,0:T(8,128)(2,1)}, bf16[512,1536]{1,0:T(8,128)(2,1)}, bf16[512,1664]{1,0:T(8,128)(2,1)}) custom-call(s32[3]{0:T(128)} %pad_add_fusion.place_ref, bf16[256,1664]{1,0:T(8,128)(2,1)} %get-tuple-element.167.near_ref, bf16[256,1664]{1,0:T(8,128)(2,1)} %copy-done.4, bf16[256,1664]{1,0:T(8,128)(2,1)} %copy-done, ...), custom_call_target="tpu_custom_call" | custom-call | tf_op jit(solution)/shard_map/experts/pallas_call | solution.py:885
  181.9 24.2 %collective-permute-done.21.rest_2_ = bf16[2,2304,128]{2,1,0:T(8,128)(2,1)S(1)} collective-permute-done((bf16[2,2304,128]{2,1,0:T(8,128)(2,1)}, bf16[2,2304,128]{2,1,0:T(8,128)(2,1)S(1)}, u32[]{:S(2)}, u32[]{:S(2)}) %collective-permute-start.21) | collective-permute-done | bytes 1179680 | tf_op jit(solution)/shard_map/ppermute | solution.py:1248
  206.1 2.8 collective-permute-done.22.rest_3_
  210.0 18.6 %experts.5 = (bf16[4,2,128,384]{3,2,1,0:T(8,128)(2,1)}, f32[256,1536]{1,0:T(8,128)}, f32[256,1664]{1,0:T(8,128)}, bf16[256,1536]{1,0:T(8,128)(2,1)}, bf16[256,1664]{1,0:T(8,128)(2,1)}) custom-call(s32[3]{0:T(128)} %pad_add_fusion.place_ref, bf16[256,1664]{1,0:T(8,128)(2,1)} %get-tuple-element.167.near_ref, bf16[256,1664]{1,0:T(8,128)(2,1)} %copy-done.4, ...), custom_call_target="tpu_custom_call" | custom-call | tf_op jit(solution)/shard_map/experts/pallas_call | solution.py:885
  229.1 1.5 collective-permute-start.23
  233.4 22.3 %collective-permute-done.23.got_ref = bf16[256,1664]{1,0:T(8,128)(2,1)} collective-permute-done((bf16[256,1664]{1,0:T(8,128)(2,1)}, bf16[256,1664]{1,0:T(8,128)(2,1)}, u32[]{:S(2)}, u32[]{:S(2)}) %collective-permute-start.23) | collective-permute-done | bytes 852000 | tf_op jit(solution)/shard_map/ppermute | solution.py:1242
  255.7 2.9 join.2
  258.6 1.5 collective-permute-start.26
  260.2 2.3 collective-permute-start.25
  262.4 6.4 %collective-permute-done.27 = bf16[64,1664]{1,0:T(8,128)(2,1)S(1)} collective-permute-done((bf16[64,1664]{1,0:T(8,128)(2,1)}, bf16[64,1664]{1,0:T(8,128)(2,1)S(1)}, u32[]{:S(2)}, u32[]{:S(2)}) %collective-permute-start.27) | collective-permute-done | bytes 213024 | tf_op jit(solution)/shard_map/ppermute | solution.py:1251
  268.9 6.9 %collective-permute-done.26 = bf16[64,1664]{1,0:T(8,128)(2,1)S(1)} collective-permute-done((bf16[64,1664]{1,0:T(8,128)(2,1)}, bf16[64,1664]{1,0:T(8,128)(2,1)S(1)}, u32[]{:S(2)}, u32[]{:S(2)}) %collective-permute-start.26) | collective-permute-done | bytes 213024 | tf_op jit(solution)/shard_map/ppermute | solution.py:1251
  276.9 2.3 collective-permute-start.31
  279.3 4.3 collective-permute-start.28
  285.5 13.6 %weight_grads.3 = (f32[2,4,5,1536,128]{4,3,2,1,0:T(8,128)}, f32[2,4,5,128,768]{4,3,2,1,0:T(8,128)}, f32[8,128]{1,0:T(8,128)}) custom-call(s32[3]{0:T(128)} %pad_add_fusion.place_ref, bf16[4,512,768]{2,1,0:T(8,128)(2,1)} %bitcast.159, bf16[512,896]{1,0:T(8,128)(2,1)} %copy-done.2, bf16[512,896]{1,0:T(8,128)(2,1)} %collective-permute-done.12.grads1, ...), custom_call_target="tpu_custom_call" | custom-call | tf_op jit(solution)/shard_map/weight_grads/pallas_call | solution.py:1175
  299.1 3.4 collective-permute-done.29.rest_2_
  304.1 2.7 join.3
  306.8 6.0 %collective-permute-start.34 = (bf16[64,1536]{1,0:T(8,128)(2,1)}, bf16[64,1536]{1,0:T(8,128)(2,1)S(1)}, u32[]{:S(2)}, u32[]{:S(2)}) collective-permute-start(bf16[64,1536]{1,0:T(8,128)(2,1)} %get-tuple-element.220), channel_id=1, source_target_pairs={{3,0},{0,1},{1,2},{2,3},{7,4},{4,5},{5,6},{6,7},{11,8},{8,9},{9,10... | collective-permute-start | bytes 589832 | tf_op jit(solution)/shard_map/ppermute | solution.py:1251
  312.8 2.4 collective-permute-start.32
  315.3 10.2 %back.1 = (f32[256,1536]{1,0:T(8,128)}, bf16[256,1536]{1,0:T(8,128)(2,1)}, bf16[256,128]{1,0:T(8,128)(2,1)}, f32[8,1536]{1,0:T(8,128)}, bf16[256,384]{1,0:T(8,12...) custom-call(s32[3]{0:T(128)} %pad_add_fusion.place_ref, f32[256,1536]{1,0:T(8,128)} %get-tuple-element.160.mixed_ref, ...), custom_call_target="tpu_custom_call" | custom-call | tf_op jit(solution)/shard_map/back/pallas_call | solution.py:431
  330.7 2.6 collective-permute-start.39
  338.0 4.0 collective-permute-done.36.along_ref
  342.6 3.8 last.1
  347.2 2.4 collective-permute-start.42
  349.5 2.4 collective-permute-start.41
  352.7 2.0 fusion.34
  357.6 21.3 %weight_grads.4 = (f32[2,4,5,1536,128]{4,3,2,1,0:T(8,128)}, f32[2,4,5,128,768]{4,3,2,1,0:T(8,128)}, f32[8,128]{1,0:T(8,128)}) custom-call(s32[3]{0:T(128)} %pad_add_fusion.place_ref, bf16[4,512,768]{2,1,0:T(8,128)(2,1)} %bitcast.160, bf16[512,896]{1,0:T(8,128)(2,1)} %copy-done.2, ...), custom_call_target="tpu_custom_call", output_to_operand_aliasing={{0}: (9, {}), {1}: (10, {})} | custom-call | tf_op jit(solution)/shard_map/weight_grads/pallas_call | solution.py:1175
  380.3 1.4 add_convert_fusion.3.rest_0_
  381.7 1.4 convert_add_fusion
  383.2 2.0 collective-permute-done.44.rest_1_
  385.3 1.3 collective-permute-start.49
  388.7 2.0 collective-permute-start.45
  391.9 6.4 %all-gather.15.cloned.1.call-done = bf16[32,2,128,384]{3,2,1,0:T(8,128)(2,1)} async-done(((bf16[4,2,128,384]{3,2,1,0:T(8,128)(2,1)}), bf16[32,2,128,384]{3,2,1,0:T(8,128)(2,1)}) %all-gather.15.cloned.1.call-update) | async-done | bytes 6291472 | tf_op jit(solution)/shard_map/all_gather | solution.py:1412
  398.2 21.3 %weight_grads.5 = (f32[2,4,5,1536,128]{4,3,2,1,0:T(8,128)}, f32[2,4,5,128,768]{4,3,2,1,0:T(8,128)}, f32[8,128]{1,0:T(8,128)}) custom-call(s32[3]{0:T(128)} %pad_add_fusion.place_ref, bf16[4,512,768]{2,1,0:T(8,128)(2,1)} %bitcast.161, bf16[512,896]{1,0:T(8,128)(2,1)} %copy-done.2, ...), custom_call_target="tpu_custom_call", output_to_operand_aliasing={{0}: (9, {}), {1}: (10, {})} | custom-call | tf_op jit(solution)/shard_map/weight_grads/pallas_call | solution.py:1175
  420.5 1.8 collective-permute-start.53
  422.3 4.1 hidden.1
  427.3 3.3 output.1
  431.4 3.0 collective-permute-done.51
  435.9 2.1 collective-permute-done.52
  (283 shorter events, 61.1 us)
Async XLA Ops:
  7.2 91.0 %all-reduce.5.cloned.1.call-start = ((), (), s32[]{:S(2)}) async-start(), calls=%async_computation | async-start | bytes 1572864 | tf_op jit(solution)/shard_map/psum | solution.py:1352
  10.8 16.9 %collective-permute-start = (bf16[400,768]{1,0:T(8,128)(2,1)S(1)}, bf16[400,768]{1,0:T(8,128)(2,1)S(1)}, u32[]{:S(2)}, u32[]{:S(2)}) collective-permute-start(bf16[400,768]{1,0:T(8,128)(2,1)S(1)} %pad_maximum_fusion.4), channel_id=1, source_target_pairs={{0,16},{16,0},{1,17},{17,1},{2,18},{18,2},{3,19},{19,3},{4,20},{20... | collective-permute-start | bytes 1843208 | tf_op jit(solution)/shard_map/ppermute | solution.py:1242
  27.8 5.7 %collective-permute-start.1 = (bf16[400,768]{1,0:T(8,128)(2,1)S(1)}, bf16[400,768]{1,0:T(8,128)(2,1)S(1)}, u32[]{:S(2)}, u32[]{:S(2)}) collective-permute-start(bf16[400,768]{1,0:T(8,128)(2,1)S(1)} %collective-permute-done.sent_ref), channel_id=1, source_target_pairs={{0,4},{4,0},{8,12},{12,8},{1,5},{5,1},{9,13},{13,9},{2,6},{6,2},{1... | collective-permute-start | bytes 1843208 | tf_op jit(solution)/shard_map/ppermute | solution.py:1245
  29.1 9.7 %collective-permute-start.2 = (bf16[192,768]{1,0:T(8,128)(2,1)}, bf16[192,768]{1,0:T(8,128)(2,1)}, u32[]{:S(2)}, u32[]{:S(2)}) collective-permute-start(bf16[192,768]{1,0:T(8,128)(2,1)} %constant_dynamic-slice_fusion), channel_id=1, source_target_pairs={{0,16},{16,0},{1,17},{17,1},{2,18},{18,2},{3,19},{19,3},{4,20},{20... | collective-permute-start | bytes 884744 | tf_op jit(solution)/shard_map/ppermute | solution.py:1242
  31.5 51.4 %copy-start = (bf16[256,1664]{1,0:T(8,128)(2,1)}, bf16[256,1664]{1,0:T(8,128)(2,1)S(1)}, u32[]{:S(2)}) copy-start(bf16[256,1664]{1,0:T(8,128)(2,1)S(1)} %pad_maximum_fusion.2.near_out_ref.out_grad_ref) | copy-start | bytes 2555908
  38.8 7.9 %collective-permute-start.6 = (bf16[192,768]{1,0:T(8,128)(2,1)}, bf16[192,768]{1,0:T(8,128)(2,1)S(1)}, u32[]{:S(2)}, u32[]{:S(2)}) collective-permute-start(bf16[192,768]{1,0:T(8,128)(2,1)} %collective-permute-done.2.out_sent_ref), channel_id=1, source_target_pairs={{0,4},{4,0},{8,12},{12,8},{1,5},{5,1},{9,13},{13,9},{2,6},{6,2},{1... | collective-permute-start | bytes 884744 | tf_op jit(solution)/shard_map/ppermute | solution.py:1245
  39.0 6.0 %collective-permute-start.4 = (bf16[256,256]{1,0:T(8,128)(2,1)}, bf16[256,256]{1,0:T(8,128)(2,1)S(1)}, u32[]{:S(2)}, u32[]{:S(2)}) collective-permute-start(bf16[256,256]{1,0:T(8,128)(2,1)} %get-tuple-element.153.kv0), channel_id=1, source_target_pairs={{0,8},{4,12},{8,0},{12,4},{1,9},{5,13},{9,1},{13,5},{2,10},{6,14},... | collective-permute-start | bytes 393224 | tf_op jit(solution)/shard_map/ppermute | solution.py:1248
  40.6 6.1 %collective-permute-start.3 = (bf16[256,256]{1,0:T(8,128)(2,1)}, bf16[256,256]{1,0:T(8,128)(2,1)S(1)}, u32[]{:S(2)}, u32[]{:S(2)}) collective-permute-start(bf16[256,256]{1,0:T(8,128)(2,1)} %get-tuple-element.153.kv0), channel_id=1, source_target_pairs={{0,4},{4,0},{8,12},{12,8},{1,5},{5,1},{9,13},{13,9},{2,6},{6,2},{1... | collective-permute-start | bytes 393224 | tf_op jit(solution)/shard_map/ppermute | solution.py:1245
  44.9 1.7 collective-permute-start.5
  44.9 52.1 %collective-permute-start.7 = (bf16[256,1664]{1,0:T(8,128)(2,1)S(1)}, bf16[256,1664]{1,0:T(8,128)(2,1)S(1)}, u32[]{:S(2)}, u32[]{:S(2)}) collective-permute-start(bf16[256,1664]{1,0:T(8,128)(2,1)S(1)} %pad_maximum_fusion.2.near_out_ref.out_grad_ref), channel_id=1, source_target_pairs={{0,16},{16,0},{1,17},{17,1},{2,18},{18,2},{3,19},{19,3},{4,20},{20... | collective-permute-start | bytes 2555912 | tf_op jit(solution)/shard_map/ppermute | solution.py:1242
  53.3 175.3 %all-gather.9.cloned.1.call-start = ((), (), s32[]{:S(2)}) async-start(), calls=%async_computation.1 | async-start | bytes 3932160 | tf_op jit(solution)/shard_map/all_gather | solution.py:1424
  53.8 25.2 %collective-permute-start.9 = (bf16[1,2304,128]{2,1,0:T(8,128)(2,1)S(1)}, bf16[1,2304,128]{2,1,0:T(8,128)(2,1)}, u32[]{:S(2)}, u32[]{:S(2)}) collective-permute-start(bf16[1,2304,128]{2,1,0:T(8,128)(2,1)S(1)} %copy-done.32), channel_id=1, source_target_pairs={{0,16},{16,0},{1,17},{17,1},{2,18},{18,2},{3,19},{19,3},{4,20},{20... | collective-permute-start | bytes 1769480 | tf_op jit(solution)/shard_map/ppermute | solution.py:1242
  79.0 30.8 %collective-permute-start.16 = (bf16[2,2304,128]{2,1,0:T(8,128)(2,1)}, bf16[2,2304,128]{2,1,0:T(8,128)(2,1)}, u32[]{:S(2)}, u32[]{:S(2)}) collective-permute-start(bf16[2,2304,128]{2,1,0:T(8,128)(2,1)} %split_weights.7), channel_id=1, source_target_pairs={{0,16},{16,0},{1,17},{17,1},{2,18},{18,2},{3,19},{19,3},{4,20},{20... | collective-permute-start | bytes 3538952 | tf_op jit(solution)/shard_map/ppermute | solution.py:1242
  98.3 132.5 %copy-start.2 = (bf16[512,896]{1,0:T(8,128)(2,1)}, bf16[512,896]{1,0:T(8,128)(2,1)S(1)}, u32[]{:S(2)}) copy-start(bf16[512,896]{1,0:T(8,128)(2,1)S(1)} %pad_maximum_fusion.1.grads0) | copy-start | bytes 2752516
  98.3 36.1 %collective-permute-start.11 = (bf16[512,896]{1,0:T(8,128)(2,1)S(1)}, bf16[512,896]{1,0:T(8,128)(2,1)S(1)}, u32[]{:S(2)}, u32[]{:S(2)}) collective-permute-start(bf16[512,896]{1,0:T(8,128)(2,1)S(1)} %pad_maximum_fusion.1.grads0), channel_id=1, source_target_pairs={{0,8},{4,12},{8,0},{12,4},{1,9},{5,13},{9,1},{13,5},{2,10},{6,14},... | collective-permute-start | bytes 2752520 | tf_op jit(solution)/shard_map/ppermute | solution.py:1248
  99.8 34.5 %collective-permute-start.12 = (bf16[512,896]{1,0:T(8,128)(2,1)S(1)}, bf16[512,896]{1,0:T(8,128)(2,1)}, u32[]{:S(2)}, u32[]{:S(2)}) collective-permute-start(bf16[512,896]{1,0:T(8,128)(2,1)S(1)} %pad_maximum_fusion.1.grads0), channel_id=1, source_target_pairs={{0,4},{4,0},{8,12},{12,8},{1,5},{5,1},{9,13},{13,9},{2,6},{6,2},{1... | collective-permute-start | bytes 2752520 | tf_op jit(solution)/shard_map/ppermute | solution.py:1245
  104.2 30.2 %collective-permute-start.8 = (bf16[256,1664]{1,0:T(8,128)(2,1)}, bf16[256,1664]{1,0:T(8,128)(2,1)S(1)}, u32[]{:S(2)}, u32[]{:S(2)}) collective-permute-start(bf16[256,1664]{1,0:T(8,128)(2,1)} %get-tuple-element.167.near_ref), channel_id=1, source_target_pairs={{0,16},{16,0},{1,17},{17,1},{2,18},{18,2},{3,19},{19,3},{4,20},{20... | collective-permute-start | bytes 2555912 | tf_op jit(solution)/shard_map/ppermute | solution.py:1242
  105.7 28.7 %collective-permute-start.10 = (bf16[1,2304,128]{2,1,0:T(8,128)(2,1)}, bf16[1,2304,128]{2,1,0:T(8,128)(2,1)}, u32[]{:S(2)}, u32[]{:S(2)}) collective-permute-start(bf16[1,2304,128]{2,1,0:T(8,128)(2,1)} %collective-permute-done.9.rest_0_), channel_id=1, source_target_pairs={{0,8},{4,12},{8,0},{12,4},{1,9},{5,13},{9,1},{13,5},{2,10},{6,14},... | collective-permute-start | bytes 1769480 | tf_op jit(solution)/shard_map/ppermute | solution.py:1248
  109.9 48.5 %collective-permute-start.17 = (bf16[2,2304,128]{2,1,0:T(8,128)(2,1)}, bf16[2,2304,128]{2,1,0:T(8,128)(2,1)}, u32[]{:S(2)}, u32[]{:S(2)}) collective-permute-start(bf16[2,2304,128]{2,1,0:T(8,128)(2,1)} %collective-permute-done.16.rest_0_), channel_id=1, source_target_pairs={{0,8},{4,12},{8,0},{12,4},{1,9},{5,13},{9,1},{13,5},{2,10},{6,14},... | collective-permute-start | bytes 3538952 | tf_op jit(solution)/shard_map/ppermute | solution.py:1248
  134.4 96.5 %copy-start.7 = (bf16[512,896]{1,0:T(8,128)(2,1)}, bf16[512,896]{1,0:T(8,128)(2,1)S(1)}, u32[]{:S(2)}) copy-start(bf16[512,896]{1,0:T(8,128)(2,1)S(1)} %collective-permute-done.11.grads2) | copy-start | bytes 2752516
  134.4 25.9 %collective-permute-start.15 = (bf16[2,2304,128]{2,1,0:T(8,128)(2,1)}, bf16[2,2304,128]{2,1,0:T(8,128)(2,1)}, u32[]{:S(2)}, u32[]{:S(2)}) collective-permute-start(bf16[2,2304,128]{2,1,0:T(8,128)(2,1)} %split_weights.6), channel_id=1, source_target_pairs={{0,16},{16,0},{1,17},{17,1},{2,18},{18,2},{3,19},{19,3},{4,20},{20... | collective-permute-start | bytes 3538952 | tf_op jit(solution)/shard_map/ppermute | solution.py:1242
  135.9 3.0 collective-permute-start.13
  135.9 3.2 collective-permute-start.14
  160.3 116.6 %all-gather.11.cloned.1.call-start = ((), (), s32[]{:S(2)}) async-start(), calls=%async_computation.2 | async-start | bytes 3538944 | tf_op jit(solution)/shard_map/all_gather | solution.py:1412
  160.5 3.3 collective-permute-start.19
  160.6 4.9 %collective-permute-start.20 = (bf16[2,2304,128]{2,1,0:T(8,128)(2,1)}, bf16[2,2304,128]{2,1,0:T(8,128)(2,1)}, u32[]{:S(2)}, u32[]{:S(2)}) collective-permute-start(bf16[2,2304,128]{2,1,0:T(8,128)(2,1)} %collective-permute-done.17.rest_2_), channel_id=1, source_target_pairs={{0,4},{4,0},{8,12},{12,8},{1,5},{5,1},{9,13},{13,9},{2,6},{6,2},{1... | collective-permute-start | bytes 3538952 | tf_op jit(solution)/shard_map/ppermute | solution.py:1245
  161.1 45.0 %collective-permute-start.21 = (bf16[2,2304,128]{2,1,0:T(8,128)(2,1)}, bf16[2,2304,128]{2,1,0:T(8,128)(2,1)S(1)}, u32[]{:S(2)}, u32[]{:S(2)}) collective-permute-start(bf16[2,2304,128]{2,1,0:T(8,128)(2,1)} %collective-permute-done.15.rest_0_), channel_id=1, source_target_pairs={{0,8},{4,12},{8,0},{12,4},{1,9},{5,13},{9,1},{13,5},{2,10},{6,14},... | collective-permute-start | bytes 3538952 | tf_op jit(solution)/shard_map/ppermute | solution.py:1248
  162.6 43.6 %collective-permute-start.18 = (bf16[2,2304,128]{2,1,0:T(8,128)(2,1)}, bf16[2,2304,128]{2,1,0:T(8,128)(2,1)}, u32[]{:S(2)}, u32[]{:S(2)}) collective-permute-start(bf16[2,2304,128]{2,1,0:T(8,128)(2,1)} %collective-permute-done.15.rest_0_), channel_id=1, source_target_pairs={{0,4},{4,0},{8,12},{12,8},{1,5},{5,1},{9,13},{13,9},{2,6},{6,2},{1... | collective-permute-start | bytes 3538952 | tf_op jit(solution)/shard_map/ppermute | solution.py:1245
  206.1 2.8 collective-permute-start.22
  228.6 118.5 %all-gather.13.cloned.1.call-start = ((), (), s32[]{:S(2)}) async-start(), calls=%async_computation.3 | async-start | bytes 7077888 | tf_op jit(solution)/shard_map/all_gather | solution.py:1412
  228.9 3.0 collective-permute-start.24
  229.1 26.6 %collective-permute-start.23 = (bf16[256,1664]{1,0:T(8,128)(2,1)}, bf16[256,1664]{1,0:T(8,128)(2,1)}, u32[]{:S(2)}, u32[]{:S(2)}) collective-permute-start(bf16[256,1664]{1,0:T(8,128)(2,1)} %get-tuple-element.192), channel_id=1, source_target_pairs={{0,16},{16,0},{1,17},{17,1},{2,18},{18,2},{3,19},{19,3},{4,20},{20... | collective-permute-start | bytes 2555912 | tf_op jit(solution)/shard_map/ppermute | solution.py:1242
  258.6 10.3 %collective-permute-start.27 = (bf16[64,1664]{1,0:T(8,128)(2,1)}, bf16[64,1664]{1,0:T(8,128)(2,1)S(1)}, u32[]{:S(2)}, u32[]{:S(2)}) collective-permute-start(bf16[64,1664]{1,0:T(8,128)(2,1)} %get-tuple-element.200), channel_id=1, source_target_pairs={{3,0},{0,1},{1,2},{2,3},{7,4},{4,5},{5,6},{6,7},{11,8},{8,9},{9,10... | collective-permute-start | bytes 638984 | tf_op jit(solution)/shard_map/ppermute | solution.py:1251
  258.6 17.1 %collective-permute-start.26 = (bf16[64,1664]{1,0:T(8,128)(2,1)}, bf16[64,1664]{1,0:T(8,128)(2,1)S(1)}, u32[]{:S(2)}, u32[]{:S(2)}) collective-permute-start(bf16[64,1664]{1,0:T(8,128)(2,1)} %get-tuple-element.199), channel_id=1, source_target_pairs={{2,0},{3,1},{0,2},{1,3},{6,4},{7,5},{4,6},{5,7},{10,8},{11,9},{8,1... | collective-permute-start | bytes 638984 | tf_op jit(solution)/shard_map/ppermute | solution.py:1251
  260.2 15.6 %collective-permute-start.25 = (bf16[64,1664]{1,0:T(8,128)(2,1)}, bf16[64,1664]{1,0:T(8,128)(2,1)S(1)}, u32[]{:S(2)}, u32[]{:S(2)}) collective-permute-start(bf16[64,1664]{1,0:T(8,128)(2,1)} %get-tuple-element.198), channel_id=1, source_target_pairs={{1,0},{2,1},{3,2},{0,3},{5,4},{6,5},{7,6},{4,7},{9,8},{10,9},{11,1... | collective-permute-start | bytes 638984 | tf_op jit(solution)/shard_map/ppermute | solution.py:1251
  276.9 121.3 %all-gather.15.cloned.1.call-start = ((), (), s32[]{:S(2)}) async-start(), calls=%async_computation.4 | async-start | bytes 7077888 | tf_op jit(solution)/shard_map/all_gather | solution.py:1412
  276.9 26.3 %collective-permute-start.31 = (bf16[256,1536]{1,0:T(8,128)(2,1)S(1)}, bf16[256,1536]{1,0:T(8,128)(2,1)S(1)}, u32[]{:S(2)}, u32[]{:S(2)}) collective-permute-start(bf16[256,1536]{1,0:T(8,128)(2,1)S(1)} %copy-done.52), channel_id=1, source_target_pairs={{0,16},{16,0},{1,17},{17,1},{2,18},{18,2},{3,19},{19,3},{4,20},{20... | collective-permute-start | bytes 2359304 | tf_op jit(solution)/shard_map/ppermute | solution.py:1242
  279.3 19.8 %collective-permute-start.28 = (bf16[64,1664]{1,0:T(8,128)(2,1)S(1)}, bf16[64,1664]{1,0:T(8,128)(2,1)S(1)}, u32[]{:S(2)}, u32[]{:S(2)}) collective-permute-start(bf16[64,1664]{1,0:T(8,128)(2,1)S(1)} %add_convert_fusion.2.rest_0_), channel_id=1, source_target_pairs={{1,0},{2,1},{3,2},{0,3},{5,4},{6,5},{7,6},{4,7},{9,8},{10,9},{11,1... | collective-permute-start | bytes 638984 | tf_op jit(solution)/shard_map/ppermute | solution.py:1251
  283.6 19.0 %collective-permute-start.29 = (bf16[64,1664]{1,0:T(8,128)(2,1)S(1)}, bf16[64,1664]{1,0:T(8,128)(2,1)S(1)}, u32[]{:S(2)}, u32[]{:S(2)}) collective-permute-start(bf16[64,1664]{1,0:T(8,128)(2,1)S(1)} %add_convert_fusion.2.rest_0_), channel_id=1, source_target_pairs={{2,0},{3,1},{0,2},{1,3},{6,4},{7,5},{4,6},{5,7},{10,8},{11,9},{8,1... | collective-permute-start | bytes 638984 | tf_op jit(solution)/shard_map/ppermute | solution.py:1251
  284.9 17.7 %collective-permute-start.30 = (bf16[64,1664]{1,0:T(8,128)(2,1)S(1)}, bf16[64,1664]{1,0:T(8,128)(2,1)S(1)}, u32[]{:S(2)}, u32[]{:S(2)}) collective-permute-start(bf16[64,1664]{1,0:T(8,128)(2,1)S(1)} %add_convert_fusion.2.rest_0_), channel_id=1, source_target_pairs={{3,0},{0,1},{1,2},{2,3},{7,4},{4,5},{5,6},{6,7},{11,8},{8,9},{9,10... | collective-permute-start | bytes 638984 | tf_op jit(solution)/shard_map/ppermute | solution.py:1251
  306.8 19.8 %collective-permute-start.34 = (bf16[64,1536]{1,0:T(8,128)(2,1)}, bf16[64,1536]{1,0:T(8,128)(2,1)S(1)}, u32[]{:S(2)}, u32[]{:S(2)}) collective-permute-start(bf16[64,1536]{1,0:T(8,128)(2,1)} %get-tuple-element.220), channel_id=1, source_target_pairs={{3,0},{0,1},{1,2},{2,3},{7,4},{4,5},{5,6},{6,7},{11,8},{8,9},{9,10... | collective-permute-start | bytes 589832 | tf_op jit(solution)/shard_map/ppermute | solution.py:1251
  312.8 13.8 %collective-permute-start.33 = (bf16[64,1536]{1,0:T(8,128)(2,1)}, bf16[64,1536]{1,0:T(8,128)(2,1)S(1)}, u32[]{:S(2)}, u32[]{:S(2)}) collective-permute-start(bf16[64,1536]{1,0:T(8,128)(2,1)} %get-tuple-element.219), channel_id=1, source_target_pairs={{2,0},{3,1},{0,2},{1,3},{6,4},{7,5},{4,6},{5,7},{10,8},{11,9},{8,1... | collective-permute-start | bytes 589832 | tf_op jit(solution)/shard_map/ppermute | solution.py:1251
  312.8 13.8 %collective-permute-start.32 = (bf16[64,1536]{1,0:T(8,128)(2,1)}, bf16[64,1536]{1,0:T(8,128)(2,1)S(1)}, u32[]{:S(2)}, u32[]{:S(2)}) collective-permute-start(bf16[64,1536]{1,0:T(8,128)(2,1)} %get-tuple-element.218), channel_id=1, source_target_pairs={{1,0},{2,1},{3,2},{0,3},{5,4},{6,5},{7,6},{4,7},{9,8},{10,9},{11,1... | collective-permute-start | bytes 589832 | tf_op jit(solution)/shard_map/ppermute | solution.py:1251
  326.8 1.8 collective-permute-start.35
  330.5 2.8 collective-permute-start.37
  330.7 15.8 %collective-permute-start.39 = (bf16[64,1536]{1,0:T(8,128)(2,1)S(1)}, bf16[64,1536]{1,0:T(8,128)(2,1)S(1)}, u32[]{:S(2)}, u32[]{:S(2)}) collective-permute-start(bf16[64,1536]{1,0:T(8,128)(2,1)S(1)} %add_convert_fusion.4), channel_id=1, source_target_pairs={{0,1},{1,0},{2,3},{3,2},{4,5},{5,4},{6,7},{7,6},{8,9},{9,8},{10,11... | collective-permute-start | bytes 589832 | tf_op jit(solution)/shard_map/ppermute | solution.py:1529
  335.6 11.5 %collective-permute-start.38 = (bf16[224,768]{1,0:T(8,128)(2,1)S(1)}, bf16[224,768]{1,0:T(8,128)(2,1)S(1)}, u32[]{:S(2)}, u32[]{:S(2)}) collective-permute-start(bf16[224,768]{1,0:T(8,128)(2,1)S(1)} %fusion.13), channel_id=1, source_target_pairs={{0,16},{16,0},{1,17},{17,1},{2,18},{18,2},{3,19},{19,3},{4,20},{20... | collective-permute-start | bytes 1032200 | tf_op jit(solution)/shard_map/ppermute | solution.py:1242
  336.7 5.3 %collective-permute-start.36 = (bf16[256,256]{1,0:T(8,128)(2,1)S(1)}, bf16[256,256]{1,0:T(8,128)(2,1)S(1)}, u32[]{:S(2)}, u32[]{:S(2)}) collective-permute-start(bf16[256,256]{1,0:T(8,128)(2,1)S(1)} %fusion.21), channel_id=1, source_target_pairs={{0,8},{4,12},{8,0},{12,4},{1,9},{5,13},{9,1},{13,5},{2,10},{6,14},... | collective-permute-start | bytes 393224 | tf_op jit(solution)/shard_map/ppermute | solution.py:1248
  347.2 33.1 %collective-permute-start.42 = (bf16[64,1536]{1,0:T(8,128)(2,1)}, bf16[64,1536]{1,0:T(8,128)(2,1)}, u32[]{:S(2)}, u32[]{:S(2)}) collective-permute-start(bf16[64,1536]{1,0:T(8,128)(2,1)} %get-tuple-element.243), channel_id=1, source_target_pairs={{3,0},{0,1},{1,2},{2,3},{7,4},{4,5},{5,6},{6,7},{11,8},{8,9},{9,10... | collective-permute-start | bytes 589832 | tf_op jit(solution)/shard_map/ppermute | solution.py:1251
  349.5 30.7 %collective-permute-start.41 = (bf16[64,1536]{1,0:T(8,128)(2,1)}, bf16[64,1536]{1,0:T(8,128)(2,1)}, u32[]{:S(2)}, u32[]{:S(2)}) collective-permute-start(bf16[64,1536]{1,0:T(8,128)(2,1)} %get-tuple-element.242), channel_id=1, source_target_pairs={{2,0},{3,1},{0,2},{1,3},{6,4},{7,5},{4,6},{5,7},{10,8},{11,9},{8,1... | collective-permute-start | bytes 589832 | tf_op jit(solution)/shard_map/ppermute | solution.py:1251
  351.9 28.3 %collective-permute-start.40 = (bf16[64,1536]{1,0:T(8,128)(2,1)}, bf16[64,1536]{1,0:T(8,128)(2,1)}, u32[]{:S(2)}, u32[]{:S(2)}) collective-permute-start(bf16[64,1536]{1,0:T(8,128)(2,1)} %get-tuple-element.241), channel_id=1, source_target_pairs={{1,0},{2,1},{3,2},{0,3},{5,4},{6,5},{7,6},{4,7},{9,8},{10,9},{11,1... | collective-permute-start | bytes 589832 | tf_op jit(solution)/shard_map/ppermute | solution.py:1251
  355.8 26.0 %collective-permute-start.43 = (bf16[2,384,640]{2,1,0:T(8,128)(2,1)}, bf16[2,384,640]{2,1,0:T(8,128)(2,1)}, u32[]{:S(2)}, u32[]{:S(2)}) collective-permute-start(bf16[2,384,640]{2,1,0:T(8,128)(2,1)} %dynamic-slice_convert_fusion), channel_id=1, source_target_pairs={{0,4},{4,0},{8,12},{12,8},{1,5},{5,1},{9,13},{13,9},{2,6},{6,2},{1... | collective-permute-start | bytes 2949128 | tf_op jit(solution)/shard_map/ppermute | solution.py:1245
  356.6 28.6 %collective-permute-start.44 = (bf16[128,1536]{1,0:T(8,128)(2,1)}, bf16[128,1536]{1,0:T(8,128)(2,1)}, u32[]{:S(2)}, u32[]{:S(2)}) collective-permute-start(bf16[128,1536]{1,0:T(8,128)(2,1)} %maximum_select_fusion.3.rest_0_), channel_id=1, source_target_pairs={{0,2},{1,3},{2,0},{3,1},{4,6},{5,7},{6,4},{7,5},{8,10},{9,11},{10,... | collective-permute-start | bytes 1179656 | tf_op jit(solution)/shard_map/ppermute | solution.py:1591
  385.3 34.3 %collective-permute-start.49 = (bf16[384,640]{1,0:T(8,128)(2,1)S(1)}, bf16[384,640]{1,0:T(8,128)(2,1)S(1)}, u32[]{:S(2)}, u32[]{:S(2)}) collective-permute-start(bf16[384,640]{1,0:T(8,128)(2,1)S(1)} %fusion.9), channel_id=1, source_target_pairs={{0,16},{16,0},{1,17},{17,1},{2,18},{18,2},{3,19},{19,3},{4,20},{20... | collective-permute-start | bytes 1474568 | tf_op jit(solution)/shard_map/ppermute | solution.py:1242
  387.4 32.2 %collective-permute-start.48 = (bf16[224,768]{1,0:T(8,128)(2,1)}, bf16[224,768]{1,0:T(8,128)(2,1)S(1)}, u32[]{:S(2)}, u32[]{:S(2)}) collective-permute-start(bf16[224,768]{1,0:T(8,128)(2,1)} %convert_element_type.160), channel_id=1, source_target_pairs={{0,8},{4,12},{8,0},{12,4},{1,9},{5,13},{9,1},{13,5},{2,10},{6,14},... | collective-permute-start | bytes 1032200 | tf_op jit(solution)/shard_map/ppermute | solution.py:1248
  388.7 30.8 %collective-permute-start.45 = (bf16[64,1536]{1,0:T(8,128)(2,1)S(1)}, bf16[64,1536]{1,0:T(8,128)(2,1)}, u32[]{:S(2)}, u32[]{:S(2)}) collective-permute-start(bf16[64,1536]{1,0:T(8,128)(2,1)S(1)} %add_convert_fusion.3.rest_0_), channel_id=1, source_target_pairs={{1,0},{2,1},{3,2},{0,3},{5,4},{6,5},{7,6},{4,7},{9,8},{10,9},{11,1... | collective-permute-start | bytes 589832 | tf_op jit(solution)/shard_map/ppermute | solution.py:1251
  390.7 28.8 %collective-permute-start.46 = (bf16[64,1536]{1,0:T(8,128)(2,1)S(1)}, bf16[64,1536]{1,0:T(8,128)(2,1)}, u32[]{:S(2)}, u32[]{:S(2)}) collective-permute-start(bf16[64,1536]{1,0:T(8,128)(2,1)S(1)} %add_convert_fusion.3.rest_0_), channel_id=1, source_target_pairs={{2,0},{3,1},{0,2},{1,3},{6,4},{7,5},{4,6},{5,7},{10,8},{11,9},{8,1... | collective-permute-start | bytes 589832 | tf_op jit(solution)/shard_map/ppermute | solution.py:1251
  390.8 28.8 %collective-permute-start.47 = (bf16[64,1536]{1,0:T(8,128)(2,1)S(1)}, bf16[64,1536]{1,0:T(8,128)(2,1)}, u32[]{:S(2)}, u32[]{:S(2)}) collective-permute-start(bf16[64,1536]{1,0:T(8,128)(2,1)S(1)} %add_convert_fusion.3.rest_0_), channel_id=1, source_target_pairs={{3,0},{0,1},{1,2},{2,3},{7,4},{4,5},{5,6},{6,7},{11,8},{8,9},{9,10... | collective-permute-start | bytes 589832 | tf_op jit(solution)/shard_map/ppermute | solution.py:1251
  420.5 14.1 %collective-permute-start.53 = (bf16[384,640]{1,0:T(8,128)(2,1)}, bf16[384,640]{1,0:T(8,128)(2,1)}, u32[]{:S(2)}, u32[]{:S(2)}) collective-permute-start(bf16[384,640]{1,0:T(8,128)(2,1)} %fusion.5), channel_id=1, source_target_pairs={{0,8},{4,12},{8,0},{12,4},{1,9},{5,13},{9,1},{13,5},{2,10},{6,14},... | collective-permute-start | bytes 1474568 | tf_op jit(solution)/shard_map/ppermute | solution.py:1248
  427.2 3.4 collective-permute-start.50
  430.7 3.7 collective-permute-start.51
  431.0 7.6 %collective-permute-start.55 = (bf16[224,768]{1,0:T(8,128)(2,1)S(1)}, bf16[224,768]{1,0:T(8,128)(2,1)S(1)}, u32[]{:S(2)}, u32[]{:S(2)}) collective-permute-start(bf16[224,768]{1,0:T(8,128)(2,1)S(1)} %add_convert_fusion.1), channel_id=1, source_target_pairs={{0,4},{4,0},{8,12},{12,8},{1,5},{5,1},{9,13},{13,9},{2,6},{6,2},{1... | collective-permute-start | bytes 1032200 | tf_op jit(solution)/shard_map/ppermute | solution.py:1245
  434.4 3.6 collective-permute-start.52
  435.8 5.3 %collective-permute-start.54 = (bf16[384,640]{1,0:T(8,128)(2,1)S(1)}, bf16[384,640]{1,0:T(8,128)(2,1)S(1)}, u32[]{:S(2)}, u32[]{:S(2)}) collective-permute-start(bf16[384,640]{1,0:T(8,128)(2,1)S(1)} %add_convert_fusion), channel_id=1, source_target_pairs={{0,4},{4,0},{8,12},{12,8},{1,5},{5,1},{9,13},{13,9},{2,6},{6,2},{1... | collective-permute-start | bytes 1474568 | tf_op jit(solution)/shard_map/ppermute | solution.py:1245
  (50 other events, 331.5 us)
Sparse Core Ops, SparseCore 0:
  53.4 44.7 all-reduce.4
  160.4 44.7 all-gather.8
  228.8 35.9 all-gather.10
  277.0 54.2 all-gather.12
  347.3 50.9 all-gather.14
